TPU v7x, 128 devices: a whole 4x4x4 slice. The times are simulated.
128 devices in a mesh: gx: 8 (over x, core), gy: 16 (over y, z).
Axes of the slice: x: 4, y: 4, z: 4, core: 2. Of those that a mesh axis runs over, the one named last changes fastest.
Arguments:
- estimate: float32 [16, 1024, 2048], P(None, 'gx', 'gy'), may hold values from 0.5 to 2
- measured: bfloat16 [2, 16, 1024, 2048], P(None, None, 'gx', 'gy'), may hold values from 0.25 to 4
- kernels: float32 [2, 4, 2, 17], replicated, may hold values from 0.2 to 2
- depth_band: int32 [16], replicated, may hold values from 0 to 3
- group_shift: int32 [2, 64], replicated, may hold values from 0 to 127, as said below
- group_length: int32 [2, 64], replicated, may hold values from 1 to 3, 128 in all within a row
Outputs:
- updated: float32 [16, 1024, 2048], P(None, 'gx', 'gy')
Inputs may be any that keep to these rules, and one draw needn't show every extreme that they name: `group_shift`: in each row the 64 values are distinct, and 0 and 127 are among them. `group_length`: each row sums to 128, and its largest entry is 3.
All inputs are finite; a program needn't handle non-finite values.
Results may differ from a plain program's by a relative error of at most 0.00035.
Values may be sent and summed in bfloat16 or wider, within the bound.
No kernel may reach another device: no remote copies, remote signals or barrier semaphores. Data moves between devices by JAX's collectives and lax.ppermute only.
A program may use at most 64 MiB of HBM per device.

v0:
```python
import functools

import jax
import jax.numpy as jnp
from jax import lax
from jax.experimental import pallas as pl
from jax.experimental.pallas import tpu as pltpu
from jax.sharding import PartitionSpec as P

HW = 8
CAP = 3
LANES = 256
F32 = jnp.float32
BF16 = jnp.bfloat16

VMEM = pl.BlockSpec(memory_space=pltpu.VMEM)
SMEM = pl.BlockSpec(memory_space=pltpu.SMEM)


def call(kernel, ins, out_shape, scratch=()):
    return pl.pallas_call(
        kernel,
        in_specs=ins,
        out_specs=jax.tree.map(lambda _: VMEM, out_shape),
        out_shape=out_shape,
        scratch_shapes=list(scratch),
        compiler_params=pltpu.CompilerParams(vmem_limit_bytes=48 * 2**20),
    )


def split(x):
    high = x.astype(BF16)
    return high, (x - high.astype(F32)).astype(BF16)


def dot(a, b, dims=((1,), (0,))):
    return lax.dot_general(a, b, (dims, ((), ())), preferred_element_type=F32)


def dot3(a, b, dims=((1,), (0,))):
    return dot(a[0], b[0], dims) + (dot(a[1], b[0], dims) + dot(a[0], b[1], dims))


NT = ((1,), (1,))


def pack_kernel(devices, me_ref, shift_ref, length_ref, measured_ref, out_ref, rows_ref):
    views, depth, tile_rows, tile_cols = measured_ref.shape
    groups = shift_ref.shape[1]
    rows_ref[:, tile_rows:] = jnp.zeros((views, rows_ref.shape[1] - tile_rows) + rows_ref.shape[2:], BF16)
    lane = lax.broadcasted_iota(jnp.int32, (tile_cols, tile_cols), 1)
    sub = lax.broadcasted_iota(jnp.int32, (tile_cols, tile_cols), 0)
    turn = (lane + sub == tile_cols - 1).astype(BF16)
    me = me_ref[0]
    for view in range(views):
        for r0 in range(0, tile_rows, 16):
            x = measured_ref[view, :, r0 : r0 + 16, :]
            if view % 2 == 1:
                x = dot(x.reshape(depth * 16, tile_cols), turn).reshape(depth, 16, tile_cols)
            x = jnp.transpose(x.astype(F32), (1, 0, 2))
            rows_ref[view, r0 : r0 + 16] = x.astype(BF16)

        def group(g, start, view=view):
            base = lax.rem(me + shift_ref[view, g], devices) * (views * CAP) + view * CAP
            for k in range(CAP):
                out_ref[base + k] = rows_ref[view, start + k]
            return start + length_ref[view, g]

        lax.fori_loop(0, groups, group, 0, unroll=4)


def unpack_kernel(devices, me_ref, shift_ref, length_ref, arrived_ref, recip_ref, out_ref, rows_ref):
    views, depth, tile_rows, tile_cols = out_ref.shape
    groups = shift_ref.shape[1]
    me = me_ref[0]
    for view in range(views):

        def group(g, start, view=view):
            source = lax.rem(me - shift_ref[view, g] + devices, devices)
            base = source * (views * CAP) + view * CAP
            for k in range(CAP):
                rows_ref[view, start + k] = arrived_ref[base + k].astype(F32)
            return start + length_ref[view, g]

        lax.fori_loop(0, groups, group, 0, unroll=4)
        for r0 in range(0, tile_rows, 16):
            x = jnp.transpose(rows_ref[view, r0 : r0 + 16], (1, 0, 2))
            out_ref[view, :, r0 : r0 + 16, :] = (x * recip_ref[view, :, r0 : r0 + 16, :]).astype(BF16)


def band(taps, size):
    wide = jnp.broadcast_to(taps, (size, LANES))
    inner = pltpu.roll(wide, LANES - HW, 1, stride=1, stride_axis=0)
    before = pltpu.roll(wide, size + HW, 1, stride=1, stride_axis=0)
    lane = lax.broadcasted_iota(jnp.int32, (size, LANES), 1)
    out = jnp.where(lane < size + HW, inner, jnp.where(lane < size + 2 * HW, before, 0.0))
    return out[:, : size + 2 * HW]


def forward_kernel(band_ref, taps_ref, padded_ref, recip_ref, adjoint_ref, fwd_ref):
    views, depth, tile_rows, tile_cols = recip_ref.shape
    bands = taps_ref.shape[2]
    for view in range(views):
        for b in range(bands):
            for axis in range(2):
                for way, ref in ((0, fwd_ref), (1, adjoint_ref)):
                    high, low = split(band(taps_ref[way, view, b, axis : axis + 1, :], tile_rows))
                    ref[view, b, axis, 0] = high
                    ref[view, b, axis, 1] = low

    def plane(z, carry):
        b = band_ref[z]
        cells = split(padded_ref[z])
        for view in range(views):
            rows = (fwd_ref[view, b, 0, 0], fwd_ref[view, b, 0, 1])
            cols = (fwd_ref[view, b, 1, 0], fwd_ref[view, b, 1, 1])
            blurred = dot3(split(dot3(rows, cells)), cols, NT)
            recip_ref[view, z] = 1.0 / blurred.astype(BF16).astype(F32)
        return carry

    lax.fori_loop(0, depth, plane, 0)


def adjoint_kernel(band_ref, adjoint_ref, ratio_ref, estimate_ref, out_ref):
    views = ratio_ref.shape[0]
    depth = ratio_ref.shape[1]

    def plane(z, carry):
        b = band_ref[z]
        total = None
        for view in range(views):
            cells = ratio_ref[view, z]
            rows = (adjoint_ref[view, b, 0, 0], adjoint_ref[view, b, 0, 1])
            blurred = dot(cells, adjoint_ref[view, b, 1, 0], NT) + dot(cells, adjoint_ref[view, b, 1, 1], NT)
            part = dot3(rows, split(blurred))
            total = part if total is None else total + part
        out_ref[z] = estimate_ref[z] * (total * (1.0 / views))
        return carry

    lax.fori_loop(0, depth, plane, 0)


def padded(cells, sides):
    for axis, dim in sides:
        count = lax.axis_size(axis)
        ends = count - 1
        head = lax.slice_in_dim(cells, 0, HW, axis=dim)
        tail = lax.slice_in_dim(cells, cells.shape[dim] - HW, cells.shape[dim], axis=dim)
        before = lax.ppermute(tail, axis, [(i, i + 1) for i in range(ends)])
        after = lax.ppermute(head, axis, [(i + 1, i) for i in range(ends)])
        cells = jnp.concatenate([cells, after, before], axis=dim)
    return cells


def body(estimate, measured, kernels, depth_band, group_shift, group_length):
    devices = lax.axis_size("gx") * lax.axis_size("gy")
    me = (lax.axis_index("gx") * lax.axis_size("gy") + lax.axis_index("gy")).reshape(1).astype(jnp.int32)
    views, depth, tile_rows, tile_cols = measured.shape
    spare = tile_rows + 8
    outgoing = call(
        functools.partial(pack_kernel, devices),
        [SMEM, SMEM, SMEM, VMEM],
        jax.ShapeDtypeStruct((devices * views * CAP, depth, tile_cols), BF16),
        [pltpu.VMEM((views, spare, depth, tile_cols), BF16)],
    )(me, group_shift, group_length, measured)
    arrived = lax.all_to_all(outgoing, ("gx", "gy"), split_axis=0, concat_axis=0, tiled=True)

    norm = kernels / jnp.sum(kernels, axis=3, keepdims=True)
    tap_rows = jnp.stack([norm, norm[..., ::-1]])
    tap_rows = jnp.pad(tap_rows, ((0, 0),) * 4 + ((0, LANES - kernels.shape[3]),))
    cells = padded(estimate, (("gx", 1), ("gy", 2)))
    matrices = (views, kernels.shape[1], 2, 2, tile_rows, tile_rows + 2 * HW)
    recip, adjoint = call(
        forward_kernel,
        [SMEM, VMEM, VMEM],
        (jax.ShapeDtypeStruct(measured.shape, F32), jax.ShapeDtypeStruct(matrices, BF16)),
        [pltpu.VMEM(matrices, BF16)],
    )(depth_band, tap_rows, cells)

    ratio = call(
        functools.partial(unpack_kernel, devices),
        [SMEM, SMEM, SMEM, VMEM, VMEM],
        jax.ShapeDtypeStruct(measured.shape, BF16),
        [pltpu.VMEM((views, spare, depth, tile_cols), F32)],
    )(me, group_shift, group_length, arrived, recip)
    ratio = padded(ratio, (("gx", 2), ("gy", 3)))
    return call(
        adjoint_kernel,
        [SMEM, VMEM, VMEM, VMEM],
        jax.ShapeDtypeStruct(estimate.shape, F32),
    )(depth_band, adjoint, ratio, estimate)


def solution(mesh):
    return jax.shard_map(
        body,
        mesh=mesh,
        in_specs=(P(None, "gx", "gy"), P(None, None, "gx", "gy"), P(), P(), P(), P()),
        out_specs=P(None, "gx", "gy"),
        check_vma=False,
    )
```

profile of v0, /device:TPU:30, one launch (start us, length us, event | category | flops | bytes accessed | tf_op | source)
XLA Modules:
  0.0 136.6 jit_solution(536416834168262858)
XLA Ops:
  2.6 3.6 %shard_map.65 = bf16[768,16,128]{2,1,0:T(8,128)(2,1)} custom-call(s32[1]{0:T(128)} %bitcast.2.me_ref, s32[2,64]{1,0:T(2,128)S(1)} %copy-done.6, s32[2,64]{1,0:T(2,128)S(1)} %copy-done.8, bf16[2,16,128,128]{3,2,1,0:T(8,128)(2,1)S(1)} %copy-done.5), custom_call_target="tpu_custom_call" | custom-call | tf_op jit(solution)/shard_map/pallas_call | solution.py:160
  6.2 10.6 %all-to-all-start = ((bf16[768,16,128]{2,1,0:T(8,128)(2,1)}), bf16[768,16,128]{2,1,0:T(8,128)(2,1)}, u32[]{:S(2)}, u32[]{:S(2)}) async-start(bf16[768,16,128]{2,1,0:T(8,128)(2,1)} %shard_map.65), calls=%async_computation | async-start | bytes 6291456 | tf_op jit(solution)/shard_map/all_to_all | solution.py:166
  16.9 2.1 %collective-permute-start.1 = (f32[16,8,128]{2,1,0:T(8,128)S(1)}, f32[16,8,128]{2,1,0:T(8,128)S(1)}, u32[]{:S(2)}, u32[]{:S(2)}) collective-permute-start(f32[16,8,128]{2,1,0:T(8,128)S(1)} %get-tuple-element.15), channel_id=1, source_target_pairs={{0,16},{16,32},{32,48},{48,64},{64,80},{80,96},{96,112},{1,17},{17... | collective-permute-start | bytes 196616 | tf_op jit(solution)/shard_map/ppermute | solution.py:149
  18.9 3.5 %collective-permute-start = (f32[16,8,128]{2,1,0:T(8,128)S(1)}, f32[16,8,128]{2,1,0:T(8,128)S(1)}, u32[]{:S(2)}, u32[]{:S(2)}) collective-permute-start(f32[16,8,128]{2,1,0:T(8,128)S(1)} %get-tuple-element.16), channel_id=1, source_target_pairs={{16,0},{32,16},{48,32},{64,48},{80,64},{96,80},{112,96},{17,1},{33... | collective-permute-start | bytes 196616 | tf_op jit(solution)/shard_map/ppermute | solution.py:150
  23.5 27.2 %collective-permute-done = f32[16,8,128]{2,1,0:T(8,128)S(1)} collective-permute-done((f32[16,8,128]{2,1,0:T(8,128)S(1)}, f32[16,8,128]{2,1,0:T(8,128)S(1)}, u32[]{:S(2)}, u32[]{:S(2)}) %collective-permute-start) | collective-permute-done | bytes 65568 | tf_op jit(solution)/shard_map/ppermute | solution.py:150
  50.7 1.3 collective-permute-done.1
  52.0 1.4 %fusion.1 = (f32[16,144,8]{2,1,0:T(8,128)}, f32[16,144,8]{2,1,0:T(8,128)S(1)}) fusion(f32[16,144,128]{2,1,0:T(8,128)S(1)} %constant_dynamic-update-slice_fusion), kind=kLoop, calls=%fused_computation.9 | loop fusion | bytes 294912 | tf_op jit(solution)/shard_map/slice | solution.py:147
  53.4 1.8 %copy.7 = f32[16,144,8]{1,2,0:T(8,128)S(1)} copy(f32[16,144,8]{2,1,0:T(8,128)} %get-tuple-element.11) | data formatting | bytes 147456 | tf_op jit(solution)/shard_map/slice | solution.py:147
  56.5 3.6 %collective-permute-start.3 = (f32[16,144,8]{1,2,0:T(8,128)}, f32[16,144,8]{1,2,0:T(8,128)}, u32[]{:S(2)}, u32[]{:S(2)}) collective-permute-start(f32[16,144,8]{1,2,0:T(8,128)} %copy.8), channel_id=1, source_target_pairs={{0,1},{1,2},{2,3},{3,4},{4,5},{5,6},{6,7},{7,8},{8,9},{9,10},{10,1... | collective-permute-start | bytes 221192 | tf_op jit(solution)/shard_map/ppermute | solution.py:149
  60.1 4.3 %collective-permute-start.2 = (f32[16,144,8]{1,2,0:T(8,128)S(1)}, f32[16,144,8]{1,2,0:T(8,128)}, u32[]{:S(2)}, u32[]{:S(2)}) collective-permute-start(f32[16,144,8]{1,2,0:T(8,128)S(1)} %copy.7), channel_id=1, source_target_pairs={{1,0},{2,1},{3,2},{4,3},{5,4},{6,5},{7,6},{8,7},{9,8},{10,9},{11,1... | collective-permute-start | bytes 221192 | tf_op jit(solution)/shard_map/ppermute | solution.py:150
  65.1 1.9 %collective-permute-done.2 = f32[16,144,8]{1,2,0:T(8,128)} collective-permute-done((f32[16,144,8]{1,2,0:T(8,128)S(1)}, f32[16,144,8]{1,2,0:T(8,128)}, u32[]{:S(2)}, u32[]{:S(2)}) %collective-permute-start.2) | collective-permute-done | bytes 73760 | tf_op jit(solution)/shard_map/ppermute | solution.py:150
  67.1 1.3 copy.9
  68.4 2.3 %copy.10 = f32[16,144,8]{2,1,0:T(8,128)} copy(f32[16,144,8]{1,2,0:T(8,128)} %collective-permute-done.3) | data formatting | bytes 147456 | tf_op jit(solution)/shard_map/ppermute | solution.py:149
  70.7 3.2 %pad_maximum_fusion.padded_ref = f32[16,144,144]{2,1,0:T(8,128)} fusion(f32[16,144,8]{2,1,0:T(8,128)} %copy.10, f32[16,144,8]{2,1,0:T(8,128)S(1)} %copy.9, f32[16,144,128]{2,1,0:T(8,128)S(1)} %constant_dynamic-update-slice_fusion), kind=kLoop, calls=%fused_computation | loop fusion | flops 663552 | bytes 2654208 | tf_op jit(solution)/shard_map/concatenate | solution.py:151
  73.9 11.4 %shard_map.64 = (f32[2,16,128,128]{3,2,1,0:T(8,128)S(1)}, bf16[2,4,2,2,128,144]{5,4,3,2,1,0:T(8,128)(2,1)S(1)}) custom-call(s32[16]{0:T(128)S(1)} %copy-done.10, f32[2,2,4,2,256]{4,3,2,1,0:T(2,128)S(1)} %select_maximum_fusion.taps_ref, f32[16,144,144]{2,1,0:T(8,128)} %pad_maximum_fusion.padded_ref), custom_call_target="tpu_custom_call" | custom-call | tf_op jit(solution)/shard_map/pallas_call | solution.py:173
  85.3 1.4 copy-done.1
  86.7 1.4 %copy-done.3 = f32[2,16,128,128]{3,2,1,0:T(8,128)} copy-done((f32[2,16,128,128]{3,2,1,0:T(8,128)}, f32[2,16,128,128]{3,2,1,0:T(8,128)S(1)}, u32[]{:S(2)}) %copy-start.3) | copy-done | bytes 2097176
  88.1 1.6 %copy-done.4 = f32[2,16,128,128]{3,2,1,0:T(8,128)S(1)} copy-done((f32[2,16,128,128]{3,2,1,0:T(8,128)S(1)}, f32[2,16,128,128]{3,2,1,0:T(8,128)}, u32[]{:S(2)}) %copy-start.4) | copy-done | bytes 2097176
  89.7 3.1 %shard_map.66 = bf16[2,16,128,128]{3,2,1,0:T(8,128)(2,1)S(1)} custom-call(s32[1]{0:T(128)} %bitcast.2.me_ref, s32[2,64]{1,0:T(2,128)S(1)} %copy-done.7, s32[2,64]{1,0:T(2,128)S(1)} %copy-done.9, bf16[768,16,128]{2,1,0:T(8,128)(2,1)} %all-to-all-done.arrived_ref, f32[2,16,128,128]{3,2,1,0:T(8,128)S(1)} %copy-done.4), custom_call_target="tpu_custom_call" | custom-call | tf_op jit(solution)/shard_map/pallas_call | solution.py:180
  92.9 3.0 %collective-permute-start.4 = (bf16[2,16,8,128]{3,2,1,0:T(8,128)(2,1)S(1)}, bf16[2,16,8,128]{3,2,1,0:T(8,128)(2,1)S(1)}, u32[]{:S(2)}, u32[]{:S(2)}) collective-permute-start(bf16[2,16,8,128]{3,2,1,0:T(8,128)(2,1)S(1)} %get-tuple-element.13), channel_id=1, source_target_pairs={{16,0},{32,16},{48,32},{64,48},{80,64},{96,80},{112,96},{17,1},{33... | collective-permute-start | bytes 196616 | tf_op jit(solution)/shard_map/ppermute | solution.py:150
  95.8 1.9 %collective-permute-start.5 = (bf16[2,16,8,128]{3,2,1,0:T(8,128)(2,1)S(1)}, bf16[2,16,8,128]{3,2,1,0:T(8,128)(2,1)S(1)}, u32[]{:S(2)}, u32[]{:S(2)}) collective-permute-start(bf16[2,16,8,128]{3,2,1,0:T(8,128)(2,1)S(1)} %get-tuple-element.14), channel_id=1, source_target_pairs={{0,16},{16,32},{32,48},{48,64},{64,80},{80,96},{96,112},{1,17},{17... | collective-permute-start | bytes 196616 | tf_op jit(solution)/shard_map/ppermute | solution.py:149
  97.8 3.6 %collective-permute-done.5 = bf16[2,16,8,128]{3,2,1,0:T(8,128)(2,1)S(1)} collective-permute-done((bf16[2,16,8,128]{3,2,1,0:T(8,128)(2,1)S(1)}, bf16[2,16,8,128]{3,2,1,0:T(8,128)(2,1)S(1)}, u32[]{:S(2)}, u32[]{:S(2)}) %collective-permute-start.5) | collective-permute-done | bytes 65568 | tf_op jit(solution)/shard_map/ppermute | solution.py:149
  101.5 1.5 %fusion = (bf16[2,16,144,8]{3,2,1,0:T(8,128)(2,1)}, bf16[2,16,144,8]{3,2,1,0:T(8,128)(2,1)S(1)}) fusion(bf16[2,16,144,128]{3,2,1,0:T(8,128)(2,1)S(1)} %pad_maximum_fusion.2), kind=kLoop, calls=%fused_computation.8 | loop fusion | bytes 294912 | tf_op jit(solution)/shard_map/slice | solution.py:147
  103.0 1.8 %copy.11 = bf16[2,16,144,8]{2,3,1,0:T(8,128)(2,1)S(1)} copy(bf16[2,16,144,8]{3,2,1,0:T(8,128)(2,1)} %get-tuple-element.9) | data formatting | bytes 147456 | tf_op jit(solution)/shard_map/slice | solution.py:147
  104.8 6.4 %collective-permute-start.6 = (bf16[2,16,144,8]{2,3,1,0:T(8,128)(2,1)S(1)}, bf16[2,16,144,8]{2,3,1,0:T(8,128)(2,1)}, u32[]{:S(2)}, u32[]{:S(2)}) collective-permute-start(bf16[2,16,144,8]{2,3,1,0:T(8,128)(2,1)S(1)} %copy.11), channel_id=1, source_target_pairs={{1,0},{2,1},{3,2},{4,3},{5,4},{6,5},{7,6},{8,7},{9,8},{10,9},{11,1... | collective-permute-start | bytes 221192 | tf_op jit(solution)/shard_map/ppermute | solution.py:150
  111.3 1.3 copy.12
  112.5 1.9 %collective-permute-start.7 = (bf16[2,16,144,8]{2,3,1,0:T(8,128)(2,1)}, bf16[2,16,144,8]{2,3,1,0:T(8,128)(2,1)}, u32[]{:S(2)}, u32[]{:S(2)}) collective-permute-start(bf16[2,16,144,8]{2,3,1,0:T(8,128)(2,1)} %copy.12), channel_id=1, source_target_pairs={{0,1},{1,2},{2,3},{3,4},{4,5},{5,6},{6,7},{7,8},{8,9},{9,10},{10,1... | collective-permute-start | bytes 221192 | tf_op jit(solution)/shard_map/ppermute | solution.py:149
  114.4 1.4 %copy.13 = bf16[2,16,144,8]{3,2,1,0:T(8,128)(2,1)S(1)} copy(bf16[2,16,144,8]{2,3,1,0:T(8,128)(2,1)} %collective-permute-done.6) | data formatting | bytes 147456 | tf_op jit(solution)/shard_map/ppermute | solution.py:150
  115.8 5.9 %collective-permute-done.7 = bf16[2,16,144,8]{2,3,1,0:T(8,128)(2,1)} collective-permute-done((bf16[2,16,144,8]{2,3,1,0:T(8,128)(2,1)}, bf16[2,16,144,8]{2,3,1,0:T(8,128)(2,1)}, u32[]{:S(2)}, u32[]{:S(2)}) %collective-permute-start.7) | collective-permute-done | bytes 73760 | tf_op jit(solution)/shard_map/ppermute | solution.py:149
  121.8 2.3 %copy.14 = bf16[2,16,144,8]{3,2,1,0:T(8,128)(2,1)} copy(bf16[2,16,144,8]{2,3,1,0:T(8,128)(2,1)} %collective-permute-done.7) | data formatting | bytes 147456 | tf_op jit(solution)/shard_map/ppermute | solution.py:149
  124.1 2.4 %pad_maximum_fusion.1.ratio_ref = bf16[2,16,144,144]{3,2,1,0:T(8,128)(2,1)S(1)} fusion(bf16[2,16,144,8]{3,2,1,0:T(8,128)(2,1)} %copy.14, bf16[2,16,144,8]{3,2,1,0:T(8,128)(2,1)S(1)} %copy.13, bf16[2,16,8,128]{3,2,1,0:T(8,128)(2,1)S(1)} %collective-permute-done.5, bf16[2,16,8,128]{3,2,1,0:T(8,128)(2,1)S(1)} %collective-permute-done.4, ...), kind=kLoop, calls=%fused_computation.1 | loop fusion | flops 6635520 | bytes 2654208 | tf_op jit(solution)/shard_map/concatenate | solution.py:151
  126.5 10.1 %shard_map.67 = f32[16,128,128]{2,1,0:T(8,128)} custom-call(s32[16]{0:T(128)S(1)} %copy-done.10, bf16[2,4,2,2,128,144]{5,4,3,2,1,0:T(8,128)(2,1)S(1)} %copy-done.2, bf16[2,16,144,144]{3,2,1,0:T(8,128)(2,1)S(1)} %pad_maximum_fusion.1.ratio_ref, f32[16,128,128]{2,1,0:T(8,128)S(1)} %copy-done), custom_call_target="tpu_custom_call" | custom-call | tf_op jit(solution)/shard_map/pallas_call | solution.py:187
  (37 shorter events, 5.7 us)
Async XLA Ops:
  0.0 1.2 copy-start.5
  1.2 0.7 copy-start.6
  1.9 0.7 copy-start.8
  6.2 10.6 %copy-start = (f32[16,128,128]{2,1,0:T(8,128)S(1)}, f32[16,128,128]{2,1,0:T(8,128)}, u32[]{:S(2)}) copy-start(f32[16,128,128]{2,1,0:T(8,128)} %estimate_ref.1) | copy-start | bytes 3145732
  6.2 16.3 %copy-start.11 = (f32[2,4,2,17]{3,2,1,0:T(2,128)S(1)}, f32[2,4,2,17]{3,2,1,0:T(2,128)}, u32[]{:S(2)}) copy-start(f32[2,4,2,17]{3,2,1,0:T(2,128)} %param.8) | copy-start | bytes 3268
  6.2 81.9 %all-to-all-start = ((bf16[768,16,128]{2,1,0:T(8,128)(2,1)}), bf16[768,16,128]{2,1,0:T(8,128)(2,1)}, u32[]{:S(2)}, u32[]{:S(2)}) async-start(bf16[768,16,128]{2,1,0:T(8,128)(2,1)} %shard_map.65), calls=%async_computation | async-start | bytes 6291456 | tf_op jit(solution)/shard_map/all_to_all | solution.py:166
  16.9 35.2 %collective-permute-start.1 = (f32[16,8,128]{2,1,0:T(8,128)S(1)}, f32[16,8,128]{2,1,0:T(8,128)S(1)}, u32[]{:S(2)}, u32[]{:S(2)}) collective-permute-start(f32[16,8,128]{2,1,0:T(8,128)S(1)} %get-tuple-element.15), channel_id=1, source_target_pairs={{0,16},{16,32},{32,48},{48,64},{64,80},{80,96},{96,112},{1,17},{17... | collective-permute-start | bytes 196616 | tf_op jit(solution)/shard_map/ppermute | solution.py:149
  18.9 31.8 %collective-permute-start = (f32[16,8,128]{2,1,0:T(8,128)S(1)}, f32[16,8,128]{2,1,0:T(8,128)S(1)}, u32[]{:S(2)}, u32[]{:S(2)}) collective-permute-start(f32[16,8,128]{2,1,0:T(8,128)S(1)} %get-tuple-element.16), channel_id=1, source_target_pairs={{16,0},{32,16},{48,32},{64,48},{80,64},{96,80},{112,96},{17,1},{33... | collective-permute-start | bytes 196616 | tf_op jit(solution)/shard_map/ppermute | solution.py:150
  56.5 11.9 %collective-permute-start.3 = (f32[16,144,8]{1,2,0:T(8,128)}, f32[16,144,8]{1,2,0:T(8,128)}, u32[]{:S(2)}, u32[]{:S(2)}) collective-permute-start(f32[16,144,8]{1,2,0:T(8,128)} %copy.8), channel_id=1, source_target_pairs={{0,1},{1,2},{2,3},{3,4},{4,5},{5,6},{6,7},{7,8},{8,9},{9,10},{10,1... | collective-permute-start | bytes 221192 | tf_op jit(solution)/shard_map/ppermute | solution.py:149
  60.1 7.0 %collective-permute-start.2 = (f32[16,144,8]{1,2,0:T(8,128)S(1)}, f32[16,144,8]{1,2,0:T(8,128)}, u32[]{:S(2)}, u32[]{:S(2)}) collective-permute-start(f32[16,144,8]{1,2,0:T(8,128)S(1)} %copy.7), channel_id=1, source_target_pairs={{1,0},{2,1},{3,2},{4,3},{5,4},{6,5},{7,6},{8,7},{9,8},{10,9},{11,1... | collective-permute-start | bytes 221192 | tf_op jit(solution)/shard_map/ppermute | solution.py:150
  70.7 3.2 %copy-start.10 = (s32[16]{0:T(128)S(1)}, s32[16]{0:T(128)}, u32[]{:S(2)}) copy-start(s32[16]{0:T(128)} %band_ref.3) | copy-start | bytes 196
  73.9 14.2 %copy-start.7 = (s32[2,64]{1,0:T(2,128)S(1)}, s32[2,64]{1,0:T(2,128)}, u32[]{:S(2)}) copy-start(s32[2,64]{1,0:T(2,128)} %shift_ref.3) | copy-start | bytes 1540
  73.9 14.2 %copy-start.9 = (s32[2,64]{1,0:T(2,128)S(1)}, s32[2,64]{1,0:T(2,128)}, u32[]{:S(2)}) copy-start(s32[2,64]{1,0:T(2,128)} %length_ref.3) | copy-start | bytes 1540
  85.3 1.4 %copy-start.1 = (bf16[2,4,2,2,128,144]{5,4,3,2,1,0:T(8,128)(2,1)}, bf16[2,4,2,2,128,144]{5,4,3,2,1,0:T(8,128)(2,1)S(1)}, u32[]{:S(2)}) copy-start(bf16[2,4,2,2,128,144]{5,4,3,2,1,0:T(8,128)(2,1)S(1)} %get-tuple-element.7.adjoint_ref) | copy-start | bytes 3538948
  86.7 1.4 %copy-start.3 = (f32[2,16,128,128]{3,2,1,0:T(8,128)}, f32[2,16,128,128]{3,2,1,0:T(8,128)S(1)}, u32[]{:S(2)}) copy-start(f32[2,16,128,128]{3,2,1,0:T(8,128)S(1)} %get-tuple-element.8.recip_ref) | copy-start | bytes 6291460
  88.1 1.6 %copy-start.4 = (f32[2,16,128,128]{3,2,1,0:T(8,128)S(1)}, f32[2,16,128,128]{3,2,1,0:T(8,128)}, u32[]{:S(2)}) copy-start(f32[2,16,128,128]{3,2,1,0:T(8,128)} %copy-done.3) | copy-start | bytes 6291460
  92.9 4.9 %collective-permute-start.4 = (bf16[2,16,8,128]{3,2,1,0:T(8,128)(2,1)S(1)}, bf16[2,16,8,128]{3,2,1,0:T(8,128)(2,1)S(1)}, u32[]{:S(2)}, u32[]{:S(2)}) collective-permute-start(bf16[2,16,8,128]{3,2,1,0:T(8,128)(2,1)S(1)} %get-tuple-element.13), channel_id=1, source_target_pairs={{16,0},{32,16},{48,32},{64,48},{80,64},{96,80},{112,96},{17,1},{33... | collective-permute-start | bytes 196616 | tf_op jit(solution)/shard_map/ppermute | solution.py:150
  95.8 5.6 %collective-permute-start.5 = (bf16[2,16,8,128]{3,2,1,0:T(8,128)(2,1)S(1)}, bf16[2,16,8,128]{3,2,1,0:T(8,128)(2,1)S(1)}, u32[]{:S(2)}, u32[]{:S(2)}) collective-permute-start(bf16[2,16,8,128]{3,2,1,0:T(8,128)(2,1)S(1)} %get-tuple-element.14), channel_id=1, source_target_pairs={{0,16},{16,32},{32,48},{48,64},{64,80},{80,96},{96,112},{1,17},{17... | collective-permute-start | bytes 196616 | tf_op jit(solution)/shard_map/ppermute | solution.py:149
  104.8 9.6 %collective-permute-start.6 = (bf16[2,16,144,8]{2,3,1,0:T(8,128)(2,1)S(1)}, bf16[2,16,144,8]{2,3,1,0:T(8,128)(2,1)}, u32[]{:S(2)}, u32[]{:S(2)}) collective-permute-start(bf16[2,16,144,8]{2,3,1,0:T(8,128)(2,1)S(1)} %copy.11), channel_id=1, source_target_pairs={{1,0},{2,1},{3,2},{4,3},{5,4},{6,5},{7,6},{8,7},{9,8},{10,9},{11,1... | collective-permute-start | bytes 221192 | tf_op jit(solution)/shard_map/ppermute | solution.py:150
  112.5 9.3 %collective-permute-start.7 = (bf16[2,16,144,8]{2,3,1,0:T(8,128)(2,1)}, bf16[2,16,144,8]{2,3,1,0:T(8,128)(2,1)}, u32[]{:S(2)}, u32[]{:S(2)}) collective-permute-start(bf16[2,16,144,8]{2,3,1,0:T(8,128)(2,1)} %copy.12), channel_id=1, source_target_pairs={{0,1},{1,2},{2,3},{3,4},{4,5},{5,6},{6,7},{7,8},{8,9},{9,10},{10,1... | collective-permute-start | bytes 221192 | tf_op jit(solution)/shard_map/ppermute | solution.py:149
  124.1 2.4 %copy-start.2 = (bf16[2,4,2,2,128,144]{5,4,3,2,1,0:T(8,128)(2,1)S(1)}, bf16[2,4,2,2,128,144]{5,4,3,2,1,0:T(8,128)(2,1)}, u32[]{:S(2)}) copy-start(bf16[2,4,2,2,128,144]{5,4,3,2,1,0:T(8,128)(2,1)} %copy-done.1) | copy-start | bytes 3538948
where the time goes:
time: 138 us; the launch traced here: 137 us
  waiting for transfers between devices  40 us (29%)
  starting transfers between devices  37.4 us (27%)
  Pallas kernels  28.2 us (20%)
  local copies, waits for them, and re-layouts  24.1 us (17%)
  other arithmetic  6.67 us (5%)
    ppermute x4, waiting for transfers between devices, padded(): after = lax.ppermute(head, axis, [(i + 1, i) for i in range(ends)])  29.2 us
    ppermute x4, starting transfers between devices, padded(): after = lax.ppermute(head, axis, [(i + 1, i) for i in range(ends)])  17.2 us
    pallas_call x1, Pallas kernels, body(): call(forward_kernel, [SMEM, VMEM, VMEM], (jax.ShapeDtypeStruct(measured.s...  11.4 us
    ppermute x4, waiting for transfers between devices, padded(): before = lax.ppermute(tail, axis, [(i, i + 1) for i in range(ends)])  10.9 us
    all_to_all x1, starting transfers between devices, body(): lax.all_to_all(outgoing, ('gx', 'gy'), split_axis=0, concat_axis=0, tiled...  10.6 us
    pallas_call x1, Pallas kernels, body(): call(adjoint_kernel, [SMEM, VMEM, VMEM, VMEM], jax.ShapeDtypeStruct(estim...  10.1 us
    ppermute x4, starting transfers between devices, padded(): before = lax.ppermute(tail, axis, [(i, i + 1) for i in range(ends)])  9.52 us
    unnamed x26, local copies, waits for them, and re-layouts  7.02 us
  transfers between devices with their start and end apart: 9, of which 5 were waited for; matrix products, arithmetic and copies ran while one was open for 11% of the time, Pallas kernels for 8%

commit v1 on v0

v1 whole, which is shorter than its diff:
```python
import functools

import jax
import jax.numpy as jnp
from jax import lax
from jax.experimental import pallas as pl
from jax.experimental.pallas import tpu as pltpu
from jax.sharding import PartitionSpec as P

HW = 8
CAP = 3
LANES = 256
F32 = jnp.float32
BF16 = jnp.bfloat16

VMEM = pl.BlockSpec(memory_space=pltpu.VMEM)
SMEM = pl.BlockSpec(memory_space=pltpu.SMEM)
NN = ((1,), (0,))
NT = ((1,), (1,))


def call(kernel, ins, out_shape, scratch=()):
    return pl.pallas_call(
        kernel,
        in_specs=ins,
        out_specs=jax.tree.map(lambda _: VMEM, out_shape),
        out_shape=out_shape,
        scratch_shapes=list(scratch),
        compiler_params=pltpu.CompilerParams(vmem_limit_bytes=16 * 2**20),
    )


def dot(a, b, dims=NN):
    return lax.dot_general(a, b, (dims, ((), ())), preferred_element_type=F32)


def split(x):
    high = x.astype(BF16)
    return high, (x - high.astype(F32)).astype(BF16)


def stacked(x, axis):
    return jnp.concatenate(split(x), axis=axis)


def halves(x):
    n = x.shape[0] // 2
    return x[:n] + x[n:]


def quarters(x):
    n, m = x.shape[0] // 2, x.shape[1] // 2
    return x[:n, :m] + (x[n:, :m] + x[:n, m:])


def joined(after, before):
    return jnp.concatenate([after.astype(F32), before.astype(F32)], axis=0).astype(BF16)


def edge_picker(cols):
    lane = lax.broadcasted_iota(jnp.int32, (2 * HW, cols), 1)
    sub = lax.broadcasted_iota(jnp.int32, (2 * HW, cols), 0)
    return (lane == jnp.where(sub < HW, sub, sub + cols - 2 * HW)).astype(BF16)


def pack_kernel(devices, me_ref, shift_ref, length_ref, measured_ref, estimate_ref, out_ref, cols_ref, rows_ref):
    views, depth, tile_rows, tile_cols = measured_ref.shape
    groups = shift_ref.shape[1]
    rows_ref[:, tile_rows:] = jnp.zeros((views, rows_ref.shape[1] - tile_rows) + rows_ref.shape[2:], BF16)
    lane = lax.broadcasted_iota(jnp.int32, (tile_cols, tile_cols), 1)
    sub = lax.broadcasted_iota(jnp.int32, (tile_cols, tile_cols), 0)
    turn = (lane + sub == tile_cols - 1).astype(BF16)
    me = me_ref[0]
    for view in range(views):
        for r0 in range(0, tile_rows, 16):
            x = measured_ref[view, :, r0 : r0 + 16, :]
            if view % 2 == 1:
                x = dot(x.reshape(depth * 16, tile_cols), turn).reshape(depth, 16, tile_cols)
            x = jnp.transpose(x.astype(F32), (1, 0, 2))
            rows_ref[view, r0 : r0 + 16] = x.astype(BF16)

        def group(g, start, view=view):
            base = lax.rem(me + shift_ref[view, g], devices) * (views * CAP) + view * CAP
            for k in range(CAP):
                out_ref[base + k] = rows_ref[view, start + k]
            return start + length_ref[view, g]

        lax.fori_loop(0, groups, group, 0, unroll=4)
    pick = edge_picker(tile_cols)
    for z in range(depth):
        cols_ref[z] = dot(pick, estimate_ref[z].astype(BF16), NT).astype(BF16)


def slab_kernel(cols_ref, after_ref, before_ref, head_ref, tail_ref):
    tile_rows = cols_ref.shape[-1]
    pick = edge_picker(after_ref.shape[-1])

    def plane(i, carry):
        corner = dot(pick, joined(after_ref[i], before_ref[i]), NT).astype(BF16)
        head_ref[i, :, :tile_rows] = cols_ref[i, :HW]
        tail_ref[i, :, :tile_rows] = cols_ref[i, HW:]
        head_ref[i, :, tile_rows:] = corner[:HW]
        tail_ref[i, :, tile_rows:] = corner[HW:]
        return carry

    lax.fori_loop(0, cols_ref.shape[0], plane, 0, unroll=8)


def edges_kernel(devices, me_ref, shift_ref, length_ref, arrived_ref, recip_ref, top_ref, bottom_ref, rows_ref):
    views, depth, tile_rows, tile_cols = recip_ref.shape
    groups = shift_ref.shape[1]
    me = me_ref[0]
    low = tile_rows - CAP * HW
    for view in range(views):
        ending = tile_rows - low
        for g in range(groups - HW, groups):
            ending = ending - length_ref[view, g]
        for side, (first, start) in enumerate(((0, 0), (groups - HW, ending))):
            for g in range(first, first + HW):
                source = lax.rem(me - shift_ref[view, g] + devices, devices)
                base = source * (views * CAP) + view * CAP
                for k in range(CAP):
                    rows_ref[view, side, start + k] = arrived_ref[base + k].astype(F32)
                start = start + length_ref[view, g]
        x = jnp.transpose(rows_ref[view, 0, :HW], (1, 0, 2))
        top_ref[view] = (x * recip_ref[view, :, :HW, :]).astype(BF16)
        x = jnp.transpose(rows_ref[view, 1, (CAP - 1) * HW : CAP * HW], (1, 0, 2))
        bottom_ref[view] = (x * recip_ref[view, :, tile_rows - HW :, :]).astype(BF16)


def unpack_kernel(devices, me_ref, shift_ref, length_ref, arrived_ref, recip_ref, out_ref, cols_ref, rows_ref):
    views, depth, tile_rows, tile_cols = out_ref.shape
    groups = shift_ref.shape[1]
    me = me_ref[0]
    pick = edge_picker(tile_cols)
    for view in range(views):

        def group(g, start, view=view):
            source = lax.rem(me - shift_ref[view, g] + devices, devices)
            base = source * (views * CAP) + view * CAP
            for k in range(CAP):
                rows_ref[view, start + k] = arrived_ref[base + k].astype(F32)
            return start + length_ref[view, g]

        lax.fori_loop(0, groups, group, 0, unroll=4)
        for r0 in range(0, tile_rows, 16):
            x = jnp.transpose(rows_ref[view, r0 : r0 + 16], (1, 0, 2))
            out_ref[view, :, r0 : r0 + 16, :] = (x * recip_ref[view, :, r0 : r0 + 16, :]).astype(BF16)
        for z in range(depth):
            cols_ref[view, z] = dot(pick, out_ref[view, z], NT).astype(BF16)


def band(taps, size):
    wide = jnp.broadcast_to(taps, (size, LANES))
    inner = pltpu.roll(wide, LANES - HW, 1, stride=1, stride_axis=0)
    before = pltpu.roll(wide, size + HW, 1, stride=1, stride_axis=0)
    lane = lax.broadcasted_iota(jnp.int32, (size, LANES), 1)
    return jnp.where(lane < size + HW, inner, jnp.where(lane < size + 2 * HW, before, 0.0))


def blur_far(rows, far, across):
    return quarters(dot(stacked(halves(dot(rows, far, NT)), 0), across))


def forward_kernel(
    band_ref, taps_ref, cells_ref, after_ref, before_ref, right_ref, left_ref,
    recip_ref, rows_ref, cols_ref, far_ref, fwd_rows, fwd_cols, fwd_far,
):
    views, depth, tile_rows, tile_cols = recip_ref.shape
    bands = taps_ref.shape[2]
    for way, refs in ((0, (fwd_rows, fwd_cols, fwd_far)), (1, (rows_ref, cols_ref, far_ref))):
        for view in range(views):
            for b in range(bands):
                along = band(taps_ref[way, view, b, 0:1, :], tile_rows)
                refs[0][view, b] = stacked(along[:, : tile_rows + 2 * HW], 0)
                across = band(taps_ref[way, view, b, 1:2, :], tile_cols)
                refs[1][view, b] = stacked(across[:, :tile_cols].T, 1)
                refs[2][view, b] = stacked(across[:, tile_cols:].T[: 2 * HW], 1)

    def plane(z, carry):
        b = band_ref[z]
        cells = stacked(cells_ref[z], 1)
        ends = joined(after_ref[z], before_ref[z])
        far = joined(right_ref[z], left_ref[z])
        for view in range(views):
            rows = fwd_rows[view, b]
            blurred = quarters(dot(rows[:, :tile_rows], cells)) + halves(dot(rows[:, tile_rows:], ends))
            blurred = quarters(dot(stacked(blurred, 0), fwd_cols[view, b])) + blur_far(rows, far, fwd_far[view, b])
            recip_ref[view, z] = 1.0 / blurred.astype(BF16).astype(F32)
        return carry

    lax.fori_loop(0, depth, plane, 0)


def near_kernel(band_ref, rows_ref, cols_ref, ratio_ref, after_ref, before_ref, out_ref):
    views, depth = ratio_ref.shape[:2]

    def plane(z, carry):
        b = band_ref[z]
        total = None
        for view in range(views):
            cells = jnp.concatenate([ratio_ref[view, z], joined(after_ref[view, z], before_ref[view, z])], axis=0)
            blurred = dot(cells, cols_ref[view, b])
            half = blurred.shape[1] // 2
            blurred = blurred[:, :half] + blurred[:, half:]
            part = quarters(dot(rows_ref[view, b], stacked(blurred, 1)))
            total = part if total is None else total + part
        out_ref[z] = total
        return carry

    lax.fori_loop(0, depth, plane, 0, unroll=2)


def far_kernel(band_ref, rows_ref, far_ref, near_ref, right_ref, left_ref, estimate_ref, out_ref):
    views, depth = right_ref.shape[:2]

    def plane(z, carry):
        b = band_ref[z]
        total = near_ref[z]
        for view in range(views):
            total = total + blur_far(rows_ref[view, b], joined(right_ref[view, z], left_ref[view, z]), far_ref[view, b])
        out_ref[z] = estimate_ref[z] * (total * (1.0 / views))
        return carry

    lax.fori_loop(0, depth, plane, 0, unroll=2)


def swap(head, tail, axis):
    ends = lax.axis_size(axis) - 1
    after = lax.ppermute(head, axis, [(i + 1, i) for i in range(ends)])
    before = lax.ppermute(tail, axis, [(i, i + 1) for i in range(ends)])
    return after, before


def slabs(cols, after, before):
    lead = cols.shape[:-2]
    shape = (cols.size // (cols.shape[-1] * cols.shape[-2]), HW, cols.shape[-1] + 2 * HW)
    merge = lambda x: x.reshape((shape[0],) + x.shape[-2:])
    out = jax.ShapeDtypeStruct(shape, BF16)
    head, tail = call(slab_kernel, [VMEM] * 3, (out, out))(merge(cols), merge(after), merge(before))
    return head.reshape(lead + shape[1:]), tail.reshape(lead + shape[1:])


def body(estimate, measured, kernels, depth_band, group_shift, group_length):
    devices = lax.axis_size("gx") * lax.axis_size("gy")
    me = (lax.axis_index("gx") * lax.axis_size("gy") + lax.axis_index("gy")).reshape(1).astype(jnp.int32)
    views, depth, tile_rows, tile_cols = measured.shape
    bands = kernels.shape[1]
    spare = tile_rows + 8
    whole = jax.ShapeDtypeStruct(measured.shape, BF16)
    edge_cols = jax.ShapeDtypeStruct((views, depth, 2 * HW, tile_rows), BF16)
    edge_rows = jax.ShapeDtypeStruct((views, depth, HW, tile_cols), BF16)

    after, before = swap(
        estimate[:, :HW].astype(BF16), estimate[:, tile_rows - HW :].astype(BF16), "gx"
    )
    outgoing, cols = call(
        functools.partial(pack_kernel, devices),
        [SMEM, SMEM, SMEM, VMEM, VMEM],
        (
            jax.ShapeDtypeStruct((devices * views * CAP, depth, tile_cols), BF16),
            jax.ShapeDtypeStruct(edge_cols.shape[1:], BF16),
        ),
        [pltpu.VMEM((views, spare, depth, tile_cols), BF16)],
    )(me, group_shift, group_length, measured, estimate)
    right, left = swap(*slabs(cols, after, before), "gy")
    outgoing, right, left = lax.optimization_barrier((outgoing, right, left))
    arrived = lax.all_to_all(outgoing, ("gx", "gy"), split_axis=0, concat_axis=0, tiled=True)

    norm = kernels / jnp.sum(kernels, axis=3, keepdims=True)
    tap_rows = jnp.stack([norm, norm[..., ::-1]])
    tap_rows = jnp.pad(tap_rows, ((0, 0),) * 4 + ((0, LANES - kernels.shape[3]),))
    matrices = [
        (views, bands, 2 * tile_rows, tile_rows + 2 * HW),
        (views, bands, tile_cols, 2 * tile_cols),
        (views, bands, 2 * HW, 2 * tile_cols),
    ]
    recip, rows_mat, cols_mat, far_mat = call(
        forward_kernel,
        [SMEM] + [VMEM] * 6,
        (jax.ShapeDtypeStruct(measured.shape, F32), *(jax.ShapeDtypeStruct(m, BF16) for m in matrices)),
        [pltpu.VMEM(m, BF16) for m in matrices],
    )(depth_band, tap_rows, estimate, after, before, right, left)

    top, bottom = call(
        functools.partial(edges_kernel, devices),
        [SMEM, SMEM, SMEM, VMEM, VMEM],
        (edge_rows, edge_rows),
        [pltpu.VMEM((views, 2, CAP * HW + 8, depth, tile_cols), F32)],
    )(me, group_shift, group_length, arrived, recip)
    after, before = swap(top, bottom, "gx")
    ratio, cols = call(
        functools.partial(unpack_kernel, devices),
        [SMEM, SMEM, SMEM, VMEM, VMEM],
        (whole, edge_cols),
        [pltpu.VMEM((views, spare, depth, tile_cols), F32)],
    )(me, group_shift, group_length, arrived, recip)
    right, left = swap(*slabs(cols, after, before), "gy")
    near = call(
        near_kernel,
        [SMEM] + [VMEM] * 5,
        jax.ShapeDtypeStruct(estimate.shape, F32),
    )(depth_band, rows_mat, cols_mat, ratio, after, before)
    return call(
        far_kernel,
        [SMEM] + [VMEM] * 6,
        jax.ShapeDtypeStruct(estimate.shape, F32),
    )(depth_band, rows_mat, far_mat, near, right, left, estimate)


def solution(mesh):
    return jax.shard_map(
        body,
        mesh=mesh,
        in_specs=(P(None, "gx", "gy"), P(None, None, "gx", "gy"), P(), P(), P(), P()),
        out_specs=P(None, "gx", "gy"),
        check_vma=False,
    )
```

time: 138 us -> 110 us (0.80)
  waiting for transfers between devices: 40 us -> 25.9 us
  local copies, waits for them, and re-layouts: 24.1 us -> 11.5 us
  Pallas kernels: 28.2 us -> 35.6 us
  other arithmetic: 6.67 us -> 1.58 us
  starting transfers between devices: 37.4 us -> 32.6 us
    ppermute x8, waiting for transfers between devices: 40 us -> 7.32 us  [the longest x4 7.29 us: swap(): before = lax.ppermute(tail, axis, [(i, i + 1) for i in range(ends)])]
    all_to_all x1, waiting for transfers between devices: 0.01 us -> 18.6 us  [body(): lax.all_to_all(outgoing, ('gx', 'gy'), split_axis=0, concat_axis=0, tiled...]
    slice x8 -> x1, local copies, waits for them, and re-layouts: 9 us -> 0.01 us  [body(): estimate[:, tile_rows - HW:].astype(BF16)]
    pallas_call x3 -> x7, Pallas kernels: 25.1 us -> 33.5 us  [the longest x1 15.6 us: body(): call(forward_kernel, [SMEM] + [VMEM] * 6, (jax.ShapeDtypeStruct(measured....]
    ppermute x4 -> x0, local copies, waits for them, and re-layouts: 7.4 us -> none  [the longest x2 4.68 us: padded(): before = lax.ppermute(tail, axis, [(i, i + 1) for i in range(ends)])]
    concatenate x3 -> x0, other arithmetic: 5.69 us -> none  [padded(): cells = jnp.concatenate([cells, after, before], axis=dim)]
    unnamed x26 -> x34, local copies, waits for them, and re-layouts: 7.02 us -> 11.4 us
    all_to_all x1, starting transfers between devices: 10.6 us -> 6.59 us  [body(): lax.all_to_all(outgoing, ('gx', 'gy'), split_axis=0, concat_axis=0, tiled...]
  transfers between devices with their start and end apart: 9 -> 9, of which waited for: 5 -> 3; matrix products, arithmetic and copies ran while one was open for 11% -> 0% of each run, Pallas kernels for 8% -> 25%
where the time goes in v1:
time: 110 us; the launch traced here: 108 us
  Pallas kernels  35.6 us (32%)
  starting transfers between devices  32.6 us (30%)
  waiting for transfers between devices  25.9 us (24%)
  local copies, waits for them, and re-layouts  11.5 us (10%)
  other arithmetic  1.58 us (1%)
    all_to_all x1, waiting for transfers between devices, body(): lax.all_to_all(outgoing, ('gx', 'gy'), split_axis=0, concat_axis=0, tiled...  18.6 us
    ppermute x4, starting transfers between devices, swap(): after = lax.ppermute(head, axis, [(i + 1, i) for i in range(ends)])  17 us
    pallas_call x1, Pallas kernels, body(): call(forward_kernel, [SMEM] + [VMEM] * 6, (jax.ShapeDtypeStruct(measured....  15.6 us
    unnamed x34, local copies, waits for them, and re-layouts  11.4 us
    ppermute x4, starting transfers between devices, swap(): before = lax.ppermute(tail, axis, [(i, i + 1) for i in range(ends)])  8.97 us
    ppermute x4, waiting for transfers between devices, swap(): before = lax.ppermute(tail, axis, [(i, i + 1) for i in range(ends)])  7.29 us
    pallas_call x1, Pallas kernels, body(): call(far_kernel, [SMEM] + [VMEM] * 6, jax.ShapeDtypeStruct(estimate.shape...  7.13 us
    pallas_call x1, Pallas kernels, body(): call(near_kernel, [SMEM] + [VMEM] * 5, jax.ShapeDtypeStruct(estimate.shap...  6.87 us
  transfers between devices with their start and end apart: 9, of which 3 were waited for; matrix products, arithmetic and copies ran while one was open for 0% of the time, Pallas kernels for 25%

profile of v1, /device:TPU:30, one launch (start us, length us, event | category | flops | bytes accessed | tf_op | source)
XLA Modules:
  0.0 107.5 jit_solution(16173101404855296308)
XLA Ops:
  0.0 1.3 %convert.4 = bf16[16,128,128]{2,1,0:T(8,128)(2,1)S(1)} convert(f32[16,128,128]{2,1,0:T(8,128)} %estimate_ref.3) | non-fusion elementwise | flops 262144 | bytes 1572864 | tf_op jit(solution)/shard_map/convert.1
  1.3 1.9 %collective-permute-start.1 = (bf16[16,8,128]{2,1,0:T(8,128)(2,1)S(1)}, bf16[16,8,128]{2,1,0:T(8,128)(2,1)S(1)}, u32[]{:S(2)}, u32[]{:S(2)}) collective-permute-start(bf16[16,8,128]{2,1,0:T(8,128)(2,1)S(1)} %get-tuple-element.39), channel_id=1, source_target_pairs={{0,16},{16,32},{32,48},{48,64},{64,80},{80,96},{96,112},{1,17},{17... | collective-permute-start | bytes 98312 | tf_op jit(solution)/shard_map/ppermute | solution.py:231
  3.3 3.6 %collective-permute-start = (bf16[16,8,128]{2,1,0:T(8,128)(2,1)S(1)}, bf16[16,8,128]{2,1,0:T(8,128)(2,1)S(1)}, u32[]{:S(2)}, u32[]{:S(2)}) collective-permute-start(bf16[16,8,128]{2,1,0:T(8,128)(2,1)S(1)} %get-tuple-element.40), channel_id=1, source_target_pairs={{16,0},{32,16},{48,32},{64,48},{80,64},{96,80},{112,96},{17,1},{33... | collective-permute-start | bytes 98312 | tf_op jit(solution)/shard_map/ppermute | solution.py:230
  6.9 1.2 %copy-done = f32[16,128,128]{2,1,0:T(8,128)S(1)} copy-done((f32[16,128,128]{2,1,0:T(8,128)S(1)}, f32[16,128,128]{2,1,0:T(8,128)}, u32[]{:S(2)}) %copy-start) | copy-done | bytes 1048600
  8.2 1.2 %copy-done.8 = bf16[2,16,128,128]{3,2,1,0:T(8,128)(2,1)S(1)} copy-done((bf16[2,16,128,128]{3,2,1,0:T(8,128)(2,1)S(1)}, bf16[2,16,128,128]{3,2,1,0:T(8,128)(2,1)}, u32[]{:S(2)}) %copy-start.8) | copy-done | bytes 1048600
  9.4 0.7 copy-done.11
  10.1 0.7 copy-done.13
  10.7 2.3 %shard_map.64 = (bf16[768,16,128]{2,1,0:T(8,128)(2,1)S(1)}, bf16[16,16,128]{2,1,0:T(8,128)(2,1)S(1)}) custom-call(s32[1]{0:T(128)} %bitcast.2.me_ref, s32[2,64]{1,0:T(2,128)S(1)} %copy-done.11, s32[2,64]{1,0:T(2,128)S(1)} %copy-done.13, bf16[2,16,128,128]{3,2,1,0:T(8,128)(2,1)S(1)} %copy-done.8, f32[16,128,128]{2,1,0:T(8,128)S(1)} %copy-done), custom_call_target="tpu_custom_call" | custom-call | tf_op jit(solution)/shard_map/pallas_call | solution.py:257
  13.0 1.7 %copy-done.7 = bf16[768,16,128]{2,1,0:T(8,128)(2,1)} copy-done((bf16[768,16,128]{2,1,0:T(8,128)(2,1)}, bf16[768,16,128]{2,1,0:T(8,128)(2,1)S(1)}, u32[]{:S(2)}) %copy-start.7) | copy-done | bytes 3145752
  14.7 0.3 shard_map.65
  15.0 6.1 %collective-permute-start.2 = (bf16[16,8,144]{2,1,0:T(8,128)(2,1)S(1)}, bf16[16,8,144]{2,1,0:T(8,128)(2,1)S(1)}, u32[]{:S(2)}, u32[]{:S(2)}) collective-permute-start(bf16[16,8,144]{2,1,0:T(8,128)(2,1)S(1)} %get-tuple-element.24), channel_id=1, source_target_pairs={{1,0},{2,1},{3,2},{4,3},{5,4},{6,5},{7,6},{8,7},{9,8},{10,9},{11,1... | collective-permute-start | bytes 110600 | tf_op jit(solution)/shard_map/ppermute | solution.py:230
  21.1 1.9 %collective-permute-start.3 = (bf16[16,8,144]{2,1,0:T(8,128)(2,1)S(1)}, bf16[16,8,144]{2,1,0:T(8,128)(2,1)S(1)}, u32[]{:S(2)}, u32[]{:S(2)}) collective-permute-start(bf16[16,8,144]{2,1,0:T(8,128)(2,1)S(1)} %get-tuple-element.25), channel_id=1, source_target_pairs={{0,1},{1,2},{2,3},{3,4},{4,5},{5,6},{6,7},{7,8},{8,9},{9,10},{10,1... | collective-permute-start | bytes 110600 | tf_op jit(solution)/shard_map/ppermute | solution.py:231
  23.0 6.3 %collective-permute-done.3.left_ref = bf16[16,8,144]{2,1,0:T(8,128)(2,1)S(1)} collective-permute-done((bf16[16,8,144]{2,1,0:T(8,128)(2,1)S(1)}, bf16[16,8,144]{2,1,0:T(8,128)(2,1)S(1)}, u32[]{:S(2)}, u32[]{:S(2)}) %collective-permute-start.3) | collective-permute-done | bytes 36896 | tf_op jit(solution)/shard_map/ppermute | solution.py:231
  29.4 6.6 %all-to-all-start = ((bf16[768,16,128]{2,1,0:T(8,128)(2,1)}), bf16[768,16,128]{2,1,0:T(8,128)(2,1)S(1)}, u32[]{:S(2)}, u32[]{:S(2)}) async-start(bf16[768,16,128]{2,1,0:T(8,128)(2,1)} %copy-done.7), calls=%async_computation | async-start | bytes 6291456 | tf_op jit(solution)/shard_map/all_to_all | solution.py:268
  36.2 0.1 rev.3
  36.4 1.2 %copy-done.1 = f32[16,128,128]{2,1,0:T(8,128)S(1)} copy-done((f32[16,128,128]{2,1,0:T(8,128)S(1)}, f32[16,128,128]{2,1,0:T(8,128)}, u32[]{:S(2)}) %copy-start.1) | copy-done | bytes 1048600
  37.6 15.6 %shard_map.66 = (f32[2,16,128,128]{3,2,1,0:T(8,128)S(1)}, bf16[2,4,256,144]{3,2,1,0:T(8,128)(2,1)S(1)}, bf16[2,4,128,256]{3,2,1,0:T(8,128)(2,1)S(1)}, bf16[2,4,16,256]{3,2,1,0:T(8,128)(2,1)S(1)}) custom-call(s32[16]{0:T(128)S(1)} %copy-done.15, f32[2,2,4,2,256]{4,3,2,1,0:T(2,128)S(1)} %select_maximum_fusion.taps_ref, f32[16,128,128]{2,1,0:T(8,128)S(1)} %copy-done.1, ...), custom_call_target="tpu_custom_call" | custom-call | tf_op jit(solution)/shard_map/pallas_call | solution.py:278
  53.2 1.3 %copy-done.3 = f32[2,16,128,128]{3,2,1,0:T(8,128)} copy-done((f32[2,16,128,128]{3,2,1,0:T(8,128)}, f32[2,16,128,128]{3,2,1,0:T(8,128)S(1)}, u32[]{:S(2)}) %copy-start.3) | copy-done | bytes 2097176
  54.6 1.0 copy-done.5
  55.6 0.8 copy-done.9
  56.4 18.6 %all-to-all-done.arrived_ref = bf16[768,16,128]{2,1,0:T(8,128)(2,1)S(1)} async-done(((bf16[768,16,128]{2,1,0:T(8,128)(2,1)}), bf16[768,16,128]{2,1,0:T(8,128)(2,1)S(1)}, u32[]{:S(2)}, u32[]{:S(2)}) %all-to-all-start) | async-done | bytes 3145760 | tf_op jit(solution)/shard_map/all_to_all | solution.py:268
  74.9 1.6 %copy-done.4 = f32[2,16,128,128]{3,2,1,0:T(8,128)S(1)} copy-done((f32[2,16,128,128]{3,2,1,0:T(8,128)S(1)}, f32[2,16,128,128]{3,2,1,0:T(8,128)}, u32[]{:S(2)}) %copy-start.4) | copy-done | bytes 2097176
  76.5 0.7 shard_map.68
  77.3 2.1 %collective-permute-start.4 = (bf16[2,16,8,128]{3,2,1,0:T(8,128)(2,1)S(1)}, bf16[2,16,8,128]{3,2,1,0:T(8,128)(2,1)S(1)}, u32[]{:S(2)}, u32[]{:S(2)}) collective-permute-start(bf16[2,16,8,128]{3,2,1,0:T(8,128)(2,1)S(1)} %get-tuple-element.34), channel_id=1, source_target_pairs={{16,0},{32,16},{48,32},{64,48},{80,64},{96,80},{112,96},{17,1},{33... | collective-permute-start | bytes 196616 | tf_op jit(solution)/shard_map/ppermute | solution.py:230
  79.3 2.4 %collective-permute-start.5 = (bf16[2,16,8,128]{3,2,1,0:T(8,128)(2,1)S(1)}, bf16[2,16,8,128]{3,2,1,0:T(8,128)(2,1)S(1)}, u32[]{:S(2)}, u32[]{:S(2)}) collective-permute-start(bf16[2,16,8,128]{3,2,1,0:T(8,128)(2,1)S(1)} %get-tuple-element.35), channel_id=1, source_target_pairs={{0,16},{16,32},{32,48},{48,64},{64,80},{80,96},{96,112},{1,17},{17... | collective-permute-start | bytes 196616 | tf_op jit(solution)/shard_map/ppermute | solution.py:231
  81.7 2.2 %shard_map.67 = (bf16[2,16,128,128]{3,2,1,0:T(8,128)(2,1)S(1)}, bf16[2,16,16,128]{3,2,1,0:T(8,128)(2,1)S(1)}) custom-call(s32[1]{0:T(128)} %bitcast.2.me_ref, s32[2,64]{1,0:T(2,128)S(1)} %copy-done.12, s32[2,64]{1,0:T(2,128)S(1)} %copy-done.14, bf16[768,16,128]{2,1,0:T(8,128)(2,1)S(1)} %all-to-all-done.arrived_ref, f32[2,16,128,128]{3,2,1,0:T(8,128)S(1)} %copy-done.4), custom_call_target="tpu_custom_call" | custom-call | tf_op jit(solution)/shard_map/pallas_call | solution.py:292
  84.0 1.0 collective-permute-done.5.before_ref
  84.9 0.6 shard_map.70
  85.5 2.7 %collective-permute-start.7 = (bf16[2,16,8,144]{3,2,1,0:T(8,128)(2,1)S(1)}, bf16[2,16,8,144]{3,2,1,0:T(8,128)(2,1)S(1)}, u32[]{:S(2)}, u32[]{:S(2)}) collective-permute-start(bf16[2,16,8,144]{3,2,1,0:T(8,128)(2,1)S(1)} %bitcast.13), channel_id=1, source_target_pairs={{0,1},{1,2},{2,3},{3,4},{4,5},{5,6},{6,7},{7,8},{8,9},{9,10},{10,1... | collective-permute-start | bytes 221192 | tf_op jit(solution)/shard_map/ppermute | solution.py:231
  88.2 5.2 %collective-permute-start.6 = (bf16[2,16,8,144]{3,2,1,0:T(8,128)(2,1)S(1)}, bf16[2,16,8,144]{3,2,1,0:T(8,128)(2,1)S(1)}, u32[]{:S(2)}, u32[]{:S(2)}) collective-permute-start(bf16[2,16,8,144]{3,2,1,0:T(8,128)(2,1)S(1)} %bitcast.12), channel_id=1, source_target_pairs={{1,0},{2,1},{3,2},{4,3},{5,4},{6,5},{7,6},{8,7},{9,8},{10,9},{11,1... | collective-permute-start | bytes 221192 | tf_op jit(solution)/shard_map/ppermute | solution.py:230
  93.5 6.9 %shard_map.69.near_ref = f32[16,128,128]{2,1,0:T(8,128)S(1)} custom-call(s32[16]{0:T(128)S(1)} %copy-done.15, bf16[2,4,256,144]{3,2,1,0:T(8,128)(2,1)S(1)} %copy-done.6, bf16[2,4,128,256]{3,2,1,0:T(8,128)(2,1)S(1)} %copy-done.10, bf16[2,16,128,128]{3,2,1,0:T(8,128)(2,1)S(1)} %get-tuple-element.33.ratio_ref, ...), custom_call_target="tpu_custom_call" | custom-call | tf_op jit(solution)/shard_map/pallas_call | solution.py:299
  100.4 7.1 %shard_map.71 = f32[16,128,128]{2,1,0:T(8,128)} custom-call(s32[16]{0:T(128)S(1)} %copy-done.15, bf16[2,4,256,144]{3,2,1,0:T(8,128)(2,1)S(1)} %copy-done.6, bf16[2,4,16,256]{3,2,1,0:T(8,128)(2,1)S(1)} %get-tuple-element.29.far_ref, f32[16,128,128]{2,1,0:T(8,128)S(1)} %shard_map.69.near_ref, bf16[2,16,8,144]{3,2,1,0:T(8,128)(2,1)S(1)} %collective-permute-done.6.right_ref, ...), custom_call_target="tpu_custom_call" | custom-call | tf_op jit(solution)/shard_map/pallas_call | solution.py:304
  (35 shorter events, 0.4 us)
Async XLA Ops:
  1.3 13.3 %collective-permute-start.1 = (bf16[16,8,128]{2,1,0:T(8,128)(2,1)S(1)}, bf16[16,8,128]{2,1,0:T(8,128)(2,1)S(1)}, u32[]{:S(2)}, u32[]{:S(2)}) collective-permute-start(bf16[16,8,128]{2,1,0:T(8,128)(2,1)S(1)} %get-tuple-element.39), channel_id=1, source_target_pairs={{0,16},{16,32},{32,48},{48,64},{64,80},{80,96},{96,112},{1,17},{17... | collective-permute-start | bytes 98312 | tf_op jit(solution)/shard_map/ppermute | solution.py:231
  3.3 11.4 %collective-permute-start = (bf16[16,8,128]{2,1,0:T(8,128)(2,1)S(1)}, bf16[16,8,128]{2,1,0:T(8,128)(2,1)S(1)}, u32[]{:S(2)}, u32[]{:S(2)}) collective-permute-start(bf16[16,8,128]{2,1,0:T(8,128)(2,1)S(1)} %get-tuple-element.40), channel_id=1, source_target_pairs={{16,0},{32,16},{48,32},{64,48},{80,64},{96,80},{112,96},{17,1},{33... | collective-permute-start | bytes 98312 | tf_op jit(solution)/shard_map/ppermute | solution.py:230
  6.9 1.2 %copy-start = (f32[16,128,128]{2,1,0:T(8,128)S(1)}, f32[16,128,128]{2,1,0:T(8,128)}, u32[]{:S(2)}) copy-start(f32[16,128,128]{2,1,0:T(8,128)} %estimate_ref.3) | copy-start | bytes 3145732
  8.1 1.2 %copy-start.8 = (bf16[2,16,128,128]{3,2,1,0:T(8,128)(2,1)S(1)}, bf16[2,16,128,128]{3,2,1,0:T(8,128)(2,1)}, u32[]{:S(2)}) copy-start(bf16[2,16,128,128]{3,2,1,0:T(8,128)(2,1)} %measured_ref.1) | copy-start | bytes 3145732
  9.4 0.7 copy-start.11
  10.1 0.7 copy-start.13
  13.0 1.7 %copy-start.7 = (bf16[768,16,128]{2,1,0:T(8,128)(2,1)}, bf16[768,16,128]{2,1,0:T(8,128)(2,1)S(1)}, u32[]{:S(2)}) copy-start(bf16[768,16,128]{2,1,0:T(8,128)(2,1)S(1)} %get-tuple-element.31) | copy-start | bytes 9437188
  15.0 8.1 %collective-permute-start.2 = (bf16[16,8,144]{2,1,0:T(8,128)(2,1)S(1)}, bf16[16,8,144]{2,1,0:T(8,128)(2,1)S(1)}, u32[]{:S(2)}, u32[]{:S(2)}) collective-permute-start(bf16[16,8,144]{2,1,0:T(8,128)(2,1)S(1)} %get-tuple-element.24), channel_id=1, source_target_pairs={{1,0},{2,1},{3,2},{4,3},{5,4},{6,5},{7,6},{8,7},{9,8},{10,9},{11,1... | collective-permute-start | bytes 110600 | tf_op jit(solution)/shard_map/ppermute | solution.py:230
  21.1 8.3 %collective-permute-start.3 = (bf16[16,8,144]{2,1,0:T(8,128)(2,1)S(1)}, bf16[16,8,144]{2,1,0:T(8,128)(2,1)S(1)}, u32[]{:S(2)}, u32[]{:S(2)}) collective-permute-start(bf16[16,8,144]{2,1,0:T(8,128)(2,1)S(1)} %get-tuple-element.25), channel_id=1, source_target_pairs={{0,1},{1,2},{2,3},{3,4},{4,5},{5,6},{6,7},{7,8},{8,9},{9,10},{10,1... | collective-permute-start | bytes 110600 | tf_op jit(solution)/shard_map/ppermute | solution.py:231
  29.4 6.6 %copy-start.16 = (f32[2,4,2,17]{3,2,1,0:T(2,128)S(1)}, f32[2,4,2,17]{3,2,1,0:T(2,128)}, u32[]{:S(2)}) copy-start(f32[2,4,2,17]{3,2,1,0:T(2,128)} %param.8) | copy-start | bytes 3268
  29.4 7.0 %copy-start.15 = (s32[16]{0:T(128)S(1)}, s32[16]{0:T(128)}, u32[]{:S(2)}) copy-start(s32[16]{0:T(128)} %band_ref.5) | copy-start | bytes 196
  29.4 45.5 %copy-start.12 = (s32[2,64]{1,0:T(2,128)S(1)}, s32[2,64]{1,0:T(2,128)}, u32[]{:S(2)}) copy-start(s32[2,64]{1,0:T(2,128)} %shift_ref.5) | copy-start | bytes 1540
  29.4 45.5 %copy-start.14 = (s32[2,64]{1,0:T(2,128)S(1)}, s32[2,64]{1,0:T(2,128)}, u32[]{:S(2)}) copy-start(s32[2,64]{1,0:T(2,128)} %length_ref.5) | copy-start | bytes 1540
  29.4 45.5 %all-to-all-start = ((bf16[768,16,128]{2,1,0:T(8,128)(2,1)}), bf16[768,16,128]{2,1,0:T(8,128)(2,1)S(1)}, u32[]{:S(2)}, u32[]{:S(2)}) async-start(bf16[768,16,128]{2,1,0:T(8,128)(2,1)} %copy-done.7), calls=%async_computation | async-start | bytes 6291456 | tf_op jit(solution)/shard_map/all_to_all | solution.py:268
  36.4 1.2 %copy-start.1 = (f32[16,128,128]{2,1,0:T(8,128)S(1)}, f32[16,128,128]{2,1,0:T(8,128)}, u32[]{:S(2)}) copy-start(f32[16,128,128]{2,1,0:T(8,128)} %estimate_ref.3) | copy-start | bytes 3145732
  53.2 1.3 %copy-start.3 = (f32[2,16,128,128]{3,2,1,0:T(8,128)}, f32[2,16,128,128]{3,2,1,0:T(8,128)S(1)}, u32[]{:S(2)}) copy-start(f32[2,16,128,128]{3,2,1,0:T(8,128)S(1)} %get-tuple-element.32.recip_ref) | copy-start | bytes 6291460
  54.6 1.0 copy-start.5
  55.5 0.8 copy-start.9
  74.9 1.6 %copy-start.4 = (f32[2,16,128,128]{3,2,1,0:T(8,128)S(1)}, f32[2,16,128,128]{3,2,1,0:T(8,128)}, u32[]{:S(2)}) copy-start(f32[2,16,128,128]{3,2,1,0:T(8,128)} %copy-done.3) | copy-start | bytes 6291460
  77.2 16.2 %copy-start.6 = (bf16[2,4,256,144]{3,2,1,0:T(8,128)(2,1)S(1)}, bf16[2,4,256,144]{3,2,1,0:T(8,128)(2,1)}, u32[]{:S(2)}) copy-start(bf16[2,4,256,144]{3,2,1,0:T(8,128)(2,1)} %copy-done.5) | copy-start | bytes 1769476
  77.3 16.2 %copy-start.10 = (bf16[2,4,128,256]{3,2,1,0:T(8,128)(2,1)S(1)}, bf16[2,4,128,256]{3,2,1,0:T(8,128)(2,1)}, u32[]{:S(2)}) copy-start(bf16[2,4,128,256]{3,2,1,0:T(8,128)(2,1)} %copy-done.9) | copy-start | bytes 1572868
  77.3 6.7 %collective-permute-start.4 = (bf16[2,16,8,128]{3,2,1,0:T(8,128)(2,1)S(1)}, bf16[2,16,8,128]{3,2,1,0:T(8,128)(2,1)S(1)}, u32[]{:S(2)}, u32[]{:S(2)}) collective-permute-start(bf16[2,16,8,128]{3,2,1,0:T(8,128)(2,1)S(1)} %get-tuple-element.34), channel_id=1, source_target_pairs={{16,0},{32,16},{48,32},{64,48},{80,64},{96,80},{112,96},{17,1},{33... | collective-permute-start | bytes 196616 | tf_op jit(solution)/shard_map/ppermute | solution.py:230
  79.3 5.6 %collective-permute-start.5 = (bf16[2,16,8,128]{3,2,1,0:T(8,128)(2,1)S(1)}, bf16[2,16,8,128]{3,2,1,0:T(8,128)(2,1)S(1)}, u32[]{:S(2)}, u32[]{:S(2)}) collective-permute-start(bf16[2,16,8,128]{3,2,1,0:T(8,128)(2,1)S(1)} %get-tuple-element.35), channel_id=1, source_target_pairs={{0,16},{16,32},{32,48},{48,64},{64,80},{80,96},{96,112},{1,17},{17... | collective-permute-start | bytes 196616 | tf_op jit(solution)/shard_map/ppermute | solution.py:231
  83.9 16.5 %copy-start.2 = (f32[16,128,128]{2,1,0:T(8,128)S(1)}, f32[16,128,128]{2,1,0:T(8,128)}, u32[]{:S(2)}) copy-start(f32[16,128,128]{2,1,0:T(8,128)} %estimate_ref.3) | copy-start | bytes 3145732
  85.5 14.9 %collective-permute-start.7 = (bf16[2,16,8,144]{3,2,1,0:T(8,128)(2,1)S(1)}, bf16[2,16,8,144]{3,2,1,0:T(8,128)(2,1)S(1)}, u32[]{:S(2)}, u32[]{:S(2)}) collective-permute-start(bf16[2,16,8,144]{3,2,1,0:T(8,128)(2,1)S(1)} %bitcast.13), channel_id=1, source_target_pairs={{0,1},{1,2},{2,3},{3,4},{4,5},{5,6},{6,7},{7,8},{8,9},{9,10},{10,1... | collective-permute-start | bytes 221192 | tf_op jit(solution)/shard_map/ppermute | solution.py:231
  88.2 12.1 %collective-permute-start.6 = (bf16[2,16,8,144]{3,2,1,0:T(8,128)(2,1)S(1)}, bf16[2,16,8,144]{3,2,1,0:T(8,128)(2,1)S(1)}, u32[]{:S(2)}, u32[]{:S(2)}) collective-permute-start(bf16[2,16,8,144]{3,2,1,0:T(8,128)(2,1)S(1)} %bitcast.12), channel_id=1, source_target_pairs={{1,0},{2,1},{3,2},{4,3},{5,4},{6,5},{7,6},{8,7},{9,8},{10,9},{11,1... | collective-permute-start | bytes 221192 | tf_op jit(solution)/shard_map/ppermute | solution.py:230

commit v2 on v1

v2 whole, which is shorter than its diff:
```python
import functools

import jax
import jax.numpy as jnp
from jax import lax
from jax.experimental import pallas as pl
from jax.experimental.pallas import tpu as pltpu
from jax.sharding import PartitionSpec as P

HW = 8
CAP = 3
LANES = 256
F32 = jnp.float32
BF16 = jnp.bfloat16

VMEM = pl.BlockSpec(memory_space=pltpu.VMEM)
SMEM = pl.BlockSpec(memory_space=pltpu.SMEM)
HBM = pl.BlockSpec(memory_space=pltpu.HBM)
NN = ((1,), (0,))
NT = ((1,), (1,))


def call(kernel, ins, out_shape, scratch=()):
    return pl.pallas_call(
        kernel,
        in_specs=ins,
        out_specs=jax.tree.map(lambda _: VMEM, out_shape),
        out_shape=out_shape,
        scratch_shapes=list(scratch),
        compiler_params=pltpu.CompilerParams(vmem_limit_bytes=16 * 2**20),
    )


def dot(a, b, dims=NN):
    return lax.dot_general(a, b, (dims, ((), ())), preferred_element_type=F32)


def split(x):
    high = x.astype(BF16)
    return high, (x - high.astype(F32)).astype(BF16)


def stacked(x, axis):
    return jnp.concatenate(split(x), axis=axis)


def halves(x):
    n = x.shape[0] // 2
    return x[:n] + x[n:]


def quarters(x):
    n, m = x.shape[0] // 2, x.shape[1] // 2
    return x[:n, :m] + (x[n:, :m] + x[:n, m:])


def halo(odd_ref, first, second):
    first, second = first.astype(F32), second.astype(F32)
    odd = odd_ref[0] == 1
    after = jnp.where(odd, second, first)
    before = jnp.where(odd, first, second)
    return jnp.concatenate([after, before], axis=0).astype(BF16)


def edge_picker(cols):
    lane = lax.broadcasted_iota(jnp.int32, (2 * HW, cols), 1)
    sub = lax.broadcasted_iota(jnp.int32, (2 * HW, cols), 0)
    return (lane == jnp.where(sub < HW, sub, sub + cols - 2 * HW)).astype(BF16)


def pack_kernel(
    devices, me_ref, shift_hbm, length_hbm, measured_hbm, _, out_ref, rows_ref, measured_ref, shift_ref, length_ref, sems
):
    views, depth, tile_rows, tile_cols = measured_ref.shape
    groups = shift_ref.shape[1]
    loads = [pltpu.make_async_copy(measured_hbm.at[v], measured_ref.at[v], sems.at[v]) for v in range(views)]
    tables = [
        pltpu.make_async_copy(shift_hbm, shift_ref, sems.at[views]),
        pltpu.make_async_copy(length_hbm, length_ref, sems.at[views + 1]),
    ]
    for copy in loads + tables:
        copy.start()
    rows_ref[:, tile_rows:] = jnp.zeros((views, rows_ref.shape[1] - tile_rows) + rows_ref.shape[2:], BF16)
    lane = lax.broadcasted_iota(jnp.int32, (tile_cols, tile_cols), 1)
    sub = lax.broadcasted_iota(jnp.int32, (tile_cols, tile_cols), 0)
    turn = (lane + sub == tile_cols - 1).astype(BF16)
    me = me_ref[0]
    for view in range(views):
        loads[view].wait()
        for r0 in range(0, tile_rows, 16):
            x = measured_ref[view, :, r0 : r0 + 16, :]
            if view % 2 == 1:
                x = dot(x.reshape(depth * 16, tile_cols), turn).reshape(depth, 16, tile_cols)
            x = jnp.transpose(x.astype(F32), (1, 0, 2))
            rows_ref[view, r0 : r0 + 16] = x.astype(BF16)
        if view == 0:
            for copy in tables:
                copy.wait()

        def group(g, start, view=view):
            base = lax.rem(me + shift_ref[view, g], devices) * (views * CAP) + view * CAP
            for k in range(CAP):
                out_ref[base + k] = rows_ref[view, start + k]
            return start + length_ref[view, g]

        lax.fori_loop(0, groups, group, 0, unroll=4)


def cols_kernel(cells_ref, out_ref):
    pick = edge_picker(cells_ref.shape[-1])
    for z in range(cells_ref.shape[0]):
        out_ref[z] = dot(pick, cells_ref[z].astype(BF16), NT).astype(BF16)


def slab_kernel(odd_x_ref, odd_y_ref, cols_ref, even_ref, odd_ref, first_ref, second_ref):
    tile_rows = cols_ref.shape[-1]
    pick = edge_picker(even_ref.shape[-1])
    odd = odd_y_ref[0] == 1

    def plane(i, carry):
        ends = halo(odd_x_ref, even_ref[i], odd_ref[i])
        corner = dot(pick, ends, NT)
        cols = cols_ref[i].astype(F32)
        for ref, flag in ((first_ref, odd), (second_ref, jnp.logical_not(odd))):
            ref[i, :, :tile_rows] = jnp.where(flag, cols[:HW], cols[HW:]).astype(BF16)
            ref[i, :, tile_rows:] = jnp.where(flag, corner[:HW], corner[HW:]).astype(BF16)
        return carry

    lax.fori_loop(0, cols_ref.shape[0], plane, 0, unroll=8)


def edges_kernel(
    devices, tile_rows, me_ref, odd_ref, shift_ref, length_ref, arrived_ref, recip_ref, first_ref, second_ref, rows_ref
):
    views = recip_ref.shape[0]
    odd = odd_ref[0] == 1
    groups = shift_ref.shape[1]
    me = me_ref[0]
    low = tile_rows - CAP * HW
    for view in range(views):
        ending = tile_rows - low
        for g in range(groups - HW, groups):
            ending = ending - length_ref[view, g]
        for side, (first, start) in enumerate(((0, 0), (groups - HW, ending))):
            for g in range(first, first + HW):
                source = lax.rem(me - shift_ref[view, g] + devices, devices)
                base = source * (views * CAP) + view * CAP
                for k in range(CAP):
                    rows_ref[view, side, start + k] = arrived_ref[base + k].astype(F32)
                start = start + length_ref[view, g]
        head = jnp.transpose(rows_ref[view, 0, :HW], (1, 0, 2)) * recip_ref[view, :, :HW]
        tail = rows_ref[view, 1, (CAP - 1) * HW : CAP * HW]
        tail = jnp.transpose(tail, (1, 0, 2)) * recip_ref[view, :, HW:]
        first_ref[view] = jnp.where(odd, head, tail).astype(BF16)
        second_ref[view] = jnp.where(odd, tail, head).astype(BF16)


def unpack_kernel(devices, me_ref, shift_ref, length_ref, arrived_ref, recip_ref, out_ref, cols_ref, rows_ref):
    views, depth, tile_rows, tile_cols = out_ref.shape
    groups = shift_ref.shape[1]
    me = me_ref[0]
    pick = edge_picker(tile_cols)
    for view in range(views):

        def group(g, start, view=view):
            source = lax.rem(me - shift_ref[view, g] + devices, devices)
            base = source * (views * CAP) + view * CAP
            for k in range(CAP):
                rows_ref[view, start + k] = arrived_ref[base + k].astype(F32)
            return start + length_ref[view, g]

        lax.fori_loop(0, groups, group, 0, unroll=4)
        for r0 in range(0, tile_rows, 16):
            x = jnp.transpose(rows_ref[view, r0 : r0 + 16], (1, 0, 2))
            out_ref[view, :, r0 : r0 + 16, :] = (x * recip_ref[view, :, r0 : r0 + 16, :]).astype(BF16)
        for z in range(depth):
            cols_ref[view, z] = dot(pick, out_ref[view, z], NT).astype(BF16)


def band(taps, size):
    wide = jnp.broadcast_to(taps, (size, LANES))
    inner = pltpu.roll(wide, LANES - HW, 1, stride=1, stride_axis=0)
    before = pltpu.roll(wide, size + HW, 1, stride=1, stride_axis=0)
    lane = lax.broadcasted_iota(jnp.int32, (size, LANES), 1)
    return jnp.where(lane < size + HW, inner, jnp.where(lane < size + 2 * HW, before, 0.0))


def blur_far(rows, far, across):
    return quarters(dot(stacked(halves(dot(rows, far, NT)), 0), across))


def forward_kernel(
    band_ref, odd_x_ref, odd_y_ref, taps_ref, cells_ref, even_x_ref, other_x_ref, even_y_ref, other_y_ref,
    recip_ref, edge_ref, rows_ref, ends_ref, cols_ref, turned_ref, far_ref, fwd_rows, fwd_cols, fwd_far,
):
    views, depth, tile_rows, tile_cols = recip_ref.shape
    bands = taps_ref.shape[2]
    for view in range(views):
        for b in range(bands):
            along = band(taps_ref[0, view, b, 0:1, :], tile_rows)
            fwd_rows[view, b] = stacked(along[:, : tile_rows + 2 * HW], 0)
            across = band(taps_ref[0, view, b, 1:2, :], tile_cols)
            fwd_cols[view, b] = stacked(across[:, :tile_cols].T, 1)
            fwd_far[view, b] = stacked(across[:, tile_cols:].T[: 2 * HW], 1)
    for b in range(bands):
        ends = jnp.zeros((tile_rows, LANES - tile_rows), F32)
        for view in range(views):
            along = band(taps_ref[1, view, b, 0:1, :], tile_rows)
            rows_ref[b, :, view * tile_rows : (view + 1) * tile_rows] = stacked(along[:, :tile_rows], 0)
            beyond = along[:, tile_rows:]
            ends = ends + (pltpu.roll(beyond, 2 * HW * view, 1) if view else beyond)
            turned_ref[view, b, :tile_rows] = stacked(along[:, :tile_rows].T, 1)
            turned_ref[view, b, tile_rows:] = stacked(beyond.T[: 2 * HW], 1)
            across = band(taps_ref[1, view, b, 1:2, :], tile_cols)
            cols_ref[view, b] = stacked(across[:, :tile_cols].T, 1)
            high, low = split(across[:, tile_cols:].T[: 2 * HW])
            far_ref[b, view] = jnp.concatenate([high, high, low], axis=0)
        ends = jnp.concatenate([ends[:HW], ends[tile_rows - HW :]], axis=0)
        ends_ref[b] = stacked(ends[:, : 2 * HW * views], 0)

    def plane(z, carry):
        b = band_ref[z]
        cells = stacked(cells_ref[z], 1)
        ends = halo(odd_x_ref, even_x_ref[z], other_x_ref[z])
        far = halo(odd_y_ref, even_y_ref[z], other_y_ref[z])
        for view in range(views):
            rows = fwd_rows[view, b]
            blurred = quarters(dot(rows[:, :tile_rows], cells)) + halves(dot(rows[:, tile_rows:], ends))
            blurred = quarters(dot(stacked(blurred, 0), fwd_cols[view, b])) + blur_far(rows, far, fwd_far[view, b])
            recip = 1.0 / blurred.astype(BF16).astype(F32)
            recip_ref[view, z] = recip
            edge_ref[view, z, :HW] = recip[:HW]
            edge_ref[view, z, HW:] = recip[tile_rows - HW :]
        return carry

    lax.fori_loop(0, depth, plane, 0, unroll=2)


def near_kernel(band_ref, odd_ref, rows_ref, ends_ref, cols_ref, ratio_ref, even_ref, other_ref, out_ref):
    views, depth, tile_rows, tile_cols = ratio_ref.shape

    def plane(z, carry):
        b = band_ref[z]
        inner, outer = [], []
        for view in range(views):
            ends = halo(odd_ref, even_ref[view, z], other_ref[view, z])
            blurred = dot(jnp.concatenate([ratio_ref[view, z], ends], axis=0), cols_ref[view, b])
            blurred = stacked(blurred[:, :tile_cols] + blurred[:, tile_cols:], 1)
            inner.append(blurred[:tile_rows])
            outer.append(blurred[tile_rows:])
        out_ref[z] = quarters(dot(rows_ref[b], jnp.concatenate(inner, axis=0)))
        ends = quarters(dot(ends_ref[b], jnp.concatenate(outer, axis=0)))
        out_ref[z, :HW] += ends[:HW]
        out_ref[z, tile_rows - HW :] += ends[HW:]
        return carry

    lax.fori_loop(0, depth, plane, 0, unroll=4)


def far_kernel(band_ref, odd_ref, turned_ref, far_ref, near_ref, even_ref, other_ref, estimate_ref, out_ref, slab_ref, along_ref):
    views, bands = turned_ref.shape[:2]
    depth, tile_rows, tile_cols = near_ref.shape
    for view in range(views):
        for z in range(depth):
            slab_ref[z * 2 * HW : (z + 1) * 2 * HW] = halo(odd_ref, even_ref[view, z], other_ref[view, z])
        for b in range(bands):
            along = dot(slab_ref[...], turned_ref[view, b])
            along_ref[view, b] = along[:, :tile_rows] + along[:, tile_rows:]

    def plane(z, carry):
        b = band_ref[z]
        parts = []
        for view in range(views):
            high, low = split(along_ref[view, b, pl.ds(pl.multiple_of(z * 2 * HW, 2 * HW), 2 * HW), :])
            parts += [high, low, high]
        across = far_ref[b].reshape(views * 6 * HW, tile_cols)
        total = near_ref[z] + dot(jnp.concatenate(parts, axis=0), across, ((0,), (0,)))
        out_ref[z] = estimate_ref[z] * (total * (1.0 / views))
        return carry

    lax.fori_loop(0, depth, plane, 0, unroll=4)


def swap(first, second, axis):
    count = lax.axis_size(axis)
    pairs = lambda begin: [p for i in range(begin, count - 1, 2) for p in ((i, i + 1), (i + 1, i))]
    return lax.ppermute(first, axis, pairs(0)), lax.ppermute(second, axis, pairs(1))


def slabs(odd_x, odd_y, cols, first, second):
    lead = cols.shape[:-2]
    shape = (cols.size // (cols.shape[-1] * cols.shape[-2]), HW, cols.shape[-1] + 2 * HW)
    merge = lambda x: x.reshape((shape[0],) + x.shape[-2:])
    out = jax.ShapeDtypeStruct(shape, BF16)
    pair = call(slab_kernel, [SMEM] * 2 + [VMEM] * 3, (out, out))(odd_x, odd_y, merge(cols), merge(first), merge(second))
    return [x.reshape(lead + shape[1:]) for x in pair]


def body(estimate, measured, kernels, depth_band, group_shift, group_length):
    devices = lax.axis_size("gx") * lax.axis_size("gy")
    gx, gy = lax.axis_index("gx").astype(jnp.int32), lax.axis_index("gy").astype(jnp.int32)
    me = (gx * lax.axis_size("gy") + gy).reshape(1)
    odd_x, odd_y = (gx % 2).reshape(1), (gy % 2).reshape(1)
    views, depth, tile_rows, tile_cols = measured.shape
    bands = kernels.shape[1]
    spare = tile_rows + 8
    like = jax.ShapeDtypeStruct
    whole = like(measured.shape, BF16)
    edge_cols = like((views, depth, 2 * HW, tile_rows), BF16)
    edge_rows = like((views, depth, HW, tile_cols), BF16)

    head, tail = estimate[:, :HW], estimate[:, tile_rows - HW :]
    even = gx % 2 == 0
    ex, ox = swap(jnp.where(even, tail, head), jnp.where(even, head, tail), "gx")
    cols = call(cols_kernel, [VMEM], like(edge_cols.shape[1:], BF16))(estimate)
    edges = slabs(odd_x, odd_y, cols, ex, ox)
    ey, oy = swap(*edges, "gy")
    outgoing = call(
        functools.partial(pack_kernel, devices),
        [SMEM, HBM, HBM, HBM, VMEM],
        like((devices * views * CAP, depth, tile_cols), BF16),
        [
            pltpu.VMEM((views, spare, depth, tile_cols), BF16),
            pltpu.VMEM(measured.shape, BF16),
            pltpu.SMEM(group_shift.shape, jnp.int32),
            pltpu.SMEM(group_length.shape, jnp.int32),
            pltpu.SemaphoreType.DMA((views + 2,)),
        ],
    )(me, group_shift, group_length, measured, edges[0])
    outgoing, ey, oy = lax.optimization_barrier((outgoing, ey, oy))
    arrived = lax.all_to_all(outgoing, ("gx", "gy"), split_axis=0, concat_axis=0, tiled=True)

    norm = kernels / jnp.sum(kernels, axis=3, keepdims=True)
    tap_rows = jnp.stack([norm, norm[..., ::-1]])
    tap_rows = jnp.pad(tap_rows, ((0, 0),) * 4 + ((0, LANES - kernels.shape[3]),))
    recip, edge_recip, rows_mat, ends_mat, cols_mat, turned_mat, far_mat = call(
        forward_kernel,
        [SMEM] * 3 + [VMEM] * 6,
        (
            like(measured.shape, F32),
            like((views, depth, 2 * HW, tile_cols), F32),
            like((bands, 2 * tile_rows, views * tile_rows), BF16),
            like((bands, 4 * HW, views * 2 * HW), BF16),
            like((views, bands, tile_cols, 2 * tile_cols), BF16),
            like((views, bands, tile_rows + 2 * HW, 2 * tile_rows), BF16),
            like((bands, views, 6 * HW, tile_cols), BF16),
        ),
        [
            pltpu.VMEM((views, bands, 2 * tile_rows, tile_rows + 2 * HW), BF16),
            pltpu.VMEM((views, bands, tile_cols, 2 * tile_cols), BF16),
            pltpu.VMEM((views, bands, 2 * HW, 2 * tile_cols), BF16),
        ],
    )(depth_band, odd_x, odd_y, tap_rows, estimate, ex, ox, ey, oy)

    ex, ox = swap(
        *call(
            functools.partial(edges_kernel, devices, tile_rows),
            [SMEM] * 4 + [VMEM] * 2,
            (edge_rows, edge_rows),
            [pltpu.VMEM((views, 2, CAP * HW + 8, depth, tile_cols), F32)],
        )(me, odd_x, group_shift, group_length, arrived, edge_recip),
        "gx",
    )
    ratio, cols = call(
        functools.partial(unpack_kernel, devices),
        [SMEM, SMEM, SMEM, VMEM, VMEM],
        (whole, edge_cols),
        [pltpu.VMEM((views, spare, depth, tile_cols), F32)],
    )(me, group_shift, group_length, arrived, recip)
    ey, oy = swap(*slabs(odd_x, odd_y, cols, ex, ox), "gy")
    near = call(
        near_kernel,
        [SMEM] * 2 + [VMEM] * 6,
        like(estimate.shape, F32),
    )(depth_band, odd_x, rows_mat, ends_mat, cols_mat, ratio, ex, ox)
    return call(
        far_kernel,
        [SMEM] * 2 + [VMEM] * 6,
        like(estimate.shape, F32),
        [
            pltpu.VMEM((depth * 2 * HW, tile_rows + 2 * HW), BF16),
            pltpu.VMEM((views, bands, depth * 2 * HW, tile_rows), F32),
        ],
    )(depth_band, odd_y, turned_mat, far_mat, near, ey, oy, estimate)


def solution(mesh):
    return jax.shard_map(
        body,
        mesh=mesh,
        in_specs=(P(None, "gx", "gy"), P(None, None, "gx", "gy"), P(), P(), P(), P()),
        out_specs=P(None, "gx", "gy"),
        check_vma=False,
    )
```

time: 110 us -> 89.8 us (0.82)
  the two profiles are of different devices: /device:TPU:30 before, /device:TPU:9 now
where the time goes in v2:
time: 89.8 us; the launch traced here: 89.3 us
  Pallas kernels  27.8 us (31%)
  starting transfers between devices  26.7 us (30%)
  waiting for transfers between devices  18.6 us (21%)
  local copies, waits for them, and re-layouts  14.7 us (16%)
  other arithmetic  1.16 us (1%)
    all_to_all x1, waiting for transfers between devices, body(): lax.all_to_all(outgoing, ('gx', 'gy'), split_axis=0, concat_axis=0, tiled...  17 us
    ppermute x4, starting transfers between devices, swap(): lax.ppermute(second, axis, pairs(1))  15.1 us
    unnamed x54, local copies, waits for them, and re-layouts  14.6 us
    pallas_call x1, Pallas kernels, body(): call(forward_kernel, [SMEM] * 3 + [VMEM] * 6, (like(measured.shape, F32),...  13.9 us
    all_to_all x1, starting transfers between devices, body(): lax.all_to_all(outgoing, ('gx', 'gy'), split_axis=0, concat_axis=0, tiled...  9.08 us
    pallas_call x1, Pallas kernels, body(): call(near_kernel, [SMEM] * 2 + [VMEM] * 6, like(estimate.shape, F32))  4.96 us
    pallas_call x1, Pallas kernels, body(): call(far_kernel, [SMEM] * 2 + [VMEM] * 6, like(estimate.shape, F32), [plt...  2.85 us
    ppermute x4, starting transfers between devices, swap(): lax.ppermute(first, axis, pairs(0))  2.6 us
  transfers between devices with their start and end apart: 9, of which 3 were waited for; matrix products, arithmetic and copies ran while one was open for 0% of the time, Pallas kernels for 26%

profile of v2, /device:TPU:9, one launch (start us, length us, event | category | flops | bytes accessed | tf_op | source)
XLA Modules:
  0.0 89.3 jit_solution(11504733658850896093)
XLA Ops:
  0.0 0.9 slice_select_fusion
  0.9 3.7 %collective-permute-start.1 = (f32[16,8,128]{2,1,0:T(8,128)S(1)}, f32[16,8,128]{2,1,0:T(8,128)S(1)}, u32[]{:S(2)}, u32[]{:S(2)}) collective-permute-start(f32[16,8,128]{2,1,0:T(8,128)S(1)} %get-tuple-element.41), channel_id=1, source_target_pairs={{16,32},{32,16},{48,64},{64,48},{80,96},{96,80},{17,33},{33,17},{4... | collective-permute-start | bytes 196616 | tf_op jit(solution)/shard_map/ppermute | solution.py:287
  4.7 1.2 %copy-done.1 = f32[16,128,128]{2,1,0:T(8,128)S(1)} copy-done((f32[16,128,128]{2,1,0:T(8,128)S(1)}, f32[16,128,128]{2,1,0:T(8,128)}, u32[]{:S(2)}) %copy-start.1) | copy-done | bytes 1048600
  6.8 5.5 %collective-permute-start.3 = (bf16[16,8,144]{2,1,0:T(8,128)(2,1)S(1)}, bf16[16,8,144]{2,1,0:T(8,128)(2,1)S(1)}, u32[]{:S(2)}, u32[]{:S(2)}) collective-permute-start(bf16[16,8,144]{2,1,0:T(8,128)(2,1)S(1)} %get-tuple-element.24), channel_id=1, source_target_pairs={{1,2},{2,1},{3,4},{4,3},{5,6},{6,5},{7,8},{8,7},{9,10},{10,9},{11,... | collective-permute-start | bytes 110600 | tf_op jit(solution)/shard_map/ppermute | solution.py:287
  12.5 1.2 %copy-done.6 = bf16[2,16,128,128]{3,2,1,0:T(8,128)(2,1)S(1)} copy-done((bf16[2,16,128,128]{3,2,1,0:T(8,128)(2,1)S(1)}, bf16[2,16,128,128]{3,2,1,0:T(8,128)(2,1)}, u32[]{:S(2)}) %copy-start.6) | copy-done | bytes 1048600
  13.7 0.7 copy-done.21
  14.4 0.7 copy-done.23
  15.1 1.8 %shard_map.66 = bf16[768,16,128]{2,1,0:T(8,128)(2,1)S(1)} custom-call(s32[1]{0:T(128)} %bitcast.4.me_ref, s32[2,64]{1,0:T(2,128)S(1)} %copy-done.21, s32[2,64]{1,0:T(2,128)S(1)} %copy-done.23, bf16[2,16,128,128]{3,2,1,0:T(8,128)(2,1)S(1)} %copy-done.6, bf16[16,8,144]{2,1,0:T(8,128)(2,1)S(1)} %get-tuple-element.23._), custom_call_target="tpu_custom_call" | custom-call | tf_op jit(solution)/shard_map/pallas_call | solution.py:318
  16.8 1.6 %copy-done = bf16[768,16,128]{2,1,0:T(8,128)(2,1)} copy-done((bf16[768,16,128]{2,1,0:T(8,128)(2,1)}, bf16[768,16,128]{2,1,0:T(8,128)(2,1)S(1)}, u32[]{:S(2)}) %copy-start) | copy-done | bytes 3145752
  18.5 0.6 copy-done.15
  19.1 0.6 copy-done.17
  19.7 9.1 %all-to-all-start = ((bf16[768,16,128]{2,1,0:T(8,128)(2,1)}), bf16[768,16,128]{2,1,0:T(8,128)(2,1)S(1)}, u32[]{:S(2)}, u32[]{:S(2)}) async-start(bf16[768,16,128]{2,1,0:T(8,128)(2,1)} %copy-done), calls=%async_computation | async-start | bytes 6291456 | tf_op jit(solution)/shard_map/all_to_all | solution.py:331
  29.3 1.2 %copy-done.2 = f32[16,128,128]{2,1,0:T(8,128)S(1)} copy-done((f32[16,128,128]{2,1,0:T(8,128)S(1)}, f32[16,128,128]{2,1,0:T(8,128)}, u32[]{:S(2)}) %copy-start.2) | copy-done | bytes 1048600
  30.5 0.8 copy-done.16
  31.3 0.8 copy-done.18
  32.1 13.9 %shard_map.67 = (f32[2,16,128,128]{3,2,1,0:T(8,128)S(1)}, f32[2,16,16,128]{3,2,1,0:T(8,128)S(1)}, bf16[4,256,256]{2,1,0:T(8,128)(2,1)S(1)}, bf16[4,32,32]{2,1,0:...) custom-call(s32[16]{0:T(128)S(1)} %copy-done.25, ...), custom_call_target="tpu_custom_call" | custom-call | tf_op jit(solution)/shard_map/pallas_call | solution.py:336
  46.1 1.3 %copy-done.4 = f32[2,16,128,128]{3,2,1,0:T(8,128)} copy-done((f32[2,16,128,128]{3,2,1,0:T(8,128)}, f32[2,16,128,128]{3,2,1,0:T(8,128)S(1)}, u32[]{:S(2)}) %copy-start.4) | copy-done | bytes 2097176
  47.4 0.8 copy-done.7
  48.2 0.8 copy-done.9
  49.0 0.8 copy-done.11
  49.8 0.6 copy-done.13
  50.5 0.6 copy-done.19
  51.1 17.0 %all-to-all-done.arrived_ref = bf16[768,16,128]{2,1,0:T(8,128)(2,1)S(1)} async-done(((bf16[768,16,128]{2,1,0:T(8,128)(2,1)}), bf16[768,16,128]{2,1,0:T(8,128)(2,1)S(1)}, u32[]{:S(2)}, u32[]{:S(2)}) %all-to-all-start) | async-done | bytes 3145760 | tf_op jit(solution)/shard_map/all_to_all | solution.py:331
  68.1 0.7 shard_map.69
  68.8 2.3 %collective-permute-start.4 = (bf16[2,16,8,128]{3,2,1,0:T(8,128)(2,1)S(1)}, bf16[2,16,8,128]{3,2,1,0:T(8,128)(2,1)S(1)}, u32[]{:S(2)}, u32[]{:S(2)}) collective-permute-start(bf16[2,16,8,128]{3,2,1,0:T(8,128)(2,1)S(1)} %get-tuple-element.36), channel_id=1, source_target_pairs={{0,16},{16,0},{32,48},{48,32},{64,80},{80,64},{96,112},{112,96},{1... | collective-permute-start | bytes 196616 | tf_op jit(solution)/shard_map/ppermute | solution.py:287
  71.2 1.9 %collective-permute-start.5 = (bf16[2,16,8,128]{3,2,1,0:T(8,128)(2,1)S(1)}, bf16[2,16,8,128]{3,2,1,0:T(8,128)(2,1)S(1)}, u32[]{:S(2)}, u32[]{:S(2)}) collective-permute-start(bf16[2,16,8,128]{3,2,1,0:T(8,128)(2,1)S(1)} %get-tuple-element.37), channel_id=1, source_target_pairs={{16,32},{32,16},{48,64},{64,48},{80,96},{96,80},{17,33},{33,17},{4... | collective-permute-start | bytes 196616 | tf_op jit(solution)/shard_map/ppermute | solution.py:287
  73.1 2.3 %shard_map.68 = (bf16[2,16,128,128]{3,2,1,0:T(8,128)(2,1)S(1)}, bf16[2,16,16,128]{3,2,1,0:T(8,128)(2,1)S(1)}) custom-call(s32[1]{0:T(128)} %bitcast.4.me_ref, s32[2,64]{1,0:T(2,128)S(1)} %copy-done.22, s32[2,64]{1,0:T(2,128)S(1)} %copy-done.24, bf16[768,16,128]{2,1,0:T(8,128)(2,1)S(1)} %all-to-all-done.arrived_ref, f32[2,16,128,128]{3,2,1,0:T(8,128)S(1)} %copy-done.5), custom_call_target="tpu_custom_call" | custom-call | tf_op jit(solution)/shard_map/pallas_call | solution.py:364
  75.4 1.3 %collective-permute-done.5.other_ref = bf16[2,16,8,128]{3,2,1,0:T(8,128)(2,1)S(1)} collective-permute-done((bf16[2,16,8,128]{3,2,1,0:T(8,128)(2,1)S(1)}, bf16[2,16,8,128]{3,2,1,0:T(8,128)(2,1)S(1)}, u32[]{:S(2)}, u32[]{:S(2)}) %collective-permute-start.5) | collective-permute-done | bytes 65568 | tf_op jit(solution)/shard_map/ppermute | solution.py:287
  76.8 0.6 shard_map.71
  77.4 3.9 %collective-permute-start.7 = (bf16[2,16,8,144]{3,2,1,0:T(8,128)(2,1)S(1)}, bf16[2,16,8,144]{3,2,1,0:T(8,128)(2,1)S(1)}, u32[]{:S(2)}, u32[]{:S(2)}) collective-permute-start(bf16[2,16,8,144]{3,2,1,0:T(8,128)(2,1)S(1)} %bitcast.15), channel_id=1, source_target_pairs={{1,2},{2,1},{3,4},{4,3},{5,6},{6,5},{7,8},{8,7},{9,10},{10,9},{11,... | collective-permute-start | bytes 221192 | tf_op jit(solution)/shard_map/ppermute | solution.py:287
  81.4 5.0 %shard_map.70.near_ref = f32[16,128,128]{2,1,0:T(8,128)S(1)} custom-call(s32[16]{0:T(128)S(1)} %copy-done.25, s32[1]{0:T(128)} %bitcast.1.odd_x_ref.odd_ref, bf16[4,256,256]{2,1,0:T(8,128)(2,1)S(1)} %copy-done.10, bf16[4,32,32]{2,1,0:T(8,128)(2,1)S(1)} %copy-done.20, bf16[2,4,128,256]{3,2,1,0:T(8,128)(2,1)S(1)} %copy-done.12, ...), custom_call_target="tpu_custom_call" | custom-call | tf_op jit(solution)/shard_map/pallas_call | solution.py:371
  86.4 2.9 %shard_map.72 = f32[16,128,128]{2,1,0:T(8,128)} custom-call(s32[16]{0:T(128)S(1)} %copy-done.25, s32[1]{0:T(128)} %bitcast.odd_y_ref.odd_ref, bf16[2,4,144,256]{3,2,1,0:T(8,128)(2,1)S(1)} %copy-done.8, bf16[4,2,48,128]{3,2,1,0:T(8,128)(2,1)S(1)} %copy-done.14, f32[16,128,128]{2,1,0:T(8,128)S(1)} %shard_map.70.near_ref, ...), custom_call_target="tpu_custom_call" | custom-call | tf_op jit(solution)/shard_map/pallas_call | solution.py:376
  (55 shorter events, 1.6 us)
Async XLA Ops:
  0.9 5.6 %collective-permute-start.1 = (f32[16,8,128]{2,1,0:T(8,128)S(1)}, f32[16,8,128]{2,1,0:T(8,128)S(1)}, u32[]{:S(2)}, u32[]{:S(2)}) collective-permute-start(f32[16,8,128]{2,1,0:T(8,128)S(1)} %get-tuple-element.41), channel_id=1, source_target_pairs={{16,32},{32,16},{48,64},{64,48},{80,96},{96,80},{17,33},{33,17},{4... | collective-permute-start | bytes 196616 | tf_op jit(solution)/shard_map/ppermute | solution.py:287
  4.6 1.9 %collective-permute-start = (f32[16,8,128]{2,1,0:T(8,128)S(1)}, f32[16,8,128]{2,1,0:T(8,128)S(1)}, u32[]{:S(2)}, u32[]{:S(2)}) collective-permute-start(f32[16,8,128]{2,1,0:T(8,128)S(1)} %get-tuple-element.42), channel_id=1, source_target_pairs={{0,16},{16,0},{32,48},{48,32},{64,80},{80,64},{96,112},{112,96},{1... | collective-permute-start | bytes 196616 | tf_op jit(solution)/shard_map/ppermute | solution.py:287
  4.7 1.2 %copy-start.1 = (f32[16,128,128]{2,1,0:T(8,128)S(1)}, f32[16,128,128]{2,1,0:T(8,128)}, u32[]{:S(2)}) copy-start(f32[16,128,128]{2,1,0:T(8,128)} %estimate_ref.1) | copy-start | bytes 3145732
  6.8 11.7 %collective-permute-start.3 = (bf16[16,8,144]{2,1,0:T(8,128)(2,1)S(1)}, bf16[16,8,144]{2,1,0:T(8,128)(2,1)S(1)}, u32[]{:S(2)}, u32[]{:S(2)}) collective-permute-start(bf16[16,8,144]{2,1,0:T(8,128)(2,1)S(1)} %get-tuple-element.24), channel_id=1, source_target_pairs={{1,2},{2,1},{3,4},{4,3},{5,6},{6,5},{7,8},{8,7},{9,10},{10,9},{11,... | collective-permute-start | bytes 110600 | tf_op jit(solution)/shard_map/ppermute | solution.py:287
  12.4 6.7 %collective-permute-start.2 = (bf16[16,8,144]{2,1,0:T(8,128)(2,1)S(1)}, bf16[16,8,144]{2,1,0:T(8,128)(2,1)S(1)}, u32[]{:S(2)}, u32[]{:S(2)}) collective-permute-start(bf16[16,8,144]{2,1,0:T(8,128)(2,1)S(1)} %get-tuple-element.23._), channel_id=1, source_target_pairs={{0,1},{1,0},{2,3},{3,2},{4,5},{5,4},{6,7},{7,6},{8,9},{9,8},{10,11... | collective-permute-start | bytes 110600 | tf_op jit(solution)/shard_map/ppermute | solution.py:287
  12.5 1.2 %copy-start.6 = (bf16[2,16,128,128]{3,2,1,0:T(8,128)(2,1)S(1)}, bf16[2,16,128,128]{3,2,1,0:T(8,128)(2,1)}, u32[]{:S(2)}) copy-start(bf16[2,16,128,128]{3,2,1,0:T(8,128)(2,1)} %measured_hbm.1) | copy-start | bytes 3145732
  13.7 0.7 copy-start.21
  14.4 0.7 copy-start.23
  16.8 1.6 %copy-start = (bf16[768,16,128]{2,1,0:T(8,128)(2,1)}, bf16[768,16,128]{2,1,0:T(8,128)(2,1)S(1)}, u32[]{:S(2)}) copy-start(bf16[768,16,128]{2,1,0:T(8,128)(2,1)S(1)} %shard_map.66) | copy-start | bytes 9437188
  18.5 10.4 %copy-start.26 = (f32[2,4,2,17]{3,2,1,0:T(2,128)S(1)}, f32[2,4,2,17]{3,2,1,0:T(2,128)}, u32[]{:S(2)}) copy-start(f32[2,4,2,17]{3,2,1,0:T(2,128)} %param.8) | copy-start | bytes 3268
  18.5 10.8 %copy-start.25 = (s32[16]{0:T(128)S(1)}, s32[16]{0:T(128)}, u32[]{:S(2)}) copy-start(s32[16]{0:T(128)} %band_ref.5) | copy-start | bytes 196
  18.5 49.6 %copy-start.22 = (s32[2,64]{1,0:T(2,128)S(1)}, s32[2,64]{1,0:T(2,128)}, u32[]{:S(2)}) copy-start(s32[2,64]{1,0:T(2,128)} %shift_ref.3) | copy-start | bytes 1540
  18.5 49.6 %copy-start.24 = (s32[2,64]{1,0:T(2,128)S(1)}, s32[2,64]{1,0:T(2,128)}, u32[]{:S(2)}) copy-start(s32[2,64]{1,0:T(2,128)} %length_ref.3) | copy-start | bytes 1540
  19.7 48.3 %all-to-all-start = ((bf16[768,16,128]{2,1,0:T(8,128)(2,1)}), bf16[768,16,128]{2,1,0:T(8,128)(2,1)S(1)}, u32[]{:S(2)}, u32[]{:S(2)}) async-start(bf16[768,16,128]{2,1,0:T(8,128)(2,1)} %copy-done), calls=%async_computation | async-start | bytes 6291456 | tf_op jit(solution)/shard_map/all_to_all | solution.py:331
  29.2 1.2 %copy-start.2 = (f32[16,128,128]{2,1,0:T(8,128)S(1)}, f32[16,128,128]{2,1,0:T(8,128)}, u32[]{:S(2)}) copy-start(f32[16,128,128]{2,1,0:T(8,128)} %estimate_ref.1) | copy-start | bytes 3145732
  30.5 0.8 copy-start.16
  31.3 0.8 copy-start.18
  46.1 1.3 %copy-start.4 = (f32[2,16,128,128]{3,2,1,0:T(8,128)}, f32[2,16,128,128]{3,2,1,0:T(8,128)S(1)}, u32[]{:S(2)}) copy-start(f32[2,16,128,128]{3,2,1,0:T(8,128)S(1)} %get-tuple-element.33.recip_ref) | copy-start | bytes 6291460
  47.4 0.8 copy-start.7
  48.2 0.8 copy-start.9
  49.0 0.8 copy-start.11
  68.1 5.0 %copy-start.5 = (f32[2,16,128,128]{3,2,1,0:T(8,128)S(1)}, f32[2,16,128,128]{3,2,1,0:T(8,128)}, u32[]{:S(2)}) copy-start(f32[2,16,128,128]{3,2,1,0:T(8,128)} %copy-done.4) | copy-start | bytes 6291460
  68.8 12.6 %copy-start.10 = (bf16[4,256,256]{2,1,0:T(8,128)(2,1)S(1)}, bf16[4,256,256]{2,1,0:T(8,128)(2,1)}, u32[]{:S(2)}) copy-start(bf16[4,256,256]{2,1,0:T(8,128)(2,1)} %copy-done.9) | copy-start | bytes 1572868
  68.8 12.6 %copy-start.12 = (bf16[2,4,128,256]{3,2,1,0:T(8,128)(2,1)S(1)}, bf16[2,4,128,256]{3,2,1,0:T(8,128)(2,1)}, u32[]{:S(2)}) copy-start(bf16[2,4,128,256]{3,2,1,0:T(8,128)(2,1)} %copy-done.11) | copy-start | bytes 1572868
  68.8 12.6 %copy-start.20 = (bf16[4,32,32]{2,1,0:T(8,128)(2,1)S(1)}, bf16[4,32,32]{2,1,0:T(8,128)(2,1)}, u32[]{:S(2)}) copy-start(bf16[4,32,32]{2,1,0:T(8,128)(2,1)} %copy-done.19) | copy-start | bytes 24580
  68.8 6.6 %collective-permute-start.4 = (bf16[2,16,8,128]{3,2,1,0:T(8,128)(2,1)S(1)}, bf16[2,16,8,128]{3,2,1,0:T(8,128)(2,1)S(1)}, u32[]{:S(2)}, u32[]{:S(2)}) collective-permute-start(bf16[2,16,8,128]{3,2,1,0:T(8,128)(2,1)S(1)} %get-tuple-element.36), channel_id=1, source_target_pairs={{0,16},{16,0},{32,48},{48,32},{64,80},{80,64},{96,112},{112,96},{1... | collective-permute-start | bytes 196616 | tf_op jit(solution)/shard_map/ppermute | solution.py:287
  71.2 5.6 %collective-permute-start.5 = (bf16[2,16,8,128]{3,2,1,0:T(8,128)(2,1)S(1)}, bf16[2,16,8,128]{3,2,1,0:T(8,128)(2,1)S(1)}, u32[]{:S(2)}, u32[]{:S(2)}) collective-permute-start(bf16[2,16,8,128]{3,2,1,0:T(8,128)(2,1)S(1)} %get-tuple-element.37), channel_id=1, source_target_pairs={{16,32},{32,16},{48,64},{64,48},{80,96},{96,80},{17,33},{33,17},{4... | collective-permute-start | bytes 196616 | tf_op jit(solution)/shard_map/ppermute | solution.py:287
  73.1 13.3 %copy-start.3 = (f32[16,128,128]{2,1,0:T(8,128)S(1)}, f32[16,128,128]{2,1,0:T(8,128)}, u32[]{:S(2)}) copy-start(f32[16,128,128]{2,1,0:T(8,128)} %estimate_ref.1) | copy-start | bytes 3145732
  73.1 13.3 %copy-start.8 = (bf16[2,4,144,256]{3,2,1,0:T(8,128)(2,1)S(1)}, bf16[2,4,144,256]{3,2,1,0:T(8,128)(2,1)}, u32[]{:S(2)}) copy-start(bf16[2,4,144,256]{3,2,1,0:T(8,128)(2,1)} %copy-done.7) | copy-start | bytes 1769476
  73.1 13.3 %copy-start.14 = (bf16[4,2,48,128]{3,2,1,0:T(8,128)(2,1)S(1)}, bf16[4,2,48,128]{3,2,1,0:T(8,128)(2,1)}, u32[]{:S(2)}) copy-start(bf16[4,2,48,128]{3,2,1,0:T(8,128)(2,1)} %copy-done.13) | copy-start | bytes 294916
  77.4 9.0 %collective-permute-start.7 = (bf16[2,16,8,144]{3,2,1,0:T(8,128)(2,1)S(1)}, bf16[2,16,8,144]{3,2,1,0:T(8,128)(2,1)S(1)}, u32[]{:S(2)}, u32[]{:S(2)}) collective-permute-start(bf16[2,16,8,144]{3,2,1,0:T(8,128)(2,1)S(1)} %bitcast.15), channel_id=1, source_target_pairs={{1,2},{2,1},{3,4},{4,3},{5,6},{6,5},{7,8},{8,7},{9,10},{10,9},{11,... | collective-permute-start | bytes 221192 | tf_op jit(solution)/shard_map/ppermute | solution.py:287
  81.3 5.1 %collective-permute-start.6 = (bf16[2,16,8,144]{3,2,1,0:T(8,128)(2,1)S(1)}, bf16[2,16,8,144]{3,2,1,0:T(8,128)(2,1)S(1)}, u32[]{:S(2)}, u32[]{:S(2)}) collective-permute-start(bf16[2,16,8,144]{3,2,1,0:T(8,128)(2,1)S(1)} %bitcast.14), channel_id=1, source_target_pairs={{0,1},{1,0},{2,3},{3,2},{4,5},{5,4},{6,7},{7,6},{8,9},{9,8},{10,11... | collective-permute-start | bytes 221192 | tf_op jit(solution)/shard_map/ppermute | solution.py:287
  (4 other events, 2.5 us)

commit v3 on v2

--- a/solution.py
+++ b/solution.py
@@ -20,14 +20,14 @@
 NT = ((1,), (1,))
 
 
-def call(kernel, ins, out_shape, scratch=()):
+def call(kernel, ins, out_shape, scratch=(), out_space=VMEM, limit=16):
     return pl.pallas_call(
         kernel,
         in_specs=ins,
-        out_specs=jax.tree.map(lambda _: VMEM, out_shape),
+        out_specs=jax.tree.map(lambda _: out_space, out_shape),
         out_shape=out_shape,
         scratch_shapes=list(scratch),
-        compiler_params=pltpu.CompilerParams(vmem_limit_bytes=16 * 2**20),
+        compiler_params=pltpu.CompilerParams(vmem_limit_bytes=limit * 2**20),
     )
 
 
@@ -69,7 +69,8 @@
 
 
 def pack_kernel(
-    devices, me_ref, shift_hbm, length_hbm, measured_hbm, _, out_ref, rows_ref, measured_ref, shift_ref, length_ref, sems
+    devices, me_ref, shift_hbm, length_hbm, measured_hbm, _, out_hbm,
+    rows_ref, measured_ref, out_ref, shift_ref, length_ref, sems,
 ):
     views, depth, tile_rows, tile_cols = measured_ref.shape
     groups = shift_ref.shape[1]
@@ -78,6 +79,7 @@
         pltpu.make_async_copy(shift_hbm, shift_ref, sems.at[views]),
         pltpu.make_async_copy(length_hbm, length_ref, sems.at[views + 1]),
     ]
+    leave = [pltpu.make_async_copy(out_ref.at[v], out_hbm.at[:, v], sems.at[views + 2 + v]) for v in range(views)]
     for copy in loads + tables:
         copy.start()
     rows_ref[:, tile_rows:] = jnp.zeros((views, rows_ref.shape[1] - tile_rows) + rows_ref.shape[2:], BF16)
@@ -98,12 +100,15 @@
                 copy.wait()
 
         def group(g, start, view=view):
-            base = lax.rem(me + shift_ref[view, g], devices) * (views * CAP) + view * CAP
+            peer = lax.rem(me + shift_ref[view, g], devices)
             for k in range(CAP):
-                out_ref[base + k] = rows_ref[view, start + k]
+                out_ref[view, peer, k] = rows_ref[view, start + k]
             return start + length_ref[view, g]
 
         lax.fori_loop(0, groups, group, 0, unroll=4)
+        leave[view].start()
+    for copy in leave:
+        copy.wait()
 
 
 def cols_kernel(cells_ref, out_ref):
@@ -126,7 +131,7 @@
             ref[i, :, tile_rows:] = jnp.where(flag, corner[:HW], corner[HW:]).astype(BF16)
         return carry
 
-    lax.fori_loop(0, cols_ref.shape[0], plane, 0, unroll=8)
+    lax.fori_loop(0, cols_ref.shape[0], plane, 0, unroll=True)
 
 
 def edges_kernel(
@@ -169,7 +174,7 @@
                 rows_ref[view, start + k] = arrived_ref[base + k].astype(F32)
             return start + length_ref[view, g]
 
-        lax.fori_loop(0, groups, group, 0, unroll=4)
+        lax.fori_loop(0, groups, group, 0, unroll=True)
         for r0 in range(0, tile_rows, 16):
             x = jnp.transpose(rows_ref[view, r0 : r0 + 16], (1, 0, 2))
             out_ref[view, :, r0 : r0 + 16, :] = (x * recip_ref[view, :, r0 : r0 + 16, :]).astype(BF16)
@@ -236,49 +241,61 @@
     lax.fori_loop(0, depth, plane, 0, unroll=2)
 
 
-def near_kernel(band_ref, odd_ref, rows_ref, ends_ref, cols_ref, ratio_ref, even_ref, other_ref, out_ref):
+def near_kernel(
+    band_ref, odd_ref, rows_ref, ends_ref, cols_ref, ratio_ref, even_ref, other_ref, out_ref, inner_ref, outer_ref
+):
     views, depth, tile_rows, tile_cols = ratio_ref.shape
 
-    def plane(z, carry):
+    def across(cells, weights):
+        blurred = dot(cells, weights)
+        return stacked(blurred[:, :tile_cols] + blurred[:, tile_cols:], 1)
+
+    for z in range(depth):
         b = band_ref[z]
-        inner, outer = [], []
         for view in range(views):
+            inner_ref[z, view * tile_rows : (view + 1) * tile_rows] = across(ratio_ref[view, z], cols_ref[view, b])
             ends = halo(odd_ref, even_ref[view, z], other_ref[view, z])
-            blurred = dot(jnp.concatenate([ratio_ref[view, z], ends], axis=0), cols_ref[view, b])
-            blurred = stacked(blurred[:, :tile_cols] + blurred[:, tile_cols:], 1)
-            inner.append(blurred[:tile_rows])
-            outer.append(blurred[tile_rows:])
-        out_ref[z] = quarters(dot(rows_ref[b], jnp.concatenate(inner, axis=0)))
-        ends = quarters(dot(ends_ref[b], jnp.concatenate(outer, axis=0)))
+            outer_ref[z, view * 2 * HW : (view + 1) * 2 * HW] = across(ends, cols_ref[view, b])
+    for z in range(depth):
+        b = band_ref[z]
+        out_ref[z] = quarters(dot(rows_ref[b], inner_ref[z]))
+        ends = quarters(dot(ends_ref[b], outer_ref[z]))
         out_ref[z, :HW] += ends[:HW]
         out_ref[z, tile_rows - HW :] += ends[HW:]
-        return carry
-
-    lax.fori_loop(0, depth, plane, 0, unroll=4)
-
-
-def far_kernel(band_ref, odd_ref, turned_ref, far_ref, near_ref, even_ref, other_ref, estimate_ref, out_ref, slab_ref, along_ref):
+
+
+def far_kernel(
+    band_ref, odd_ref, turned_ref, far_ref, near_ref, even_ref, other_ref, estimate_ref, out_hbm,
+    slab_ref, along_ref, out_ref, sems,
+):
     views, bands = turned_ref.shape[:2]
     depth, tile_rows, tile_cols = near_ref.shape
+    step = depth // sems.shape[0]
     for view in range(views):
         for z in range(depth):
-            slab_ref[z * 2 * HW : (z + 1) * 2 * HW] = halo(odd_ref, even_ref[view, z], other_ref[view, z])
+            slab_ref[view, z * 2 * HW : (z + 1) * 2 * HW] = halo(odd_ref, even_ref[view, z], other_ref[view, z])
+    for view in range(views):
         for b in range(bands):
-            along = dot(slab_ref[...], turned_ref[view, b])
-            along_ref[view, b] = along[:, :tile_rows] + along[:, tile_rows:]
-
-    def plane(z, carry):
+            along = dot(slab_ref[view], turned_ref[view, b])
+            high, low = split(along[:, :tile_rows] + along[:, tile_rows:])
+            along_ref[view, b, 0] = high
+            along_ref[view, b, 1] = low
+    leave = []
+    for z in range(depth):
         b = band_ref[z]
         parts = []
         for view in range(views):
-            high, low = split(along_ref[view, b, pl.ds(pl.multiple_of(z * 2 * HW, 2 * HW), 2 * HW), :])
+            high, low = (along_ref[view, b, part, z * 2 * HW : (z + 1) * 2 * HW, :] for part in range(2))
             parts += [high, low, high]
         across = far_ref[b].reshape(views * 6 * HW, tile_cols)
         total = near_ref[z] + dot(jnp.concatenate(parts, axis=0), across, ((0,), (0,)))
         out_ref[z] = estimate_ref[z] * (total * (1.0 / views))
-        return carry
-
-    lax.fori_loop(0, depth, plane, 0, unroll=4)
+        if z % step == step - 1:
+            part = pl.ds(z - step + 1, step)
+            leave.append(pltpu.make_async_copy(out_ref.at[part], out_hbm.at[part], sems.at[z // step]))
+            leave[-1].start()
+    for copy in leave:
+        copy.wait()
 
 
 def swap(first, second, axis):
@@ -318,15 +335,19 @@
     outgoing = call(
         functools.partial(pack_kernel, devices),
         [SMEM, HBM, HBM, HBM, VMEM],
-        like((devices * views * CAP, depth, tile_cols), BF16),
+        like((devices, views, CAP, depth, tile_cols), BF16),
         [
             pltpu.VMEM((views, spare, depth, tile_cols), BF16),
             pltpu.VMEM(measured.shape, BF16),
+            pltpu.VMEM((views, devices, CAP, depth, tile_cols), BF16),
             pltpu.SMEM(group_shift.shape, jnp.int32),
             pltpu.SMEM(group_length.shape, jnp.int32),
-            pltpu.SemaphoreType.DMA((views + 2,)),
+            pltpu.SemaphoreType.DMA((2 * views + 2,)),
         ],
+        HBM,
+        60,
     )(me, group_shift, group_length, measured, edges[0])
+    outgoing = outgoing.reshape(devices * views * CAP, depth, tile_cols)
     outgoing, ey, oy = lax.optimization_barrier((outgoing, ey, oy))
     arrived = lax.all_to_all(outgoing, ("gx", "gy"), split_axis=0, concat_axis=0, tiled=True)
 
@@ -372,15 +393,22 @@
         near_kernel,
         [SMEM] * 2 + [VMEM] * 6,
         like(estimate.shape, F32),
+        [
+            pltpu.VMEM((depth, views * tile_rows, 2 * tile_cols), BF16),
+            pltpu.VMEM((depth, views * 2 * HW, 2 * tile_cols), BF16),
+        ],
     )(depth_band, odd_x, rows_mat, ends_mat, cols_mat, ratio, ex, ox)
     return call(
         far_kernel,
         [SMEM] * 2 + [VMEM] * 6,
         like(estimate.shape, F32),
         [
-            pltpu.VMEM((depth * 2 * HW, tile_rows + 2 * HW), BF16),
-            pltpu.VMEM((views, bands, depth * 2 * HW, tile_rows), F32),
+            pltpu.VMEM((views, depth * 2 * HW, tile_rows + 2 * HW), BF16),
+            pltpu.VMEM((views, bands, 2, depth * 2 * HW, tile_rows), BF16),
+            pltpu.VMEM(estimate.shape, F32),
+            pltpu.SemaphoreType.DMA((4,)),
         ],
+        HBM,
     )(depth_band, odd_y, turned_mat, far_mat, near, ey, oy, estimate)
 
 

time: 89.8 us -> 86 us (0.958)
  local copies, waits for them, and re-layouts: 14.7 us -> 10.5 us
  waiting for transfers between devices: 18.6 us -> 20.7 us
  Pallas kernels: 27.8 us -> 26 us
    unnamed x54 -> x48, local copies, waits for them, and re-layouts: 14.6 us -> 10.4 us
    pallas_call x1, Pallas kernels: 1.76 us -> 4.5 us  [body(): call(functools.partial(pack_kernel, devices), [SMEM, HBM, HBM, HBM, VMEM]...]
    pallas_call x1, Pallas kernels: 4.96 us -> 2.25 us  [body(): call(near_kernel, [SMEM] * 2 + [VMEM] * 6, like(estimate.shape, F32), [pl...]
    ppermute x4, waiting for transfers between devices: 1.58 us -> 3.66 us  [swap(): lax.ppermute(second, axis, pairs(1))]
  transfers between devices with their start and end apart: 9 -> 9, of which waited for: 3 -> 4; matrix products, arithmetic and copies ran while one was open for 0% -> 0% of each run, Pallas kernels for 26% -> 27%
where the time goes in v3:
time: 86 us; the launch traced here: 85.4 us
  starting transfers between devices  26.8 us (31%)
  Pallas kernels  26 us (30%)
  waiting for transfers between devices  20.7 us (24%)
  local copies, waits for them, and re-layouts  10.5 us (12%)
  other arithmetic  1.16 us (1%)
    all_to_all x1, waiting for transfers between devices, body(): lax.all_to_all(outgoing, ('gx', 'gy'), split_axis=0, concat_axis=0, tiled...  17 us
    ppermute x4, starting transfers between devices, swap(): lax.ppermute(second, axis, pairs(1))  15.1 us
    pallas_call x1, Pallas kernels, body(): call(forward_kernel, [SMEM] * 3 + [VMEM] * 6, (like(measured.shape, F32),...  13.9 us
    unnamed x48, local copies, waits for them, and re-layouts  10.4 us
    all_to_all x1, starting transfers between devices, body(): lax.all_to_all(outgoing, ('gx', 'gy'), split_axis=0, concat_axis=0, tiled...  9.08 us
    pallas_call x1, Pallas kernels, body(): call(functools.partial(pack_kernel, devices), [SMEM, HBM, HBM, HBM, VMEM]...  4.5 us
    ppermute x4, waiting for transfers between devices, swap(): lax.ppermute(second, axis, pairs(1))  3.66 us
    ppermute x4, starting transfers between devices, swap(): lax.ppermute(first, axis, pairs(0))  2.6 us
  transfers between devices with their start and end apart: 9, of which 4 were waited for; matrix products, arithmetic and copies ran while one was open for 0% of the time, Pallas kernels for 27%

profile of v3, /device:TPU:9, one launch (start us, length us, event | category | flops | bytes accessed | tf_op | source)
XLA Modules:
  0.0 85.4 jit_solution(14313462618215615661)
XLA Ops:
  0.0 0.9 %slice_select_fusion = (f32[16,8,128]{2,1,0:T(8,128)S(1)}, f32[16,8,128]{2,1,0:T(8,128)S(1)}) fusion(f32[16,128,128]{2,1,0:T(8,128)} %estimate_ref.1, pred[]{:T(512)S(6)} %eq.7), kind=kLoop, calls=%fused_computation | loop fusion | flops 32768 | bytes 262145 | tf_op jit(solution)/shard_map/jit(_where)/select_n | solution.py:331
  0.9 3.7 %collective-permute-start.1 = (f32[16,8,128]{2,1,0:T(8,128)S(1)}, f32[16,8,128]{2,1,0:T(8,128)S(1)}, u32[]{:S(2)}, u32[]{:S(2)}) collective-permute-start(f32[16,8,128]{2,1,0:T(8,128)S(1)} %get-tuple-element.41), channel_id=1, source_target_pairs={{16,32},{32,16},{48,64},{64,48},{80,96},{96,80},{17,33},{33,17},{4... | collective-permute-start | bytes 196616 | tf_op jit(solution)/shard_map/ppermute | solution.py:304
  4.7 1.2 %copy-done = f32[16,128,128]{2,1,0:T(8,128)S(1)} copy-done((f32[16,128,128]{2,1,0:T(8,128)S(1)}, f32[16,128,128]{2,1,0:T(8,128)}, u32[]{:S(2)}) %copy-start) | copy-done | bytes 1048600
  5.9 0.4 shard_map.64.cols_ref
  6.3 0.2 collective-permute-done.1.odd_ref.other_x_ref
  6.5 0.2 shard_map.65
  6.7 5.6 %collective-permute-start.3 = (bf16[16,8,144]{2,1,0:T(8,128)(2,1)S(1)}, bf16[16,8,144]{2,1,0:T(8,128)(2,1)S(1)}, u32[]{:S(2)}, u32[]{:S(2)}) collective-permute-start(bf16[16,8,144]{2,1,0:T(8,128)(2,1)S(1)} %get-tuple-element.24), channel_id=1, source_target_pairs={{1,2},{2,1},{3,4},{4,3},{5,6},{6,5},{7,8},{8,7},{9,10},{10,9},{11,... | collective-permute-start | bytes 110600 | tf_op jit(solution)/shard_map/ppermute | solution.py:304
  12.4 4.5 %shard_map.66 = bf16[128,2,3,16,128]{4,3,2,1,0:T(8,128)(2,1)} custom-call(s32[1]{0:T(128)} %bitcast.4.me_ref, s32[2,64]{1,0:T(2,128)} %shift_ref.3, s32[2,64]{1,0:T(2,128)} %length_ref.3, bf16[2,16,128,128]{3,2,1,0:T(8,128)(2,1)} %measured_hbm.1, bf16[16,8,144]{2,1,0:T(8,128)(2,1)} %copy-done.13), custom_call_target="tpu_custom_call" | custom-call | tf_op jit(solution)/shard_map/pallas_call | solution.py:335
  16.9 0.6 copy-done.14
  17.5 0.6 copy-done.16
  18.2 9.1 %all-to-all-start = ((bf16[768,16,128]{2,1,0:T(8,128)(2,1)}), bf16[768,16,128]{2,1,0:T(8,128)(2,1)S(1)}, u32[]{:S(2)}, u32[]{:S(2)}) async-start(bf16[768,16,128]{2,1,0:T(8,128)(2,1)} %bitcast.17), calls=%async_computation | async-start | bytes 6291456 | tf_op jit(solution)/shard_map/all_to_all | solution.py:352
  27.7 1.2 %copy-done.1 = f32[16,128,128]{2,1,0:T(8,128)S(1)} copy-done((f32[16,128,128]{2,1,0:T(8,128)S(1)}, f32[16,128,128]{2,1,0:T(8,128)}, u32[]{:S(2)}) %copy-start.1) | copy-done | bytes 1048600
  28.9 0.8 copy-done.15
  29.7 0.8 copy-done.17
  30.6 13.9 %shard_map.67 = (f32[2,16,128,128]{3,2,1,0:T(8,128)S(1)}, f32[2,16,16,128]{3,2,1,0:T(8,128)S(1)}, bf16[4,256,256]{2,1,0:T(8,128)(2,1)S(1)}, bf16[4,32,32]{2,1,0:...) custom-call(s32[16]{0:T(128)S(1)} %copy-done.22, ...), custom_call_target="tpu_custom_call" | custom-call | tf_op jit(solution)/shard_map/pallas_call | solution.py:357
  44.5 1.3 %copy-done.3 = f32[2,16,128,128]{3,2,1,0:T(8,128)} copy-done((f32[2,16,128,128]{3,2,1,0:T(8,128)}, f32[2,16,128,128]{3,2,1,0:T(8,128)S(1)}, u32[]{:S(2)}) %copy-start.3) | copy-done | bytes 2097176
  45.8 0.8 copy-done.5
  46.6 0.8 copy-done.7
  47.4 0.8 copy-done.9
  48.2 0.6 copy-done.11
  48.9 0.6 copy-done.18
  49.5 17.0 %all-to-all-done.arrived_ref = bf16[768,16,128]{2,1,0:T(8,128)(2,1)S(1)} async-done(((bf16[768,16,128]{2,1,0:T(8,128)(2,1)}), bf16[768,16,128]{2,1,0:T(8,128)(2,1)S(1)}, u32[]{:S(2)}, u32[]{:S(2)}) %all-to-all-start) | async-done | bytes 3145760 | tf_op jit(solution)/shard_map/all_to_all | solution.py:352
  66.5 0.7 shard_map.69
  67.3 2.3 %collective-permute-start.4 = (bf16[2,16,8,128]{3,2,1,0:T(8,128)(2,1)S(1)}, bf16[2,16,8,128]{3,2,1,0:T(8,128)(2,1)S(1)}, u32[]{:S(2)}, u32[]{:S(2)}) collective-permute-start(bf16[2,16,8,128]{3,2,1,0:T(8,128)(2,1)S(1)} %get-tuple-element.36), channel_id=1, source_target_pairs={{0,16},{16,0},{32,48},{48,32},{64,80},{80,64},{96,112},{112,96},{1... | collective-permute-start | bytes 196616 | tf_op jit(solution)/shard_map/ppermute | solution.py:304
  69.6 1.9 %collective-permute-start.5 = (bf16[2,16,8,128]{3,2,1,0:T(8,128)(2,1)S(1)}, bf16[2,16,8,128]{3,2,1,0:T(8,128)(2,1)S(1)}, u32[]{:S(2)}, u32[]{:S(2)}) collective-permute-start(bf16[2,16,8,128]{3,2,1,0:T(8,128)(2,1)S(1)} %get-tuple-element.37), channel_id=1, source_target_pairs={{16,32},{32,16},{48,64},{64,48},{80,96},{96,80},{17,33},{33,17},{4... | collective-permute-start | bytes 196616 | tf_op jit(solution)/shard_map/ppermute | solution.py:304
  71.6 1.7 %shard_map.68 = (bf16[2,16,128,128]{3,2,1,0:T(8,128)(2,1)S(1)}, bf16[2,16,16,128]{3,2,1,0:T(8,128)(2,1)S(1)}) custom-call(s32[1]{0:T(128)} %bitcast.4.me_ref, s32[2,64]{1,0:T(2,128)S(1)} %copy-done.20, s32[2,64]{1,0:T(2,128)S(1)} %copy-done.21, bf16[768,16,128]{2,1,0:T(8,128)(2,1)S(1)} %all-to-all-done.arrived_ref, f32[2,16,128,128]{3,2,1,0:T(8,128)S(1)} %copy-done.4), custom_call_target="tpu_custom_call" | custom-call | tf_op jit(solution)/shard_map/pallas_call | solution.py:385
  73.3 1.9 %collective-permute-done.5.other_ref = bf16[2,16,8,128]{3,2,1,0:T(8,128)(2,1)S(1)} collective-permute-done((bf16[2,16,8,128]{3,2,1,0:T(8,128)(2,1)S(1)}, bf16[2,16,8,128]{3,2,1,0:T(8,128)(2,1)S(1)}, u32[]{:S(2)}, u32[]{:S(2)}) %collective-permute-start.5) | collective-permute-done | bytes 65568 | tf_op jit(solution)/shard_map/ppermute | solution.py:304
  75.2 0.2 shard_map.71
  75.4 3.9 %collective-permute-start.7 = (bf16[2,16,8,144]{3,2,1,0:T(8,128)(2,1)S(1)}, bf16[2,16,8,144]{3,2,1,0:T(8,128)(2,1)S(1)}, u32[]{:S(2)}, u32[]{:S(2)}) collective-permute-start(bf16[2,16,8,144]{3,2,1,0:T(8,128)(2,1)S(1)} %bitcast.16), channel_id=1, source_target_pairs={{1,2},{2,1},{3,4},{4,3},{5,6},{6,5},{7,8},{8,7},{9,10},{10,9},{11,... | collective-permute-start | bytes 221192 | tf_op jit(solution)/shard_map/ppermute | solution.py:304
  79.5 2.3 %shard_map.70.near_ref = f32[16,128,128]{2,1,0:T(8,128)S(1)} custom-call(s32[16]{0:T(128)S(1)} %copy-done.22, s32[1]{0:T(128)} %bitcast.1.odd_x_ref.odd_ref, bf16[4,256,256]{2,1,0:T(8,128)(2,1)S(1)} %copy-done.8, bf16[4,32,32]{2,1,0:T(8,128)(2,1)S(1)} %copy-done.19, bf16[2,4,128,256]{3,2,1,0:T(8,128)(2,1)S(1)} %copy-done.10, ...), custom_call_target="tpu_custom_call" | custom-call | tf_op jit(solution)/shard_map/pallas_call | solution.py:392
  81.7 1.5 %collective-permute-done.7.other_ref = bf16[2,16,8,144]{3,2,1,0:T(8,128)(2,1)S(1)} collective-permute-done((bf16[2,16,8,144]{3,2,1,0:T(8,128)(2,1)S(1)}, bf16[2,16,8,144]{3,2,1,0:T(8,128)(2,1)S(1)}, u32[]{:S(2)}, u32[]{:S(2)}) %collective-permute-start.7) | collective-permute-done | bytes 73760 | tf_op jit(solution)/shard_map/ppermute | solution.py:304
  83.2 2.2 %shard_map.72 = f32[16,128,128]{2,1,0:T(8,128)} custom-call(s32[16]{0:T(128)S(1)} %copy-done.22, s32[1]{0:T(128)} %bitcast.odd_y_ref.odd_ref, bf16[2,4,144,256]{3,2,1,0:T(8,128)(2,1)S(1)} %copy-done.6, bf16[4,2,48,128]{3,2,1,0:T(8,128)(2,1)S(1)} %copy-done.12, f32[16,128,128]{2,1,0:T(8,128)S(1)} %shard_map.70.near_ref, ...), custom_call_target="tpu_custom_call" | custom-call | tf_op jit(solution)/shard_map/pallas_call | solution.py:401
  (49 shorter events, 0.7 us)
Async XLA Ops:
  0.9 5.6 %collective-permute-start.1 = (f32[16,8,128]{2,1,0:T(8,128)S(1)}, f32[16,8,128]{2,1,0:T(8,128)S(1)}, u32[]{:S(2)}, u32[]{:S(2)}) collective-permute-start(f32[16,8,128]{2,1,0:T(8,128)S(1)} %get-tuple-element.41), channel_id=1, source_target_pairs={{16,32},{32,16},{48,64},{64,48},{80,96},{96,80},{17,33},{33,17},{4... | collective-permute-start | bytes 196616 | tf_op jit(solution)/shard_map/ppermute | solution.py:304
  4.6 1.9 %collective-permute-start = (f32[16,8,128]{2,1,0:T(8,128)S(1)}, f32[16,8,128]{2,1,0:T(8,128)S(1)}, u32[]{:S(2)}, u32[]{:S(2)}) collective-permute-start(f32[16,8,128]{2,1,0:T(8,128)S(1)} %get-tuple-element.42), channel_id=1, source_target_pairs={{0,16},{16,0},{32,48},{48,32},{64,80},{80,64},{96,112},{112,96},{1... | collective-permute-start | bytes 196616 | tf_op jit(solution)/shard_map/ppermute | solution.py:304
  4.7 1.2 %copy-start = (f32[16,128,128]{2,1,0:T(8,128)S(1)}, f32[16,128,128]{2,1,0:T(8,128)}, u32[]{:S(2)}) copy-start(f32[16,128,128]{2,1,0:T(8,128)} %estimate_ref.1) | copy-start | bytes 3145732
  6.7 5.7 %copy-start.13 = (bf16[16,8,144]{2,1,0:T(8,128)(2,1)}, bf16[16,8,144]{2,1,0:T(8,128)(2,1)S(1)}, u32[]{:S(2)}) copy-start(bf16[16,8,144]{2,1,0:T(8,128)(2,1)S(1)} %get-tuple-element.23._) | copy-start | bytes 110596
  6.7 10.2 %collective-permute-start.3 = (bf16[16,8,144]{2,1,0:T(8,128)(2,1)S(1)}, bf16[16,8,144]{2,1,0:T(8,128)(2,1)S(1)}, u32[]{:S(2)}, u32[]{:S(2)}) collective-permute-start(bf16[16,8,144]{2,1,0:T(8,128)(2,1)S(1)} %get-tuple-element.24), channel_id=1, source_target_pairs={{1,2},{2,1},{3,4},{4,3},{5,6},{6,5},{7,8},{8,7},{9,10},{10,9},{11,... | collective-permute-start | bytes 110600 | tf_op jit(solution)/shard_map/ppermute | solution.py:304
  12.3 5.3 %collective-permute-start.2 = (bf16[16,8,144]{2,1,0:T(8,128)(2,1)S(1)}, bf16[16,8,144]{2,1,0:T(8,128)(2,1)S(1)}, u32[]{:S(2)}, u32[]{:S(2)}) collective-permute-start(bf16[16,8,144]{2,1,0:T(8,128)(2,1)S(1)} %get-tuple-element.23._), channel_id=1, source_target_pairs={{0,1},{1,0},{2,3},{3,2},{4,5},{5,4},{6,7},{7,6},{8,9},{9,8},{10,11... | collective-permute-start | bytes 110600 | tf_op jit(solution)/shard_map/ppermute | solution.py:304
  16.9 0.6 copy-start.14
  17.5 0.6 copy-start.16
  18.1 9.1 %copy-start.23 = (f32[2,4,2,17]{3,2,1,0:T(2,128)S(1)}, f32[2,4,2,17]{3,2,1,0:T(2,128)}, u32[]{:S(2)}) copy-start(f32[2,4,2,17]{3,2,1,0:T(2,128)} %param.8) | copy-start | bytes 3268
  18.1 9.5 %copy-start.22 = (s32[16]{0:T(128)S(1)}, s32[16]{0:T(128)}, u32[]{:S(2)}) copy-start(s32[16]{0:T(128)} %band_ref.5) | copy-start | bytes 196
  18.1 48.3 %copy-start.20 = (s32[2,64]{1,0:T(2,128)S(1)}, s32[2,64]{1,0:T(2,128)}, u32[]{:S(2)}) copy-start(s32[2,64]{1,0:T(2,128)} %shift_ref.3) | copy-start | bytes 1540
  18.1 48.3 %copy-start.21 = (s32[2,64]{1,0:T(2,128)S(1)}, s32[2,64]{1,0:T(2,128)}, u32[]{:S(2)}) copy-start(s32[2,64]{1,0:T(2,128)} %length_ref.3) | copy-start | bytes 1540
  18.2 48.3 %all-to-all-start = ((bf16[768,16,128]{2,1,0:T(8,128)(2,1)}), bf16[768,16,128]{2,1,0:T(8,128)(2,1)S(1)}, u32[]{:S(2)}, u32[]{:S(2)}) async-start(bf16[768,16,128]{2,1,0:T(8,128)(2,1)} %bitcast.17), calls=%async_computation | async-start | bytes 6291456 | tf_op jit(solution)/shard_map/all_to_all | solution.py:352
  27.7 1.2 %copy-start.1 = (f32[16,128,128]{2,1,0:T(8,128)S(1)}, f32[16,128,128]{2,1,0:T(8,128)}, u32[]{:S(2)}) copy-start(f32[16,128,128]{2,1,0:T(8,128)} %estimate_ref.1) | copy-start | bytes 3145732
  28.9 0.8 copy-start.15
  29.7 0.8 copy-start.17
  44.5 1.3 %copy-start.3 = (f32[2,16,128,128]{3,2,1,0:T(8,128)}, f32[2,16,128,128]{3,2,1,0:T(8,128)S(1)}, u32[]{:S(2)}) copy-start(f32[2,16,128,128]{3,2,1,0:T(8,128)S(1)} %get-tuple-element.33.recip_ref) | copy-start | bytes 6291460
  45.8 0.8 copy-start.5
  46.6 0.8 copy-start.7
  47.4 0.8 copy-start.9
  48.2 0.6 copy-start.11
  66.5 5.0 %copy-start.4 = (f32[2,16,128,128]{3,2,1,0:T(8,128)S(1)}, f32[2,16,128,128]{3,2,1,0:T(8,128)}, u32[]{:S(2)}) copy-start(f32[2,16,128,128]{3,2,1,0:T(8,128)} %copy-done.3) | copy-start | bytes 6291460
  67.2 12.2 %copy-start.8 = (bf16[4,256,256]{2,1,0:T(8,128)(2,1)S(1)}, bf16[4,256,256]{2,1,0:T(8,128)(2,1)}, u32[]{:S(2)}) copy-start(bf16[4,256,256]{2,1,0:T(8,128)(2,1)} %copy-done.7) | copy-start | bytes 1572868
  67.2 12.2 %copy-start.10 = (bf16[2,4,128,256]{3,2,1,0:T(8,128)(2,1)S(1)}, bf16[2,4,128,256]{3,2,1,0:T(8,128)(2,1)}, u32[]{:S(2)}) copy-start(bf16[2,4,128,256]{3,2,1,0:T(8,128)(2,1)} %copy-done.9) | copy-start | bytes 1572868
  67.2 12.2 %copy-start.19 = (bf16[4,32,32]{2,1,0:T(8,128)(2,1)S(1)}, bf16[4,32,32]{2,1,0:T(8,128)(2,1)}, u32[]{:S(2)}) copy-start(bf16[4,32,32]{2,1,0:T(8,128)(2,1)} %copy-done.18) | copy-start | bytes 24580
  67.3 6.0 %collective-permute-start.4 = (bf16[2,16,8,128]{3,2,1,0:T(8,128)(2,1)S(1)}, bf16[2,16,8,128]{3,2,1,0:T(8,128)(2,1)S(1)}, u32[]{:S(2)}, u32[]{:S(2)}) collective-permute-start(bf16[2,16,8,128]{3,2,1,0:T(8,128)(2,1)S(1)} %get-tuple-element.36), channel_id=1, source_target_pairs={{0,16},{16,0},{32,48},{48,32},{64,80},{80,64},{96,112},{112,96},{1... | collective-permute-start | bytes 196616 | tf_op jit(solution)/shard_map/ppermute | solution.py:304
  69.6 5.6 %collective-permute-start.5 = (bf16[2,16,8,128]{3,2,1,0:T(8,128)(2,1)S(1)}, bf16[2,16,8,128]{3,2,1,0:T(8,128)(2,1)S(1)}, u32[]{:S(2)}, u32[]{:S(2)}) collective-permute-start(bf16[2,16,8,128]{3,2,1,0:T(8,128)(2,1)S(1)} %get-tuple-element.37), channel_id=1, source_target_pairs={{16,32},{32,16},{48,64},{64,48},{80,96},{96,80},{17,33},{33,17},{4... | collective-permute-start | bytes 196616 | tf_op jit(solution)/shard_map/ppermute | solution.py:304
  71.5 11.7 %copy-start.2 = (f32[16,128,128]{2,1,0:T(8,128)S(1)}, f32[16,128,128]{2,1,0:T(8,128)}, u32[]{:S(2)}) copy-start(f32[16,128,128]{2,1,0:T(8,128)} %estimate_ref.1) | copy-start | bytes 3145732
  71.5 11.7 %copy-start.6 = (bf16[2,4,144,256]{3,2,1,0:T(8,128)(2,1)S(1)}, bf16[2,4,144,256]{3,2,1,0:T(8,128)(2,1)}, u32[]{:S(2)}) copy-start(bf16[2,4,144,256]{3,2,1,0:T(8,128)(2,1)} %copy-done.5) | copy-start | bytes 1769476
  71.6 11.7 %copy-start.12 = (bf16[4,2,48,128]{3,2,1,0:T(8,128)(2,1)S(1)}, bf16[4,2,48,128]{3,2,1,0:T(8,128)(2,1)}, u32[]{:S(2)}) copy-start(bf16[4,2,48,128]{3,2,1,0:T(8,128)(2,1)} %copy-done.11) | copy-start | bytes 294916
  75.4 7.8 %collective-permute-start.7 = (bf16[2,16,8,144]{3,2,1,0:T(8,128)(2,1)S(1)}, bf16[2,16,8,144]{3,2,1,0:T(8,128)(2,1)S(1)}, u32[]{:S(2)}, u32[]{:S(2)}) collective-permute-start(bf16[2,16,8,144]{3,2,1,0:T(8,128)(2,1)S(1)} %bitcast.16), channel_id=1, source_target_pairs={{1,2},{2,1},{3,4},{4,3},{5,6},{6,5},{7,8},{8,7},{9,10},{10,9},{11,... | collective-permute-start | bytes 221192 | tf_op jit(solution)/shard_map/ppermute | solution.py:304
  79.3 3.9 %collective-permute-start.6 = (bf16[2,16,8,144]{3,2,1,0:T(8,128)(2,1)S(1)}, bf16[2,16,8,144]{3,2,1,0:T(8,128)(2,1)S(1)}, u32[]{:S(2)}, u32[]{:S(2)}) collective-permute-start(bf16[2,16,8,144]{3,2,1,0:T(8,128)(2,1)S(1)} %bitcast.15), channel_id=1, source_target_pairs={{0,1},{1,0},{2,3},{3,2},{4,5},{5,4},{6,7},{7,6},{8,9},{9,8},{10,11... | collective-permute-start | bytes 221192 | tf_op jit(solution)/shard_map/ppermute | solution.py:304
  (1 other events, 0.6 us)

commit v4 on v3

--- a/solution.py
+++ b/solution.py
@@ -70,7 +70,7 @@
 
 def pack_kernel(
     devices, me_ref, shift_hbm, length_hbm, measured_hbm, _, out_hbm,
-    rows_ref, measured_ref, out_ref, shift_ref, length_ref, sems,
+    rows_ref, measured_ref, shift_ref, length_ref, sems,
 ):
     views, depth, tile_rows, tile_cols = measured_ref.shape
     groups = shift_ref.shape[1]
@@ -79,8 +79,7 @@
         pltpu.make_async_copy(shift_hbm, shift_ref, sems.at[views]),
         pltpu.make_async_copy(length_hbm, length_ref, sems.at[views + 1]),
     ]
-    leave = [pltpu.make_async_copy(out_ref.at[v], out_hbm.at[:, v], sems.at[views + 2 + v]) for v in range(views)]
-    for copy in loads + tables:
+    for copy in tables + loads:
         copy.start()
     rows_ref[:, tile_rows:] = jnp.zeros((views, rows_ref.shape[1] - tile_rows) + rows_ref.shape[2:], BF16)
     lane = lax.broadcasted_iota(jnp.int32, (tile_cols, tile_cols), 1)
@@ -101,14 +100,14 @@
 
         def group(g, start, view=view):
             peer = lax.rem(me + shift_ref[view, g], devices)
-            for k in range(CAP):
-                out_ref[view, peer, k] = rows_ref[view, start + k]
+            blocks = rows_ref.at[view, pl.ds(start, CAP)]
+            pltpu.make_async_copy(blocks, out_hbm.at[peer, view], sems.at[views + 2 + view]).start()
             return start + length_ref[view, g]
 
-        lax.fori_loop(0, groups, group, 0, unroll=4)
-        leave[view].start()
-    for copy in leave:
-        copy.wait()
+        lax.fori_loop(0, groups, group, 0, unroll=True)
+    for view in range(views):
+        sent = out_hbm.at[pl.ds(0, groups), view]
+        pltpu.make_async_copy(sent, sent, sems.at[views + 2 + view]).wait()
 
 
 def cols_kernel(cells_ref, out_ref):
@@ -132,6 +131,23 @@
         return carry
 
     lax.fori_loop(0, cols_ref.shape[0], plane, 0, unroll=True)
+
+
+def dense_slab_kernel(odd_x_ref, odd_y_ref, cols_ref, even_ref, other_ref, first_ref, second_ref):
+    views, depth, _, tile_rows = cols_ref.shape
+    count = tile_rows // (2 * HW)
+    pick = edge_picker(even_ref.shape[-1])
+    odd = odd_y_ref[0] == 1
+    for view in range(views):
+        for i in range(first_ref.shape[1]):
+            if i < depth:
+                edge = cols_ref[view, i].astype(F32)
+            else:
+                planes = range((i - depth) * count, (i - depth + 1) * count)
+                ends = [halo(odd_x_ref, even_ref[view, z], other_ref[view, z]) for z in planes]
+                edge = dot(pick, jnp.concatenate(ends, axis=0), NT)
+            first_ref[view, i] = jnp.where(odd, edge[:HW], edge[HW:]).astype(BF16)
+            second_ref[view, i] = jnp.where(odd, edge[HW:], edge[:HW]).astype(BF16)
 
 
 def edges_kernel(
@@ -215,7 +231,9 @@
             beyond = along[:, tile_rows:]
             ends = ends + (pltpu.roll(beyond, 2 * HW * view, 1) if view else beyond)
             turned_ref[view, b, :tile_rows] = stacked(along[:, :tile_rows].T, 1)
-            turned_ref[view, b, tile_rows:] = stacked(beyond.T[: 2 * HW], 1)
+            turned = stacked(beyond.T[: 2 * HW], 1)
+            for at in range(tile_rows, 2 * tile_rows, 2 * HW):
+                turned_ref[view, b, at : at + 2 * HW] = turned
             across = band(taps_ref[1, view, b, 1:2, :], tile_cols)
             cols_ref[view, b] = stacked(across[:, :tile_cols].T, 1)
             high, low = split(across[:, tile_cols:].T[: 2 * HW])
@@ -271,9 +289,15 @@
     views, bands = turned_ref.shape[:2]
     depth, tile_rows, tile_cols = near_ref.shape
     step = depth // sems.shape[0]
+    count = tile_rows // (2 * HW)
+    owner = lax.broadcasted_iota(jnp.int32, (2 * HW, tile_rows), 1) // (2 * HW)
     for view in range(views):
         for z in range(depth):
-            slab_ref[view, z * 2 * HW : (z + 1) * 2 * HW] = halo(odd_ref, even_ref[view, z], other_ref[view, z])
+            at = pl.ds(z * 2 * HW, 2 * HW)
+            slab_ref[view, at, :tile_rows] = halo(odd_ref, even_ref[view, z], other_ref[view, z])
+            tile = depth + z // count
+            corners = halo(odd_ref, even_ref[view, tile], other_ref[view, tile])
+            slab_ref[view, at, tile_rows:] = jnp.where(owner == z % count, corners.astype(F32), 0.0).astype(BF16)
     for view in range(views):
         for b in range(bands):
             along = dot(slab_ref[view], turned_ref[view, b])
@@ -331,7 +355,7 @@
     ex, ox = swap(jnp.where(even, tail, head), jnp.where(even, head, tail), "gx")
     cols = call(cols_kernel, [VMEM], like(edge_cols.shape[1:], BF16))(estimate)
     edges = slabs(odd_x, odd_y, cols, ex, ox)
-    ey, oy = swap(*edges, "gy")
+    ey, oy = (pltpu.with_memory_space_constraint(x, pltpu.HBM) for x in swap(*edges, "gy"))
     outgoing = call(
         functools.partial(pack_kernel, devices),
         [SMEM, HBM, HBM, HBM, VMEM],
@@ -339,7 +363,6 @@
         [
             pltpu.VMEM((views, spare, depth, tile_cols), BF16),
             pltpu.VMEM(measured.shape, BF16),
-            pltpu.VMEM((views, devices, CAP, depth, tile_cols), BF16),
             pltpu.SMEM(group_shift.shape, jnp.int32),
             pltpu.SMEM(group_length.shape, jnp.int32),
             pltpu.SemaphoreType.DMA((2 * views + 2,)),
@@ -363,7 +386,7 @@
             like((bands, 2 * tile_rows, views * tile_rows), BF16),
             like((bands, 4 * HW, views * 2 * HW), BF16),
             like((views, bands, tile_cols, 2 * tile_cols), BF16),
-            like((views, bands, tile_rows + 2 * HW, 2 * tile_rows), BF16),
+            like((views, bands, 2 * tile_rows, 2 * tile_rows), BF16),
             like((bands, views, 6 * HW, tile_cols), BF16),
         ),
         [
@@ -388,7 +411,9 @@
         (whole, edge_cols),
         [pltpu.VMEM((views, spare, depth, tile_cols), F32)],
     )(me, group_shift, group_length, arrived, recip)
-    ey, oy = swap(*slabs(odd_x, odd_y, cols, ex, ox), "gy")
+    tiles = like((views, depth + depth * 2 * HW // tile_rows, HW, tile_rows), BF16)
+    edges = call(dense_slab_kernel, [SMEM] * 2 + [VMEM] * 3, (tiles, tiles))(odd_x, odd_y, cols, ex, ox)
+    ey, oy = swap(*edges, "gy")
     near = call(
         near_kernel,
         [SMEM] * 2 + [VMEM] * 6,
@@ -403,7 +428,7 @@
         [SMEM] * 2 + [VMEM] * 6,
         like(estimate.shape, F32),
         [
-            pltpu.VMEM((views, depth * 2 * HW, tile_rows + 2 * HW), BF16),
+            pltpu.VMEM((views, depth * 2 * HW, 2 * tile_rows), BF16),
             pltpu.VMEM((views, bands, 2, depth * 2 * HW, tile_rows), BF16),
             pltpu.VMEM(estimate.shape, F32),
             pltpu.SemaphoreType.DMA((4,)),

time: 86 us -> 84.4 us (0.981)
  the two profiles are of different devices: /device:TPU:9 before, /device:TPU:30 now
where the time goes in v4:
time: 84.4 us; the launch traced here: 82.8 us
  Pallas kernels  25.6 us (30%)
  waiting for transfers between devices  25.5 us (30%)
  starting transfers between devices  21.8 us (26%)
  local copies, waits for them, and re-layouts  8.35 us (10%)
  other arithmetic  1.16 us (1%)
    all_to_all x1, waiting for transfers between devices, body(): lax.all_to_all(outgoing, ('gx', 'gy'), split_axis=0, concat_axis=0, tiled...  17.9 us
    pallas_call x1, Pallas kernels, body(): call(forward_kernel, [SMEM] * 3 + [VMEM] * 6, (like(measured.shape, F32),...  14.3 us
    ppermute x4, starting transfers between devices, swap(): lax.ppermute(second, axis, pairs(1))  12.8 us
    unnamed x44, local copies, waits for them, and re-layouts  8.24 us
    all_to_all x1, starting transfers between devices, body(): lax.all_to_all(outgoing, ('gx', 'gy'), split_axis=0, concat_axis=0, tiled...  8.04 us
    ppermute x4, waiting for transfers between devices, swap(): lax.ppermute(second, axis, pairs(1))  7.21 us
    pallas_call x1, Pallas kernels, body(): call(functools.partial(pack_kernel, devices), [SMEM, HBM, HBM, HBM, VMEM]...  3.77 us
    pallas_call x1, Pallas kernels, body(): call(near_kernel, [SMEM] * 2 + [VMEM] * 6, like(estimate.shape, F32), [pl...  2.25 us
  transfers between devices with their start and end apart: 9, of which 5 were waited for; matrix products, arithmetic and copies ran while one was open for 0% of the time, Pallas kernels for 27%

profile of v4, /device:TPU:30, one launch (start us, length us, event | category | flops | bytes accessed | tf_op | source)
XLA Modules:
  0.0 82.8 jit_solution(12834943642564195103)
XLA Ops:
  0.0 0.9 %slice_select_fusion = (f32[16,8,128]{2,1,0:T(8,128)S(1)}, f32[16,8,128]{2,1,0:T(8,128)S(1)}) fusion(f32[16,128,128]{2,1,0:T(8,128)} %estimate_ref.1, pred[]{:T(512)S(6)} %eq.7), kind=kLoop, calls=%fused_computation | loop fusion | flops 32768 | bytes 262145 | tf_op jit(solution)/shard_map/jit(_where)/select_n | solution.py:355
  0.9 2.2 %collective-permute-start.1 = (f32[16,8,128]{2,1,0:T(8,128)S(1)}, f32[16,8,128]{2,1,0:T(8,128)S(1)}, u32[]{:S(2)}, u32[]{:S(2)}) collective-permute-start(f32[16,8,128]{2,1,0:T(8,128)S(1)} %get-tuple-element.41), channel_id=1, source_target_pairs={{16,32},{32,16},{48,64},{64,48},{80,96},{96,80},{17,33},{33,17},{4... | collective-permute-start | bytes 196616 | tf_op jit(solution)/shard_map/ppermute | solution.py:328
  3.2 1.2 %copy-done = f32[16,128,128]{2,1,0:T(8,128)S(1)} copy-done((f32[16,128,128]{2,1,0:T(8,128)S(1)}, f32[16,128,128]{2,1,0:T(8,128)}, u32[]{:S(2)}) %copy-start) | copy-done | bytes 1048600
  4.4 0.4 shard_map.64.cols_ref
  4.8 1.7 %collective-permute-done.1.odd_ref.other_x_ref = f32[16,8,128]{2,1,0:T(8,128)S(1)} collective-permute-done((f32[16,8,128]{2,1,0:T(8,128)S(1)}, f32[16,8,128]{2,1,0:T(8,128)S(1)}, u32[]{:S(2)}, u32[]{:S(2)}) %collective-permute-start.1) | collective-permute-done | bytes 65568 | tf_op jit(solution)/shard_map/ppermute | solution.py:328
  6.5 0.2 shard_map.65
  6.7 6.1 %collective-permute-start.3 = (bf16[16,8,144]{2,1,0:T(8,128)(2,1)S(1)}, bf16[16,8,144]{2,1,0:T(8,128)(2,1)S(1)}, u32[]{:S(2)}, u32[]{:S(2)}) collective-permute-start(bf16[16,8,144]{2,1,0:T(8,128)(2,1)S(1)} %get-tuple-element.24), channel_id=1, source_target_pairs={{1,2},{2,1},{3,4},{4,3},{5,6},{6,5},{7,8},{8,7},{9,10},{10,9},{11,... | collective-permute-start | bytes 110600 | tf_op jit(solution)/shard_map/ppermute | solution.py:328
  12.9 3.8 %shard_map.66 = bf16[128,2,3,16,128]{4,3,2,1,0:T(8,128)(2,1)} custom-call(s32[1]{0:T(128)} %bitcast.4.me_ref, s32[2,64]{1,0:T(2,128)} %shift_ref.3, s32[2,64]{1,0:T(2,128)} %length_ref.3, bf16[2,16,128,128]{3,2,1,0:T(8,128)(2,1)} %measured_hbm.1, bf16[16,8,144]{2,1,0:T(8,128)(2,1)} %copy-done.13), custom_call_target="tpu_custom_call" | custom-call | tf_op jit(solution)/shard_map/pallas_call | solution.py:359
  16.7 0.4 collective-permute-done.2.even_y_ref
  17.2 0.1 copy-done.20
  17.3 0.5 copy-done.21
  17.8 8.0 %all-to-all-start = ((bf16[768,16,128]{2,1,0:T(8,128)(2,1)}), bf16[768,16,128]{2,1,0:T(8,128)(2,1)S(1)}, u32[]{:S(2)}, u32[]{:S(2)}) async-start(bf16[768,16,128]{2,1,0:T(8,128)(2,1)} %bitcast.7), calls=%async_computation | async-start | bytes 6291456 | tf_op jit(solution)/shard_map/all_to_all | solution.py:375
  26.0 0.1 rev.3
  26.3 1.2 %copy-done.1 = f32[16,128,128]{2,1,0:T(8,128)S(1)} copy-done((f32[16,128,128]{2,1,0:T(8,128)S(1)}, f32[16,128,128]{2,1,0:T(8,128)}, u32[]{:S(2)}) %copy-start.1) | copy-done | bytes 1048600
  27.5 14.3 %shard_map.67 = (f32[2,16,128,128]{3,2,1,0:T(8,128)S(1)}, f32[2,16,16,128]{3,2,1,0:T(8,128)S(1)}, bf16[4,256,256]{2,1,0:T(8,128)(2,1)S(1)}, bf16[4,32,32]{2,1,0:...) custom-call(s32[16]{0:T(128)S(1)} %copy-done.18, ...), custom_call_target="tpu_custom_call" | custom-call | tf_op jit(solution)/shard_map/pallas_call | solution.py:380
  41.8 1.3 %copy-done.3 = f32[2,16,128,128]{3,2,1,0:T(8,128)} copy-done((f32[2,16,128,128]{3,2,1,0:T(8,128)}, f32[2,16,128,128]{3,2,1,0:T(8,128)S(1)}, u32[]{:S(2)}) %copy-start.3) | copy-done | bytes 2097176
  43.1 1.0 %copy-done.5 = bf16[2,4,256,256]{3,2,1,0:T(8,128)(2,1)} copy-done((bf16[2,4,256,256]{3,2,1,0:T(8,128)(2,1)}, bf16[2,4,256,256]{3,2,1,0:T(8,128)(2,1)S(1)}, u32[]{:S(2)}) %copy-start.5) | copy-done | bytes 1048600
  44.1 0.8 copy-done.7
  44.9 0.8 copy-done.9
  45.7 0.6 copy-done.11
  46.3 0.6 copy-done.14
  46.9 17.9 %all-to-all-done.arrived_ref = bf16[768,16,128]{2,1,0:T(8,128)(2,1)S(1)} async-done(((bf16[768,16,128]{2,1,0:T(8,128)(2,1)}), bf16[768,16,128]{2,1,0:T(8,128)(2,1)S(1)}, u32[]{:S(2)}, u32[]{:S(2)}) %all-to-all-start) | async-done | bytes 3145760 | tf_op jit(solution)/shard_map/all_to_all | solution.py:375
  64.8 0.7 shard_map.69
  65.6 2.2 %collective-permute-start.5 = (bf16[2,16,8,128]{3,2,1,0:T(8,128)(2,1)S(1)}, bf16[2,16,8,128]{3,2,1,0:T(8,128)(2,1)S(1)}, u32[]{:S(2)}, u32[]{:S(2)}) collective-permute-start(bf16[2,16,8,128]{3,2,1,0:T(8,128)(2,1)S(1)} %get-tuple-element.37), channel_id=1, source_target_pairs={{16,32},{32,16},{48,64},{64,48},{80,96},{96,80},{17,33},{33,17},{4... | collective-permute-start | bytes 196616 | tf_op jit(solution)/shard_map/ppermute | solution.py:328
  67.9 1.7 %shard_map.68 = (bf16[2,16,128,128]{3,2,1,0:T(8,128)(2,1)S(1)}, bf16[2,16,16,128]{3,2,1,0:T(8,128)(2,1)S(1)}) custom-call(s32[1]{0:T(128)} %bitcast.4.me_ref, s32[2,64]{1,0:T(2,128)S(1)} %copy-done.16, s32[2,64]{1,0:T(2,128)S(1)} %copy-done.17, bf16[768,16,128]{2,1,0:T(8,128)(2,1)S(1)} %all-to-all-done.arrived_ref, f32[2,16,128,128]{3,2,1,0:T(8,128)S(1)} %copy-done.4), custom_call_target="tpu_custom_call" | custom-call | tf_op jit(solution)/shard_map/pallas_call | solution.py:408
  69.6 1.7 %collective-permute-done.5.other_ref = bf16[2,16,8,128]{3,2,1,0:T(8,128)(2,1)S(1)} collective-permute-done((bf16[2,16,8,128]{3,2,1,0:T(8,128)(2,1)S(1)}, bf16[2,16,8,128]{3,2,1,0:T(8,128)(2,1)S(1)}, u32[]{:S(2)}, u32[]{:S(2)}) %collective-permute-start.5) | collective-permute-done | bytes 65568 | tf_op jit(solution)/shard_map/ppermute | solution.py:328
  71.4 0.2 shard_map.71
  71.5 0.7 collective-permute-start.6
  72.2 2.3 %collective-permute-start.7 = (bf16[2,18,8,128]{3,2,1,0:T(8,128)(2,1)S(1)}, bf16[2,18,8,128]{3,2,1,0:T(8,128)(2,1)S(1)}, u32[]{:S(2)}, u32[]{:S(2)}) collective-permute-start(bf16[2,18,8,128]{3,2,1,0:T(8,128)(2,1)S(1)} %get-tuple-element.40), channel_id=1, source_target_pairs={{1,2},{2,1},{3,4},{4,3},{5,6},{6,5},{7,8},{8,7},{9,10},{10,9},{11,... | collective-permute-start | bytes 221192 | tf_op jit(solution)/shard_map/ppermute | solution.py:328
  74.5 2.2 %shard_map.70.near_ref = f32[16,128,128]{2,1,0:T(8,128)S(1)} custom-call(s32[16]{0:T(128)S(1)} %copy-done.18, s32[1]{0:T(128)} %bitcast.1.odd_x_ref.odd_ref, bf16[4,256,256]{2,1,0:T(8,128)(2,1)S(1)} %copy-done.8, bf16[4,32,32]{2,1,0:T(8,128)(2,1)S(1)} %copy-done.15, bf16[2,4,128,256]{3,2,1,0:T(8,128)(2,1)S(1)} %copy-done.10, ...), custom_call_target="tpu_custom_call" | custom-call | tf_op jit(solution)/shard_map/pallas_call | solution.py:417
  76.8 3.8 %collective-permute-done.7.other_ref = bf16[2,18,8,128]{3,2,1,0:T(8,128)(2,1)S(1)} collective-permute-done((bf16[2,18,8,128]{3,2,1,0:T(8,128)(2,1)S(1)}, bf16[2,18,8,128]{3,2,1,0:T(8,128)(2,1)S(1)}, u32[]{:S(2)}, u32[]{:S(2)}) %collective-permute-start.7) | collective-permute-done | bytes 73760 | tf_op jit(solution)/shard_map/ppermute | solution.py:328
  80.6 2.2 %shard_map.72 = f32[16,128,128]{2,1,0:T(8,128)} custom-call(s32[16]{0:T(128)S(1)} %copy-done.18, s32[1]{0:T(128)} %bitcast.odd_y_ref.odd_ref, bf16[2,4,256,256]{3,2,1,0:T(8,128)(2,1)S(1)} %copy-done.6, bf16[4,2,48,128]{3,2,1,0:T(8,128)(2,1)S(1)} %copy-done.12, f32[16,128,128]{2,1,0:T(8,128)S(1)} %shard_map.70.near_ref, ...), custom_call_target="tpu_custom_call" | custom-call | tf_op jit(solution)/shard_map/pallas_call | solution.py:426
  (45 shorter events, 0.6 us)
Async XLA Ops:
  0.9 5.6 %collective-permute-start.1 = (f32[16,8,128]{2,1,0:T(8,128)S(1)}, f32[16,8,128]{2,1,0:T(8,128)S(1)}, u32[]{:S(2)}, u32[]{:S(2)}) collective-permute-start(f32[16,8,128]{2,1,0:T(8,128)S(1)} %get-tuple-element.41), channel_id=1, source_target_pairs={{16,32},{32,16},{48,64},{64,48},{80,96},{96,80},{17,33},{33,17},{4... | collective-permute-start | bytes 196616 | tf_op jit(solution)/shard_map/ppermute | solution.py:328
  3.1 3.4 %collective-permute-start = (f32[16,8,128]{2,1,0:T(8,128)S(1)}, f32[16,8,128]{2,1,0:T(8,128)S(1)}, u32[]{:S(2)}, u32[]{:S(2)}) collective-permute-start(f32[16,8,128]{2,1,0:T(8,128)S(1)} %get-tuple-element.42), channel_id=1, source_target_pairs={{0,16},{16,0},{32,48},{48,32},{64,80},{80,64},{96,112},{112,96},{1... | collective-permute-start | bytes 196616 | tf_op jit(solution)/shard_map/ppermute | solution.py:328
  3.2 1.2 %copy-start = (f32[16,128,128]{2,1,0:T(8,128)S(1)}, f32[16,128,128]{2,1,0:T(8,128)}, u32[]{:S(2)}) copy-start(f32[16,128,128]{2,1,0:T(8,128)} %estimate_ref.1) | copy-start | bytes 3145732
  6.6 6.2 %copy-start.13 = (bf16[16,8,144]{2,1,0:T(8,128)(2,1)}, bf16[16,8,144]{2,1,0:T(8,128)(2,1)S(1)}, u32[]{:S(2)}) copy-start(bf16[16,8,144]{2,1,0:T(8,128)(2,1)S(1)} %get-tuple-element.23._) | copy-start | bytes 110596
  6.7 10.0 %collective-permute-start.3 = (bf16[16,8,144]{2,1,0:T(8,128)(2,1)S(1)}, bf16[16,8,144]{2,1,0:T(8,128)(2,1)S(1)}, u32[]{:S(2)}, u32[]{:S(2)}) collective-permute-start(bf16[16,8,144]{2,1,0:T(8,128)(2,1)S(1)} %get-tuple-element.24), channel_id=1, source_target_pairs={{1,2},{2,1},{3,4},{4,3},{5,6},{6,5},{7,8},{8,7},{9,10},{10,9},{11,... | collective-permute-start | bytes 110600 | tf_op jit(solution)/shard_map/ppermute | solution.py:328
  12.8 4.3 %collective-permute-start.2 = (bf16[16,8,144]{2,1,0:T(8,128)(2,1)S(1)}, bf16[16,8,144]{2,1,0:T(8,128)(2,1)S(1)}, u32[]{:S(2)}, u32[]{:S(2)}) collective-permute-start(bf16[16,8,144]{2,1,0:T(8,128)(2,1)S(1)} %get-tuple-element.23._), channel_id=1, source_target_pairs={{0,1},{1,0},{2,3},{3,2},{4,5},{5,4},{6,7},{7,6},{8,9},{9,8},{10,11... | collective-permute-start | bytes 110600 | tf_op jit(solution)/shard_map/ppermute | solution.py:328
  16.7 0.6 copy-start.20
  17.1 0.6 copy-start.21
  17.1 8.7 %copy-start.19 = (f32[2,4,2,17]{3,2,1,0:T(2,128)S(1)}, f32[2,4,2,17]{3,2,1,0:T(2,128)}, u32[]{:S(2)}) copy-start(f32[2,4,2,17]{3,2,1,0:T(2,128)} %param.8) | copy-start | bytes 3268
  17.1 9.1 %copy-start.18 = (s32[16]{0:T(128)S(1)}, s32[16]{0:T(128)}, u32[]{:S(2)}) copy-start(s32[16]{0:T(128)} %band_ref.5) | copy-start | bytes 196
  17.1 47.6 %copy-start.16 = (s32[2,64]{1,0:T(2,128)S(1)}, s32[2,64]{1,0:T(2,128)}, u32[]{:S(2)}) copy-start(s32[2,64]{1,0:T(2,128)} %shift_ref.3) | copy-start | bytes 1540
  17.1 47.6 %copy-start.17 = (s32[2,64]{1,0:T(2,128)S(1)}, s32[2,64]{1,0:T(2,128)}, u32[]{:S(2)}) copy-start(s32[2,64]{1,0:T(2,128)} %length_ref.3) | copy-start | bytes 1540
  17.8 47.0 %all-to-all-start = ((bf16[768,16,128]{2,1,0:T(8,128)(2,1)}), bf16[768,16,128]{2,1,0:T(8,128)(2,1)S(1)}, u32[]{:S(2)}, u32[]{:S(2)}) async-start(bf16[768,16,128]{2,1,0:T(8,128)(2,1)} %bitcast.7), calls=%async_computation | async-start | bytes 6291456 | tf_op jit(solution)/shard_map/all_to_all | solution.py:375
  26.2 1.2 %copy-start.1 = (f32[16,128,128]{2,1,0:T(8,128)S(1)}, f32[16,128,128]{2,1,0:T(8,128)}, u32[]{:S(2)}) copy-start(f32[16,128,128]{2,1,0:T(8,128)} %estimate_ref.1) | copy-start | bytes 3145732
  41.8 1.4 %copy-start.3 = (f32[2,16,128,128]{3,2,1,0:T(8,128)}, f32[2,16,128,128]{3,2,1,0:T(8,128)S(1)}, u32[]{:S(2)}) copy-start(f32[2,16,128,128]{3,2,1,0:T(8,128)S(1)} %get-tuple-element.33.recip_ref) | copy-start | bytes 6291460
  43.1 1.0 %copy-start.5 = (bf16[2,4,256,256]{3,2,1,0:T(8,128)(2,1)}, bf16[2,4,256,256]{3,2,1,0:T(8,128)(2,1)S(1)}, u32[]{:S(2)}) copy-start(bf16[2,4,256,256]{3,2,1,0:T(8,128)(2,1)S(1)} %get-tuple-element.27.turned_ref) | copy-start | bytes 3145732
  44.1 0.8 copy-start.7
  44.9 0.8 copy-start.9
  45.7 0.6 copy-start.11
  46.3 0.6 copy-start.14
  64.8 3.1 %copy-start.4 = (f32[2,16,128,128]{3,2,1,0:T(8,128)S(1)}, f32[2,16,128,128]{3,2,1,0:T(8,128)}, u32[]{:S(2)}) copy-start(f32[2,16,128,128]{3,2,1,0:T(8,128)} %copy-done.3) | copy-start | bytes 6291460
  65.5 9.0 %copy-start.8 = (bf16[4,256,256]{2,1,0:T(8,128)(2,1)S(1)}, bf16[4,256,256]{2,1,0:T(8,128)(2,1)}, u32[]{:S(2)}) copy-start(bf16[4,256,256]{2,1,0:T(8,128)(2,1)} %copy-done.7) | copy-start | bytes 1572868
  65.5 9.0 %copy-start.10 = (bf16[2,4,128,256]{3,2,1,0:T(8,128)(2,1)S(1)}, bf16[2,4,128,256]{3,2,1,0:T(8,128)(2,1)}, u32[]{:S(2)}) copy-start(bf16[2,4,128,256]{3,2,1,0:T(8,128)(2,1)} %copy-done.9) | copy-start | bytes 1572868
  65.5 9.0 %copy-start.15 = (bf16[4,32,32]{2,1,0:T(8,128)(2,1)S(1)}, bf16[4,32,32]{2,1,0:T(8,128)(2,1)}, u32[]{:S(2)}) copy-start(bf16[4,32,32]{2,1,0:T(8,128)(2,1)} %copy-done.14) | copy-start | bytes 24580
  65.5 4.1 %collective-permute-start.4 = (bf16[2,16,8,128]{3,2,1,0:T(8,128)(2,1)S(1)}, bf16[2,16,8,128]{3,2,1,0:T(8,128)(2,1)S(1)}, u32[]{:S(2)}, u32[]{:S(2)}) collective-permute-start(bf16[2,16,8,128]{3,2,1,0:T(8,128)(2,1)S(1)} %get-tuple-element.36), channel_id=1, source_target_pairs={{0,16},{16,0},{32,48},{48,32},{64,80},{80,64},{96,112},{112,96},{1... | collective-permute-start | bytes 196616 | tf_op jit(solution)/shard_map/ppermute | solution.py:328
  65.6 5.7 %collective-permute-start.5 = (bf16[2,16,8,128]{3,2,1,0:T(8,128)(2,1)S(1)}, bf16[2,16,8,128]{3,2,1,0:T(8,128)(2,1)S(1)}, u32[]{:S(2)}, u32[]{:S(2)}) collective-permute-start(bf16[2,16,8,128]{3,2,1,0:T(8,128)(2,1)S(1)} %get-tuple-element.37), channel_id=1, source_target_pairs={{16,32},{32,16},{48,64},{64,48},{80,96},{96,80},{17,33},{33,17},{4... | collective-permute-start | bytes 196616 | tf_op jit(solution)/shard_map/ppermute | solution.py:328
  67.9 12.7 %copy-start.2 = (f32[16,128,128]{2,1,0:T(8,128)S(1)}, f32[16,128,128]{2,1,0:T(8,128)}, u32[]{:S(2)}) copy-start(f32[16,128,128]{2,1,0:T(8,128)} %estimate_ref.1) | copy-start | bytes 3145732
  67.9 12.7 %copy-start.6 = (bf16[2,4,256,256]{3,2,1,0:T(8,128)(2,1)S(1)}, bf16[2,4,256,256]{3,2,1,0:T(8,128)(2,1)}, u32[]{:S(2)}) copy-start(bf16[2,4,256,256]{3,2,1,0:T(8,128)(2,1)} %copy-done.5) | copy-start | bytes 3145732
  67.9 12.7 %copy-start.12 = (bf16[4,2,48,128]{3,2,1,0:T(8,128)(2,1)S(1)}, bf16[4,2,48,128]{3,2,1,0:T(8,128)(2,1)}, u32[]{:S(2)}) copy-start(bf16[4,2,48,128]{3,2,1,0:T(8,128)(2,1)} %copy-done.11) | copy-start | bytes 294916
  71.5 5.3 %collective-permute-start.6 = (bf16[2,18,8,128]{3,2,1,0:T(8,128)(2,1)S(1)}, bf16[2,18,8,128]{3,2,1,0:T(8,128)(2,1)S(1)}, u32[]{:S(2)}, u32[]{:S(2)}) collective-permute-start(bf16[2,18,8,128]{3,2,1,0:T(8,128)(2,1)S(1)} %get-tuple-element.39), channel_id=1, source_target_pairs={{0,1},{1,0},{2,3},{3,2},{4,5},{5,4},{6,7},{7,6},{8,9},{9,8},{10,11... | collective-permute-start | bytes 221192 | tf_op jit(solution)/shard_map/ppermute | solution.py:328
  72.2 8.3 %collective-permute-start.7 = (bf16[2,18,8,128]{3,2,1,0:T(8,128)(2,1)S(1)}, bf16[2,18,8,128]{3,2,1,0:T(8,128)(2,1)S(1)}, u32[]{:S(2)}, u32[]{:S(2)}) collective-permute-start(bf16[2,18,8,128]{3,2,1,0:T(8,128)(2,1)S(1)} %get-tuple-element.40), channel_id=1, source_target_pairs={{1,2},{2,1},{3,4},{4,3},{5,6},{6,5},{7,8},{8,7},{9,10},{10,9},{11,... | collective-permute-start | bytes 221192 | tf_op jit(solution)/shard_map/ppermute | solution.py:328

commit v5 on v4

--- a/solution.py
+++ b/solution.py
@@ -69,7 +69,7 @@
 
 
 def pack_kernel(
-    devices, me_ref, shift_hbm, length_hbm, measured_hbm, _, out_hbm,
+    devices, me_ref, shift_hbm, length_hbm, measured_hbm, out_hbm,
     rows_ref, measured_ref, shift_ref, length_ref, sems,
 ):
     views, depth, tile_rows, tile_cols = measured_ref.shape
@@ -116,23 +116,6 @@
         out_ref[z] = dot(pick, cells_ref[z].astype(BF16), NT).astype(BF16)
 
 
-def slab_kernel(odd_x_ref, odd_y_ref, cols_ref, even_ref, odd_ref, first_ref, second_ref):
-    tile_rows = cols_ref.shape[-1]
-    pick = edge_picker(even_ref.shape[-1])
-    odd = odd_y_ref[0] == 1
-
-    def plane(i, carry):
-        ends = halo(odd_x_ref, even_ref[i], odd_ref[i])
-        corner = dot(pick, ends, NT)
-        cols = cols_ref[i].astype(F32)
-        for ref, flag in ((first_ref, odd), (second_ref, jnp.logical_not(odd))):
-            ref[i, :, :tile_rows] = jnp.where(flag, cols[:HW], cols[HW:]).astype(BF16)
-            ref[i, :, tile_rows:] = jnp.where(flag, corner[:HW], corner[HW:]).astype(BF16)
-        return carry
-
-    lax.fori_loop(0, cols_ref.shape[0], plane, 0, unroll=True)
-
-
 def dense_slab_kernel(odd_x_ref, odd_y_ref, cols_ref, even_ref, other_ref, first_ref, second_ref):
     views, depth, _, tile_rows = cols_ref.shape
     count = tile_rows // (2 * HW)
@@ -144,17 +127,20 @@
                 edge = cols_ref[view, i].astype(F32)
             else:
                 planes = range((i - depth) * count, (i - depth + 1) * count)
-                ends = [halo(odd_x_ref, even_ref[view, z], other_ref[view, z]) for z in planes]
+                lead = () if len(even_ref.shape) == 3 else (view,)
+                ends = [halo(odd_x_ref, even_ref[*lead, z], other_ref[*lead, z]) for z in planes]
                 edge = dot(pick, jnp.concatenate(ends, axis=0), NT)
             first_ref[view, i] = jnp.where(odd, edge[:HW], edge[HW:]).astype(BF16)
             second_ref[view, i] = jnp.where(odd, edge[HW:], edge[:HW]).astype(BF16)
 
 
 def edges_kernel(
-    devices, tile_rows, me_ref, odd_ref, shift_ref, length_ref, arrived_ref, recip_ref, first_ref, second_ref, rows_ref
-):
-    views = recip_ref.shape[0]
-    odd = odd_ref[0] == 1
+    devices, tile_rows, me_ref, odd_x_ref, odd_y_ref, band_ref, shift_ref, length_ref,
+    arrived_ref, edge_ref, turned_ref, far_ref, even_ref, other_ref,
+    first_ref, second_ref, along_ref, rows_ref, slab_ref, recip_ref,
+):
+    views, depth = edge_ref.shape[:2]
+    odd = odd_x_ref[0] == 1
     groups = shift_ref.shape[1]
     me = me_ref[0]
     low = tile_rows - CAP * HW
@@ -169,14 +155,26 @@
                 for k in range(CAP):
                     rows_ref[view, side, start + k] = arrived_ref[base + k].astype(F32)
                 start = start + length_ref[view, g]
-        head = jnp.transpose(rows_ref[view, 0, :HW], (1, 0, 2)) * recip_ref[view, :, :HW]
+    weights = [turned_ref.at[view] for view in range(views)]
+    far_products(odd_y_ref, even_ref.at[0], other_ref.at[0], weights, slab_ref, [along_ref.at[v] for v in range(views)])
+    pick = edge_picker(tile_rows)
+    for view in range(views):
+        for z in range(depth):
+            b = band_ref[z]
+            along = jnp.concatenate(far_parts(along_ref, view, b, z), axis=0)
+            blurred = edge_ref[view, z] + dot(dot(pick, along, NT).astype(BF16), far_ref[b, view])
+            recip_ref[z] = 1.0 / blurred.astype(BF16).astype(F32)
+        head = jnp.transpose(rows_ref[view, 0, :HW], (1, 0, 2)) * recip_ref[:, :HW]
         tail = rows_ref[view, 1, (CAP - 1) * HW : CAP * HW]
-        tail = jnp.transpose(tail, (1, 0, 2)) * recip_ref[view, :, HW:]
+        tail = jnp.transpose(tail, (1, 0, 2)) * recip_ref[:, HW:]
         first_ref[view] = jnp.where(odd, head, tail).astype(BF16)
         second_ref[view] = jnp.where(odd, tail, head).astype(BF16)
 
 
-def unpack_kernel(devices, me_ref, shift_ref, length_ref, arrived_ref, recip_ref, out_ref, cols_ref, rows_ref):
+def unpack_kernel(
+    devices, me_ref, band_ref, shift_ref, length_ref, arrived_ref, blurred_ref, far_ref, along_ref,
+    out_ref, cols_ref, rows_ref, recip_ref,
+):
     views, depth, tile_rows, tile_cols = out_ref.shape
     groups = shift_ref.shape[1]
     me = me_ref[0]
@@ -191,9 +189,14 @@
             return start + length_ref[view, g]
 
         lax.fori_loop(0, groups, group, 0, unroll=True)
+        for z in range(depth):
+            b = band_ref[z]
+            along = jnp.concatenate(far_parts(along_ref, view, b, z), axis=0)
+            blurred = blurred_ref[view, z] + dot(along, far_ref[b, view], ((0,), (0,)))
+            recip_ref[z] = 1.0 / blurred.astype(BF16).astype(F32)
         for r0 in range(0, tile_rows, 16):
             x = jnp.transpose(rows_ref[view, r0 : r0 + 16], (1, 0, 2))
-            out_ref[view, :, r0 : r0 + 16, :] = (x * recip_ref[view, :, r0 : r0 + 16, :]).astype(BF16)
+            out_ref[view, :, r0 : r0 + 16, :] = (x * recip_ref[:, r0 : r0 + 16, :]).astype(BF16)
         for z in range(depth):
             cols_ref[view, z] = dot(pick, out_ref[view, z], NT).astype(BF16)
 
@@ -206,54 +209,72 @@
     return jnp.where(lane < size + HW, inner, jnp.where(lane < size + 2 * HW, before, 0.0))
 
 
-def blur_far(rows, far, across):
-    return quarters(dot(stacked(halves(dot(rows, far, NT)), 0), across))
+def far_products(odd_ref, even_ref, other_ref, weights, slab_ref, along_ref):
+    depth = slab_ref.shape[0] // (2 * HW)
+    tile_rows = slab_ref.shape[1] // 2
+    count = tile_rows // (2 * HW)
+    owner = lax.broadcasted_iota(jnp.int32, (2 * HW, tile_rows), 1) // (2 * HW)
+    for z in range(depth):
+        at = pl.ds(z * 2 * HW, 2 * HW)
+        slab_ref[at, :tile_rows] = halo(odd_ref, even_ref[z], other_ref[z])
+        corners = halo(odd_ref, even_ref[depth + z // count], other_ref[depth + z // count])
+        slab_ref[at, tile_rows:] = jnp.where(owner == z % count, corners.astype(F32), 0.0).astype(BF16)
+    for turned_ref, out_ref in zip(weights, along_ref):
+        for b in range(turned_ref.shape[0]):
+            along = dot(slab_ref[...], turned_ref[b])
+            high, low = split(along[:, :tile_rows] + along[:, tile_rows:])
+            out_ref[b, 0] = high
+            out_ref[b, 1] = low
+
+
+def far_parts(along_ref, view, b, z):
+    at = pl.ds(z * 2 * HW, 2 * HW)
+    high, low = along_ref[view, b, 0, at, :], along_ref[view, b, 1, at, :]
+    return [high, low, high]
 
 
 def forward_kernel(
-    band_ref, odd_x_ref, odd_y_ref, taps_ref, cells_ref, even_x_ref, other_x_ref, even_y_ref, other_y_ref,
-    recip_ref, edge_ref, rows_ref, ends_ref, cols_ref, turned_ref, far_ref, fwd_rows, fwd_cols, fwd_far,
-):
-    views, depth, tile_rows, tile_cols = recip_ref.shape
+    band_ref, odd_ref, taps_ref, cells_ref, even_ref, other_ref,
+    blurred_ref, edge_ref, fwd_turned_ref, fwd_far_ref, rows_ref, ends_ref, cols_ref, turned_ref, far_ref, fwd_rows, fwd_cols,
+):
+    views, depth, tile_rows, tile_cols = blurred_ref.shape
     bands = taps_ref.shape[2]
-    for view in range(views):
-        for b in range(bands):
-            along = band(taps_ref[0, view, b, 0:1, :], tile_rows)
-            fwd_rows[view, b] = stacked(along[:, : tile_rows + 2 * HW], 0)
-            across = band(taps_ref[0, view, b, 1:2, :], tile_cols)
-            fwd_cols[view, b] = stacked(across[:, :tile_cols].T, 1)
-            fwd_far[view, b] = stacked(across[:, tile_cols:].T[: 2 * HW], 1)
     for b in range(bands):
         ends = jnp.zeros((tile_rows, LANES - tile_rows), F32)
         for view in range(views):
-            along = band(taps_ref[1, view, b, 0:1, :], tile_rows)
-            rows_ref[b, :, view * tile_rows : (view + 1) * tile_rows] = stacked(along[:, :tile_rows], 0)
-            beyond = along[:, tile_rows:]
-            ends = ends + (pltpu.roll(beyond, 2 * HW * view, 1) if view else beyond)
-            turned_ref[view, b, :tile_rows] = stacked(along[:, :tile_rows].T, 1)
-            turned = stacked(beyond.T[: 2 * HW], 1)
-            for at in range(tile_rows, 2 * tile_rows, 2 * HW):
-                turned_ref[view, b, at : at + 2 * HW] = turned
-            across = band(taps_ref[1, view, b, 1:2, :], tile_cols)
-            cols_ref[view, b] = stacked(across[:, :tile_cols].T, 1)
-            high, low = split(across[:, tile_cols:].T[: 2 * HW])
-            far_ref[b, view] = jnp.concatenate([high, high, low], axis=0)
+            for way in range(2):
+                along = band(taps_ref[way, view, b, 0:1, :], tile_rows)
+                across = band(taps_ref[way, view, b, 1:2, :], tile_cols)
+                beyond = along[:, tile_rows:]
+                turned, far = ((fwd_turned_ref, fwd_far_ref), (turned_ref, far_ref))[way]
+                turned[view, b, :tile_rows] = stacked(along[:, :tile_rows].T, 1)
+                corner = stacked(beyond.T[: 2 * HW], 1)
+                for at in range(tile_rows, 2 * tile_rows, 2 * HW):
+                    turned[view, b, at : at + 2 * HW] = corner
+                high, low = split(across[:, tile_cols:].T[: 2 * HW])
+                far[b, view] = jnp.concatenate([high, high, low], axis=0)
+                inner = stacked(across[:, :tile_cols].T, 1)
+                if way == 0:
+                    fwd_rows[view, b] = stacked(along[:, : tile_rows + 2 * HW], 0)
+                    fwd_cols[view, b] = inner
+                else:
+                    rows_ref[b, :, view * tile_rows : (view + 1) * tile_rows] = stacked(along[:, :tile_rows], 0)
+                    ends = ends + (pltpu.roll(beyond, 2 * HW * view, 1) if view else beyond)
+                    cols_ref[view, b] = inner
         ends = jnp.concatenate([ends[:HW], ends[tile_rows - HW :]], axis=0)
         ends_ref[b] = stacked(ends[:, : 2 * HW * views], 0)
 
     def plane(z, carry):
         b = band_ref[z]
         cells = stacked(cells_ref[z], 1)
-        ends = halo(odd_x_ref, even_x_ref[z], other_x_ref[z])
-        far = halo(odd_y_ref, even_y_ref[z], other_y_ref[z])
+        ends = halo(odd_ref, even_ref[z], other_ref[z])
         for view in range(views):
             rows = fwd_rows[view, b]
             blurred = quarters(dot(rows[:, :tile_rows], cells)) + halves(dot(rows[:, tile_rows:], ends))
-            blurred = quarters(dot(stacked(blurred, 0), fwd_cols[view, b])) + blur_far(rows, far, fwd_far[view, b])
-            recip = 1.0 / blurred.astype(BF16).astype(F32)
-            recip_ref[view, z] = recip
-            edge_ref[view, z, :HW] = recip[:HW]
-            edge_ref[view, z, HW:] = recip[tile_rows - HW :]
+            blurred = quarters(dot(stacked(blurred, 0), fwd_cols[view, b]))
+            blurred_ref[view, z] = blurred
+            edge_ref[view, z, :HW] = blurred[:HW]
+            edge_ref[view, z, HW:] = blurred[tile_rows - HW :]
         return carry
 
     lax.fori_loop(0, depth, plane, 0, unroll=2)
@@ -289,28 +310,14 @@
     views, bands = turned_ref.shape[:2]
     depth, tile_rows, tile_cols = near_ref.shape
     step = depth // sems.shape[0]
-    count = tile_rows // (2 * HW)
-    owner = lax.broadcasted_iota(jnp.int32, (2 * HW, tile_rows), 1) // (2 * HW)
-    for view in range(views):
-        for z in range(depth):
-            at = pl.ds(z * 2 * HW, 2 * HW)
-            slab_ref[view, at, :tile_rows] = halo(odd_ref, even_ref[view, z], other_ref[view, z])
-            tile = depth + z // count
-            corners = halo(odd_ref, even_ref[view, tile], other_ref[view, tile])
-            slab_ref[view, at, tile_rows:] = jnp.where(owner == z % count, corners.astype(F32), 0.0).astype(BF16)
-    for view in range(views):
-        for b in range(bands):
-            along = dot(slab_ref[view], turned_ref[view, b])
-            high, low = split(along[:, :tile_rows] + along[:, tile_rows:])
-            along_ref[view, b, 0] = high
-            along_ref[view, b, 1] = low
+    for view in range(views):
+        far_products(odd_ref, even_ref.at[view], other_ref.at[view], [turned_ref.at[view]], slab_ref.at[view], [along_ref.at[view]])
     leave = []
     for z in range(depth):
         b = band_ref[z]
         parts = []
         for view in range(views):
-            high, low = (along_ref[view, b, part, z * 2 * HW : (z + 1) * 2 * HW, :] for part in range(2))
-            parts += [high, low, high]
+            parts += far_parts(along_ref, view, b, z)
         across = far_ref[b].reshape(views * 6 * HW, tile_cols)
         total = near_ref[z] + dot(jnp.concatenate(parts, axis=0), across, ((0,), (0,)))
         out_ref[z] = estimate_ref[z] * (total * (1.0 / views))
@@ -326,15 +333,6 @@
     count = lax.axis_size(axis)
     pairs = lambda begin: [p for i in range(begin, count - 1, 2) for p in ((i, i + 1), (i + 1, i))]
     return lax.ppermute(first, axis, pairs(0)), lax.ppermute(second, axis, pairs(1))
-
-
-def slabs(odd_x, odd_y, cols, first, second):
-    lead = cols.shape[:-2]
-    shape = (cols.size // (cols.shape[-1] * cols.shape[-2]), HW, cols.shape[-1] + 2 * HW)
-    merge = lambda x: x.reshape((shape[0],) + x.shape[-2:])
-    out = jax.ShapeDtypeStruct(shape, BF16)
-    pair = call(slab_kernel, [SMEM] * 2 + [VMEM] * 3, (out, out))(odd_x, odd_y, merge(cols), merge(first), merge(second))
-    return [x.reshape(lead + shape[1:]) for x in pair]
 
 
 def body(estimate, measured, kernels, depth_band, group_shift, group_length):
@@ -353,12 +351,9 @@
     head, tail = estimate[:, :HW], estimate[:, tile_rows - HW :]
     even = gx % 2 == 0
     ex, ox = swap(jnp.where(even, tail, head), jnp.where(even, head, tail), "gx")
-    cols = call(cols_kernel, [VMEM], like(edge_cols.shape[1:], BF16))(estimate)
-    edges = slabs(odd_x, odd_y, cols, ex, ox)
-    ey, oy = (pltpu.with_memory_space_constraint(x, pltpu.HBM) for x in swap(*edges, "gy"))
     outgoing = call(
         functools.partial(pack_kernel, devices),
-        [SMEM, HBM, HBM, HBM, VMEM],
+        [SMEM, HBM, HBM, HBM],
         like((devices, views, CAP, depth, tile_cols), BF16),
         [
             pltpu.VMEM((views, spare, depth, tile_cols), BF16),
@@ -369,51 +364,63 @@
         ],
         HBM,
         60,
-    )(me, group_shift, group_length, measured, edges[0])
+    )(me, group_shift, group_length, measured)
     outgoing = outgoing.reshape(devices * views * CAP, depth, tile_cols)
-    outgoing, ey, oy = lax.optimization_barrier((outgoing, ey, oy))
+    ex, ox = (pltpu.with_memory_space_constraint(x, pltpu.HBM) for x in (ex, ox))
+    outgoing, ex, ox, cells = lax.optimization_barrier((outgoing, ex, ox, estimate))
     arrived = lax.all_to_all(outgoing, ("gx", "gy"), split_axis=0, concat_axis=0, tiled=True)
+
+    cols = call(cols_kernel, [VMEM], like(edge_cols.shape[1:], BF16))(cells)
+    tiles = depth + depth * 2 * HW // tile_rows
+    dense = lambda lead, *args: call(
+        dense_slab_kernel, [SMEM] * 2 + [VMEM] * 3, (like((lead, tiles, HW, tile_rows), BF16),) * 2
+    )(odd_x, odd_y, *args)
+    ey, oy = swap(*dense(1, cols[None], ex, ox), "gy")
 
     norm = kernels / jnp.sum(kernels, axis=3, keepdims=True)
     tap_rows = jnp.stack([norm, norm[..., ::-1]])
     tap_rows = jnp.pad(tap_rows, ((0, 0),) * 4 + ((0, LANES - kernels.shape[3]),))
-    recip, edge_recip, rows_mat, ends_mat, cols_mat, turned_mat, far_mat = call(
+    turned_like = like((views, bands, 2 * tile_rows, 2 * tile_rows), BF16)
+    far_like = like((bands, views, 6 * HW, tile_cols), BF16)
+    blurred, edge_blurred, fwd_turned, fwd_far, rows_mat, ends_mat, cols_mat, turned_mat, far_mat = call(
         forward_kernel,
-        [SMEM] * 3 + [VMEM] * 6,
+        [SMEM] * 2 + [VMEM] * 4,
         (
             like(measured.shape, F32),
             like((views, depth, 2 * HW, tile_cols), F32),
+            turned_like,
+            far_like,
             like((bands, 2 * tile_rows, views * tile_rows), BF16),
             like((bands, 4 * HW, views * 2 * HW), BF16),
             like((views, bands, tile_cols, 2 * tile_cols), BF16),
-            like((views, bands, 2 * tile_rows, 2 * tile_rows), BF16),
-            like((bands, views, 6 * HW, tile_cols), BF16),
+            turned_like,
+            far_like,
         ),
         [
             pltpu.VMEM((views, bands, 2 * tile_rows, tile_rows + 2 * HW), BF16),
             pltpu.VMEM((views, bands, tile_cols, 2 * tile_cols), BF16),
-            pltpu.VMEM((views, bands, 2 * HW, 2 * tile_cols), BF16),
         ],
-    )(depth_band, odd_x, odd_y, tap_rows, estimate, ex, ox, ey, oy)
-
-    ex, ox = swap(
-        *call(
-            functools.partial(edges_kernel, devices, tile_rows),
-            [SMEM] * 4 + [VMEM] * 2,
-            (edge_rows, edge_rows),
-            [pltpu.VMEM((views, 2, CAP * HW + 8, depth, tile_cols), F32)],
-        )(me, odd_x, group_shift, group_length, arrived, edge_recip),
-        "gx",
-    )
+    )(depth_band, odd_x, tap_rows, cells, ex, ox)
+
+    along_like = like((views, bands, 2, depth * 2 * HW, tile_rows), BF16)
+    first, second, along = call(
+        functools.partial(edges_kernel, devices, tile_rows),
+        [SMEM] * 6 + [VMEM] * 6,
+        (edge_rows, edge_rows, along_like),
+        [
+            pltpu.VMEM((views, 2, CAP * HW + 8, depth, tile_cols), F32),
+            pltpu.VMEM((depth * 2 * HW, 2 * tile_rows), BF16),
+            pltpu.VMEM((depth, 2 * HW, tile_cols), F32),
+        ],
+    )(me, odd_x, odd_y, depth_band, group_shift, group_length, arrived, edge_blurred, fwd_turned, fwd_far, ey, oy)
+    ex, ox = swap(first, second, "gx")
     ratio, cols = call(
         functools.partial(unpack_kernel, devices),
-        [SMEM, SMEM, SMEM, VMEM, VMEM],
+        [SMEM] * 4 + [VMEM] * 4,
         (whole, edge_cols),
-        [pltpu.VMEM((views, spare, depth, tile_cols), F32)],
-    )(me, group_shift, group_length, arrived, recip)
-    tiles = like((views, depth + depth * 2 * HW // tile_rows, HW, tile_rows), BF16)
-    edges = call(dense_slab_kernel, [SMEM] * 2 + [VMEM] * 3, (tiles, tiles))(odd_x, odd_y, cols, ex, ox)
-    ey, oy = swap(*edges, "gy")
+        [pltpu.VMEM((views, spare, depth, tile_cols), F32), pltpu.VMEM(estimate.shape, F32)],
+    )(me, depth_band, group_shift, group_length, arrived, blurred, fwd_far, along)
+    ey, oy = swap(*dense(views, cols, ex, ox), "gy")
     near = call(
         near_kernel,
         [SMEM] * 2 + [VMEM] * 6,

time: 84.4 us -> 83.1 us (0.985)
  waiting for transfers between devices: 25.5 us -> 16.5 us
  local copies, waits for them, and re-layouts: 8.35 us -> 12.1 us
  starting transfers between devices: 21.8 us -> 24.5 us
  Pallas kernels: 25.6 us -> 27.5 us
    all_to_all x1, waiting for transfers between devices: 17.9 us -> 0.01 us  [body(): lax.all_to_all(outgoing, ('gx', 'gy'), split_axis=0, concat_axis=0, tiled...]
    ppermute x4, waiting for transfers between devices: 0.44 us -> 7.83 us  [swap(): lax.ppermute(first, axis, pairs(0))]
    unnamed x44 -> x50, local copies, waits for them, and re-layouts: 8.24 us -> 12 us
    all_to_all x1, starting transfers between devices: 8.04 us -> 10.9 us  [body(): lax.all_to_all(outgoing, ('gx', 'gy'), split_axis=0, concat_axis=0, tiled...]
    pallas_call x7, Pallas kernels: 21.2 us -> 22.9 us  [the longest x1 11.1 us: body(): call(forward_kernel, [SMEM] * 2 + [VMEM] * 4, (like(measured.shape, F32),...]
    ppermute x4, waiting for transfers between devices: 7.21 us -> 8.72 us  [swap(): lax.ppermute(second, axis, pairs(1))]
    ppermute x4, starting transfers between devices: 12.8 us -> 11.7 us  [swap(): lax.ppermute(second, axis, pairs(1))]
    ppermute x4, starting transfers between devices: 0.93 us -> 1.87 us  [swap(): lax.ppermute(first, axis, pairs(0))]
  transfers between devices with their start and end apart: 9 -> 9, of which waited for: 5 -> 5; matrix products, arithmetic and copies ran while one was open for 0% -> 0% of each run, Pallas kernels for 27% -> 24%
where the time goes in v5:
time: 83.1 us; the launch traced here: 82.1 us
  Pallas kernels  27.5 us (33%)
  starting transfers between devices  24.5 us (29%)
  waiting for transfers between devices  16.5 us (20%)
  local copies, waits for them, and re-layouts  12.1 us (15%)
  other arithmetic  1.16 us (1%)
    unnamed x50, local copies, waits for them, and re-layouts  12 us
    ppermute x4, starting transfers between devices, swap(): lax.ppermute(second, axis, pairs(1))  11.7 us
    pallas_call x1, Pallas kernels, body(): call(forward_kernel, [SMEM] * 2 + [VMEM] * 4, (like(measured.shape, F32),...  11.1 us
    all_to_all x1, starting transfers between devices, body(): lax.all_to_all(outgoing, ('gx', 'gy'), split_axis=0, concat_axis=0, tiled...  10.9 us
    ppermute x4, waiting for transfers between devices, swap(): lax.ppermute(second, axis, pairs(1))  8.72 us
    ppermute x4, waiting for transfers between devices, swap(): lax.ppermute(first, axis, pairs(0))  7.83 us
    pallas_call x1, Pallas kernels, body(): call(functools.partial(edges_kernel, devices, tile_rows), [SMEM] * 6 + [V...  5.09 us
    pallas_call x1, Pallas kernels, body(): call(functools.partial(pack_kernel, devices), [SMEM, HBM, HBM, HBM], like...  2.93 us
  transfers between devices with their start and end apart: 9, of which 5 were waited for; matrix products, arithmetic and copies ran while one was open for 0% of the time, Pallas kernels for 24%

profile of v5, /device:TPU:30, one launch (start us, length us, event | category | flops | bytes accessed | tf_op | source)
XLA Modules:
  0.0 82.1 jit_solution(715152666190277090)
XLA Ops:
  0.0 0.9 %slice_select_fusion = (f32[16,8,128]{2,1,0:T(8,128)S(1)}, f32[16,8,128]{2,1,0:T(8,128)S(1)}) fusion(f32[16,128,128]{2,1,0:T(8,128)} %estimate_ref.1, pred[]{:T(512)S(6)} %eq.7), kind=kLoop, calls=%fused_computation | loop fusion | flops 32768 | bytes 262145 | tf_op jit(solution)/shard_map/jit(_where)/select_n | solution.py:353
  0.9 2.2 %collective-permute-start.1 = (f32[16,8,128]{2,1,0:T(8,128)S(1)}, f32[16,8,128]{2,1,0:T(8,128)S(1)}, u32[]{:S(2)}, u32[]{:S(2)}) collective-permute-start(f32[16,8,128]{2,1,0:T(8,128)S(1)} %get-tuple-element.49), channel_id=1, source_target_pairs={{16,32},{32,16},{48,64},{64,48},{80,96},{96,80},{17,33},{33,17},{4... | collective-permute-start | bytes 196616 | tf_op jit(solution)/shard_map/ppermute | solution.py:335
  3.2 2.9 %shard_map.64 = bf16[128,2,3,16,128]{4,3,2,1,0:T(8,128)(2,1)} custom-call(s32[1]{0:T(128)} %bitcast.4.me_ref, s32[2,64]{1,0:T(2,128)} %shift_ref.3, s32[2,64]{1,0:T(2,128)} %length_ref.3, bf16[2,16,128,128]{3,2,1,0:T(8,128)(2,1)} %measured_hbm.1), custom_call_target="tpu_custom_call" | custom-call | tf_op jit(solution)/shard_map/pallas_call | solution.py:354
  6.5 0.6 copy-done.22
  7.1 10.9 %all-to-all-start = ((bf16[768,16,128]{2,1,0:T(8,128)(2,1)}), bf16[768,16,128]{2,1,0:T(8,128)(2,1)S(1)}, u32[]{:S(2)}, u32[]{:S(2)}) async-start(bf16[768,16,128]{2,1,0:T(8,128)(2,1)} %bitcast.9), calls=%async_computation | async-start | bytes 6291456 | tf_op jit(solution)/shard_map/all_to_all | solution.py:371
  18.5 1.2 %copy-done = f32[16,128,128]{2,1,0:T(8,128)S(1)} copy-done((f32[16,128,128]{2,1,0:T(8,128)S(1)}, f32[16,128,128]{2,1,0:T(8,128)}, u32[]{:S(2)}) %copy-start) | copy-done | bytes 1048600
  19.7 0.4 shard_map.66
  20.0 1.1 %shard_map.67 = (bf16[1,18,8,128]{3,2,1,0:T(8,128)(2,1)S(1)}, bf16[1,18,8,128]{3,2,1,0:T(8,128)(2,1)S(1)}) custom-call(s32[1]{0:T(128)} %bitcast.1.odd_ref.odd_x_ref, s32[1]{0:T(128)} %bitcast.odd_y_ref.odd_ref, bf16[1,16,16,128]{3,2,1,0:T(8,128)(2,1)S(1)} %bitcast.8, f32[16,8,128]{2,1,0:T(8,128)} %copy-done.23, f32[16,8,128]{2,1,0:T(8,128)} %copy-done.22), custom_call_target="tpu_custom_call" | custom-call | tf_op jit(solution)/shard_map/pallas_call | solution.py:375
  21.1 1.7 %collective-permute-start.2 = (bf16[1,18,8,128]{3,2,1,0:T(8,128)(2,1)S(1)}, bf16[1,18,8,128]{3,2,1,0:T(8,128)(2,1)S(1)}, u32[]{:S(2)}, u32[]{:S(2)}) collective-permute-start(bf16[1,18,8,128]{3,2,1,0:T(8,128)(2,1)S(1)} %get-tuple-element.40), channel_id=1, source_target_pairs={{0,1},{1,0},{2,3},{3,2},{4,5},{5,4},{6,7},{7,6},{8,9},{9,8},{10,11... | collective-permute-start | bytes 110600 | tf_op jit(solution)/shard_map/ppermute | solution.py:335
  22.8 4.5 %collective-permute-start.3 = (bf16[1,18,8,128]{3,2,1,0:T(8,128)(2,1)S(1)}, bf16[1,18,8,128]{3,2,1,0:T(8,128)(2,1)S(1)}, u32[]{:S(2)}, u32[]{:S(2)}) collective-permute-start(bf16[1,18,8,128]{3,2,1,0:T(8,128)(2,1)S(1)} %get-tuple-element.41), channel_id=1, source_target_pairs={{1,2},{2,1},{3,4},{4,3},{5,6},{6,5},{7,8},{8,7},{9,10},{10,9},{11,... | collective-permute-start | bytes 110600 | tf_op jit(solution)/shard_map/ppermute | solution.py:335
  27.3 1.2 %copy-done.1 = f32[16,128,128]{2,1,0:T(8,128)S(1)} copy-done((f32[16,128,128]{2,1,0:T(8,128)S(1)}, f32[16,128,128]{2,1,0:T(8,128)}, u32[]{:S(2)}) %copy-start.1) | copy-done | bytes 1048600
  28.6 11.1 %shard_map.65 = (f32[2,16,128,128]{3,2,1,0:T(8,128)S(1)}, f32[2,16,16,128]{3,2,1,0:T(8,128)S(1)}, bf16[2,4,256,256]{3,2,1,0:T(8,128)(2,1)S(1)}, bf16[4,2,48,128]...) custom-call(s32[16]{0:T(128)S(1)} %copy-done.19, ...), custom_call_target="tpu_custom_call" | custom-call | tf_op jit(solution)/shard_map/pallas_call | solution.py:385
  39.7 1.3 %copy-done.3 = f32[2,16,128,128]{3,2,1,0:T(8,128)} copy-done((f32[2,16,128,128]{3,2,1,0:T(8,128)}, f32[2,16,128,128]{3,2,1,0:T(8,128)S(1)}, u32[]{:S(2)}) %copy-start.3) | copy-done | bytes 2097176
  41.0 1.0 %copy-done.5 = bf16[2,4,256,256]{3,2,1,0:T(8,128)(2,1)} copy-done((bf16[2,4,256,256]{3,2,1,0:T(8,128)(2,1)}, bf16[2,4,256,256]{3,2,1,0:T(8,128)(2,1)S(1)}, u32[]{:S(2)}) %copy-start.5) | copy-done | bytes 1048600
  42.0 1.0 %copy-done.7 = bf16[2,4,256,256]{3,2,1,0:T(8,128)(2,1)} copy-done((bf16[2,4,256,256]{3,2,1,0:T(8,128)(2,1)}, bf16[2,4,256,256]{3,2,1,0:T(8,128)(2,1)S(1)}, u32[]{:S(2)}) %copy-start.7) | copy-done | bytes 1048600
  43.0 0.8 copy-done.9
  43.8 0.8 copy-done.11
  44.6 0.6 copy-done.13
  45.2 0.6 copy-done.17
  45.9 7.8 %collective-permute-done.2.even_ref = bf16[1,18,8,128]{3,2,1,0:T(8,128)(2,1)S(1)} collective-permute-done((bf16[1,18,8,128]{3,2,1,0:T(8,128)(2,1)S(1)}, bf16[1,18,8,128]{3,2,1,0:T(8,128)(2,1)S(1)}, u32[]{:S(2)}, u32[]{:S(2)}) %collective-permute-start.2) | collective-permute-done | bytes 36896 | tf_op jit(solution)/shard_map/ppermute | solution.py:335
  53.7 4.1 %collective-permute-done.3.other_ref = bf16[1,18,8,128]{3,2,1,0:T(8,128)(2,1)S(1)} collective-permute-done((bf16[1,18,8,128]{3,2,1,0:T(8,128)(2,1)S(1)}, bf16[1,18,8,128]{3,2,1,0:T(8,128)(2,1)S(1)}, u32[]{:S(2)}, u32[]{:S(2)}) %collective-permute-start.3) | collective-permute-done | bytes 36896 | tf_op jit(solution)/shard_map/ppermute | solution.py:335
  57.8 0.6 copy-done.15
  58.4 1.4 %copy-done.8 = bf16[2,4,256,256]{3,2,1,0:T(8,128)(2,1)S(1)} copy-done((bf16[2,4,256,256]{3,2,1,0:T(8,128)(2,1)S(1)}, bf16[2,4,256,256]{3,2,1,0:T(8,128)(2,1)}, u32[]{:S(2)}) %copy-start.8) | copy-done | bytes 1048600
  59.8 0.8 copy-done.16
  60.6 5.1 %shard_map.68 = (bf16[2,16,8,128]{3,2,1,0:T(8,128)(2,1)S(1)}, bf16[2,16,8,128]{3,2,1,0:T(8,128)(2,1)S(1)}, bf16[2,4,2,256,128]{4,3,2,1,0:T(8,128)(2,1)S(1)}) custom-call(s32[1]{0:T(128)} %bitcast.4.me_ref, s32[1]{0:T(128)} %bitcast.1.odd_ref.odd_x_ref, s32[1]{0:T(128)} %bitcast.odd_y_ref.odd_ref, s32[16]{0:T(128)S(1)} %copy-done.19, s32[2,64]{1,0:T(2,128)S(1)} %copy-done.20, ...), custom_call_target="tpu_custom_call" | custom-call | tf_op jit(solution)/shard_map/pallas_call | solution.py:406
  65.7 2.5 %collective-permute-start.5 = (bf16[2,16,8,128]{3,2,1,0:T(8,128)(2,1)S(1)}, bf16[2,16,8,128]{3,2,1,0:T(8,128)(2,1)S(1)}, u32[]{:S(2)}, u32[]{:S(2)}) collective-permute-start(bf16[2,16,8,128]{3,2,1,0:T(8,128)(2,1)S(1)} %get-tuple-element.45), channel_id=1, source_target_pairs={{16,32},{32,16},{48,64},{64,48},{80,96},{96,80},{17,33},{33,17},{4... | collective-permute-start | bytes 196616 | tf_op jit(solution)/shard_map/ppermute | solution.py:335
  68.3 2.2 %shard_map.69 = (bf16[2,16,128,128]{3,2,1,0:T(8,128)(2,1)S(1)}, bf16[2,16,16,128]{3,2,1,0:T(8,128)(2,1)S(1)}) custom-call(s32[1]{0:T(128)} %bitcast.4.me_ref, s32[16]{0:T(128)S(1)} %copy-done.19, s32[2,64]{1,0:T(2,128)S(1)} %copy-done.20, s32[2,64]{1,0:T(2,128)S(1)} %copy-done.21, bf16[768,16,128]{2,1,0:T(8,128)(2,1)S(1)} %all-to-all-done.arrived_ref, ...), custom_call_target="tpu_custom_call" | custom-call | tf_op jit(solution)/shard_map/pallas_call | solution.py:417
  70.5 0.8 collective-permute-done.5.other_ref
  71.5 2.5 %collective-permute-start.7 = (bf16[2,18,8,128]{3,2,1,0:T(8,128)(2,1)S(1)}, bf16[2,18,8,128]{3,2,1,0:T(8,128)(2,1)S(1)}, u32[]{:S(2)}, u32[]{:S(2)}) collective-permute-start(bf16[2,18,8,128]{3,2,1,0:T(8,128)(2,1)S(1)} %get-tuple-element.48), channel_id=1, source_target_pairs={{1,2},{2,1},{3,4},{4,3},{5,6},{6,5},{7,8},{8,7},{9,10},{10,9},{11,... | collective-permute-start | bytes 221192 | tf_op jit(solution)/shard_map/ppermute | solution.py:335
  74.0 2.3 %shard_map.70.near_ref = f32[16,128,128]{2,1,0:T(8,128)S(1)} custom-call(s32[16]{0:T(128)S(1)} %copy-done.19, s32[1]{0:T(128)} %bitcast.1.odd_ref.odd_x_ref, bf16[4,256,256]{2,1,0:T(8,128)(2,1)S(1)} %copy-done.10, bf16[4,32,32]{2,1,0:T(8,128)(2,1)S(1)} %copy-done.18, bf16[2,4,128,256]{3,2,1,0:T(8,128)(2,1)S(1)} %copy-done.12, ...), custom_call_target="tpu_custom_call" | custom-call | tf_op jit(solution)/shard_map/pallas_call | solution.py:424
  76.4 3.5 %collective-permute-done.7.other_ref = bf16[2,18,8,128]{3,2,1,0:T(8,128)(2,1)S(1)} collective-permute-done((bf16[2,18,8,128]{3,2,1,0:T(8,128)(2,1)S(1)}, bf16[2,18,8,128]{3,2,1,0:T(8,128)(2,1)S(1)}, u32[]{:S(2)}, u32[]{:S(2)}) %collective-permute-start.7) | collective-permute-done | bytes 73760 | tf_op jit(solution)/shard_map/ppermute | solution.py:335
  79.9 2.2 %shard_map.72 = f32[16,128,128]{2,1,0:T(8,128)} custom-call(s32[16]{0:T(128)S(1)} %copy-done.19, s32[1]{0:T(128)} %bitcast.odd_y_ref.odd_ref, bf16[2,4,256,256]{3,2,1,0:T(8,128)(2,1)S(1)} %copy-done.6, bf16[4,2,48,128]{3,2,1,0:T(8,128)(2,1)S(1)} %copy-done.14, f32[16,128,128]{2,1,0:T(8,128)S(1)} %shard_map.70.near_ref, ...), custom_call_target="tpu_custom_call" | custom-call | tf_op jit(solution)/shard_map/pallas_call | solution.py:433
  (51 shorter events, 1.2 us)
Async XLA Ops:
  0.9 5.6 %collective-permute-start.1 = (f32[16,8,128]{2,1,0:T(8,128)S(1)}, f32[16,8,128]{2,1,0:T(8,128)S(1)}, u32[]{:S(2)}, u32[]{:S(2)}) collective-permute-start(f32[16,8,128]{2,1,0:T(8,128)S(1)} %get-tuple-element.49), channel_id=1, source_target_pairs={{16,32},{32,16},{48,64},{64,48},{80,96},{96,80},{17,33},{33,17},{4... | collective-permute-start | bytes 196616 | tf_op jit(solution)/shard_map/ppermute | solution.py:335
  3.1 3.4 %collective-permute-start = (f32[16,8,128]{2,1,0:T(8,128)S(1)}, f32[16,8,128]{2,1,0:T(8,128)S(1)}, u32[]{:S(2)}, u32[]{:S(2)}) collective-permute-start(f32[16,8,128]{2,1,0:T(8,128)S(1)} %get-tuple-element.50), channel_id=1, source_target_pairs={{0,16},{16,0},{32,48},{48,32},{64,80},{80,64},{96,112},{112,96},{1... | collective-permute-start | bytes 196616 | tf_op jit(solution)/shard_map/ppermute | solution.py:335
  6.5 0.6 copy-start.22
  6.5 0.6 copy-start.23
  6.5 11.6 %copy-start.24 = (f32[2,4,2,17]{3,2,1,0:T(2,128)S(1)}, f32[2,4,2,17]{3,2,1,0:T(2,128)}, u32[]{:S(2)}) copy-start(f32[2,4,2,17]{3,2,1,0:T(2,128)} %param.8) | copy-start | bytes 3268
  6.5 20.8 %copy-start.19 = (s32[16]{0:T(128)S(1)}, s32[16]{0:T(128)}, u32[]{:S(2)}) copy-start(s32[16]{0:T(128)} %band_ref.9) | copy-start | bytes 196
  6.5 51.9 %copy-start.20 = (s32[2,64]{1,0:T(2,128)S(1)}, s32[2,64]{1,0:T(2,128)}, u32[]{:S(2)}) copy-start(s32[2,64]{1,0:T(2,128)} %shift_ref.3) | copy-start | bytes 1540
  6.5 51.9 %copy-start.21 = (s32[2,64]{1,0:T(2,128)S(1)}, s32[2,64]{1,0:T(2,128)}, u32[]{:S(2)}) copy-start(s32[2,64]{1,0:T(2,128)} %length_ref.3) | copy-start | bytes 1540
  7.1 51.3 %all-to-all-start = ((bf16[768,16,128]{2,1,0:T(8,128)(2,1)}), bf16[768,16,128]{2,1,0:T(8,128)(2,1)S(1)}, u32[]{:S(2)}, u32[]{:S(2)}) async-start(bf16[768,16,128]{2,1,0:T(8,128)(2,1)} %bitcast.9), calls=%async_computation | async-start | bytes 6291456 | tf_op jit(solution)/shard_map/all_to_all | solution.py:371
  18.4 1.2 %copy-start = (f32[16,128,128]{2,1,0:T(8,128)S(1)}, f32[16,128,128]{2,1,0:T(8,128)}, u32[]{:S(2)}) copy-start(f32[16,128,128]{2,1,0:T(8,128)} %estimate_ref.1) | copy-start | bytes 3145732
  21.1 32.6 %collective-permute-start.2 = (bf16[1,18,8,128]{3,2,1,0:T(8,128)(2,1)S(1)}, bf16[1,18,8,128]{3,2,1,0:T(8,128)(2,1)S(1)}, u32[]{:S(2)}, u32[]{:S(2)}) collective-permute-start(bf16[1,18,8,128]{3,2,1,0:T(8,128)(2,1)S(1)} %get-tuple-element.40), channel_id=1, source_target_pairs={{0,1},{1,0},{2,3},{3,2},{4,5},{5,4},{6,7},{7,6},{8,9},{9,8},{10,11... | collective-permute-start | bytes 110600 | tf_op jit(solution)/shard_map/ppermute | solution.py:335
  22.8 35.0 %collective-permute-start.3 = (bf16[1,18,8,128]{3,2,1,0:T(8,128)(2,1)S(1)}, bf16[1,18,8,128]{3,2,1,0:T(8,128)(2,1)S(1)}, u32[]{:S(2)}, u32[]{:S(2)}) collective-permute-start(bf16[1,18,8,128]{3,2,1,0:T(8,128)(2,1)S(1)} %get-tuple-element.41), channel_id=1, source_target_pairs={{1,2},{2,1},{3,4},{4,3},{5,6},{6,5},{7,8},{8,7},{9,10},{10,9},{11,... | collective-permute-start | bytes 110600 | tf_op jit(solution)/shard_map/ppermute | solution.py:335
  27.3 1.2 %copy-start.1 = (f32[16,128,128]{2,1,0:T(8,128)S(1)}, f32[16,128,128]{2,1,0:T(8,128)}, u32[]{:S(2)}) copy-start(f32[16,128,128]{2,1,0:T(8,128)} %estimate_ref.1) | copy-start | bytes 3145732
  39.7 1.3 %copy-start.3 = (f32[2,16,128,128]{3,2,1,0:T(8,128)}, f32[2,16,128,128]{3,2,1,0:T(8,128)S(1)}, u32[]{:S(2)}) copy-start(f32[2,16,128,128]{3,2,1,0:T(8,128)S(1)} %get-tuple-element.36.blurred_ref) | copy-start | bytes 6291460
  41.0 1.0 %copy-start.5 = (bf16[2,4,256,256]{3,2,1,0:T(8,128)(2,1)}, bf16[2,4,256,256]{3,2,1,0:T(8,128)(2,1)S(1)}, u32[]{:S(2)}) copy-start(bf16[2,4,256,256]{3,2,1,0:T(8,128)(2,1)S(1)} %get-tuple-element.30.turned_ref) | copy-start | bytes 3145732
  42.0 1.0 %copy-start.7 = (bf16[2,4,256,256]{3,2,1,0:T(8,128)(2,1)}, bf16[2,4,256,256]{3,2,1,0:T(8,128)(2,1)S(1)}, u32[]{:S(2)}) copy-start(bf16[2,4,256,256]{3,2,1,0:T(8,128)(2,1)S(1)} %get-tuple-element.39.turned_ref) | copy-start | bytes 3145732
  43.0 0.8 copy-start.9
  43.8 0.8 copy-start.11
  44.6 0.6 copy-start.13
  58.4 9.9 %copy-start.4 = (f32[2,16,128,128]{3,2,1,0:T(8,128)S(1)}, f32[2,16,128,128]{3,2,1,0:T(8,128)}, u32[]{:S(2)}) copy-start(f32[2,16,128,128]{3,2,1,0:T(8,128)} %copy-done.3) | copy-start | bytes 6291460
  58.4 1.4 %copy-start.8 = (bf16[2,4,256,256]{3,2,1,0:T(8,128)(2,1)S(1)}, bf16[2,4,256,256]{3,2,1,0:T(8,128)(2,1)}, u32[]{:S(2)}) copy-start(bf16[2,4,256,256]{3,2,1,0:T(8,128)(2,1)} %copy-done.7) | copy-start | bytes 3145732
  59.8 0.8 copy-start.16
  65.6 4.9 %collective-permute-start.4 = (bf16[2,16,8,128]{3,2,1,0:T(8,128)(2,1)S(1)}, bf16[2,16,8,128]{3,2,1,0:T(8,128)(2,1)S(1)}, u32[]{:S(2)}, u32[]{:S(2)}) collective-permute-start(bf16[2,16,8,128]{3,2,1,0:T(8,128)(2,1)S(1)} %get-tuple-element.44), channel_id=1, source_target_pairs={{0,16},{16,0},{32,48},{48,32},{64,80},{80,64},{96,112},{112,96},{1... | collective-permute-start | bytes 196616 | tf_op jit(solution)/shard_map/ppermute | solution.py:335
  65.7 5.6 %collective-permute-start.5 = (bf16[2,16,8,128]{3,2,1,0:T(8,128)(2,1)S(1)}, bf16[2,16,8,128]{3,2,1,0:T(8,128)(2,1)S(1)}, u32[]{:S(2)}, u32[]{:S(2)}) collective-permute-start(bf16[2,16,8,128]{3,2,1,0:T(8,128)(2,1)S(1)} %get-tuple-element.45), channel_id=1, source_target_pairs={{16,32},{32,16},{48,64},{64,48},{80,96},{96,80},{17,33},{33,17},{4... | collective-permute-start | bytes 196616 | tf_op jit(solution)/shard_map/ppermute | solution.py:335
  68.3 5.7 %copy-start.10 = (bf16[4,256,256]{2,1,0:T(8,128)(2,1)S(1)}, bf16[4,256,256]{2,1,0:T(8,128)(2,1)}, u32[]{:S(2)}) copy-start(bf16[4,256,256]{2,1,0:T(8,128)(2,1)} %copy-done.9) | copy-start | bytes 1572868
  68.3 5.7 %copy-start.12 = (bf16[2,4,128,256]{3,2,1,0:T(8,128)(2,1)S(1)}, bf16[2,4,128,256]{3,2,1,0:T(8,128)(2,1)}, u32[]{:S(2)}) copy-start(bf16[2,4,128,256]{3,2,1,0:T(8,128)(2,1)} %copy-done.11) | copy-start | bytes 1572868
  68.3 5.7 %copy-start.18 = (bf16[4,32,32]{2,1,0:T(8,128)(2,1)S(1)}, bf16[4,32,32]{2,1,0:T(8,128)(2,1)}, u32[]{:S(2)}) copy-start(bf16[4,32,32]{2,1,0:T(8,128)(2,1)} %copy-done.17) | copy-start | bytes 24580
  70.5 9.4 %copy-start.2 = (f32[16,128,128]{2,1,0:T(8,128)S(1)}, f32[16,128,128]{2,1,0:T(8,128)}, u32[]{:S(2)}) copy-start(f32[16,128,128]{2,1,0:T(8,128)} %estimate_ref.1) | copy-start | bytes 3145732
  70.5 9.4 %copy-start.6 = (bf16[2,4,256,256]{3,2,1,0:T(8,128)(2,1)S(1)}, bf16[2,4,256,256]{3,2,1,0:T(8,128)(2,1)}, u32[]{:S(2)}) copy-start(bf16[2,4,256,256]{3,2,1,0:T(8,128)(2,1)} %copy-done.5) | copy-start | bytes 3145732
  70.5 9.3 %copy-start.14 = (bf16[4,2,48,128]{3,2,1,0:T(8,128)(2,1)S(1)}, bf16[4,2,48,128]{3,2,1,0:T(8,128)(2,1)}, u32[]{:S(2)}) copy-start(bf16[4,2,48,128]{3,2,1,0:T(8,128)(2,1)} %copy-done.13) | copy-start | bytes 294916
  71.5 4.9 %collective-permute-start.6 = (bf16[2,18,8,128]{3,2,1,0:T(8,128)(2,1)S(1)}, bf16[2,18,8,128]{3,2,1,0:T(8,128)(2,1)S(1)}, u32[]{:S(2)}, u32[]{:S(2)}) collective-permute-start(bf16[2,18,8,128]{3,2,1,0:T(8,128)(2,1)S(1)} %get-tuple-element.47), channel_id=1, source_target_pairs={{0,1},{1,0},{2,3},{3,2},{4,5},{5,4},{6,7},{7,6},{8,9},{9,8},{10,11... | collective-permute-start | bytes 221192 | tf_op jit(solution)/shard_map/ppermute | solution.py:335
  71.5 8.4 %collective-permute-start.7 = (bf16[2,18,8,128]{3,2,1,0:T(8,128)(2,1)S(1)}, bf16[2,18,8,128]{3,2,1,0:T(8,128)(2,1)S(1)}, u32[]{:S(2)}, u32[]{:S(2)}) collective-permute-start(bf16[2,18,8,128]{3,2,1,0:T(8,128)(2,1)S(1)} %get-tuple-element.48), channel_id=1, source_target_pairs={{1,2},{2,1},{3,4},{4,3},{5,6},{6,5},{7,8},{8,7},{9,10},{10,9},{11,... | collective-permute-start | bytes 221192 | tf_op jit(solution)/shard_map/ppermute | solution.py:335
  (2 other events, 1.2 us)

commit v6 on v5

--- a/solution.py
+++ b/solution.py
@@ -135,12 +135,10 @@
 
 
 def edges_kernel(
-    devices, tile_rows, me_ref, odd_x_ref, odd_y_ref, band_ref, shift_ref, length_ref,
-    arrived_ref, edge_ref, turned_ref, far_ref, even_ref, other_ref,
-    first_ref, second_ref, along_ref, rows_ref, slab_ref, recip_ref,
-):
-    views, depth = edge_ref.shape[:2]
-    odd = odd_x_ref[0] == 1
+    devices, tile_rows, me_ref, odd_ref, shift_ref, length_ref, arrived_ref, recip_ref, first_ref, second_ref, rows_ref
+):
+    views = recip_ref.shape[0]
+    odd = odd_ref[0] == 1
     groups = shift_ref.shape[1]
     me = me_ref[0]
     low = tile_rows - CAP * HW
@@ -155,26 +153,14 @@
                 for k in range(CAP):
                     rows_ref[view, side, start + k] = arrived_ref[base + k].astype(F32)
                 start = start + length_ref[view, g]
-    weights = [turned_ref.at[view] for view in range(views)]
-    far_products(odd_y_ref, even_ref.at[0], other_ref.at[0], weights, slab_ref, [along_ref.at[v] for v in range(views)])
-    pick = edge_picker(tile_rows)
-    for view in range(views):
-        for z in range(depth):
-            b = band_ref[z]
-            along = jnp.concatenate(far_parts(along_ref, view, b, z), axis=0)
-            blurred = edge_ref[view, z] + dot(dot(pick, along, NT).astype(BF16), far_ref[b, view])
-            recip_ref[z] = 1.0 / blurred.astype(BF16).astype(F32)
-        head = jnp.transpose(rows_ref[view, 0, :HW], (1, 0, 2)) * recip_ref[:, :HW]
+        head = jnp.transpose(rows_ref[view, 0, :HW], (1, 0, 2)) * recip_ref[view, :, :HW]
         tail = rows_ref[view, 1, (CAP - 1) * HW : CAP * HW]
-        tail = jnp.transpose(tail, (1, 0, 2)) * recip_ref[:, HW:]
+        tail = jnp.transpose(tail, (1, 0, 2)) * recip_ref[view, :, HW:]
         first_ref[view] = jnp.where(odd, head, tail).astype(BF16)
         second_ref[view] = jnp.where(odd, tail, head).astype(BF16)
 
 
-def unpack_kernel(
-    devices, me_ref, band_ref, shift_ref, length_ref, arrived_ref, blurred_ref, far_ref, along_ref,
-    out_ref, cols_ref, rows_ref, recip_ref,
-):
+def unpack_kernel(devices, me_ref, shift_ref, length_ref, arrived_ref, recip_ref, out_ref, cols_ref, rows_ref):
     views, depth, tile_rows, tile_cols = out_ref.shape
     groups = shift_ref.shape[1]
     me = me_ref[0]
@@ -189,14 +175,9 @@
             return start + length_ref[view, g]
 
         lax.fori_loop(0, groups, group, 0, unroll=True)
-        for z in range(depth):
-            b = band_ref[z]
-            along = jnp.concatenate(far_parts(along_ref, view, b, z), axis=0)
-            blurred = blurred_ref[view, z] + dot(along, far_ref[b, view], ((0,), (0,)))
-            recip_ref[z] = 1.0 / blurred.astype(BF16).astype(F32)
         for r0 in range(0, tile_rows, 16):
             x = jnp.transpose(rows_ref[view, r0 : r0 + 16], (1, 0, 2))
-            out_ref[view, :, r0 : r0 + 16, :] = (x * recip_ref[:, r0 : r0 + 16, :]).astype(BF16)
+            out_ref[view, :, r0 : r0 + 16, :] = (x * recip_ref[view, :, r0 : r0 + 16, :]).astype(BF16)
         for z in range(depth):
             cols_ref[view, z] = dot(pick, out_ref[view, z], NT).astype(BF16)
 
@@ -235,7 +216,7 @@
 
 def forward_kernel(
     band_ref, odd_ref, taps_ref, cells_ref, even_ref, other_ref,
-    blurred_ref, edge_ref, fwd_turned_ref, fwd_far_ref, rows_ref, ends_ref, cols_ref, turned_ref, far_ref, fwd_rows, fwd_cols,
+    blurred_ref, fwd_turned_ref, fwd_far_ref, rows_ref, ends_ref, cols_ref, turned_ref, far_ref, fwd_rows, fwd_cols,
 ):
     views, depth, tile_rows, tile_cols = blurred_ref.shape
     bands = taps_ref.shape[2]
@@ -273,11 +254,26 @@
             blurred = quarters(dot(rows[:, :tile_rows], cells)) + halves(dot(rows[:, tile_rows:], ends))
             blurred = quarters(dot(stacked(blurred, 0), fwd_cols[view, b]))
             blurred_ref[view, z] = blurred
-            edge_ref[view, z, :HW] = blurred[:HW]
-            edge_ref[view, z, HW:] = blurred[tile_rows - HW :]
         return carry
 
     lax.fori_loop(0, depth, plane, 0, unroll=2)
+
+
+def recip_kernel(
+    band_ref, odd_ref, turned_ref, far_ref, even_ref, other_ref, blurred_ref, out_ref, edge_ref, slab_ref, along_ref
+):
+    views, depth, tile_rows, tile_cols = blurred_ref.shape
+    weights = [turned_ref.at[view] for view in range(views)]
+    far_products(odd_ref, even_ref.at[0], other_ref.at[0], weights, slab_ref, [along_ref.at[v] for v in range(views)])
+    for view in range(views):
+        for z in range(depth):
+            b = band_ref[z]
+            along = jnp.concatenate(far_parts(along_ref, view, b, z), axis=0)
+            blurred = blurred_ref[view, z] + dot(along, far_ref[b, view], ((0,), (0,)))
+            recip = 1.0 / blurred.astype(BF16).astype(F32)
+            out_ref[view, z] = recip
+            edge_ref[view, z, :HW] = recip[:HW]
+            edge_ref[view, z, HW:] = recip[tile_rows - HW :]
 
 
 def near_kernel(
@@ -382,12 +378,11 @@
     tap_rows = jnp.pad(tap_rows, ((0, 0),) * 4 + ((0, LANES - kernels.shape[3]),))
     turned_like = like((views, bands, 2 * tile_rows, 2 * tile_rows), BF16)
     far_like = like((bands, views, 6 * HW, tile_cols), BF16)
-    blurred, edge_blurred, fwd_turned, fwd_far, rows_mat, ends_mat, cols_mat, turned_mat, far_mat = call(
+    blurred, fwd_turned, fwd_far, rows_mat, ends_mat, cols_mat, turned_mat, far_mat = call(
         forward_kernel,
         [SMEM] * 2 + [VMEM] * 4,
         (
             like(measured.shape, F32),
-            like((views, depth, 2 * HW, tile_cols), F32),
             turned_like,
             far_like,
             like((bands, 2 * tile_rows, views * tile_rows), BF16),
@@ -402,24 +397,29 @@
         ],
     )(depth_band, odd_x, tap_rows, cells, ex, ox)
 
-    along_like = like((views, bands, 2, depth * 2 * HW, tile_rows), BF16)
-    first, second, along = call(
+    recip, edge_recip = call(
+        recip_kernel,
+        [SMEM] * 2 + [VMEM] * 5,
+        (like(measured.shape, F32), like((views, depth, 2 * HW, tile_cols), F32)),
+        [
+            pltpu.VMEM((depth * 2 * HW, 2 * tile_rows), BF16),
+            pltpu.VMEM((views, bands, 2, depth * 2 * HW, tile_rows), BF16),
+        ],
+    )(depth_band, odd_y, fwd_turned, fwd_far, ey, oy, blurred)
+
+    first, second = call(
         functools.partial(edges_kernel, devices, tile_rows),
-        [SMEM] * 6 + [VMEM] * 6,
-        (edge_rows, edge_rows, along_like),
-        [
-            pltpu.VMEM((views, 2, CAP * HW + 8, depth, tile_cols), F32),
-            pltpu.VMEM((depth * 2 * HW, 2 * tile_rows), BF16),
-            pltpu.VMEM((depth, 2 * HW, tile_cols), F32),
-        ],
-    )(me, odd_x, odd_y, depth_band, group_shift, group_length, arrived, edge_blurred, fwd_turned, fwd_far, ey, oy)
+        [SMEM] * 4 + [VMEM] * 2,
+        (edge_rows, edge_rows),
+        [pltpu.VMEM((views, 2, CAP * HW + 8, depth, tile_cols), F32)],
+    )(me, odd_x, group_shift, group_length, arrived, edge_recip)
     ex, ox = swap(first, second, "gx")
     ratio, cols = call(
         functools.partial(unpack_kernel, devices),
-        [SMEM] * 4 + [VMEM] * 4,
+        [SMEM] * 3 + [VMEM] * 2,
         (whole, edge_cols),
-        [pltpu.VMEM((views, spare, depth, tile_cols), F32), pltpu.VMEM(estimate.shape, F32)],
-    )(me, depth_band, group_shift, group_length, arrived, blurred, fwd_far, along)
+        [pltpu.VMEM((views, spare, depth, tile_cols), F32)],
+    )(me, group_shift, group_length, arrived, recip)
     ey, oy = swap(*dense(views, cols, ex, ox), "gy")
     near = call(
         near_kernel,

time: 83.1 us -> 78.5 us (0.945)
  local copies, waits for them, and re-layouts: 12.1 us -> 7.13 us
  waiting for transfers between devices: 16.5 us -> 20.9 us
  Pallas kernels: 27.5 us -> 24.3 us
    unnamed x50 -> x34, local copies, waits for them, and re-layouts: 12 us -> 7.03 us
    ppermute x4, waiting for transfers between devices: 7.83 us -> 11.3 us  [swap(): lax.ppermute(first, axis, pairs(0))]
    pallas_call x2 -> x3, Pallas kernels: 7.28 us -> 4.06 us  [the longest x1 1.79 us: body(): call(functools.partial(unpack_kernel, devices), [SMEM] * 3 + [VMEM] * 2,...]
  transfers between devices with their start and end apart: 9 -> 9, of which waited for: 5 -> 5; matrix products, arithmetic and copies ran while one was open for 0% -> 0% of each run, Pallas kernels for 24% -> 27%
where the time goes in v6:
time: 78.5 us; the launch traced here: 78.1 us
  starting transfers between devices  24.3 us (31%)
  Pallas kernels  24.3 us (31%)
  waiting for transfers between devices  20.9 us (27%)
  local copies, waits for them, and re-layouts  7.13 us (9%)
  other arithmetic  1.16 us (1%)
    ppermute x4, starting transfers between devices, swap(): lax.ppermute(second, axis, pairs(1))  11.4 us
    ppermute x4, waiting for transfers between devices, swap(): lax.ppermute(first, axis, pairs(0))  11.3 us
    pallas_call x1, Pallas kernels, body(): call(forward_kernel, [SMEM] * 2 + [VMEM] * 4, (like(measured.shape, F32),...  11.1 us
    all_to_all x1, starting transfers between devices, body(): lax.all_to_all(outgoing, ('gx', 'gy'), split_axis=0, concat_axis=0, tiled...  11 us
    ppermute x4, waiting for transfers between devices, swap(): lax.ppermute(second, axis, pairs(1))  9.52 us
    unnamed x34, local copies, waits for them, and re-layouts  7.03 us
    pallas_call x1, Pallas kernels, body(): call(functools.partial(pack_kernel, devices), [SMEM, HBM, HBM, HBM], like...  2.96 us
    pallas_call x1, Pallas kernels, body(): call(near_kernel, [SMEM] * 2 + [VMEM] * 6, like(estimate.shape, F32), [pl...  2.31 us
  transfers between devices with their start and end apart: 9, of which 5 were waited for; matrix products, arithmetic and copies ran while one was open for 0% of the time, Pallas kernels for 27%

profile of v6, /device:TPU:30, one launch (start us, length us, event | category | flops | bytes accessed | tf_op | source)
XLA Modules:
  0.0 78.1 jit_solution(5791142016832588233)
XLA Ops:
  0.0 0.9 %slice_select_fusion = (f32[16,8,128]{2,1,0:T(8,128)S(1)}, f32[16,8,128]{2,1,0:T(8,128)S(1)}) fusion(f32[16,128,128]{2,1,0:T(8,128)} %estimate_ref.1, pred[]{:T(512)S(6)} %eq.7), kind=kLoop, calls=%fused_computation | loop fusion | flops 32768 | bytes 262145 | tf_op jit(solution)/shard_map/jit(_where)/select_n | solution.py:349
  0.9 2.2 %collective-permute-start.1 = (f32[16,8,128]{2,1,0:T(8,128)S(1)}, f32[16,8,128]{2,1,0:T(8,128)S(1)}, u32[]{:S(2)}, u32[]{:S(2)}) collective-permute-start(f32[16,8,128]{2,1,0:T(8,128)S(1)} %get-tuple-element.49), channel_id=1, source_target_pairs={{16,32},{32,16},{48,64},{64,48},{80,96},{96,80},{17,33},{33,17},{4... | collective-permute-start | bytes 196616 | tf_op jit(solution)/shard_map/ppermute | solution.py:331
  3.2 3.0 %shard_map.64 = bf16[128,2,3,16,128]{4,3,2,1,0:T(8,128)(2,1)} custom-call(s32[1]{0:T(128)} %bitcast.4.me_ref, s32[2,64]{1,0:T(2,128)} %shift_ref.3, s32[2,64]{1,0:T(2,128)} %length_ref.3, bf16[2,16,128,128]{3,2,1,0:T(8,128)(2,1)} %measured_hbm.1), custom_call_target="tpu_custom_call" | custom-call | tf_op jit(solution)/shard_map/pallas_call | solution.py:350
  6.1 0.3 collective-permute-done.1.other_ref
  6.5 0.6 copy-done.14
  7.1 11.0 %all-to-all-start = ((bf16[768,16,128]{2,1,0:T(8,128)(2,1)}), bf16[768,16,128]{2,1,0:T(8,128)(2,1)S(1)}, u32[]{:S(2)}, u32[]{:S(2)}) async-start(bf16[768,16,128]{2,1,0:T(8,128)(2,1)} %bitcast.9), calls=%async_computation | async-start | bytes 6291456 | tf_op jit(solution)/shard_map/all_to_all | solution.py:367
  18.1 0.1 reduce_sum.9
  18.2 0.1 broadcast_divide_fusion
  18.3 0.1 rev.3
  18.5 1.2 %copy-done = f32[16,128,128]{2,1,0:T(8,128)S(1)} copy-done((f32[16,128,128]{2,1,0:T(8,128)S(1)}, f32[16,128,128]{2,1,0:T(8,128)}, u32[]{:S(2)}) %copy-start) | copy-done | bytes 1048600
  19.8 0.4 shard_map.66
  20.1 1.1 %shard_map.67 = (bf16[1,18,8,128]{3,2,1,0:T(8,128)(2,1)S(1)}, bf16[1,18,8,128]{3,2,1,0:T(8,128)(2,1)S(1)}) custom-call(s32[1]{0:T(128)} %bitcast.1.odd_ref.odd_x_ref, s32[1]{0:T(128)} %bitcast.odd_y_ref.odd_ref, bf16[1,16,16,128]{3,2,1,0:T(8,128)(2,1)S(1)} %bitcast.8, f32[16,8,128]{2,1,0:T(8,128)} %copy-done.15, f32[16,8,128]{2,1,0:T(8,128)} %copy-done.14), custom_call_target="tpu_custom_call" | custom-call | tf_op jit(solution)/shard_map/pallas_call | solution.py:371
  21.2 1.7 %collective-permute-start.2 = (bf16[1,18,8,128]{3,2,1,0:T(8,128)(2,1)S(1)}, bf16[1,18,8,128]{3,2,1,0:T(8,128)(2,1)S(1)}, u32[]{:S(2)}, u32[]{:S(2)}) collective-permute-start(bf16[1,18,8,128]{3,2,1,0:T(8,128)(2,1)S(1)} %get-tuple-element.38), channel_id=1, source_target_pairs={{0,1},{1,0},{2,3},{3,2},{4,5},{5,4},{6,7},{7,6},{8,9},{9,8},{10,11... | collective-permute-start | bytes 110600 | tf_op jit(solution)/shard_map/ppermute | solution.py:331
  22.9 4.5 %collective-permute-start.3 = (bf16[1,18,8,128]{3,2,1,0:T(8,128)(2,1)S(1)}, bf16[1,18,8,128]{3,2,1,0:T(8,128)(2,1)S(1)}, u32[]{:S(2)}, u32[]{:S(2)}) collective-permute-start(bf16[1,18,8,128]{3,2,1,0:T(8,128)(2,1)S(1)} %get-tuple-element.39), channel_id=1, source_target_pairs={{1,2},{2,1},{3,4},{4,3},{5,6},{6,5},{7,8},{8,7},{9,10},{10,9},{11,... | collective-permute-start | bytes 110600 | tf_op jit(solution)/shard_map/ppermute | solution.py:331
  27.4 1.2 %copy-done.1 = f32[16,128,128]{2,1,0:T(8,128)S(1)} copy-done((f32[16,128,128]{2,1,0:T(8,128)S(1)}, f32[16,128,128]{2,1,0:T(8,128)}, u32[]{:S(2)}) %copy-start.1) | copy-done | bytes 1048600
  28.6 11.1 %shard_map.65 = (f32[2,16,128,128]{3,2,1,0:T(8,128)S(1)}, bf16[2,4,256,256]{3,2,1,0:T(8,128)(2,1)S(1)}, bf16[4,2,48,128]{3,2,1,0:T(8,128)(2,1)S(1)}, bf16[4,256,...) custom-call(s32[16]{0:T(128)S(1)} %copy-done.13, ...), custom_call_target="tpu_custom_call" | custom-call | tf_op jit(solution)/shard_map/pallas_call | solution.py:381
  39.8 1.0 %copy-done.5 = bf16[2,4,256,256]{3,2,1,0:T(8,128)(2,1)} copy-done((bf16[2,4,256,256]{3,2,1,0:T(8,128)(2,1)}, bf16[2,4,256,256]{3,2,1,0:T(8,128)(2,1)S(1)}, u32[]{:S(2)}) %copy-start.5) | copy-done | bytes 1048600
  40.8 0.8 %copy-done.7 = bf16[4,256,256]{2,1,0:T(8,128)(2,1)} copy-done((bf16[4,256,256]{2,1,0:T(8,128)(2,1)}, bf16[4,256,256]{2,1,0:T(8,128)(2,1)S(1)}, u32[]{:S(2)}) %copy-start.7) | copy-done | bytes 524312
  41.6 0.8 %copy-done.9 = bf16[2,4,128,256]{3,2,1,0:T(8,128)(2,1)} copy-done((bf16[2,4,128,256]{3,2,1,0:T(8,128)(2,1)}, bf16[2,4,128,256]{3,2,1,0:T(8,128)(2,1)S(1)}, u32[]{:S(2)}) %copy-start.9) | copy-done | bytes 524312
  42.4 11.3 %collective-permute-done.2.even_ref = bf16[1,18,8,128]{3,2,1,0:T(8,128)(2,1)S(1)} collective-permute-done((bf16[1,18,8,128]{3,2,1,0:T(8,128)(2,1)S(1)}, bf16[1,18,8,128]{3,2,1,0:T(8,128)(2,1)S(1)}, u32[]{:S(2)}, u32[]{:S(2)}) %collective-permute-start.2) | collective-permute-done | bytes 36896 | tf_op jit(solution)/shard_map/ppermute | solution.py:331
  53.7 4.1 %collective-permute-done.3.other_ref = bf16[1,18,8,128]{3,2,1,0:T(8,128)(2,1)S(1)} collective-permute-done((bf16[1,18,8,128]{3,2,1,0:T(8,128)(2,1)S(1)}, bf16[1,18,8,128]{3,2,1,0:T(8,128)(2,1)S(1)}, u32[]{:S(2)}, u32[]{:S(2)}) %collective-permute-start.3) | collective-permute-done | bytes 36896 | tf_op jit(solution)/shard_map/ppermute | solution.py:331
  57.8 1.5 %shard_map.68 = (f32[2,16,128,128]{3,2,1,0:T(8,128)S(1)}, f32[2,16,16,128]{3,2,1,0:T(8,128)S(1)}) custom-call(s32[16]{0:T(128)S(1)} %copy-done.13, s32[1]{0:T(128)} %bitcast.odd_y_ref.odd_ref, bf16[2,4,256,256]{3,2,1,0:T(8,128)(2,1)S(1)} %get-tuple-element.36.turned_ref, bf16[4,2,48,128]{3,2,1,0:T(8,128)(2,1)S(1)} %get-tuple-element.37.far_ref, ...), custom_call_target="tpu_custom_call" | custom-call | tf_op jit(solution)/shard_map/pallas_call | solution.py:400
  59.4 1.3 %copy-done.3 = f32[2,16,128,128]{3,2,1,0:T(8,128)} copy-done((f32[2,16,128,128]{3,2,1,0:T(8,128)}, f32[2,16,128,128]{3,2,1,0:T(8,128)S(1)}, u32[]{:S(2)}) %copy-start.3) | copy-done | bytes 2097176
  60.7 0.7 shard_map.70
  61.6 2.5 %collective-permute-start.5 = (bf16[2,16,8,128]{3,2,1,0:T(8,128)(2,1)S(1)}, bf16[2,16,8,128]{3,2,1,0:T(8,128)(2,1)S(1)}, u32[]{:S(2)}, u32[]{:S(2)}) collective-permute-start(bf16[2,16,8,128]{3,2,1,0:T(8,128)(2,1)S(1)} %get-tuple-element.45), channel_id=1, source_target_pairs={{16,32},{32,16},{48,64},{64,48},{80,96},{96,80},{17,33},{33,17},{4... | collective-permute-start | bytes 196616 | tf_op jit(solution)/shard_map/ppermute | solution.py:331
  64.2 1.8 %shard_map.69 = (bf16[2,16,128,128]{3,2,1,0:T(8,128)(2,1)S(1)}, bf16[2,16,16,128]{3,2,1,0:T(8,128)(2,1)S(1)}) custom-call(s32[1]{0:T(128)} %bitcast.4.me_ref, s32[2,64]{1,0:T(2,128)S(1)} %copy-done.11, s32[2,64]{1,0:T(2,128)S(1)} %copy-done.12, bf16[768,16,128]{2,1,0:T(8,128)(2,1)S(1)} %all-to-all-done.arrived_ref, f32[2,16,128,128]{3,2,1,0:T(8,128)S(1)} %copy-done.4), custom_call_target="tpu_custom_call" | custom-call | tf_op jit(solution)/shard_map/pallas_call | solution.py:417
  66.0 1.3 %collective-permute-done.5.other_ref = bf16[2,16,8,128]{3,2,1,0:T(8,128)(2,1)S(1)} collective-permute-done((bf16[2,16,8,128]{3,2,1,0:T(8,128)(2,1)S(1)}, bf16[2,16,8,128]{3,2,1,0:T(8,128)(2,1)S(1)}, u32[]{:S(2)}, u32[]{:S(2)}) %collective-permute-start.5) | collective-permute-done | bytes 65568 | tf_op jit(solution)/shard_map/ppermute | solution.py:331
  67.3 0.2 shard_map.72
  67.5 2.3 %collective-permute-start.7 = (bf16[2,18,8,128]{3,2,1,0:T(8,128)(2,1)S(1)}, bf16[2,18,8,128]{3,2,1,0:T(8,128)(2,1)S(1)}, u32[]{:S(2)}, u32[]{:S(2)}) collective-permute-start(bf16[2,18,8,128]{3,2,1,0:T(8,128)(2,1)S(1)} %get-tuple-element.48), channel_id=1, source_target_pairs={{1,2},{2,1},{3,4},{4,3},{5,6},{6,5},{7,8},{8,7},{9,10},{10,9},{11,... | collective-permute-start | bytes 221192 | tf_op jit(solution)/shard_map/ppermute | solution.py:331
  69.8 2.3 %shard_map.71.near_ref = f32[16,128,128]{2,1,0:T(8,128)S(1)} custom-call(s32[16]{0:T(128)S(1)} %copy-done.13, s32[1]{0:T(128)} %bitcast.1.odd_ref.odd_x_ref, bf16[4,256,256]{2,1,0:T(8,128)(2,1)S(1)} %copy-done.8, bf16[4,32,32]{2,1,0:T(8,128)(2,1)S(1)} %get-tuple-element.33.ends_ref, bf16[2,4,128,256]{3,2,1,0:T(8,128)(2,1)S(1)} %copy-done.10, ...), custom_call_target="tpu_custom_call" | custom-call | tf_op jit(solution)/shard_map/pallas_call | solution.py:424
  72.1 3.7 %collective-permute-done.7.other_ref = bf16[2,18,8,128]{3,2,1,0:T(8,128)(2,1)S(1)} collective-permute-done((bf16[2,18,8,128]{3,2,1,0:T(8,128)(2,1)S(1)}, bf16[2,18,8,128]{3,2,1,0:T(8,128)(2,1)S(1)}, u32[]{:S(2)}, u32[]{:S(2)}) %collective-permute-start.7) | collective-permute-done | bytes 73760 | tf_op jit(solution)/shard_map/ppermute | solution.py:331
  75.9 2.2 %shard_map.73 = f32[16,128,128]{2,1,0:T(8,128)} custom-call(s32[16]{0:T(128)S(1)} %copy-done.13, s32[1]{0:T(128)} %bitcast.odd_y_ref.odd_ref, bf16[2,4,256,256]{3,2,1,0:T(8,128)(2,1)S(1)} %copy-done.6, bf16[4,2,48,128]{3,2,1,0:T(8,128)(2,1)S(1)} %get-tuple-element.31.far_ref, f32[16,128,128]{2,1,0:T(8,128)S(1)} %shard_map.71.near_ref, ...), custom_call_target="tpu_custom_call" | custom-call | tf_op jit(solution)/shard_map/pallas_call | solution.py:433
  (36 shorter events, 0.4 us)
Async XLA Ops:
  0.9 5.6 %collective-permute-start.1 = (f32[16,8,128]{2,1,0:T(8,128)S(1)}, f32[16,8,128]{2,1,0:T(8,128)S(1)}, u32[]{:S(2)}, u32[]{:S(2)}) collective-permute-start(f32[16,8,128]{2,1,0:T(8,128)S(1)} %get-tuple-element.49), channel_id=1, source_target_pairs={{16,32},{32,16},{48,64},{64,48},{80,96},{96,80},{17,33},{33,17},{4... | collective-permute-start | bytes 196616 | tf_op jit(solution)/shard_map/ppermute | solution.py:331
  3.1 3.4 %collective-permute-start = (f32[16,8,128]{2,1,0:T(8,128)S(1)}, f32[16,8,128]{2,1,0:T(8,128)S(1)}, u32[]{:S(2)}, u32[]{:S(2)}) collective-permute-start(f32[16,8,128]{2,1,0:T(8,128)S(1)} %get-tuple-element.50), channel_id=1, source_target_pairs={{0,16},{16,0},{32,48},{48,32},{64,80},{80,64},{96,112},{112,96},{1... | collective-permute-start | bytes 196616 | tf_op jit(solution)/shard_map/ppermute | solution.py:331
  6.5 0.6 copy-start.14
  6.5 0.6 copy-start.15
  6.5 11.7 %copy-start.16 = (f32[2,4,2,17]{3,2,1,0:T(2,128)S(1)}, f32[2,4,2,17]{3,2,1,0:T(2,128)}, u32[]{:S(2)}) copy-start(f32[2,4,2,17]{3,2,1,0:T(2,128)} %param.8) | copy-start | bytes 3268
  6.5 20.9 %copy-start.13 = (s32[16]{0:T(128)S(1)}, s32[16]{0:T(128)}, u32[]{:S(2)}) copy-start(s32[16]{0:T(128)} %band_ref.7) | copy-start | bytes 196
  7.1 53.6 %all-to-all-start = ((bf16[768,16,128]{2,1,0:T(8,128)(2,1)}), bf16[768,16,128]{2,1,0:T(8,128)(2,1)S(1)}, u32[]{:S(2)}, u32[]{:S(2)}) async-start(bf16[768,16,128]{2,1,0:T(8,128)(2,1)} %bitcast.9), calls=%async_computation | async-start | bytes 6291456 | tf_op jit(solution)/shard_map/all_to_all | solution.py:367
  18.1 42.6 %copy-start.11 = (s32[2,64]{1,0:T(2,128)S(1)}, s32[2,64]{1,0:T(2,128)}, u32[]{:S(2)}) copy-start(s32[2,64]{1,0:T(2,128)} %shift_ref.3) | copy-start | bytes 1540
  18.1 42.6 %copy-start.12 = (s32[2,64]{1,0:T(2,128)S(1)}, s32[2,64]{1,0:T(2,128)}, u32[]{:S(2)}) copy-start(s32[2,64]{1,0:T(2,128)} %length_ref.3) | copy-start | bytes 1540
  18.5 1.2 %copy-start = (f32[16,128,128]{2,1,0:T(8,128)S(1)}, f32[16,128,128]{2,1,0:T(8,128)}, u32[]{:S(2)}) copy-start(f32[16,128,128]{2,1,0:T(8,128)} %estimate_ref.1) | copy-start | bytes 3145732
  21.2 32.6 %collective-permute-start.2 = (bf16[1,18,8,128]{3,2,1,0:T(8,128)(2,1)S(1)}, bf16[1,18,8,128]{3,2,1,0:T(8,128)(2,1)S(1)}, u32[]{:S(2)}, u32[]{:S(2)}) collective-permute-start(bf16[1,18,8,128]{3,2,1,0:T(8,128)(2,1)S(1)} %get-tuple-element.38), channel_id=1, source_target_pairs={{0,1},{1,0},{2,3},{3,2},{4,5},{5,4},{6,7},{7,6},{8,9},{9,8},{10,11... | collective-permute-start | bytes 110600 | tf_op jit(solution)/shard_map/ppermute | solution.py:331
  22.9 34.9 %collective-permute-start.3 = (bf16[1,18,8,128]{3,2,1,0:T(8,128)(2,1)S(1)}, bf16[1,18,8,128]{3,2,1,0:T(8,128)(2,1)S(1)}, u32[]{:S(2)}, u32[]{:S(2)}) collective-permute-start(bf16[1,18,8,128]{3,2,1,0:T(8,128)(2,1)S(1)} %get-tuple-element.39), channel_id=1, source_target_pairs={{1,2},{2,1},{3,4},{4,3},{5,6},{6,5},{7,8},{8,7},{9,10},{10,9},{11,... | collective-permute-start | bytes 110600 | tf_op jit(solution)/shard_map/ppermute | solution.py:331
  27.4 1.2 %copy-start.1 = (f32[16,128,128]{2,1,0:T(8,128)S(1)}, f32[16,128,128]{2,1,0:T(8,128)}, u32[]{:S(2)}) copy-start(f32[16,128,128]{2,1,0:T(8,128)} %estimate_ref.1) | copy-start | bytes 3145732
  39.8 1.0 %copy-start.5 = (bf16[2,4,256,256]{3,2,1,0:T(8,128)(2,1)}, bf16[2,4,256,256]{3,2,1,0:T(8,128)(2,1)S(1)}, u32[]{:S(2)}) copy-start(bf16[2,4,256,256]{3,2,1,0:T(8,128)(2,1)S(1)} %get-tuple-element.30.turned_ref) | copy-start | bytes 3145732
  40.8 0.8 %copy-start.7 = (bf16[4,256,256]{2,1,0:T(8,128)(2,1)}, bf16[4,256,256]{2,1,0:T(8,128)(2,1)S(1)}, u32[]{:S(2)}) copy-start(bf16[4,256,256]{2,1,0:T(8,128)(2,1)S(1)} %get-tuple-element.32.rows_ref) | copy-start | bytes 1572868
  41.6 0.8 %copy-start.9 = (bf16[2,4,128,256]{3,2,1,0:T(8,128)(2,1)}, bf16[2,4,128,256]{3,2,1,0:T(8,128)(2,1)S(1)}, u32[]{:S(2)}) copy-start(bf16[2,4,128,256]{3,2,1,0:T(8,128)(2,1)S(1)} %get-tuple-element.34.cols_ref) | copy-start | bytes 1572868
  59.4 1.3 %copy-start.3 = (f32[2,16,128,128]{3,2,1,0:T(8,128)}, f32[2,16,128,128]{3,2,1,0:T(8,128)S(1)}, u32[]{:S(2)}) copy-start(f32[2,16,128,128]{3,2,1,0:T(8,128)S(1)} %get-tuple-element.41.recip_ref) | copy-start | bytes 6291460
  60.7 3.4 %copy-start.4 = (f32[2,16,128,128]{3,2,1,0:T(8,128)S(1)}, f32[2,16,128,128]{3,2,1,0:T(8,128)}, u32[]{:S(2)}) copy-start(f32[2,16,128,128]{3,2,1,0:T(8,128)} %copy-done.3) | copy-start | bytes 6291460
  61.5 8.3 %copy-start.8 = (bf16[4,256,256]{2,1,0:T(8,128)(2,1)S(1)}, bf16[4,256,256]{2,1,0:T(8,128)(2,1)}, u32[]{:S(2)}) copy-start(bf16[4,256,256]{2,1,0:T(8,128)(2,1)} %copy-done.7) | copy-start | bytes 1572868
  61.5 8.3 %copy-start.10 = (bf16[2,4,128,256]{3,2,1,0:T(8,128)(2,1)S(1)}, bf16[2,4,128,256]{3,2,1,0:T(8,128)(2,1)}, u32[]{:S(2)}) copy-start(bf16[2,4,128,256]{3,2,1,0:T(8,128)(2,1)} %copy-done.9) | copy-start | bytes 1572868
  61.5 4.5 %collective-permute-start.4 = (bf16[2,16,8,128]{3,2,1,0:T(8,128)(2,1)S(1)}, bf16[2,16,8,128]{3,2,1,0:T(8,128)(2,1)S(1)}, u32[]{:S(2)}, u32[]{:S(2)}) collective-permute-start(bf16[2,16,8,128]{3,2,1,0:T(8,128)(2,1)S(1)} %get-tuple-element.44), channel_id=1, source_target_pairs={{0,16},{16,0},{32,48},{48,32},{64,80},{80,64},{96,112},{112,96},{1... | collective-permute-start | bytes 196616 | tf_op jit(solution)/shard_map/ppermute | solution.py:331
  61.6 5.7 %collective-permute-start.5 = (bf16[2,16,8,128]{3,2,1,0:T(8,128)(2,1)S(1)}, bf16[2,16,8,128]{3,2,1,0:T(8,128)(2,1)S(1)}, u32[]{:S(2)}, u32[]{:S(2)}) collective-permute-start(bf16[2,16,8,128]{3,2,1,0:T(8,128)(2,1)S(1)} %get-tuple-element.45), channel_id=1, source_target_pairs={{16,32},{32,16},{48,64},{64,48},{80,96},{96,80},{17,33},{33,17},{4... | collective-permute-start | bytes 196616 | tf_op jit(solution)/shard_map/ppermute | solution.py:331
  64.2 11.7 %copy-start.2 = (f32[16,128,128]{2,1,0:T(8,128)S(1)}, f32[16,128,128]{2,1,0:T(8,128)}, u32[]{:S(2)}) copy-start(f32[16,128,128]{2,1,0:T(8,128)} %estimate_ref.1) | copy-start | bytes 3145732
  64.2 11.7 %copy-start.6 = (bf16[2,4,256,256]{3,2,1,0:T(8,128)(2,1)S(1)}, bf16[2,4,256,256]{3,2,1,0:T(8,128)(2,1)}, u32[]{:S(2)}) copy-start(bf16[2,4,256,256]{3,2,1,0:T(8,128)(2,1)} %copy-done.5) | copy-start | bytes 3145732
  67.5 4.6 %collective-permute-start.6 = (bf16[2,18,8,128]{3,2,1,0:T(8,128)(2,1)S(1)}, bf16[2,18,8,128]{3,2,1,0:T(8,128)(2,1)S(1)}, u32[]{:S(2)}, u32[]{:S(2)}) collective-permute-start(bf16[2,18,8,128]{3,2,1,0:T(8,128)(2,1)S(1)} %get-tuple-element.47), channel_id=1, source_target_pairs={{0,1},{1,0},{2,3},{3,2},{4,5},{5,4},{6,7},{7,6},{8,9},{9,8},{10,11... | collective-permute-start | bytes 221192 | tf_op jit(solution)/shard_map/ppermute | solution.py:331
  67.5 8.4 %collective-permute-start.7 = (bf16[2,18,8,128]{3,2,1,0:T(8,128)(2,1)S(1)}, bf16[2,18,8,128]{3,2,1,0:T(8,128)(2,1)S(1)}, u32[]{:S(2)}, u32[]{:S(2)}) collective-permute-start(bf16[2,18,8,128]{3,2,1,0:T(8,128)(2,1)S(1)} %get-tuple-element.48), channel_id=1, source_target_pairs={{1,2},{2,1},{3,4},{4,3},{5,6},{6,5},{7,8},{8,7},{9,10},{10,9},{11,... | collective-permute-start | bytes 221192 | tf_op jit(solution)/shard_map/ppermute | solution.py:331

commit v7 on v6

--- a/solution.py
+++ b/solution.py
@@ -10,6 +10,7 @@
 HW = 8
 CAP = 3
 LANES = 256
+LAST = 2**20
 F32 = jnp.float32
 BF16 = jnp.bfloat16
 
@@ -54,11 +55,15 @@
     return x[:n, :m] + (x[n:, :m] + x[:n, m:])
 
 
-def halo(odd_ref, first, second):
+def is_odd(place_ref):
+    return place_ref[0] % 2 == 1
+
+
+def halo(place_ref, first, second):
     first, second = first.astype(F32), second.astype(F32)
-    odd = odd_ref[0] == 1
-    after = jnp.where(odd, second, first)
-    before = jnp.where(odd, first, second)
+    odd = is_odd(place_ref)
+    after = jnp.where(place_ref[0] >= LAST, 0.0, jnp.where(odd, second, first))
+    before = jnp.where(place_ref[0] == 0, 0.0, jnp.where(odd, first, second))
     return jnp.concatenate([after, before], axis=0).astype(BF16)
 
 
@@ -116,11 +121,11 @@
         out_ref[z] = dot(pick, cells_ref[z].astype(BF16), NT).astype(BF16)
 
 
-def dense_slab_kernel(odd_x_ref, odd_y_ref, cols_ref, even_ref, other_ref, first_ref, second_ref):
+def dense_slab_kernel(place_x_ref, place_y_ref, cols_ref, even_ref, other_ref, first_ref, second_ref):
     views, depth, _, tile_rows = cols_ref.shape
     count = tile_rows // (2 * HW)
     pick = edge_picker(even_ref.shape[-1])
-    odd = odd_y_ref[0] == 1
+    odd = is_odd(place_y_ref)
     for view in range(views):
         for i in range(first_ref.shape[1]):
             if i < depth:
@@ -128,17 +133,17 @@
             else:
                 planes = range((i - depth) * count, (i - depth + 1) * count)
                 lead = () if len(even_ref.shape) == 3 else (view,)
-                ends = [halo(odd_x_ref, even_ref[*lead, z], other_ref[*lead, z]) for z in planes]
+                ends = [halo(place_x_ref, even_ref[*lead, z], other_ref[*lead, z]) for z in planes]
                 edge = dot(pick, jnp.concatenate(ends, axis=0), NT)
             first_ref[view, i] = jnp.where(odd, edge[:HW], edge[HW:]).astype(BF16)
             second_ref[view, i] = jnp.where(odd, edge[HW:], edge[:HW]).astype(BF16)
 
 
 def edges_kernel(
-    devices, tile_rows, me_ref, odd_ref, shift_ref, length_ref, arrived_ref, recip_ref, first_ref, second_ref, rows_ref
+    devices, tile_rows, me_ref, place_ref, shift_ref, length_ref, arrived_ref, recip_ref, first_ref, second_ref, rows_ref
 ):
     views = recip_ref.shape[0]
-    odd = odd_ref[0] == 1
+    odd = is_odd(place_ref)
     groups = shift_ref.shape[1]
     me = me_ref[0]
     low = tile_rows - CAP * HW
@@ -190,15 +195,15 @@
     return jnp.where(lane < size + HW, inner, jnp.where(lane < size + 2 * HW, before, 0.0))
 
 
-def far_products(odd_ref, even_ref, other_ref, weights, slab_ref, along_ref):
+def far_products(place_ref, even_ref, other_ref, weights, slab_ref, along_ref):
     depth = slab_ref.shape[0] // (2 * HW)
     tile_rows = slab_ref.shape[1] // 2
     count = tile_rows // (2 * HW)
     owner = lax.broadcasted_iota(jnp.int32, (2 * HW, tile_rows), 1) // (2 * HW)
     for z in range(depth):
         at = pl.ds(z * 2 * HW, 2 * HW)
-        slab_ref[at, :tile_rows] = halo(odd_ref, even_ref[z], other_ref[z])
-        corners = halo(odd_ref, even_ref[depth + z // count], other_ref[depth + z // count])
+        slab_ref[at, :tile_rows] = halo(place_ref, even_ref[z], other_ref[z])
+        corners = halo(place_ref, even_ref[depth + z // count], other_ref[depth + z // count])
         slab_ref[at, tile_rows:] = jnp.where(owner == z % count, corners.astype(F32), 0.0).astype(BF16)
     for turned_ref, out_ref in zip(weights, along_ref):
         for b in range(turned_ref.shape[0]):
@@ -215,7 +220,7 @@
 
 
 def forward_kernel(
-    band_ref, odd_ref, taps_ref, cells_ref, even_ref, other_ref,
+    band_ref, place_ref, taps_ref, cells_ref, even_ref, other_ref,
     blurred_ref, fwd_turned_ref, fwd_far_ref, rows_ref, ends_ref, cols_ref, turned_ref, far_ref, fwd_rows, fwd_cols,
 ):
     views, depth, tile_rows, tile_cols = blurred_ref.shape
@@ -248,7 +253,7 @@
     def plane(z, carry):
         b = band_ref[z]
         cells = stacked(cells_ref[z], 1)
-        ends = halo(odd_ref, even_ref[z], other_ref[z])
+        ends = halo(place_ref, even_ref[z], other_ref[z])
         for view in range(views):
             rows = fwd_rows[view, b]
             blurred = quarters(dot(rows[:, :tile_rows], cells)) + halves(dot(rows[:, tile_rows:], ends))
@@ -260,11 +265,11 @@
 
 
 def recip_kernel(
-    band_ref, odd_ref, turned_ref, far_ref, even_ref, other_ref, blurred_ref, out_ref, edge_ref, slab_ref, along_ref
+    band_ref, place_ref, turned_ref, far_ref, even_ref, other_ref, blurred_ref, out_ref, edge_ref, slab_ref, along_ref
 ):
     views, depth, tile_rows, tile_cols = blurred_ref.shape
     weights = [turned_ref.at[view] for view in range(views)]
-    far_products(odd_ref, even_ref.at[0], other_ref.at[0], weights, slab_ref, [along_ref.at[v] for v in range(views)])
+    far_products(place_ref, even_ref.at[0], other_ref.at[0], weights, slab_ref, [along_ref.at[v] for v in range(views)])
     for view in range(views):
         for z in range(depth):
             b = band_ref[z]
@@ -277,7 +282,7 @@
 
 
 def near_kernel(
-    band_ref, odd_ref, rows_ref, ends_ref, cols_ref, ratio_ref, even_ref, other_ref, out_ref, inner_ref, outer_ref
+    band_ref, place_ref, rows_ref, ends_ref, cols_ref, ratio_ref, even_ref, other_ref, out_ref, inner_ref, outer_ref
 ):
     views, depth, tile_rows, tile_cols = ratio_ref.shape
 
@@ -289,7 +294,7 @@
         b = band_ref[z]
         for view in range(views):
             inner_ref[z, view * tile_rows : (view + 1) * tile_rows] = across(ratio_ref[view, z], cols_ref[view, b])
-            ends = halo(odd_ref, even_ref[view, z], other_ref[view, z])
+            ends = halo(place_ref, even_ref[view, z], other_ref[view, z])
             outer_ref[z, view * 2 * HW : (view + 1) * 2 * HW] = across(ends, cols_ref[view, b])
     for z in range(depth):
         b = band_ref[z]
@@ -300,14 +305,14 @@
 
 
 def far_kernel(
-    band_ref, odd_ref, turned_ref, far_ref, near_ref, even_ref, other_ref, estimate_ref, out_hbm,
+    band_ref, place_ref, turned_ref, far_ref, near_ref, even_ref, other_ref, estimate_ref, out_hbm,
     slab_ref, along_ref, out_ref, sems,
 ):
     views, bands = turned_ref.shape[:2]
     depth, tile_rows, tile_cols = near_ref.shape
     step = depth // sems.shape[0]
     for view in range(views):
-        far_products(odd_ref, even_ref.at[view], other_ref.at[view], [turned_ref.at[view]], slab_ref.at[view], [along_ref.at[view]])
+        far_products(place_ref, even_ref.at[view], other_ref.at[view], [turned_ref.at[view]], slab_ref.at[view], [along_ref.at[view]])
     leave = []
     for z in range(depth):
         b = band_ref[z]
@@ -327,15 +332,19 @@
 
 def swap(first, second, axis):
     count = lax.axis_size(axis)
-    pairs = lambda begin: [p for i in range(begin, count - 1, 2) for p in ((i, i + 1), (i + 1, i))]
+    pairs = lambda begin: [p for i in range(begin, count, 2) for p in ((i, (i + 1) % count), ((i + 1) % count, i))]
     return lax.ppermute(first, axis, pairs(0)), lax.ppermute(second, axis, pairs(1))
+
+
+def place(count, at):
+    return jnp.where(at == count - 1, at + LAST, at).reshape(1)
 
 
 def body(estimate, measured, kernels, depth_band, group_shift, group_length):
     devices = lax.axis_size("gx") * lax.axis_size("gy")
     gx, gy = lax.axis_index("gx").astype(jnp.int32), lax.axis_index("gy").astype(jnp.int32)
     me = (gx * lax.axis_size("gy") + gy).reshape(1)
-    odd_x, odd_y = (gx % 2).reshape(1), (gy % 2).reshape(1)
+    place_x, place_y = (place(lax.axis_size(axis), at) for axis, at in (("gx", gx), ("gy", gy)))
     views, depth, tile_rows, tile_cols = measured.shape
     bands = kernels.shape[1]
     spare = tile_rows + 8
@@ -370,7 +379,7 @@
     tiles = depth + depth * 2 * HW // tile_rows
     dense = lambda lead, *args: call(
         dense_slab_kernel, [SMEM] * 2 + [VMEM] * 3, (like((lead, tiles, HW, tile_rows), BF16),) * 2
-    )(odd_x, odd_y, *args)
+    )(place_x, place_y, *args)
     ey, oy = swap(*dense(1, cols[None], ex, ox), "gy")
 
     norm = kernels / jnp.sum(kernels, axis=3, keepdims=True)
@@ -395,7 +404,7 @@
             pltpu.VMEM((views, bands, 2 * tile_rows, tile_rows + 2 * HW), BF16),
             pltpu.VMEM((views, bands, tile_cols, 2 * tile_cols), BF16),
         ],
-    )(depth_band, odd_x, tap_rows, cells, ex, ox)
+    )(depth_band, place_x, tap_rows, cells, ex, ox)
 
     recip, edge_recip = call(
         recip_kernel,
@@ -405,14 +414,14 @@
             pltpu.VMEM((depth * 2 * HW, 2 * tile_rows), BF16),
             pltpu.VMEM((views, bands, 2, depth * 2 * HW, tile_rows), BF16),
         ],
-    )(depth_band, odd_y, fwd_turned, fwd_far, ey, oy, blurred)
+    )(depth_band, place_y, fwd_turned, fwd_far, ey, oy, blurred)
 
     first, second = call(
         functools.partial(edges_kernel, devices, tile_rows),
         [SMEM] * 4 + [VMEM] * 2,
         (edge_rows, edge_rows),
         [pltpu.VMEM((views, 2, CAP * HW + 8, depth, tile_cols), F32)],
-    )(me, odd_x, group_shift, group_length, arrived, edge_recip)
+    )(me, place_x, group_shift, group_length, arrived, edge_recip)
     ex, ox = swap(first, second, "gx")
     ratio, cols = call(
         functools.partial(unpack_kernel, devices),
@@ -429,7 +438,7 @@
             pltpu.VMEM((depth, views * tile_rows, 2 * tile_cols), BF16),
             pltpu.VMEM((depth, views * 2 * HW, 2 * tile_cols), BF16),
         ],
-    )(depth_band, odd_x, rows_mat, ends_mat, cols_mat, ratio, ex, ox)
+    )(depth_band, place_x, rows_mat, ends_mat, cols_mat, ratio, ex, ox)
     return call(
         far_kernel,
         [SMEM] * 2 + [VMEM] * 6,
@@ -441,7 +450,7 @@
             pltpu.SemaphoreType.DMA((4,)),
         ],
         HBM,
-    )(depth_band, odd_y, turned_mat, far_mat, near, ey, oy, estimate)
+    )(depth_band, place_y, turned_mat, far_mat, near, ey, oy, estimate)
 
 
 def solution(mesh):

time: 78.5 us -> 77.3 us (0.985)
  the two profiles are of different devices: /device:TPU:30 before, /device:TPU:0 now
where the time goes in v7:
time: 77.3 us; the launch traced here: 76.9 us
  Pallas kernels  24.3 us (31%)
  starting transfers between devices  24 us (31%)
  waiting for transfers between devices  19.9 us (26%)
  local copies, waits for them, and re-layouts  7.11 us (9%)
  other arithmetic  1.16 us (2%)
    ppermute x4, waiting for transfers between devices, swap(): lax.ppermute(second, axis, pairs(1))  19.4 us
    ppermute x4, starting transfers between devices, swap(): lax.ppermute(second, axis, pairs(1))  12.7 us
    pallas_call x1, Pallas kernels, body(): call(forward_kernel, [SMEM] * 2 + [VMEM] * 4, (like(measured.shape, F32),...  11.1 us
    all_to_all x1, starting transfers between devices, body(): lax.all_to_all(outgoing, ('gx', 'gy'), split_axis=0, concat_axis=0, tiled...  10.1 us
    unnamed x34, local copies, waits for them, and re-layouts  7 us
    pallas_call x1, Pallas kernels, body(): call(functools.partial(pack_kernel, devices), [SMEM, HBM, HBM, HBM], like...  2.99 us
    pallas_call x1, Pallas kernels, body(): call(near_kernel, [SMEM] * 2 + [VMEM] * 6, like(estimate.shape, F32), [pl...  2.29 us
    pallas_call x1, Pallas kernels, body(): call(far_kernel, [SMEM] * 2 + [VMEM] * 6, like(estimate.shape, F32), [plt...  2.21 us
  transfers between devices with their start and end apart: 9, of which 4 were waited for; matrix products, arithmetic and copies ran while one was open for 0% of the time, Pallas kernels for 28%

profile of v7, /device:TPU:0, one launch (start us, length us, event | category | flops | bytes accessed | tf_op | source)
XLA Modules:
  0.0 76.9 jit_solution(13402081903730159440)
XLA Ops:
  0.0 0.9 %slice_select_fusion = (f32[16,8,128]{2,1,0:T(8,128)S(1)}, f32[16,8,128]{2,1,0:T(8,128)S(1)}) fusion(f32[16,128,128]{2,1,0:T(8,128)} %estimate_ref.1, pred[]{:T(512)S(6)} %eq.13), kind=kLoop, calls=%fused_computation | loop fusion | flops 32768 | bytes 262145 | tf_op jit(solution)/shard_map/jit(_where)/select_n | solution.py:358
  0.9 2.4 %collective-permute-start.1 = (f32[16,8,128]{2,1,0:T(8,128)S(1)}, f32[16,8,128]{2,1,0:T(8,128)S(1)}, u32[]{:S(2)}, u32[]{:S(2)}) collective-permute-start(f32[16,8,128]{2,1,0:T(8,128)S(1)} %get-tuple-element.49), channel_id=1, source_target_pairs={{16,32},{32,16},{48,64},{64,48},{80,96},{96,80},{112,0},{0,112},{1... | collective-permute-start | bytes 196616 | tf_op jit(solution)/shard_map/ppermute | solution.py:336
  3.3 3.0 %shard_map.64 = bf16[128,2,3,16,128]{4,3,2,1,0:T(8,128)(2,1)} custom-call(s32[1]{0:T(128)} %bitcast.4.me_ref, s32[2,64]{1,0:T(2,128)} %shift_ref.3, s32[2,64]{1,0:T(2,128)} %length_ref.3, bf16[2,16,128,128]{3,2,1,0:T(8,128)(2,1)} %measured_hbm.1), custom_call_target="tpu_custom_call" | custom-call | tf_op jit(solution)/shard_map/pallas_call | solution.py:359
  6.3 0.6 copy-done.14
  6.9 10.1 %all-to-all-start = ((bf16[768,16,128]{2,1,0:T(8,128)(2,1)}), bf16[768,16,128]{2,1,0:T(8,128)(2,1)S(1)}, u32[]{:S(2)}, u32[]{:S(2)}) async-start(bf16[768,16,128]{2,1,0:T(8,128)(2,1)} %bitcast.9), calls=%async_computation | async-start | bytes 6291456 | tf_op jit(solution)/shard_map/all_to_all | solution.py:376
  17.1 0.1 reduce_sum.9
  17.2 0.1 broadcast_divide_fusion
  17.3 0.1 rev.3
  17.5 1.2 %copy-done = f32[16,128,128]{2,1,0:T(8,128)S(1)} copy-done((f32[16,128,128]{2,1,0:T(8,128)S(1)}, f32[16,128,128]{2,1,0:T(8,128)}, u32[]{:S(2)}) %copy-start) | copy-done | bytes 1048600
  18.7 0.4 shard_map.66
  19.1 1.1 %shard_map.67 = (bf16[1,18,8,128]{3,2,1,0:T(8,128)(2,1)S(1)}, bf16[1,18,8,128]{3,2,1,0:T(8,128)(2,1)S(1)}) custom-call(s32[1]{0:T(128)} %bitcast.1.place_ref.place_x_ref, s32[1]{0:T(128)} %bitcast.place_y_ref.place_ref, bf16[1,16,16,128]{3,2,1,0:T(8,128)(2,1)S(1)} %bitcast.8, f32[16,8,128]{2,1,0:T(8,128)} %copy-done.15, f32[16,8,128]{2,1,0:T(8,128)} %copy-done.14), custom_call_target="tpu_custom_call" | custom-call | tf_op jit(solution)/shard_map/pallas_call | solution.py:380
  20.1 1.1 %collective-permute-start.2 = (bf16[1,18,8,128]{3,2,1,0:T(8,128)(2,1)S(1)}, bf16[1,18,8,128]{3,2,1,0:T(8,128)(2,1)S(1)}, u32[]{:S(2)}, u32[]{:S(2)}) collective-permute-start(bf16[1,18,8,128]{3,2,1,0:T(8,128)(2,1)S(1)} %get-tuple-element.38), channel_id=1, source_target_pairs={{0,1},{1,0},{2,3},{3,2},{4,5},{5,4},{6,7},{7,6},{8,9},{9,8},{10,11... | collective-permute-start | bytes 110600 | tf_op jit(solution)/shard_map/ppermute | solution.py:336
  21.2 4.6 %collective-permute-start.3 = (bf16[1,18,8,128]{3,2,1,0:T(8,128)(2,1)S(1)}, bf16[1,18,8,128]{3,2,1,0:T(8,128)(2,1)S(1)}, u32[]{:S(2)}, u32[]{:S(2)}) collective-permute-start(bf16[1,18,8,128]{3,2,1,0:T(8,128)(2,1)S(1)} %get-tuple-element.39), channel_id=1, source_target_pairs={{1,2},{2,1},{3,4},{4,3},{5,6},{6,5},{7,8},{8,7},{9,10},{10,9},{11,... | collective-permute-start | bytes 110600 | tf_op jit(solution)/shard_map/ppermute | solution.py:336
  25.9 1.2 %copy-done.1 = f32[16,128,128]{2,1,0:T(8,128)S(1)} copy-done((f32[16,128,128]{2,1,0:T(8,128)S(1)}, f32[16,128,128]{2,1,0:T(8,128)}, u32[]{:S(2)}) %copy-start.1) | copy-done | bytes 1048600
  27.1 11.1 %shard_map.65 = (f32[2,16,128,128]{3,2,1,0:T(8,128)S(1)}, bf16[2,4,256,256]{3,2,1,0:T(8,128)(2,1)S(1)}, bf16[4,2,48,128]{3,2,1,0:T(8,128)(2,1)S(1)}, bf16[4,256,...) custom-call(s32[16]{0:T(128)S(1)} %copy-done.13, ...), custom_call_target="tpu_custom_call" | custom-call | tf_op jit(solution)/shard_map/pallas_call | solution.py:390
  38.3 1.0 %copy-done.5 = bf16[2,4,256,256]{3,2,1,0:T(8,128)(2,1)} copy-done((bf16[2,4,256,256]{3,2,1,0:T(8,128)(2,1)}, bf16[2,4,256,256]{3,2,1,0:T(8,128)(2,1)S(1)}, u32[]{:S(2)}) %copy-start.5) | copy-done | bytes 1048600
  39.2 0.8 %copy-done.7 = bf16[4,256,256]{2,1,0:T(8,128)(2,1)} copy-done((bf16[4,256,256]{2,1,0:T(8,128)(2,1)}, bf16[4,256,256]{2,1,0:T(8,128)(2,1)S(1)}, u32[]{:S(2)}) %copy-start.7) | copy-done | bytes 524312
  40.0 0.8 %copy-done.9 = bf16[2,4,128,256]{3,2,1,0:T(8,128)(2,1)} copy-done((bf16[2,4,128,256]{3,2,1,0:T(8,128)(2,1)}, bf16[2,4,128,256]{3,2,1,0:T(8,128)(2,1)S(1)}, u32[]{:S(2)}) %copy-start.9) | copy-done | bytes 524312
  40.9 15.6 %collective-permute-done.3.other_ref = bf16[1,18,8,128]{3,2,1,0:T(8,128)(2,1)S(1)} collective-permute-done((bf16[1,18,8,128]{3,2,1,0:T(8,128)(2,1)S(1)}, bf16[1,18,8,128]{3,2,1,0:T(8,128)(2,1)S(1)}, u32[]{:S(2)}, u32[]{:S(2)}) %collective-permute-start.3) | collective-permute-done | bytes 36896 | tf_op jit(solution)/shard_map/ppermute | solution.py:336
  56.5 1.5 %shard_map.68 = (f32[2,16,128,128]{3,2,1,0:T(8,128)S(1)}, f32[2,16,16,128]{3,2,1,0:T(8,128)S(1)}) custom-call(s32[16]{0:T(128)S(1)} %copy-done.13, s32[1]{0:T(128)} %bitcast.place_y_ref.place_ref, bf16[2,4,256,256]{3,2,1,0:T(8,128)(2,1)S(1)} %get-tuple-element.36.turned_ref, bf16[4,2,48,128]{3,2,1,0:T(8,128)(2,1)S(1)} %get-tuple-element.37.far_ref, ...), custom_call_target="tpu_custom_call" | custom-call | tf_op jit(solution)/shard_map/pallas_call | solution.py:409
  58.0 1.3 %copy-done.3 = f32[2,16,128,128]{3,2,1,0:T(8,128)} copy-done((f32[2,16,128,128]{3,2,1,0:T(8,128)}, f32[2,16,128,128]{3,2,1,0:T(8,128)S(1)}, u32[]{:S(2)}) %copy-start.3) | copy-done | bytes 2097176
  59.4 0.7 shard_map.70
  60.1 0.1 collective-permute-start.4
  60.2 4.2 %collective-permute-start.5 = (bf16[2,16,8,128]{3,2,1,0:T(8,128)(2,1)S(1)}, bf16[2,16,8,128]{3,2,1,0:T(8,128)(2,1)S(1)}, u32[]{:S(2)}, u32[]{:S(2)}) collective-permute-start(bf16[2,16,8,128]{3,2,1,0:T(8,128)(2,1)S(1)} %get-tuple-element.45), channel_id=1, source_target_pairs={{16,32},{32,16},{48,64},{64,48},{80,96},{96,80},{112,0},{0,112},{1... | collective-permute-start | bytes 196616 | tf_op jit(solution)/shard_map/ppermute | solution.py:336
  64.4 1.8 %shard_map.69 = (bf16[2,16,128,128]{3,2,1,0:T(8,128)(2,1)S(1)}, bf16[2,16,16,128]{3,2,1,0:T(8,128)(2,1)S(1)}) custom-call(s32[1]{0:T(128)} %bitcast.4.me_ref, s32[2,64]{1,0:T(2,128)S(1)} %copy-done.11, s32[2,64]{1,0:T(2,128)S(1)} %copy-done.12, bf16[768,16,128]{2,1,0:T(8,128)(2,1)S(1)} %all-to-all-done.arrived_ref, f32[2,16,128,128]{3,2,1,0:T(8,128)S(1)} %copy-done.4), custom_call_target="tpu_custom_call" | custom-call | tf_op jit(solution)/shard_map/pallas_call | solution.py:426
  66.2 0.1 collective-permute-done.5.other_ref
  66.4 0.2 shard_map.72
  66.6 1.5 %collective-permute-start.7 = (bf16[2,18,8,128]{3,2,1,0:T(8,128)(2,1)S(1)}, bf16[2,18,8,128]{3,2,1,0:T(8,128)(2,1)S(1)}, u32[]{:S(2)}, u32[]{:S(2)}) collective-permute-start(bf16[2,18,8,128]{3,2,1,0:T(8,128)(2,1)S(1)} %get-tuple-element.48), channel_id=1, source_target_pairs={{1,2},{2,1},{3,4},{4,3},{5,6},{6,5},{7,8},{8,7},{9,10},{10,9},{11,... | collective-permute-start | bytes 221192 | tf_op jit(solution)/shard_map/ppermute | solution.py:336
  68.1 2.3 %shard_map.71.near_ref = f32[16,128,128]{2,1,0:T(8,128)S(1)} custom-call(s32[16]{0:T(128)S(1)} %copy-done.13, s32[1]{0:T(128)} %bitcast.1.place_ref.place_x_ref, bf16[4,256,256]{2,1,0:T(8,128)(2,1)S(1)} %copy-done.8, bf16[4,32,32]{2,1,0:T(8,128)(2,1)S(1)} %get-tuple-element.33.ends_ref, bf16[2,4,128,256]{3,2,1,0:T(8,128)(2,1)S(1)} %copy-done.10, ...), custom_call_target="tpu_custom_call" | custom-call | tf_op jit(solution)/shard_map/pallas_call | solution.py:433
  70.4 0.5 collective-permute-done.6.even_ref
  70.9 3.6 %collective-permute-done.7.other_ref = bf16[2,18,8,128]{3,2,1,0:T(8,128)(2,1)S(1)} collective-permute-done((bf16[2,18,8,128]{3,2,1,0:T(8,128)(2,1)S(1)}, bf16[2,18,8,128]{3,2,1,0:T(8,128)(2,1)S(1)}, u32[]{:S(2)}, u32[]{:S(2)}) %collective-permute-start.7) | collective-permute-done | bytes 73760 | tf_op jit(solution)/shard_map/ppermute | solution.py:336
  74.5 2.2 %shard_map.73 = f32[16,128,128]{2,1,0:T(8,128)} custom-call(s32[16]{0:T(128)S(1)} %copy-done.13, s32[1]{0:T(128)} %bitcast.place_y_ref.place_ref, bf16[2,4,256,256]{3,2,1,0:T(8,128)(2,1)S(1)} %copy-done.6, bf16[4,2,48,128]{3,2,1,0:T(8,128)(2,1)S(1)} %get-tuple-element.31.far_ref, f32[16,128,128]{2,1,0:T(8,128)S(1)} %shard_map.71.near_ref, ...), custom_call_target="tpu_custom_call" | custom-call | tf_op jit(solution)/shard_map/pallas_call | solution.py:442
  (36 shorter events, 0.2 us)
Async XLA Ops:
  0.9 5.4 %collective-permute-start.1 = (f32[16,8,128]{2,1,0:T(8,128)S(1)}, f32[16,8,128]{2,1,0:T(8,128)S(1)}, u32[]{:S(2)}, u32[]{:S(2)}) collective-permute-start(f32[16,8,128]{2,1,0:T(8,128)S(1)} %get-tuple-element.49), channel_id=1, source_target_pairs={{16,32},{32,16},{48,64},{64,48},{80,96},{96,80},{112,0},{0,112},{1... | collective-permute-start | bytes 196616 | tf_op jit(solution)/shard_map/ppermute | solution.py:336
  3.2 3.0 %collective-permute-start = (f32[16,8,128]{2,1,0:T(8,128)S(1)}, f32[16,8,128]{2,1,0:T(8,128)S(1)}, u32[]{:S(2)}, u32[]{:S(2)}) collective-permute-start(f32[16,8,128]{2,1,0:T(8,128)S(1)} %get-tuple-element.50), channel_id=1, source_target_pairs={{0,16},{16,0},{32,48},{48,32},{64,80},{80,64},{96,112},{112,96},{1... | collective-permute-start | bytes 196616 | tf_op jit(solution)/shard_map/ppermute | solution.py:336
  6.3 0.6 copy-start.14
  6.3 0.6 copy-start.15
  6.3 10.8 %copy-start.16 = (f32[2,4,2,17]{3,2,1,0:T(2,128)S(1)}, f32[2,4,2,17]{3,2,1,0:T(2,128)}, u32[]{:S(2)}) copy-start(f32[2,4,2,17]{3,2,1,0:T(2,128)} %param.8) | copy-start | bytes 3268
  6.3 19.6 %copy-start.13 = (s32[16]{0:T(128)S(1)}, s32[16]{0:T(128)}, u32[]{:S(2)}) copy-start(s32[16]{0:T(128)} %band_ref.7) | copy-start | bytes 196
  6.9 52.5 %all-to-all-start = ((bf16[768,16,128]{2,1,0:T(8,128)(2,1)}), bf16[768,16,128]{2,1,0:T(8,128)(2,1)S(1)}, u32[]{:S(2)}, u32[]{:S(2)}) async-start(bf16[768,16,128]{2,1,0:T(8,128)(2,1)} %bitcast.9), calls=%async_computation | async-start | bytes 6291456 | tf_op jit(solution)/shard_map/all_to_all | solution.py:376
  17.0 42.3 %copy-start.11 = (s32[2,64]{1,0:T(2,128)S(1)}, s32[2,64]{1,0:T(2,128)}, u32[]{:S(2)}) copy-start(s32[2,64]{1,0:T(2,128)} %shift_ref.3) | copy-start | bytes 1540
  17.1 42.3 %copy-start.12 = (s32[2,64]{1,0:T(2,128)S(1)}, s32[2,64]{1,0:T(2,128)}, u32[]{:S(2)}) copy-start(s32[2,64]{1,0:T(2,128)} %length_ref.3) | copy-start | bytes 1540
  17.5 1.2 %copy-start = (f32[16,128,128]{2,1,0:T(8,128)S(1)}, f32[16,128,128]{2,1,0:T(8,128)}, u32[]{:S(2)}) copy-start(f32[16,128,128]{2,1,0:T(8,128)} %estimate_ref.1) | copy-start | bytes 3145732
  20.1 20.7 %collective-permute-start.2 = (bf16[1,18,8,128]{3,2,1,0:T(8,128)(2,1)S(1)}, bf16[1,18,8,128]{3,2,1,0:T(8,128)(2,1)S(1)}, u32[]{:S(2)}, u32[]{:S(2)}) collective-permute-start(bf16[1,18,8,128]{3,2,1,0:T(8,128)(2,1)S(1)} %get-tuple-element.38), channel_id=1, source_target_pairs={{0,1},{1,0},{2,3},{3,2},{4,5},{5,4},{6,7},{7,6},{8,9},{9,8},{10,11... | collective-permute-start | bytes 110600 | tf_op jit(solution)/shard_map/ppermute | solution.py:336
  21.2 35.3 %collective-permute-start.3 = (bf16[1,18,8,128]{3,2,1,0:T(8,128)(2,1)S(1)}, bf16[1,18,8,128]{3,2,1,0:T(8,128)(2,1)S(1)}, u32[]{:S(2)}, u32[]{:S(2)}) collective-permute-start(bf16[1,18,8,128]{3,2,1,0:T(8,128)(2,1)S(1)} %get-tuple-element.39), channel_id=1, source_target_pairs={{1,2},{2,1},{3,4},{4,3},{5,6},{6,5},{7,8},{8,7},{9,10},{10,9},{11,... | collective-permute-start | bytes 110600 | tf_op jit(solution)/shard_map/ppermute | solution.py:336
  25.9 1.2 %copy-start.1 = (f32[16,128,128]{2,1,0:T(8,128)S(1)}, f32[16,128,128]{2,1,0:T(8,128)}, u32[]{:S(2)}) copy-start(f32[16,128,128]{2,1,0:T(8,128)} %estimate_ref.1) | copy-start | bytes 3145732
  38.3 1.0 %copy-start.5 = (bf16[2,4,256,256]{3,2,1,0:T(8,128)(2,1)}, bf16[2,4,256,256]{3,2,1,0:T(8,128)(2,1)S(1)}, u32[]{:S(2)}) copy-start(bf16[2,4,256,256]{3,2,1,0:T(8,128)(2,1)S(1)} %get-tuple-element.30.turned_ref) | copy-start | bytes 3145732
  39.2 0.8 %copy-start.7 = (bf16[4,256,256]{2,1,0:T(8,128)(2,1)}, bf16[4,256,256]{2,1,0:T(8,128)(2,1)S(1)}, u32[]{:S(2)}) copy-start(bf16[4,256,256]{2,1,0:T(8,128)(2,1)S(1)} %get-tuple-element.32.rows_ref) | copy-start | bytes 1572868
  40.0 0.8 %copy-start.9 = (bf16[2,4,128,256]{3,2,1,0:T(8,128)(2,1)}, bf16[2,4,128,256]{3,2,1,0:T(8,128)(2,1)S(1)}, u32[]{:S(2)}) copy-start(bf16[2,4,128,256]{3,2,1,0:T(8,128)(2,1)S(1)} %get-tuple-element.34.cols_ref) | copy-start | bytes 1572868
  58.0 1.3 %copy-start.3 = (f32[2,16,128,128]{3,2,1,0:T(8,128)}, f32[2,16,128,128]{3,2,1,0:T(8,128)S(1)}, u32[]{:S(2)}) copy-start(f32[2,16,128,128]{3,2,1,0:T(8,128)S(1)} %get-tuple-element.41.recip_ref) | copy-start | bytes 6291460
  59.4 5.1 %copy-start.4 = (f32[2,16,128,128]{3,2,1,0:T(8,128)S(1)}, f32[2,16,128,128]{3,2,1,0:T(8,128)}, u32[]{:S(2)}) copy-start(f32[2,16,128,128]{3,2,1,0:T(8,128)} %copy-done.3) | copy-start | bytes 6291460
  60.1 8.0 %copy-start.8 = (bf16[4,256,256]{2,1,0:T(8,128)(2,1)S(1)}, bf16[4,256,256]{2,1,0:T(8,128)(2,1)}, u32[]{:S(2)}) copy-start(bf16[4,256,256]{2,1,0:T(8,128)(2,1)} %copy-done.7) | copy-start | bytes 1572868
  60.1 8.0 %copy-start.10 = (bf16[2,4,128,256]{3,2,1,0:T(8,128)(2,1)S(1)}, bf16[2,4,128,256]{3,2,1,0:T(8,128)(2,1)}, u32[]{:S(2)}) copy-start(bf16[2,4,128,256]{3,2,1,0:T(8,128)(2,1)} %copy-done.9) | copy-start | bytes 1572868
  60.1 6.1 %collective-permute-start.4 = (bf16[2,16,8,128]{3,2,1,0:T(8,128)(2,1)S(1)}, bf16[2,16,8,128]{3,2,1,0:T(8,128)(2,1)S(1)}, u32[]{:S(2)}, u32[]{:S(2)}) collective-permute-start(bf16[2,16,8,128]{3,2,1,0:T(8,128)(2,1)S(1)} %get-tuple-element.44), channel_id=1, source_target_pairs={{0,16},{16,0},{32,48},{48,32},{64,80},{80,64},{96,112},{112,96},{1... | collective-permute-start | bytes 196616 | tf_op jit(solution)/shard_map/ppermute | solution.py:336
  60.2 6.2 %collective-permute-start.5 = (bf16[2,16,8,128]{3,2,1,0:T(8,128)(2,1)S(1)}, bf16[2,16,8,128]{3,2,1,0:T(8,128)(2,1)S(1)}, u32[]{:S(2)}, u32[]{:S(2)}) collective-permute-start(bf16[2,16,8,128]{3,2,1,0:T(8,128)(2,1)S(1)} %get-tuple-element.45), channel_id=1, source_target_pairs={{16,32},{32,16},{48,64},{64,48},{80,96},{96,80},{112,0},{0,112},{1... | collective-permute-start | bytes 196616 | tf_op jit(solution)/shard_map/ppermute | solution.py:336
  64.4 10.1 %copy-start.2 = (f32[16,128,128]{2,1,0:T(8,128)S(1)}, f32[16,128,128]{2,1,0:T(8,128)}, u32[]{:S(2)}) copy-start(f32[16,128,128]{2,1,0:T(8,128)} %estimate_ref.1) | copy-start | bytes 3145732
  64.4 10.1 %copy-start.6 = (bf16[2,4,256,256]{3,2,1,0:T(8,128)(2,1)S(1)}, bf16[2,4,256,256]{3,2,1,0:T(8,128)(2,1)}, u32[]{:S(2)}) copy-start(bf16[2,4,256,256]{3,2,1,0:T(8,128)(2,1)} %copy-done.5) | copy-start | bytes 3145732
  66.6 4.4 %collective-permute-start.6 = (bf16[2,18,8,128]{3,2,1,0:T(8,128)(2,1)S(1)}, bf16[2,18,8,128]{3,2,1,0:T(8,128)(2,1)S(1)}, u32[]{:S(2)}, u32[]{:S(2)}) collective-permute-start(bf16[2,18,8,128]{3,2,1,0:T(8,128)(2,1)S(1)} %get-tuple-element.47), channel_id=1, source_target_pairs={{0,1},{1,0},{2,3},{3,2},{4,5},{5,4},{6,7},{7,6},{8,9},{9,8},{10,11... | collective-permute-start | bytes 221192 | tf_op jit(solution)/shard_map/ppermute | solution.py:336
  66.6 7.9 %collective-permute-start.7 = (bf16[2,18,8,128]{3,2,1,0:T(8,128)(2,1)S(1)}, bf16[2,18,8,128]{3,2,1,0:T(8,128)(2,1)S(1)}, u32[]{:S(2)}, u32[]{:S(2)}) collective-permute-start(bf16[2,18,8,128]{3,2,1,0:T(8,128)(2,1)S(1)} %get-tuple-element.48), channel_id=1, source_target_pairs={{1,2},{2,1},{3,4},{4,3},{5,6},{6,5},{7,8},{8,7},{9,10},{10,9},{11,... | collective-permute-start | bytes 221192 | tf_op jit(solution)/shard_map/ppermute | solution.py:336

commit v8 on v7

--- a/solution.py
+++ b/solution.py
@@ -330,10 +330,12 @@
         copy.wait()
 
 
-def swap(first, second, axis):
+def swap(first, second, axis, ring=True):
     count = lax.axis_size(axis)
-    pairs = lambda begin: [p for i in range(begin, count, 2) for p in ((i, (i + 1) % count), ((i + 1) % count, i))]
-    return lax.ppermute(first, axis, pairs(0)), lax.ppermute(second, axis, pairs(1))
+    chain = lambda begin: range(begin, count if ring else count - 1, 2)
+    pairs = lambda begin: [p for i in chain(begin) for p in ((i, (i + 1) % count), ((i + 1) % count, i))]
+    late = lax.ppermute(second, axis, pairs(1))
+    return lax.ppermute(first, axis, pairs(0)), late
 
 
 def place(count, at):
@@ -371,7 +373,6 @@
         60,
     )(me, group_shift, group_length, measured)
     outgoing = outgoing.reshape(devices * views * CAP, depth, tile_cols)
-    ex, ox = (pltpu.with_memory_space_constraint(x, pltpu.HBM) for x in (ex, ox))
     outgoing, ex, ox, cells = lax.optimization_barrier((outgoing, ex, ox, estimate))
     arrived = lax.all_to_all(outgoing, ("gx", "gy"), split_axis=0, concat_axis=0, tiled=True)
 
@@ -380,7 +381,7 @@
     dense = lambda lead, *args: call(
         dense_slab_kernel, [SMEM] * 2 + [VMEM] * 3, (like((lead, tiles, HW, tile_rows), BF16),) * 2
     )(place_x, place_y, *args)
-    ey, oy = swap(*dense(1, cols[None], ex, ox), "gy")
+    ey, oy = swap(*dense(1, cols[None], ex, ox), "gy", ring=False)
 
     norm = kernels / jnp.sum(kernels, axis=3, keepdims=True)
     tap_rows = jnp.stack([norm, norm[..., ::-1]])

time: 77.3 us -> 73.8 us (0.955)
  starting transfers between devices: 24 us -> 21.1 us
  waiting for transfers between devices: 19.9 us -> 21.4 us
  Pallas kernels: 24.3 us -> 23.1 us
    all_to_all x1, waiting for transfers between devices: 0.01 us -> 19.4 us  [body(): lax.all_to_all(outgoing, ('gx', 'gy'), split_axis=0, concat_axis=0, tiled...]
    ppermute x8, waiting for transfers between devices: 19.9 us -> 1.98 us  [the longest x4 1.97 us: swap(): late = lax.ppermute(second, axis, pairs(1))]
    ppermute x8, starting transfers between devices: 13.9 us -> 10.9 us  [the longest x4 9.58 us: swap(): late = lax.ppermute(second, axis, pairs(1))]
    pallas_call x2, Pallas kernels: 1.24 us -> 0.37 us  [body(): call(dense_slab_kernel, [SMEM] * 2 + [VMEM] * 3, (like((lead, tiles, HW,...]
    unnamed x34 -> x30, local copies, waits for them, and re-layouts: 7 us -> 6.41 us
  transfers between devices with their start and end apart: 9 -> 9, of which waited for: 4 -> 3; matrix products, arithmetic and copies ran while one was open for 0% -> 1% of each run, Pallas kernels for 28% -> 27%
where the time goes in v8:
time: 73.8 us; the launch traced here: 73.5 us
  Pallas kernels  23.1 us (31%)
  waiting for transfers between devices  21.4 us (29%)
  starting transfers between devices  21.1 us (29%)
  local copies, waits for them, and re-layouts  6.51 us (9%)
  other arithmetic  1.16 us (2%)
    all_to_all x1, waiting for transfers between devices, body(): lax.all_to_all(outgoing, ('gx', 'gy'), split_axis=0, concat_axis=0, tiled...  19.4 us
    pallas_call x1, Pallas kernels, body(): call(forward_kernel, [SMEM] * 2 + [VMEM] * 4, (like(measured.shape, F32),...  10.8 us
    all_to_all x1, starting transfers between devices, body(): lax.all_to_all(outgoing, ('gx', 'gy'), split_axis=0, concat_axis=0, tiled...  10.2 us
    ppermute x4, starting transfers between devices, swap(): late = lax.ppermute(second, axis, pairs(1))  9.58 us
    unnamed x30, local copies, waits for them, and re-layouts  6.41 us
    pallas_call x1, Pallas kernels, body(): call(functools.partial(pack_kernel, devices), [SMEM, HBM, HBM, HBM], like...  2.94 us
    pallas_call x1, Pallas kernels, body(): call(near_kernel, [SMEM] * 2 + [VMEM] * 6, like(estimate.shape, F32), [pl...  2.36 us
    pallas_call x1, Pallas kernels, body(): call(far_kernel, [SMEM] * 2 + [VMEM] * 6, like(estimate.shape, F32), [plt...  2.22 us
  transfers between devices with their start and end apart: 9, of which 3 were waited for; matrix products, arithmetic and copies ran while one was open for 1% of the time, Pallas kernels for 27%

profile of v8, /device:TPU:0, one launch (start us, length us, event | category | flops | bytes accessed | tf_op | source)
XLA Modules:
  0.0 73.5 jit_solution(3147577500963781291)
XLA Ops:
  0.0 0.9 %slice_select_fusion = (f32[16,8,128]{2,1,0:T(8,128)S(1)}, f32[16,8,128]{2,1,0:T(8,128)S(1)}) fusion(f32[16,128,128]{2,1,0:T(8,128)} %estimate_ref.1, pred[]{:T(512)S(6)} %eq.13), kind=kLoop, calls=%fused_computation | loop fusion | flops 32768 | bytes 262145 | tf_op jit(solution)/shard_map/jit(_where)/select_n | solution.py:360
  0.9 2.4 %collective-permute-start.1 = (f32[16,8,128]{2,1,0:T(8,128)S(1)}, f32[16,8,128]{2,1,0:T(8,128)S(1)}, u32[]{:S(2)}, u32[]{:S(2)}) collective-permute-start(f32[16,8,128]{2,1,0:T(8,128)S(1)} %get-tuple-element.49), channel_id=1, source_target_pairs={{16,32},{32,16},{48,64},{64,48},{80,96},{96,80},{112,0},{0,112},{1... | collective-permute-start | bytes 196616 | tf_op jit(solution)/shard_map/ppermute | solution.py:337
  3.3 2.9 %shard_map.64 = bf16[128,2,3,16,128]{4,3,2,1,0:T(8,128)(2,1)} custom-call(s32[1]{0:T(128)} %bitcast.4.me_ref, s32[2,64]{1,0:T(2,128)} %shift_ref.3, s32[2,64]{1,0:T(2,128)} %length_ref.3, bf16[2,16,128,128]{3,2,1,0:T(8,128)(2,1)} %measured_hbm.1), custom_call_target="tpu_custom_call" | custom-call | tf_op jit(solution)/shard_map/pallas_call | solution.py:361
  6.2 10.2 %all-to-all-start = ((bf16[768,16,128]{2,1,0:T(8,128)(2,1)}), bf16[768,16,128]{2,1,0:T(8,128)(2,1)S(1)}, u32[]{:S(2)}, u32[]{:S(2)}) async-start(bf16[768,16,128]{2,1,0:T(8,128)(2,1)} %bitcast.9), calls=%async_computation | async-start | bytes 6291456 | tf_op jit(solution)/shard_map/all_to_all | solution.py:377
  16.5 0.1 reduce_sum.9
  16.6 0.1 broadcast_divide_fusion
  16.6 0.1 rev.3
  16.8 0.1 fusion
  16.9 1.2 %copy-done = f32[16,128,128]{2,1,0:T(8,128)S(1)} copy-done((f32[16,128,128]{2,1,0:T(8,128)S(1)}, f32[16,128,128]{2,1,0:T(8,128)}, u32[]{:S(2)}) %copy-start) | copy-done | bytes 1048600
  18.1 0.4 shard_map.66
  18.4 0.2 shard_map.67
  18.6 1.1 %collective-permute-start.2 = (bf16[1,18,8,128]{3,2,1,0:T(8,128)(2,1)S(1)}, bf16[1,18,8,128]{3,2,1,0:T(8,128)(2,1)S(1)}, u32[]{:S(2)}, u32[]{:S(2)}) collective-permute-start(bf16[1,18,8,128]{3,2,1,0:T(8,128)(2,1)S(1)} %get-tuple-element.38), channel_id=1, source_target_pairs={{0,1},{1,0},{2,3},{3,2},{4,5},{5,4},{6,7},{7,6},{8,9},{9,8},{10,11... | collective-permute-start | bytes 110600 | tf_op jit(solution)/shard_map/ppermute | solution.py:338
  19.7 0.7 collective-permute-start.3
  20.4 1.2 %copy-done.1 = f32[16,128,128]{2,1,0:T(8,128)S(1)} copy-done((f32[16,128,128]{2,1,0:T(8,128)S(1)}, f32[16,128,128]{2,1,0:T(8,128)}, u32[]{:S(2)}) %copy-start.1) | copy-done | bytes 1048600
  21.6 10.8 %shard_map.65 = (f32[2,16,128,128]{3,2,1,0:T(8,128)S(1)}, bf16[2,4,256,256]{3,2,1,0:T(8,128)(2,1)S(1)}, bf16[4,2,48,128]{3,2,1,0:T(8,128)(2,1)S(1)}, bf16[4,256,...) custom-call(s32[16]{0:T(128)S(1)} %copy-done.13, ...), custom_call_target="tpu_custom_call" | custom-call | tf_op jit(solution)/shard_map/pallas_call | solution.py:391
  32.5 1.0 %copy-done.5 = bf16[2,4,256,256]{3,2,1,0:T(8,128)(2,1)} copy-done((bf16[2,4,256,256]{3,2,1,0:T(8,128)(2,1)}, bf16[2,4,256,256]{3,2,1,0:T(8,128)(2,1)S(1)}, u32[]{:S(2)}) %copy-start.5) | copy-done | bytes 1048600
  33.4 0.8 %copy-done.7 = bf16[4,256,256]{2,1,0:T(8,128)(2,1)} copy-done((bf16[4,256,256]{2,1,0:T(8,128)(2,1)}, bf16[4,256,256]{2,1,0:T(8,128)(2,1)S(1)}, u32[]{:S(2)}) %copy-start.7) | copy-done | bytes 524312
  34.2 0.8 %copy-done.9 = bf16[2,4,128,256]{3,2,1,0:T(8,128)(2,1)} copy-done((bf16[2,4,128,256]{3,2,1,0:T(8,128)(2,1)}, bf16[2,4,128,256]{3,2,1,0:T(8,128)(2,1)S(1)}, u32[]{:S(2)}) %copy-start.9) | copy-done | bytes 524312
  35.1 1.5 %shard_map.68 = (f32[2,16,128,128]{3,2,1,0:T(8,128)S(1)}, f32[2,16,16,128]{3,2,1,0:T(8,128)S(1)}) custom-call(s32[16]{0:T(128)S(1)} %copy-done.13, s32[1]{0:T(128)} %bitcast.place_y_ref.place_ref, bf16[2,4,256,256]{3,2,1,0:T(8,128)(2,1)S(1)} %get-tuple-element.36.turned_ref, bf16[4,2,48,128]{3,2,1,0:T(8,128)(2,1)S(1)} %get-tuple-element.37.far_ref, ...), custom_call_target="tpu_custom_call" | custom-call | tf_op jit(solution)/shard_map/pallas_call | solution.py:410
  36.6 1.3 %copy-done.3 = f32[2,16,128,128]{3,2,1,0:T(8,128)} copy-done((f32[2,16,128,128]{3,2,1,0:T(8,128)}, f32[2,16,128,128]{3,2,1,0:T(8,128)S(1)}, u32[]{:S(2)}) %copy-start.3) | copy-done | bytes 2097176
  38.0 19.4 %all-to-all-done.arrived_ref = bf16[768,16,128]{2,1,0:T(8,128)(2,1)S(1)} async-done(((bf16[768,16,128]{2,1,0:T(8,128)(2,1)}), bf16[768,16,128]{2,1,0:T(8,128)(2,1)S(1)}, u32[]{:S(2)}, u32[]{:S(2)}) %all-to-all-start) | async-done | bytes 3145760 | tf_op jit(solution)/shard_map/all_to_all | solution.py:377
  57.4 0.7 %shard_map.70 = (bf16[2,16,8,128]{3,2,1,0:T(8,128)(2,1)S(1)}, bf16[2,16,8,128]{3,2,1,0:T(8,128)(2,1)S(1)}) custom-call(s32[1]{0:T(128)} %bitcast.4.me_ref, s32[1]{0:T(128)} %bitcast.1.place_ref.place_x_ref, s32[2,64]{1,0:T(2,128)S(1)} %copy-done.11, s32[2,64]{1,0:T(2,128)S(1)} %copy-done.12, bf16[768,16,128]{2,1,0:T(8,128)(2,1)S(1)} %all-to-all-done.arrived_ref, ...), custom_call_target="tpu_custom_call" | custom-call | tf_op jit(solution)/shard_map/pallas_call | solution.py:420
  58.2 0.1 collective-permute-start.4
  58.3 2.6 %collective-permute-start.5 = (bf16[2,16,8,128]{3,2,1,0:T(8,128)(2,1)S(1)}, bf16[2,16,8,128]{3,2,1,0:T(8,128)(2,1)S(1)}, u32[]{:S(2)}, u32[]{:S(2)}) collective-permute-start(bf16[2,16,8,128]{3,2,1,0:T(8,128)(2,1)S(1)} %get-tuple-element.45), channel_id=1, source_target_pairs={{16,32},{32,16},{48,64},{64,48},{80,96},{96,80},{112,0},{0,112},{1... | collective-permute-start | bytes 196616 | tf_op jit(solution)/shard_map/ppermute | solution.py:337
  60.9 1.7 %shard_map.69 = (bf16[2,16,128,128]{3,2,1,0:T(8,128)(2,1)S(1)}, bf16[2,16,16,128]{3,2,1,0:T(8,128)(2,1)S(1)}) custom-call(s32[1]{0:T(128)} %bitcast.4.me_ref, s32[2,64]{1,0:T(2,128)S(1)} %copy-done.11, s32[2,64]{1,0:T(2,128)S(1)} %copy-done.12, bf16[768,16,128]{2,1,0:T(8,128)(2,1)S(1)} %all-to-all-done.arrived_ref, f32[2,16,128,128]{3,2,1,0:T(8,128)S(1)} %copy-done.4), custom_call_target="tpu_custom_call" | custom-call | tf_op jit(solution)/shard_map/pallas_call | solution.py:427
  62.7 0.6 collective-permute-done.5.other_ref
  63.3 0.2 shard_map.72
  63.4 0.1 collective-permute-start.6
  63.6 3.9 %collective-permute-start.7 = (bf16[2,18,8,128]{3,2,1,0:T(8,128)(2,1)S(1)}, bf16[2,18,8,128]{3,2,1,0:T(8,128)(2,1)S(1)}, u32[]{:S(2)}, u32[]{:S(2)}) collective-permute-start(bf16[2,18,8,128]{3,2,1,0:T(8,128)(2,1)S(1)} %get-tuple-element.48), channel_id=1, source_target_pairs={{1,2},{2,1},{3,4},{4,3},{5,6},{6,5},{7,8},{8,7},{9,10},{10,9},{11,... | collective-permute-start | bytes 221192 | tf_op jit(solution)/shard_map/ppermute | solution.py:337
  67.5 2.4 %shard_map.71.near_ref = f32[16,128,128]{2,1,0:T(8,128)S(1)} custom-call(s32[16]{0:T(128)S(1)} %copy-done.13, s32[1]{0:T(128)} %bitcast.1.place_ref.place_x_ref, bf16[4,256,256]{2,1,0:T(8,128)(2,1)S(1)} %copy-done.8, bf16[4,32,32]{2,1,0:T(8,128)(2,1)S(1)} %get-tuple-element.33.ends_ref, bf16[2,4,128,256]{3,2,1,0:T(8,128)(2,1)S(1)} %copy-done.10, ...), custom_call_target="tpu_custom_call" | custom-call | tf_op jit(solution)/shard_map/pallas_call | solution.py:434
  69.9 1.4 %collective-permute-done.7.other_ref = bf16[2,18,8,128]{3,2,1,0:T(8,128)(2,1)S(1)} collective-permute-done((bf16[2,18,8,128]{3,2,1,0:T(8,128)(2,1)S(1)}, bf16[2,18,8,128]{3,2,1,0:T(8,128)(2,1)S(1)}, u32[]{:S(2)}, u32[]{:S(2)}) %collective-permute-start.7) | collective-permute-done | bytes 73760 | tf_op jit(solution)/shard_map/ppermute | solution.py:337
  71.3 2.2 %shard_map.73 = f32[16,128,128]{2,1,0:T(8,128)} custom-call(s32[16]{0:T(128)S(1)} %copy-done.13, s32[1]{0:T(128)} %bitcast.place_y_ref.place_ref, bf16[2,4,256,256]{3,2,1,0:T(8,128)(2,1)S(1)} %copy-done.6, bf16[4,2,48,128]{3,2,1,0:T(8,128)(2,1)S(1)} %get-tuple-element.31.far_ref, f32[16,128,128]{2,1,0:T(8,128)S(1)} %shard_map.71.near_ref, ...), custom_call_target="tpu_custom_call" | custom-call | tf_op jit(solution)/shard_map/pallas_call | solution.py:443
  (32 shorter events, 0.1 us)
Async XLA Ops:
  0.9 5.3 %collective-permute-start.1 = (f32[16,8,128]{2,1,0:T(8,128)S(1)}, f32[16,8,128]{2,1,0:T(8,128)S(1)}, u32[]{:S(2)}, u32[]{:S(2)}) collective-permute-start(f32[16,8,128]{2,1,0:T(8,128)S(1)} %get-tuple-element.49), channel_id=1, source_target_pairs={{16,32},{32,16},{48,64},{64,48},{80,96},{96,80},{112,0},{0,112},{1... | collective-permute-start | bytes 196616 | tf_op jit(solution)/shard_map/ppermute | solution.py:337
  3.2 3.0 %collective-permute-start = (f32[16,8,128]{2,1,0:T(8,128)S(1)}, f32[16,8,128]{2,1,0:T(8,128)S(1)}, u32[]{:S(2)}, u32[]{:S(2)}) collective-permute-start(f32[16,8,128]{2,1,0:T(8,128)S(1)} %get-tuple-element.50), channel_id=1, source_target_pairs={{0,16},{16,0},{32,48},{48,32},{64,80},{80,64},{96,112},{112,96},{1... | collective-permute-start | bytes 196616 | tf_op jit(solution)/shard_map/ppermute | solution.py:338
  6.2 10.2 %copy-start.14 = (f32[2,4,2,17]{3,2,1,0:T(2,128)S(1)}, f32[2,4,2,17]{3,2,1,0:T(2,128)}, u32[]{:S(2)}) copy-start(f32[2,4,2,17]{3,2,1,0:T(2,128)} %param.8) | copy-start | bytes 3268
  6.2 14.2 %copy-start.13 = (s32[16]{0:T(128)S(1)}, s32[16]{0:T(128)}, u32[]{:S(2)}) copy-start(s32[16]{0:T(128)} %band_ref.7) | copy-start | bytes 196
  6.2 51.2 %all-to-all-start = ((bf16[768,16,128]{2,1,0:T(8,128)(2,1)}), bf16[768,16,128]{2,1,0:T(8,128)(2,1)S(1)}, u32[]{:S(2)}, u32[]{:S(2)}) async-start(bf16[768,16,128]{2,1,0:T(8,128)(2,1)} %bitcast.9), calls=%async_computation | async-start | bytes 6291456 | tf_op jit(solution)/shard_map/all_to_all | solution.py:377
  16.4 41.0 %copy-start.11 = (s32[2,64]{1,0:T(2,128)S(1)}, s32[2,64]{1,0:T(2,128)}, u32[]{:S(2)}) copy-start(s32[2,64]{1,0:T(2,128)} %shift_ref.3) | copy-start | bytes 1540
  16.4 41.0 %copy-start.12 = (s32[2,64]{1,0:T(2,128)S(1)}, s32[2,64]{1,0:T(2,128)}, u32[]{:S(2)}) copy-start(s32[2,64]{1,0:T(2,128)} %length_ref.3) | copy-start | bytes 1540
  16.8 1.2 %copy-start = (f32[16,128,128]{2,1,0:T(8,128)S(1)}, f32[16,128,128]{2,1,0:T(8,128)}, u32[]{:S(2)}) copy-start(f32[16,128,128]{2,1,0:T(8,128)} %estimate_ref.1) | copy-start | bytes 3145732
  18.6 16.4 %collective-permute-start.2 = (bf16[1,18,8,128]{3,2,1,0:T(8,128)(2,1)S(1)}, bf16[1,18,8,128]{3,2,1,0:T(8,128)(2,1)S(1)}, u32[]{:S(2)}, u32[]{:S(2)}) collective-permute-start(bf16[1,18,8,128]{3,2,1,0:T(8,128)(2,1)S(1)} %get-tuple-element.38), channel_id=1, source_target_pairs={{0,1},{1,0},{2,3},{3,2},{4,5},{5,4},{6,7},{7,6},{8,9},{9,8},{10,11... | collective-permute-start | bytes 110600 | tf_op jit(solution)/shard_map/ppermute | solution.py:338
  19.7 15.4 %collective-permute-start.3 = (bf16[1,18,8,128]{3,2,1,0:T(8,128)(2,1)S(1)}, bf16[1,18,8,128]{3,2,1,0:T(8,128)(2,1)S(1)}, u32[]{:S(2)}, u32[]{:S(2)}) collective-permute-start(bf16[1,18,8,128]{3,2,1,0:T(8,128)(2,1)S(1)} %get-tuple-element.39), channel_id=1, source_target_pairs={{1,2},{2,1},{3,4},{4,3},{5,6},{6,5},{7,8},{8,7},{9,10},{10,9},{11,... | collective-permute-start | bytes 110600 | tf_op jit(solution)/shard_map/ppermute | solution.py:337
  20.4 1.2 %copy-start.1 = (f32[16,128,128]{2,1,0:T(8,128)S(1)}, f32[16,128,128]{2,1,0:T(8,128)}, u32[]{:S(2)}) copy-start(f32[16,128,128]{2,1,0:T(8,128)} %estimate_ref.1) | copy-start | bytes 3145732
  32.5 1.0 %copy-start.5 = (bf16[2,4,256,256]{3,2,1,0:T(8,128)(2,1)}, bf16[2,4,256,256]{3,2,1,0:T(8,128)(2,1)S(1)}, u32[]{:S(2)}) copy-start(bf16[2,4,256,256]{3,2,1,0:T(8,128)(2,1)S(1)} %get-tuple-element.30.turned_ref) | copy-start | bytes 3145732
  33.4 0.8 %copy-start.7 = (bf16[4,256,256]{2,1,0:T(8,128)(2,1)}, bf16[4,256,256]{2,1,0:T(8,128)(2,1)S(1)}, u32[]{:S(2)}) copy-start(bf16[4,256,256]{2,1,0:T(8,128)(2,1)S(1)} %get-tuple-element.32.rows_ref) | copy-start | bytes 1572868
  34.2 0.8 %copy-start.9 = (bf16[2,4,128,256]{3,2,1,0:T(8,128)(2,1)}, bf16[2,4,128,256]{3,2,1,0:T(8,128)(2,1)S(1)}, u32[]{:S(2)}) copy-start(bf16[2,4,128,256]{3,2,1,0:T(8,128)(2,1)S(1)} %get-tuple-element.34.cols_ref) | copy-start | bytes 1572868
  36.6 1.4 %copy-start.3 = (f32[2,16,128,128]{3,2,1,0:T(8,128)}, f32[2,16,128,128]{3,2,1,0:T(8,128)S(1)}, u32[]{:S(2)}) copy-start(f32[2,16,128,128]{3,2,1,0:T(8,128)S(1)} %get-tuple-element.41.recip_ref) | copy-start | bytes 6291460
  57.4 3.5 %copy-start.4 = (f32[2,16,128,128]{3,2,1,0:T(8,128)S(1)}, f32[2,16,128,128]{3,2,1,0:T(8,128)}, u32[]{:S(2)}) copy-start(f32[2,16,128,128]{3,2,1,0:T(8,128)} %copy-done.3) | copy-start | bytes 6291460
  58.2 9.3 %copy-start.8 = (bf16[4,256,256]{2,1,0:T(8,128)(2,1)S(1)}, bf16[4,256,256]{2,1,0:T(8,128)(2,1)}, u32[]{:S(2)}) copy-start(bf16[4,256,256]{2,1,0:T(8,128)(2,1)} %copy-done.7) | copy-start | bytes 1572868
  58.2 9.3 %copy-start.10 = (bf16[2,4,128,256]{3,2,1,0:T(8,128)(2,1)S(1)}, bf16[2,4,128,256]{3,2,1,0:T(8,128)(2,1)}, u32[]{:S(2)}) copy-start(bf16[2,4,128,256]{3,2,1,0:T(8,128)(2,1)} %copy-done.9) | copy-start | bytes 1572868
  58.2 4.5 %collective-permute-start.4 = (bf16[2,16,8,128]{3,2,1,0:T(8,128)(2,1)S(1)}, bf16[2,16,8,128]{3,2,1,0:T(8,128)(2,1)S(1)}, u32[]{:S(2)}, u32[]{:S(2)}) collective-permute-start(bf16[2,16,8,128]{3,2,1,0:T(8,128)(2,1)S(1)} %get-tuple-element.44), channel_id=1, source_target_pairs={{0,16},{16,0},{32,48},{48,32},{64,80},{80,64},{96,112},{112,96},{1... | collective-permute-start | bytes 196616 | tf_op jit(solution)/shard_map/ppermute | solution.py:338
  58.3 5.0 %collective-permute-start.5 = (bf16[2,16,8,128]{3,2,1,0:T(8,128)(2,1)S(1)}, bf16[2,16,8,128]{3,2,1,0:T(8,128)(2,1)S(1)}, u32[]{:S(2)}, u32[]{:S(2)}) collective-permute-start(bf16[2,16,8,128]{3,2,1,0:T(8,128)(2,1)S(1)} %get-tuple-element.45), channel_id=1, source_target_pairs={{16,32},{32,16},{48,64},{64,48},{80,96},{96,80},{112,0},{0,112},{1... | collective-permute-start | bytes 196616 | tf_op jit(solution)/shard_map/ppermute | solution.py:337
  60.9 10.3 %copy-start.2 = (f32[16,128,128]{2,1,0:T(8,128)S(1)}, f32[16,128,128]{2,1,0:T(8,128)}, u32[]{:S(2)}) copy-start(f32[16,128,128]{2,1,0:T(8,128)} %estimate_ref.1) | copy-start | bytes 3145732
  60.9 10.3 %copy-start.6 = (bf16[2,4,256,256]{3,2,1,0:T(8,128)(2,1)S(1)}, bf16[2,4,256,256]{3,2,1,0:T(8,128)(2,1)}, u32[]{:S(2)}) copy-start(bf16[2,4,256,256]{3,2,1,0:T(8,128)(2,1)} %copy-done.5) | copy-start | bytes 3145732
  63.4 6.4 %collective-permute-start.6 = (bf16[2,18,8,128]{3,2,1,0:T(8,128)(2,1)S(1)}, bf16[2,18,8,128]{3,2,1,0:T(8,128)(2,1)S(1)}, u32[]{:S(2)}, u32[]{:S(2)}) collective-permute-start(bf16[2,18,8,128]{3,2,1,0:T(8,128)(2,1)S(1)} %get-tuple-element.47), channel_id=1, source_target_pairs={{0,1},{1,0},{2,3},{3,2},{4,5},{5,4},{6,7},{7,6},{8,9},{9,8},{10,11... | collective-permute-start | bytes 221192 | tf_op jit(solution)/shard_map/ppermute | solution.py:338
  63.6 7.7 %collective-permute-start.7 = (bf16[2,18,8,128]{3,2,1,0:T(8,128)(2,1)S(1)}, bf16[2,18,8,128]{3,2,1,0:T(8,128)(2,1)S(1)}, u32[]{:S(2)}, u32[]{:S(2)}) collective-permute-start(bf16[2,18,8,128]{3,2,1,0:T(8,128)(2,1)S(1)} %get-tuple-element.48), channel_id=1, source_target_pairs={{1,2},{2,1},{3,4},{4,3},{5,6},{6,5},{7,8},{8,7},{9,10},{10,9},{11,... | collective-permute-start | bytes 221192 | tf_op jit(solution)/shard_map/ppermute | solution.py:337

commit v9 on v8

--- a/solution.py
+++ b/solution.py
@@ -304,23 +304,67 @@
         out_ref[z, tile_rows - HW :] += ends[HW:]
 
 
-def far_kernel(
-    band_ref, place_ref, turned_ref, far_ref, near_ref, even_ref, other_ref, estimate_ref, out_hbm,
-    slab_ref, along_ref, out_ref, sems,
-):
+def half_products(place_ref, turned_ref, far_ref, cells_ref, ring_odd, slab_ref, along_ref, across_ref):
     views, bands = turned_ref.shape[:2]
-    depth, tile_rows, tile_cols = near_ref.shape
+    tile_rows = along_ref.shape[-1]
+    depth = tile_rows // HW
+    count = tile_rows // (2 * HW)
+    odd = is_odd(place_ref)
+    follows = odd if ring_odd else jnp.logical_not(odd)
+    end = jnp.logical_or(place_ref[0] == 0, place_ref[0] >= LAST)
+    owner = lax.broadcasted_iota(jnp.int32, (HW, tile_rows), 1) // (2 * HW)
+
+    def cells(view, i):
+        x = cells_ref[view, i].astype(F32)
+        return jnp.where(end, 0.0, x) if ring_odd else x
+
+    for view in range(views):
+        for z in range(0, depth, 2):
+            at = pl.ds(z * HW, 2 * HW)
+            both = (z, z + 1)
+            slab_ref[view, at, :tile_rows] = jnp.concatenate([cells(view, i) for i in both], axis=0).astype(BF16)
+            corners = [jnp.where(owner == i % count, cells(view, depth + i // count), 0.0) for i in both]
+            slab_ref[view, at, tile_rows:] = jnp.concatenate(corners, axis=0).astype(BF16)
+    for b in range(bands):
+        across = []
+        for view in range(views):
+            along = dot(slab_ref[view], turned_ref[view, b])
+            along_ref[view, b] = along[:, :tile_rows] + along[:, tile_rows:]
+            weights = far_ref[b, view].astype(F32)
+            high = jnp.where(follows, weights[:HW], weights[HW : 2 * HW])
+            low = jnp.where(follows, weights[4 * HW : 5 * HW], weights[5 * HW :])
+            across += [high, high, low]
+        across_ref[b] = jnp.concatenate(across, axis=0).astype(BF16)
+
+
+def half_part(along_ref, across_ref, b, z):
+    parts = []
+    for view in range(along_ref.shape[0]):
+        along = along_ref[view, b, z * HW : (z + 1) * HW, :]
+        high = along.astype(BF16).astype(F32)
+        parts += [high, along - high, high]
+    return dot(jnp.concatenate(parts, axis=0).astype(BF16), across_ref[b], ((0,), (0,)))
+
+
+def even_far_kernel(
+    band_ref, place_ref, turned_ref, far_ref, near_ref, cells_ref, out_ref, slab_ref, along_ref, across_ref
+):
+    half_products(place_ref, turned_ref, far_ref, cells_ref, False, slab_ref, along_ref, across_ref)
+    for z in range(near_ref.shape[0]):
+        out_ref[z] = near_ref[z] + half_part(along_ref, across_ref, band_ref[z], z)
+
+
+def odd_far_kernel(
+    band_ref, place_ref, turned_ref, far_ref, near_ref, cells_ref, estimate_ref, out_hbm,
+    slab_ref, along_ref, across_ref, out_ref, sems,
+):
+    views = turned_ref.shape[0]
+    depth = near_ref.shape[0]
     step = depth // sems.shape[0]
-    for view in range(views):
-        far_products(place_ref, even_ref.at[view], other_ref.at[view], [turned_ref.at[view]], slab_ref.at[view], [along_ref.at[view]])
+    half_products(place_ref, turned_ref, far_ref, cells_ref, True, slab_ref, along_ref, across_ref)
     leave = []
     for z in range(depth):
-        b = band_ref[z]
-        parts = []
-        for view in range(views):
-            parts += far_parts(along_ref, view, b, z)
-        across = far_ref[b].reshape(views * 6 * HW, tile_cols)
-        total = near_ref[z] + dot(jnp.concatenate(parts, axis=0), across, ((0,), (0,)))
+        total = near_ref[z] + half_part(along_ref, across_ref, band_ref[z], z)
         out_ref[z] = estimate_ref[z] * (total * (1.0 / views))
         if z % step == step - 1:
             part = pl.ds(z - step + 1, step)
@@ -440,18 +484,21 @@
             pltpu.VMEM((depth, views * 2 * HW, 2 * tile_cols), BF16),
         ],
     )(depth_band, place_x, rows_mat, ends_mat, cols_mat, ratio, ex, ox)
+    halves = [
+        pltpu.VMEM((views, depth * HW, 2 * tile_rows), BF16),
+        pltpu.VMEM((views, bands, depth * HW, tile_rows), F32),
+        pltpu.VMEM((bands, views * 3 * HW, tile_cols), BF16),
+    ]
+    near = call(
+        even_far_kernel, [SMEM] * 2 + [VMEM] * 4, like(estimate.shape, F32), halves
+    )(depth_band, place_y, turned_mat, far_mat, near, ey)
     return call(
-        far_kernel,
-        [SMEM] * 2 + [VMEM] * 6,
+        odd_far_kernel,
+        [SMEM] * 2 + [VMEM] * 5,
         like(estimate.shape, F32),
-        [
-            pltpu.VMEM((views, depth * 2 * HW, 2 * tile_rows), BF16),
-            pltpu.VMEM((views, bands, 2, depth * 2 * HW, tile_rows), BF16),
-            pltpu.VMEM(estimate.shape, F32),
-            pltpu.SemaphoreType.DMA((4,)),
-        ],
+        halves + [pltpu.VMEM(estimate.shape, F32), pltpu.SemaphoreType.DMA((4,))],
         HBM,
-    )(depth_band, place_y, turned_mat, far_mat, near, ey, oy, estimate)
+    )(depth_band, place_y, turned_mat, far_mat, near, oy, estimate)
 
 
 def solution(mesh):

time: 73.8 us -> 74 us (level)
  Pallas kernels: 23.1 us -> 24 us
  waiting for transfers between devices: 21.4 us -> 20.5 us
    pallas_call x1 -> x2, Pallas kernels: 2.22 us -> 3.33 us  [the longest x1 2.12 us: body(): call(odd_far_kernel, [SMEM] * 2 + [VMEM] * 5, like(estimate.shape, F32),...]
    ppermute x4, waiting for transfers between devices: 1.97 us -> 1.02 us  [swap(): late = lax.ppermute(second, axis, pairs(1))]
  transfers between devices with their start and end apart: 9 -> 9, of which waited for: 3 -> 3; matrix products, arithmetic and copies ran while one was open for 1% -> 1% of each run, Pallas kernels for 27% -> 28%
where the time goes in v9:
time: 74 us; the launch traced here: 73.7 us
  Pallas kernels  24 us (32%)
  starting transfers between devices  21.1 us (29%)
  waiting for transfers between devices  20.5 us (28%)
  local copies, waits for them, and re-layouts  6.51 us (9%)
  other arithmetic  1.16 us (2%)
    all_to_all x1, waiting for transfers between devices, body(): lax.all_to_all(outgoing, ('gx', 'gy'), split_axis=0, concat_axis=0, tiled...  19.4 us
    pallas_call x1, Pallas kernels, body(): call(forward_kernel, [SMEM] * 2 + [VMEM] * 4, (like(measured.shape, F32),...  10.8 us
    all_to_all x1, starting transfers between devices, body(): lax.all_to_all(outgoing, ('gx', 'gy'), split_axis=0, concat_axis=0, tiled...  10.2 us
    ppermute x4, starting transfers between devices, swap(): late = lax.ppermute(second, axis, pairs(1))  9.58 us
    unnamed x30, local copies, waits for them, and re-layouts  6.41 us
    pallas_call x1, Pallas kernels, body(): call(functools.partial(pack_kernel, devices), [SMEM, HBM, HBM, HBM], like...  2.94 us
    pallas_call x1, Pallas kernels, body(): call(near_kernel, [SMEM] * 2 + [VMEM] * 6, like(estimate.shape, F32), [pl...  2.26 us
    pallas_call x1, Pallas kernels, body(): call(odd_far_kernel, [SMEM] * 2 + [VMEM] * 5, like(estimate.shape, F32),...  2.12 us
  transfers between devices with their start and end apart: 9, of which 3 were waited for; matrix products, arithmetic and copies ran while one was open for 1% of the time, Pallas kernels for 28%

profile of v9, /device:TPU:0, one launch (start us, length us, event | category | flops | bytes accessed | tf_op | source)
XLA Modules:
  0.0 73.7 jit_solution(9168982707446904920)
XLA Ops:
  0.0 0.9 %slice_select_fusion = (f32[16,8,128]{2,1,0:T(8,128)S(1)}, f32[16,8,128]{2,1,0:T(8,128)S(1)}) fusion(f32[16,128,128]{2,1,0:T(8,128)} %estimate_ref.1, pred[]{:T(512)S(6)} %eq.13), kind=kLoop, calls=%fused_computation | loop fusion | flops 32768 | bytes 262145 | tf_op jit(solution)/shard_map/jit(_where)/select_n | solution.py:404
  0.9 2.4 %collective-permute-start.1 = (f32[16,8,128]{2,1,0:T(8,128)S(1)}, f32[16,8,128]{2,1,0:T(8,128)S(1)}, u32[]{:S(2)}, u32[]{:S(2)}) collective-permute-start(f32[16,8,128]{2,1,0:T(8,128)S(1)} %get-tuple-element.49), channel_id=1, source_target_pairs={{16,32},{32,16},{48,64},{64,48},{80,96},{96,80},{112,0},{0,112},{1... | collective-permute-start | bytes 196616 | tf_op jit(solution)/shard_map/ppermute | solution.py:381
  3.3 2.9 %shard_map.64 = bf16[128,2,3,16,128]{4,3,2,1,0:T(8,128)(2,1)} custom-call(s32[1]{0:T(128)} %bitcast.4.me_ref, s32[2,64]{1,0:T(2,128)} %shift_ref.3, s32[2,64]{1,0:T(2,128)} %length_ref.3, bf16[2,16,128,128]{3,2,1,0:T(8,128)(2,1)} %measured_hbm.1), custom_call_target="tpu_custom_call" | custom-call | tf_op jit(solution)/shard_map/pallas_call | solution.py:405
  6.2 10.2 %all-to-all-start = ((bf16[768,16,128]{2,1,0:T(8,128)(2,1)}), bf16[768,16,128]{2,1,0:T(8,128)(2,1)S(1)}, u32[]{:S(2)}, u32[]{:S(2)}) async-start(bf16[768,16,128]{2,1,0:T(8,128)(2,1)} %bitcast.9), calls=%async_computation | async-start | bytes 6291456 | tf_op jit(solution)/shard_map/all_to_all | solution.py:421
  16.5 0.1 reduce_sum.9
  16.6 0.1 broadcast_divide_fusion
  16.7 0.1 rev.3
  16.9 1.2 %copy-done = f32[16,128,128]{2,1,0:T(8,128)S(1)} copy-done((f32[16,128,128]{2,1,0:T(8,128)S(1)}, f32[16,128,128]{2,1,0:T(8,128)}, u32[]{:S(2)}) %copy-start) | copy-done | bytes 1048600
  18.1 0.4 shard_map.66
  18.5 0.2 shard_map.67
  18.6 1.1 %collective-permute-start.2 = (bf16[1,18,8,128]{3,2,1,0:T(8,128)(2,1)S(1)}, bf16[1,18,8,128]{3,2,1,0:T(8,128)(2,1)S(1)}, u32[]{:S(2)}, u32[]{:S(2)}) collective-permute-start(bf16[1,18,8,128]{3,2,1,0:T(8,128)(2,1)S(1)} %get-tuple-element.38), channel_id=1, source_target_pairs={{0,1},{1,0},{2,3},{3,2},{4,5},{5,4},{6,7},{7,6},{8,9},{9,8},{10,11... | collective-permute-start | bytes 110600 | tf_op jit(solution)/shard_map/ppermute | solution.py:382
  19.7 0.7 collective-permute-start.3
  20.4 1.2 %copy-done.1 = f32[16,128,128]{2,1,0:T(8,128)S(1)} copy-done((f32[16,128,128]{2,1,0:T(8,128)S(1)}, f32[16,128,128]{2,1,0:T(8,128)}, u32[]{:S(2)}) %copy-start.1) | copy-done | bytes 1048600
  21.6 10.8 %shard_map.65 = (f32[2,16,128,128]{3,2,1,0:T(8,128)S(1)}, bf16[2,4,256,256]{3,2,1,0:T(8,128)(2,1)S(1)}, bf16[4,2,48,128]{3,2,1,0:T(8,128)(2,1)S(1)}, bf16[4,256,...) custom-call(s32[16]{0:T(128)S(1)} %copy-done.11, ...), custom_call_target="tpu_custom_call" | custom-call | tf_op jit(solution)/shard_map/pallas_call | solution.py:435
  32.5 1.0 %copy-done.3 = bf16[2,4,256,256]{3,2,1,0:T(8,128)(2,1)} copy-done((bf16[2,4,256,256]{3,2,1,0:T(8,128)(2,1)}, bf16[2,4,256,256]{3,2,1,0:T(8,128)(2,1)S(1)}, u32[]{:S(2)}) %copy-start.3) | copy-done | bytes 1048600
  33.5 0.8 %copy-done.7 = bf16[4,256,256]{2,1,0:T(8,128)(2,1)} copy-done((bf16[4,256,256]{2,1,0:T(8,128)(2,1)}, bf16[4,256,256]{2,1,0:T(8,128)(2,1)S(1)}, u32[]{:S(2)}) %copy-start.7) | copy-done | bytes 524312
  34.3 0.8 %copy-done.9 = bf16[2,4,128,256]{3,2,1,0:T(8,128)(2,1)} copy-done((bf16[2,4,128,256]{3,2,1,0:T(8,128)(2,1)}, bf16[2,4,128,256]{3,2,1,0:T(8,128)(2,1)S(1)}, u32[]{:S(2)}) %copy-start.9) | copy-done | bytes 524312
  35.1 1.5 %shard_map.68 = (f32[2,16,128,128]{3,2,1,0:T(8,128)S(1)}, f32[2,16,16,128]{3,2,1,0:T(8,128)S(1)}) custom-call(s32[16]{0:T(128)S(1)} %copy-done.11, s32[1]{0:T(128)} %bitcast.place_y_ref.place_ref, bf16[2,4,256,256]{3,2,1,0:T(8,128)(2,1)S(1)} %get-tuple-element.36.turned_ref, bf16[4,2,48,128]{3,2,1,0:T(8,128)(2,1)S(1)} %get-tuple-element.37.far_ref, ...), custom_call_target="tpu_custom_call" | custom-call | tf_op jit(solution)/shard_map/pallas_call | solution.py:454
  36.6 1.3 %copy-done.5 = f32[2,16,128,128]{3,2,1,0:T(8,128)} copy-done((f32[2,16,128,128]{3,2,1,0:T(8,128)}, f32[2,16,128,128]{3,2,1,0:T(8,128)S(1)}, u32[]{:S(2)}) %copy-start.5) | copy-done | bytes 2097176
  38.0 19.4 %all-to-all-done.arrived_ref = bf16[768,16,128]{2,1,0:T(8,128)(2,1)S(1)} async-done(((bf16[768,16,128]{2,1,0:T(8,128)(2,1)}), bf16[768,16,128]{2,1,0:T(8,128)(2,1)S(1)}, u32[]{:S(2)}, u32[]{:S(2)}) %all-to-all-start) | async-done | bytes 3145760 | tf_op jit(solution)/shard_map/all_to_all | solution.py:421
  57.4 0.7 %shard_map.70 = (bf16[2,16,8,128]{3,2,1,0:T(8,128)(2,1)S(1)}, bf16[2,16,8,128]{3,2,1,0:T(8,128)(2,1)S(1)}) custom-call(s32[1]{0:T(128)} %bitcast.4.me_ref, s32[1]{0:T(128)} %bitcast.1.place_ref.place_x_ref, s32[2,64]{1,0:T(2,128)S(1)} %copy-done.12, s32[2,64]{1,0:T(2,128)S(1)} %copy-done.13, bf16[768,16,128]{2,1,0:T(8,128)(2,1)S(1)} %all-to-all-done.arrived_ref, ...), custom_call_target="tpu_custom_call" | custom-call | tf_op jit(solution)/shard_map/pallas_call | solution.py:464
  58.2 0.1 collective-permute-start.4
  58.3 2.6 %collective-permute-start.5 = (bf16[2,16,8,128]{3,2,1,0:T(8,128)(2,1)S(1)}, bf16[2,16,8,128]{3,2,1,0:T(8,128)(2,1)S(1)}, u32[]{:S(2)}, u32[]{:S(2)}) collective-permute-start(bf16[2,16,8,128]{3,2,1,0:T(8,128)(2,1)S(1)} %get-tuple-element.45), channel_id=1, source_target_pairs={{16,32},{32,16},{48,64},{64,48},{80,96},{96,80},{112,0},{0,112},{1... | collective-permute-start | bytes 196616 | tf_op jit(solution)/shard_map/ppermute | solution.py:381
  60.9 1.7 %shard_map.69 = (bf16[2,16,128,128]{3,2,1,0:T(8,128)(2,1)S(1)}, bf16[2,16,16,128]{3,2,1,0:T(8,128)(2,1)S(1)}) custom-call(s32[1]{0:T(128)} %bitcast.4.me_ref, s32[2,64]{1,0:T(2,128)S(1)} %copy-done.12, s32[2,64]{1,0:T(2,128)S(1)} %copy-done.13, bf16[768,16,128]{2,1,0:T(8,128)(2,1)S(1)} %all-to-all-done.arrived_ref, f32[2,16,128,128]{3,2,1,0:T(8,128)S(1)} %copy-done.6), custom_call_target="tpu_custom_call" | custom-call | tf_op jit(solution)/shard_map/pallas_call | solution.py:471
  62.6 0.6 collective-permute-done.5.other_ref
  63.3 0.2 shard_map.72
  63.5 0.1 collective-permute-start.6
  63.6 3.9 %collective-permute-start.7 = (bf16[2,18,8,128]{3,2,1,0:T(8,128)(2,1)S(1)}, bf16[2,18,8,128]{3,2,1,0:T(8,128)(2,1)S(1)}, u32[]{:S(2)}, u32[]{:S(2)}) collective-permute-start(bf16[2,18,8,128]{3,2,1,0:T(8,128)(2,1)S(1)} %get-tuple-element.48), channel_id=1, source_target_pairs={{1,2},{2,1},{3,4},{4,3},{5,6},{6,5},{7,8},{8,7},{9,10},{10,9},{11,... | collective-permute-start | bytes 221192 | tf_op jit(solution)/shard_map/ppermute | solution.py:381
  67.5 2.3 %shard_map.71.near_ref = f32[16,128,128]{2,1,0:T(8,128)S(1)} custom-call(s32[16]{0:T(128)S(1)} %copy-done.11, s32[1]{0:T(128)} %bitcast.1.place_ref.place_x_ref, bf16[4,256,256]{2,1,0:T(8,128)(2,1)S(1)} %copy-done.8, bf16[4,32,32]{2,1,0:T(8,128)(2,1)S(1)} %get-tuple-element.33.ends_ref, bf16[2,4,128,256]{3,2,1,0:T(8,128)(2,1)S(1)} %copy-done.10, ...), custom_call_target="tpu_custom_call" | custom-call | tf_op jit(solution)/shard_map/pallas_call | solution.py:478
  69.8 1.2 %shard_map.73.near_ref = f32[16,128,128]{2,1,0:T(8,128)S(1)} custom-call(s32[16]{0:T(128)S(1)} %copy-done.11, s32[1]{0:T(128)} %bitcast.place_y_ref.place_ref, bf16[2,4,256,256]{3,2,1,0:T(8,128)(2,1)S(1)} %copy-done.4, bf16[4,2,48,128]{3,2,1,0:T(8,128)(2,1)S(1)} %get-tuple-element.31.far_ref, f32[16,128,128]{2,1,0:T(8,128)S(1)} %shard_map.71.near_ref, ...), custom_call_target="tpu_custom_call" | custom-call | tf_op jit(solution)/shard_map/pallas_call | solution.py:492
  71.0 0.4 collective-permute-done.7.cells_ref
  71.4 2.1 %shard_map.74 = f32[16,128,128]{2,1,0:T(8,128)} custom-call(s32[16]{0:T(128)S(1)} %copy-done.11, s32[1]{0:T(128)} %bitcast.place_y_ref.place_ref, bf16[2,4,256,256]{3,2,1,0:T(8,128)(2,1)S(1)} %copy-done.4, bf16[4,2,48,128]{3,2,1,0:T(8,128)(2,1)S(1)} %get-tuple-element.31.far_ref, f32[16,128,128]{2,1,0:T(8,128)S(1)} %shard_map.73.near_ref, ...), custom_call_target="tpu_custom_call" | custom-call | tf_op jit(solution)/shard_map/pallas_call | solution.py:495
  (33 shorter events, 0.2 us)
Async XLA Ops:
  0.9 5.3 %collective-permute-start.1 = (f32[16,8,128]{2,1,0:T(8,128)S(1)}, f32[16,8,128]{2,1,0:T(8,128)S(1)}, u32[]{:S(2)}, u32[]{:S(2)}) collective-permute-start(f32[16,8,128]{2,1,0:T(8,128)S(1)} %get-tuple-element.49), channel_id=1, source_target_pairs={{16,32},{32,16},{48,64},{64,48},{80,96},{96,80},{112,0},{0,112},{1... | collective-permute-start | bytes 196616 | tf_op jit(solution)/shard_map/ppermute | solution.py:381
  3.2 3.0 %collective-permute-start = (f32[16,8,128]{2,1,0:T(8,128)S(1)}, f32[16,8,128]{2,1,0:T(8,128)S(1)}, u32[]{:S(2)}, u32[]{:S(2)}) collective-permute-start(f32[16,8,128]{2,1,0:T(8,128)S(1)} %get-tuple-element.50), channel_id=1, source_target_pairs={{0,16},{16,0},{32,48},{48,32},{64,80},{80,64},{96,112},{112,96},{1... | collective-permute-start | bytes 196616 | tf_op jit(solution)/shard_map/ppermute | solution.py:382
  6.2 10.2 %copy-start.14 = (f32[2,4,2,17]{3,2,1,0:T(2,128)S(1)}, f32[2,4,2,17]{3,2,1,0:T(2,128)}, u32[]{:S(2)}) copy-start(f32[2,4,2,17]{3,2,1,0:T(2,128)} %param.8) | copy-start | bytes 3268
  6.2 14.2 %copy-start.11 = (s32[16]{0:T(128)S(1)}, s32[16]{0:T(128)}, u32[]{:S(2)}) copy-start(s32[16]{0:T(128)} %band_ref.9) | copy-start | bytes 196
  6.2 51.2 %all-to-all-start = ((bf16[768,16,128]{2,1,0:T(8,128)(2,1)}), bf16[768,16,128]{2,1,0:T(8,128)(2,1)S(1)}, u32[]{:S(2)}, u32[]{:S(2)}) async-start(bf16[768,16,128]{2,1,0:T(8,128)(2,1)} %bitcast.9), calls=%async_computation | async-start | bytes 6291456 | tf_op jit(solution)/shard_map/all_to_all | solution.py:421
  16.4 41.0 %copy-start.12 = (s32[2,64]{1,0:T(2,128)S(1)}, s32[2,64]{1,0:T(2,128)}, u32[]{:S(2)}) copy-start(s32[2,64]{1,0:T(2,128)} %shift_ref.3) | copy-start | bytes 1540
  16.4 41.0 %copy-start.13 = (s32[2,64]{1,0:T(2,128)S(1)}, s32[2,64]{1,0:T(2,128)}, u32[]{:S(2)}) copy-start(s32[2,64]{1,0:T(2,128)} %length_ref.3) | copy-start | bytes 1540
  16.9 1.2 %copy-start = (f32[16,128,128]{2,1,0:T(8,128)S(1)}, f32[16,128,128]{2,1,0:T(8,128)}, u32[]{:S(2)}) copy-start(f32[16,128,128]{2,1,0:T(8,128)} %estimate_ref.1) | copy-start | bytes 3145732
  18.6 16.4 %collective-permute-start.2 = (bf16[1,18,8,128]{3,2,1,0:T(8,128)(2,1)S(1)}, bf16[1,18,8,128]{3,2,1,0:T(8,128)(2,1)S(1)}, u32[]{:S(2)}, u32[]{:S(2)}) collective-permute-start(bf16[1,18,8,128]{3,2,1,0:T(8,128)(2,1)S(1)} %get-tuple-element.38), channel_id=1, source_target_pairs={{0,1},{1,0},{2,3},{3,2},{4,5},{5,4},{6,7},{7,6},{8,9},{9,8},{10,11... | collective-permute-start | bytes 110600 | tf_op jit(solution)/shard_map/ppermute | solution.py:382
  19.7 15.4 %collective-permute-start.3 = (bf16[1,18,8,128]{3,2,1,0:T(8,128)(2,1)S(1)}, bf16[1,18,8,128]{3,2,1,0:T(8,128)(2,1)S(1)}, u32[]{:S(2)}, u32[]{:S(2)}) collective-permute-start(bf16[1,18,8,128]{3,2,1,0:T(8,128)(2,1)S(1)} %get-tuple-element.39), channel_id=1, source_target_pairs={{1,2},{2,1},{3,4},{4,3},{5,6},{6,5},{7,8},{8,7},{9,10},{10,9},{11,... | collective-permute-start | bytes 110600 | tf_op jit(solution)/shard_map/ppermute | solution.py:381
  20.4 1.2 %copy-start.1 = (f32[16,128,128]{2,1,0:T(8,128)S(1)}, f32[16,128,128]{2,1,0:T(8,128)}, u32[]{:S(2)}) copy-start(f32[16,128,128]{2,1,0:T(8,128)} %estimate_ref.1) | copy-start | bytes 3145732
  32.5 1.0 %copy-start.3 = (bf16[2,4,256,256]{3,2,1,0:T(8,128)(2,1)}, bf16[2,4,256,256]{3,2,1,0:T(8,128)(2,1)S(1)}, u32[]{:S(2)}) copy-start(bf16[2,4,256,256]{3,2,1,0:T(8,128)(2,1)S(1)} %get-tuple-element.30.turned_ref) | copy-start | bytes 3145732
  33.5 0.8 %copy-start.7 = (bf16[4,256,256]{2,1,0:T(8,128)(2,1)}, bf16[4,256,256]{2,1,0:T(8,128)(2,1)S(1)}, u32[]{:S(2)}) copy-start(bf16[4,256,256]{2,1,0:T(8,128)(2,1)S(1)} %get-tuple-element.32.rows_ref) | copy-start | bytes 1572868
  34.3 0.8 %copy-start.9 = (bf16[2,4,128,256]{3,2,1,0:T(8,128)(2,1)}, bf16[2,4,128,256]{3,2,1,0:T(8,128)(2,1)S(1)}, u32[]{:S(2)}) copy-start(bf16[2,4,128,256]{3,2,1,0:T(8,128)(2,1)S(1)} %get-tuple-element.34.cols_ref) | copy-start | bytes 1572868
  36.6 1.4 %copy-start.5 = (f32[2,16,128,128]{3,2,1,0:T(8,128)}, f32[2,16,128,128]{3,2,1,0:T(8,128)S(1)}, u32[]{:S(2)}) copy-start(f32[2,16,128,128]{3,2,1,0:T(8,128)S(1)} %get-tuple-element.41.recip_ref) | copy-start | bytes 6291460
  57.4 3.5 %copy-start.6 = (f32[2,16,128,128]{3,2,1,0:T(8,128)S(1)}, f32[2,16,128,128]{3,2,1,0:T(8,128)}, u32[]{:S(2)}) copy-start(f32[2,16,128,128]{3,2,1,0:T(8,128)} %copy-done.5) | copy-start | bytes 6291460
  58.2 9.3 %copy-start.8 = (bf16[4,256,256]{2,1,0:T(8,128)(2,1)S(1)}, bf16[4,256,256]{2,1,0:T(8,128)(2,1)}, u32[]{:S(2)}) copy-start(bf16[4,256,256]{2,1,0:T(8,128)(2,1)} %copy-done.7) | copy-start | bytes 1572868
  58.2 9.3 %copy-start.10 = (bf16[2,4,128,256]{3,2,1,0:T(8,128)(2,1)S(1)}, bf16[2,4,128,256]{3,2,1,0:T(8,128)(2,1)}, u32[]{:S(2)}) copy-start(bf16[2,4,128,256]{3,2,1,0:T(8,128)(2,1)} %copy-done.9) | copy-start | bytes 1572868
  58.2 4.4 %collective-permute-start.4 = (bf16[2,16,8,128]{3,2,1,0:T(8,128)(2,1)S(1)}, bf16[2,16,8,128]{3,2,1,0:T(8,128)(2,1)S(1)}, u32[]{:S(2)}, u32[]{:S(2)}) collective-permute-start(bf16[2,16,8,128]{3,2,1,0:T(8,128)(2,1)S(1)} %get-tuple-element.44), channel_id=1, source_target_pairs={{0,16},{16,0},{32,48},{48,32},{64,80},{80,64},{96,112},{112,96},{1... | collective-permute-start | bytes 196616 | tf_op jit(solution)/shard_map/ppermute | solution.py:382
  58.3 5.0 %collective-permute-start.5 = (bf16[2,16,8,128]{3,2,1,0:T(8,128)(2,1)S(1)}, bf16[2,16,8,128]{3,2,1,0:T(8,128)(2,1)S(1)}, u32[]{:S(2)}, u32[]{:S(2)}) collective-permute-start(bf16[2,16,8,128]{3,2,1,0:T(8,128)(2,1)S(1)} %get-tuple-element.45), channel_id=1, source_target_pairs={{16,32},{32,16},{48,64},{64,48},{80,96},{96,80},{112,0},{0,112},{1... | collective-permute-start | bytes 196616 | tf_op jit(solution)/shard_map/ppermute | solution.py:381
  60.9 8.9 %copy-start.4 = (bf16[2,4,256,256]{3,2,1,0:T(8,128)(2,1)S(1)}, bf16[2,4,256,256]{3,2,1,0:T(8,128)(2,1)}, u32[]{:S(2)}) copy-start(bf16[2,4,256,256]{3,2,1,0:T(8,128)(2,1)} %copy-done.3) | copy-start | bytes 3145732
  63.5 6.3 %collective-permute-start.6 = (bf16[2,18,8,128]{3,2,1,0:T(8,128)(2,1)S(1)}, bf16[2,18,8,128]{3,2,1,0:T(8,128)(2,1)S(1)}, u32[]{:S(2)}, u32[]{:S(2)}) collective-permute-start(bf16[2,18,8,128]{3,2,1,0:T(8,128)(2,1)S(1)} %get-tuple-element.47), channel_id=1, source_target_pairs={{0,1},{1,0},{2,3},{3,2},{4,5},{5,4},{6,7},{7,6},{8,9},{9,8},{10,11... | collective-permute-start | bytes 221192 | tf_op jit(solution)/shard_map/ppermute | solution.py:382
  63.6 7.8 %collective-permute-start.7 = (bf16[2,18,8,128]{3,2,1,0:T(8,128)(2,1)S(1)}, bf16[2,18,8,128]{3,2,1,0:T(8,128)(2,1)S(1)}, u32[]{:S(2)}, u32[]{:S(2)}) collective-permute-start(bf16[2,18,8,128]{3,2,1,0:T(8,128)(2,1)S(1)} %get-tuple-element.48), channel_id=1, source_target_pairs={{1,2},{2,1},{3,4},{4,3},{5,6},{6,5},{7,8},{8,7},{9,10},{10,9},{11,... | collective-permute-start | bytes 221192 | tf_op jit(solution)/shard_map/ppermute | solution.py:381
  67.5 3.9 %copy-start.2 = (f32[16,128,128]{2,1,0:T(8,128)S(1)}, f32[16,128,128]{2,1,0:T(8,128)}, u32[]{:S(2)}) copy-start(f32[16,128,128]{2,1,0:T(8,128)} %estimate_ref.1) | copy-start | bytes 3145732

commit v10 on v9

--- a/solution.py
+++ b/solution.py
@@ -374,10 +374,10 @@
         copy.wait()
 
 
-def swap(first, second, axis, ring=True):
+def swap(first, second, axis, everyone=True):
     count = lax.axis_size(axis)
-    chain = lambda begin: range(begin, count if ring else count - 1, 2)
-    pairs = lambda begin: [p for i in chain(begin) for p in ((i, (i + 1) % count), ((i + 1) % count, i))]
+    ends = lambda begin: [(0, 0), (count - 1, count - 1)] if begin and everyone else []
+    pairs = lambda begin: ends(begin) + [p for i in range(begin, count - 1, 2) for p in ((i, i + 1), (i + 1, i))]
     late = lax.ppermute(second, axis, pairs(1))
     return lax.ppermute(first, axis, pairs(0)), late
 
@@ -425,7 +425,7 @@
     dense = lambda lead, *args: call(
         dense_slab_kernel, [SMEM] * 2 + [VMEM] * 3, (like((lead, tiles, HW, tile_rows), BF16),) * 2
     )(place_x, place_y, *args)
-    ey, oy = swap(*dense(1, cols[None], ex, ox), "gy", ring=False)
+    ey, oy = swap(*dense(1, cols[None], ex, ox), "gy", everyone=False)
 
     norm = kernels / jnp.sum(kernels, axis=3, keepdims=True)
     tap_rows = jnp.stack([norm, norm[..., ::-1]])
@@ -496,7 +496,7 @@
         odd_far_kernel,
         [SMEM] * 2 + [VMEM] * 5,
         like(estimate.shape, F32),
-        halves + [pltpu.VMEM(estimate.shape, F32), pltpu.SemaphoreType.DMA((4,))],
+        halves + [pltpu.VMEM(estimate.shape, F32), pltpu.SemaphoreType.DMA((depth,))],
         HBM,
     )(depth_band, place_y, turned_mat, far_mat, near, oy, estimate)
 

time: 74 us -> 77.8 us (1.051)
  the two profiles are of different devices: /device:TPU:0 before, /device:TPU:30 now
where the time goes in v10:
time: 77.8 us; the launch traced here: 77.4 us
  starting transfers between devices  24.3 us (31%)
  Pallas kernels  24.1 us (31%)
  waiting for transfers between devices  21 us (27%)
  local copies, waits for them, and re-layouts  6.51 us (8%)
  other arithmetic  1.16 us (1%)
    ppermute x4, waiting for transfers between devices, swap(): return (lax.ppermute(first, axis, pairs(0)), late)  12.5 us
    ppermute x4, starting transfers between devices, swap(): late = lax.ppermute(second, axis, pairs(1))  11.4 us
    all_to_all x1, starting transfers between devices, body(): lax.all_to_all(outgoing, ('gx', 'gy'), split_axis=0, concat_axis=0, tiled...  10.9 us
    pallas_call x1, Pallas kernels, body(): call(forward_kernel, [SMEM] * 2 + [VMEM] * 4, (like(measured.shape, F32),...  10.8 us
    ppermute x4, waiting for transfers between devices, swap(): late = lax.ppermute(second, axis, pairs(1))  8.47 us
    unnamed x30, local copies, waits for them, and re-layouts  6.41 us
    pallas_call x1, Pallas kernels, body(): call(functools.partial(pack_kernel, devices), [SMEM, HBM, HBM, HBM], like...  2.96 us
    pallas_call x1, Pallas kernels, body(): call(near_kernel, [SMEM] * 2 + [VMEM] * 6, like(estimate.shape, F32), [pl...  2.25 us
  transfers between devices with their start and end apart: 9, of which 5 were waited for; matrix products, arithmetic and copies ran while one was open for 0% of the time, Pallas kernels for 27%

profile of v10, /device:TPU:30, one launch (start us, length us, event | category | flops | bytes accessed | tf_op | source)
XLA Modules:
  0.0 77.4 jit_solution(15381878951298039781)
XLA Ops:
  0.0 0.9 %slice_select_fusion = (f32[16,8,128]{2,1,0:T(8,128)S(1)}, f32[16,8,128]{2,1,0:T(8,128)S(1)}) fusion(f32[16,128,128]{2,1,0:T(8,128)} %estimate_ref.1, pred[]{:T(512)S(6)} %eq.13), kind=kLoop, calls=%fused_computation | loop fusion | flops 32768 | bytes 262145 | tf_op jit(solution)/shard_map/jit(_where)/select_n | solution.py:404
  0.9 2.2 %collective-permute-start.1 = (f32[16,8,128]{2,1,0:T(8,128)S(1)}, f32[16,8,128]{2,1,0:T(8,128)S(1)}, u32[]{:S(2)}, u32[]{:S(2)}) collective-permute-start(f32[16,8,128]{2,1,0:T(8,128)S(1)} %get-tuple-element.49), channel_id=1, source_target_pairs={{0,0},{112,112},{16,32},{32,16},{48,64},{64,48},{80,96},{96,80},{1... | collective-permute-start | bytes 196616 | tf_op jit(solution)/shard_map/ppermute | solution.py:381
  3.2 3.0 %shard_map.64 = bf16[128,2,3,16,128]{4,3,2,1,0:T(8,128)(2,1)} custom-call(s32[1]{0:T(128)} %bitcast.4.me_ref, s32[2,64]{1,0:T(2,128)} %shift_ref.3, s32[2,64]{1,0:T(2,128)} %length_ref.3, bf16[2,16,128,128]{3,2,1,0:T(8,128)(2,1)} %measured_hbm.1), custom_call_target="tpu_custom_call" | custom-call | tf_op jit(solution)/shard_map/pallas_call | solution.py:405
  6.1 0.3 collective-permute-done.1.other_ref
  6.5 10.9 %all-to-all-start = ((bf16[768,16,128]{2,1,0:T(8,128)(2,1)}), bf16[768,16,128]{2,1,0:T(8,128)(2,1)S(1)}, u32[]{:S(2)}, u32[]{:S(2)}) async-start(bf16[768,16,128]{2,1,0:T(8,128)(2,1)} %bitcast.9), calls=%async_computation | async-start | bytes 6291456 | tf_op jit(solution)/shard_map/all_to_all | solution.py:421
  17.5 0.1 reduce_sum.9
  17.6 0.1 broadcast_divide_fusion
  17.7 0.1 rev.3
  17.9 1.2 %copy-done = f32[16,128,128]{2,1,0:T(8,128)S(1)} copy-done((f32[16,128,128]{2,1,0:T(8,128)S(1)}, f32[16,128,128]{2,1,0:T(8,128)}, u32[]{:S(2)}) %copy-start) | copy-done | bytes 1048600
  19.1 0.4 shard_map.66
  19.4 0.2 shard_map.67
  19.6 1.7 %collective-permute-start.2 = (bf16[1,18,8,128]{3,2,1,0:T(8,128)(2,1)S(1)}, bf16[1,18,8,128]{3,2,1,0:T(8,128)(2,1)S(1)}, u32[]{:S(2)}, u32[]{:S(2)}) collective-permute-start(bf16[1,18,8,128]{3,2,1,0:T(8,128)(2,1)S(1)} %get-tuple-element.38), channel_id=1, source_target_pairs={{0,1},{1,0},{2,3},{3,2},{4,5},{5,4},{6,7},{7,6},{8,9},{9,8},{10,11... | collective-permute-start | bytes 110600 | tf_op jit(solution)/shard_map/ppermute | solution.py:382
  21.4 4.5 %collective-permute-start.3 = (bf16[1,18,8,128]{3,2,1,0:T(8,128)(2,1)S(1)}, bf16[1,18,8,128]{3,2,1,0:T(8,128)(2,1)S(1)}, u32[]{:S(2)}, u32[]{:S(2)}) collective-permute-start(bf16[1,18,8,128]{3,2,1,0:T(8,128)(2,1)S(1)} %get-tuple-element.39), channel_id=1, source_target_pairs={{1,2},{2,1},{3,4},{4,3},{5,6},{6,5},{7,8},{8,7},{9,10},{10,9},{11,... | collective-permute-start | bytes 110600 | tf_op jit(solution)/shard_map/ppermute | solution.py:381
  25.9 1.2 %copy-done.1 = f32[16,128,128]{2,1,0:T(8,128)S(1)} copy-done((f32[16,128,128]{2,1,0:T(8,128)S(1)}, f32[16,128,128]{2,1,0:T(8,128)}, u32[]{:S(2)}) %copy-start.1) | copy-done | bytes 1048600
  27.1 10.8 %shard_map.65 = (f32[2,16,128,128]{3,2,1,0:T(8,128)S(1)}, bf16[2,4,256,256]{3,2,1,0:T(8,128)(2,1)S(1)}, bf16[4,2,48,128]{3,2,1,0:T(8,128)(2,1)S(1)}, bf16[4,256,...) custom-call(s32[16]{0:T(128)S(1)} %copy-done.11, ...), custom_call_target="tpu_custom_call" | custom-call | tf_op jit(solution)/shard_map/pallas_call | solution.py:435
  37.9 1.0 %copy-done.3 = bf16[2,4,256,256]{3,2,1,0:T(8,128)(2,1)} copy-done((bf16[2,4,256,256]{3,2,1,0:T(8,128)(2,1)}, bf16[2,4,256,256]{3,2,1,0:T(8,128)(2,1)S(1)}, u32[]{:S(2)}) %copy-start.3) | copy-done | bytes 1048600
  38.9 0.8 %copy-done.7 = bf16[4,256,256]{2,1,0:T(8,128)(2,1)} copy-done((bf16[4,256,256]{2,1,0:T(8,128)(2,1)}, bf16[4,256,256]{2,1,0:T(8,128)(2,1)S(1)}, u32[]{:S(2)}) %copy-start.7) | copy-done | bytes 524312
  39.7 0.8 %copy-done.9 = bf16[2,4,128,256]{3,2,1,0:T(8,128)(2,1)} copy-done((bf16[2,4,128,256]{3,2,1,0:T(8,128)(2,1)}, bf16[2,4,128,256]{3,2,1,0:T(8,128)(2,1)S(1)}, u32[]{:S(2)}) %copy-start.9) | copy-done | bytes 524312
  40.5 12.5 %collective-permute-done.2.even_ref = bf16[1,18,8,128]{3,2,1,0:T(8,128)(2,1)S(1)} collective-permute-done((bf16[1,18,8,128]{3,2,1,0:T(8,128)(2,1)S(1)}, bf16[1,18,8,128]{3,2,1,0:T(8,128)(2,1)S(1)}, u32[]{:S(2)}, u32[]{:S(2)}) %collective-permute-start.2) | collective-permute-done | bytes 36896 | tf_op jit(solution)/shard_map/ppermute | solution.py:382
  53.0 4.1 %collective-permute-done.3.other_ref = bf16[1,18,8,128]{3,2,1,0:T(8,128)(2,1)S(1)} collective-permute-done((bf16[1,18,8,128]{3,2,1,0:T(8,128)(2,1)S(1)}, bf16[1,18,8,128]{3,2,1,0:T(8,128)(2,1)S(1)}, u32[]{:S(2)}, u32[]{:S(2)}) %collective-permute-start.3) | collective-permute-done | bytes 36896 | tf_op jit(solution)/shard_map/ppermute | solution.py:381
  57.2 1.5 %shard_map.68 = (f32[2,16,128,128]{3,2,1,0:T(8,128)S(1)}, f32[2,16,16,128]{3,2,1,0:T(8,128)S(1)}) custom-call(s32[16]{0:T(128)S(1)} %copy-done.11, s32[1]{0:T(128)} %bitcast.place_y_ref.place_ref, bf16[2,4,256,256]{3,2,1,0:T(8,128)(2,1)S(1)} %get-tuple-element.36.turned_ref, bf16[4,2,48,128]{3,2,1,0:T(8,128)(2,1)S(1)} %get-tuple-element.37.far_ref, ...), custom_call_target="tpu_custom_call" | custom-call | tf_op jit(solution)/shard_map/pallas_call | solution.py:454
  58.7 1.3 %copy-done.5 = f32[2,16,128,128]{3,2,1,0:T(8,128)} copy-done((f32[2,16,128,128]{3,2,1,0:T(8,128)}, f32[2,16,128,128]{3,2,1,0:T(8,128)S(1)}, u32[]{:S(2)}) %copy-start.5) | copy-done | bytes 2097176
  60.1 0.7 shard_map.70
  60.9 2.5 %collective-permute-start.5 = (bf16[2,16,8,128]{3,2,1,0:T(8,128)(2,1)S(1)}, bf16[2,16,8,128]{3,2,1,0:T(8,128)(2,1)S(1)}, u32[]{:S(2)}, u32[]{:S(2)}) collective-permute-start(bf16[2,16,8,128]{3,2,1,0:T(8,128)(2,1)S(1)} %get-tuple-element.45), channel_id=1, source_target_pairs={{0,0},{112,112},{16,32},{32,16},{48,64},{64,48},{80,96},{96,80},{1... | collective-permute-start | bytes 196616 | tf_op jit(solution)/shard_map/ppermute | solution.py:381
  63.5 1.7 %shard_map.69 = (bf16[2,16,128,128]{3,2,1,0:T(8,128)(2,1)S(1)}, bf16[2,16,16,128]{3,2,1,0:T(8,128)(2,1)S(1)}) custom-call(s32[1]{0:T(128)} %bitcast.4.me_ref, s32[2,64]{1,0:T(2,128)S(1)} %copy-done.12, s32[2,64]{1,0:T(2,128)S(1)} %copy-done.13, bf16[768,16,128]{2,1,0:T(8,128)(2,1)S(1)} %all-to-all-done.arrived_ref, f32[2,16,128,128]{3,2,1,0:T(8,128)S(1)} %copy-done.6), custom_call_target="tpu_custom_call" | custom-call | tf_op jit(solution)/shard_map/pallas_call | solution.py:471
  65.2 1.5 %collective-permute-done.5.other_ref = bf16[2,16,8,128]{3,2,1,0:T(8,128)(2,1)S(1)} collective-permute-done((bf16[2,16,8,128]{3,2,1,0:T(8,128)(2,1)S(1)}, bf16[2,16,8,128]{3,2,1,0:T(8,128)(2,1)S(1)}, u32[]{:S(2)}, u32[]{:S(2)}) %collective-permute-start.5) | collective-permute-done | bytes 65568 | tf_op jit(solution)/shard_map/ppermute | solution.py:381
  66.7 0.2 shard_map.72
  66.9 2.3 %collective-permute-start.7 = (bf16[2,18,8,128]{3,2,1,0:T(8,128)(2,1)S(1)}, bf16[2,18,8,128]{3,2,1,0:T(8,128)(2,1)S(1)}, u32[]{:S(2)}, u32[]{:S(2)}) collective-permute-start(bf16[2,18,8,128]{3,2,1,0:T(8,128)(2,1)S(1)} %get-tuple-element.48), channel_id=1, source_target_pairs={{0,0},{15,15},{1,2},{2,1},{3,4},{4,3},{5,6},{6,5},{7,8},{8,7},{9,1... | collective-permute-start | bytes 221192 | tf_op jit(solution)/shard_map/ppermute | solution.py:381
  69.2 2.3 %shard_map.71.near_ref = f32[16,128,128]{2,1,0:T(8,128)S(1)} custom-call(s32[16]{0:T(128)S(1)} %copy-done.11, s32[1]{0:T(128)} %bitcast.1.place_ref.place_x_ref, bf16[4,256,256]{2,1,0:T(8,128)(2,1)S(1)} %copy-done.8, bf16[4,32,32]{2,1,0:T(8,128)(2,1)S(1)} %get-tuple-element.33.ends_ref, bf16[2,4,128,256]{3,2,1,0:T(8,128)(2,1)S(1)} %copy-done.10, ...), custom_call_target="tpu_custom_call" | custom-call | tf_op jit(solution)/shard_map/pallas_call | solution.py:478
  71.4 1.2 %shard_map.73.near_ref = f32[16,128,128]{2,1,0:T(8,128)S(1)} custom-call(s32[16]{0:T(128)S(1)} %copy-done.11, s32[1]{0:T(128)} %bitcast.place_y_ref.place_ref, bf16[2,4,256,256]{3,2,1,0:T(8,128)(2,1)S(1)} %copy-done.4, bf16[4,2,48,128]{3,2,1,0:T(8,128)(2,1)S(1)} %get-tuple-element.31.far_ref, f32[16,128,128]{2,1,0:T(8,128)S(1)} %shard_map.71.near_ref, ...), custom_call_target="tpu_custom_call" | custom-call | tf_op jit(solution)/shard_map/pallas_call | solution.py:492
  72.6 2.6 %collective-permute-done.7.cells_ref = bf16[2,18,8,128]{3,2,1,0:T(8,128)(2,1)S(1)} collective-permute-done((bf16[2,18,8,128]{3,2,1,0:T(8,128)(2,1)S(1)}, bf16[2,18,8,128]{3,2,1,0:T(8,128)(2,1)S(1)}, u32[]{:S(2)}, u32[]{:S(2)}) %collective-permute-start.7) | collective-permute-done | bytes 73760 | tf_op jit(solution)/shard_map/ppermute | solution.py:381
  75.2 2.2 %shard_map.74 = f32[16,128,128]{2,1,0:T(8,128)} custom-call(s32[16]{0:T(128)S(1)} %copy-done.11, s32[1]{0:T(128)} %bitcast.place_y_ref.place_ref, bf16[2,4,256,256]{3,2,1,0:T(8,128)(2,1)S(1)} %copy-done.4, bf16[4,2,48,128]{3,2,1,0:T(8,128)(2,1)S(1)} %get-tuple-element.31.far_ref, f32[16,128,128]{2,1,0:T(8,128)S(1)} %shard_map.73.near_ref, ...), custom_call_target="tpu_custom_call" | custom-call | tf_op jit(solution)/shard_map/pallas_call | solution.py:495
  (33 shorter events, 0.3 us)
Async XLA Ops:
  0.9 5.6 %collective-permute-start.1 = (f32[16,8,128]{2,1,0:T(8,128)S(1)}, f32[16,8,128]{2,1,0:T(8,128)S(1)}, u32[]{:S(2)}, u32[]{:S(2)}) collective-permute-start(f32[16,8,128]{2,1,0:T(8,128)S(1)} %get-tuple-element.49), channel_id=1, source_target_pairs={{0,0},{112,112},{16,32},{32,16},{48,64},{64,48},{80,96},{96,80},{1... | collective-permute-start | bytes 196616 | tf_op jit(solution)/shard_map/ppermute | solution.py:381
  3.1 3.4 %collective-permute-start = (f32[16,8,128]{2,1,0:T(8,128)S(1)}, f32[16,8,128]{2,1,0:T(8,128)S(1)}, u32[]{:S(2)}, u32[]{:S(2)}) collective-permute-start(f32[16,8,128]{2,1,0:T(8,128)S(1)} %get-tuple-element.50), channel_id=1, source_target_pairs={{0,16},{16,0},{32,48},{48,32},{64,80},{80,64},{96,112},{112,96},{1... | collective-permute-start | bytes 196616 | tf_op jit(solution)/shard_map/ppermute | solution.py:382
  6.5 11.0 %copy-start.14 = (f32[2,4,2,17]{3,2,1,0:T(2,128)S(1)}, f32[2,4,2,17]{3,2,1,0:T(2,128)}, u32[]{:S(2)}) copy-start(f32[2,4,2,17]{3,2,1,0:T(2,128)} %param.8) | copy-start | bytes 3268
  6.5 19.4 %copy-start.11 = (s32[16]{0:T(128)S(1)}, s32[16]{0:T(128)}, u32[]{:S(2)}) copy-start(s32[16]{0:T(128)} %band_ref.9) | copy-start | bytes 196
  6.5 53.6 %all-to-all-start = ((bf16[768,16,128]{2,1,0:T(8,128)(2,1)}), bf16[768,16,128]{2,1,0:T(8,128)(2,1)S(1)}, u32[]{:S(2)}, u32[]{:S(2)}) async-start(bf16[768,16,128]{2,1,0:T(8,128)(2,1)} %bitcast.9), calls=%async_computation | async-start | bytes 6291456 | tf_op jit(solution)/shard_map/all_to_all | solution.py:421
  17.4 42.6 %copy-start.12 = (s32[2,64]{1,0:T(2,128)S(1)}, s32[2,64]{1,0:T(2,128)}, u32[]{:S(2)}) copy-start(s32[2,64]{1,0:T(2,128)} %shift_ref.3) | copy-start | bytes 1540
  17.4 42.6 %copy-start.13 = (s32[2,64]{1,0:T(2,128)S(1)}, s32[2,64]{1,0:T(2,128)}, u32[]{:S(2)}) copy-start(s32[2,64]{1,0:T(2,128)} %length_ref.3) | copy-start | bytes 1540
  17.9 1.2 %copy-start = (f32[16,128,128]{2,1,0:T(8,128)S(1)}, f32[16,128,128]{2,1,0:T(8,128)}, u32[]{:S(2)}) copy-start(f32[16,128,128]{2,1,0:T(8,128)} %estimate_ref.1) | copy-start | bytes 3145732
  19.6 33.4 %collective-permute-start.2 = (bf16[1,18,8,128]{3,2,1,0:T(8,128)(2,1)S(1)}, bf16[1,18,8,128]{3,2,1,0:T(8,128)(2,1)S(1)}, u32[]{:S(2)}, u32[]{:S(2)}) collective-permute-start(bf16[1,18,8,128]{3,2,1,0:T(8,128)(2,1)S(1)} %get-tuple-element.38), channel_id=1, source_target_pairs={{0,1},{1,0},{2,3},{3,2},{4,5},{5,4},{6,7},{7,6},{8,9},{9,8},{10,11... | collective-permute-start | bytes 110600 | tf_op jit(solution)/shard_map/ppermute | solution.py:382
  21.4 35.8 %collective-permute-start.3 = (bf16[1,18,8,128]{3,2,1,0:T(8,128)(2,1)S(1)}, bf16[1,18,8,128]{3,2,1,0:T(8,128)(2,1)S(1)}, u32[]{:S(2)}, u32[]{:S(2)}) collective-permute-start(bf16[1,18,8,128]{3,2,1,0:T(8,128)(2,1)S(1)} %get-tuple-element.39), channel_id=1, source_target_pairs={{1,2},{2,1},{3,4},{4,3},{5,6},{6,5},{7,8},{8,7},{9,10},{10,9},{11,... | collective-permute-start | bytes 110600 | tf_op jit(solution)/shard_map/ppermute | solution.py:381
  25.9 1.2 %copy-start.1 = (f32[16,128,128]{2,1,0:T(8,128)S(1)}, f32[16,128,128]{2,1,0:T(8,128)}, u32[]{:S(2)}) copy-start(f32[16,128,128]{2,1,0:T(8,128)} %estimate_ref.1) | copy-start | bytes 3145732
  37.9 1.0 %copy-start.3 = (bf16[2,4,256,256]{3,2,1,0:T(8,128)(2,1)}, bf16[2,4,256,256]{3,2,1,0:T(8,128)(2,1)S(1)}, u32[]{:S(2)}) copy-start(bf16[2,4,256,256]{3,2,1,0:T(8,128)(2,1)S(1)} %get-tuple-element.30.turned_ref) | copy-start | bytes 3145732
  38.9 0.8 %copy-start.7 = (bf16[4,256,256]{2,1,0:T(8,128)(2,1)}, bf16[4,256,256]{2,1,0:T(8,128)(2,1)S(1)}, u32[]{:S(2)}) copy-start(bf16[4,256,256]{2,1,0:T(8,128)(2,1)S(1)} %get-tuple-element.32.rows_ref) | copy-start | bytes 1572868
  39.7 0.8 %copy-start.9 = (bf16[2,4,128,256]{3,2,1,0:T(8,128)(2,1)}, bf16[2,4,128,256]{3,2,1,0:T(8,128)(2,1)S(1)}, u32[]{:S(2)}) copy-start(bf16[2,4,128,256]{3,2,1,0:T(8,128)(2,1)S(1)} %get-tuple-element.34.cols_ref) | copy-start | bytes 1572868
  58.7 1.4 %copy-start.5 = (f32[2,16,128,128]{3,2,1,0:T(8,128)}, f32[2,16,128,128]{3,2,1,0:T(8,128)S(1)}, u32[]{:S(2)}) copy-start(f32[2,16,128,128]{3,2,1,0:T(8,128)S(1)} %get-tuple-element.41.recip_ref) | copy-start | bytes 6291460
  60.1 3.4 %copy-start.6 = (f32[2,16,128,128]{3,2,1,0:T(8,128)S(1)}, f32[2,16,128,128]{3,2,1,0:T(8,128)}, u32[]{:S(2)}) copy-start(f32[2,16,128,128]{3,2,1,0:T(8,128)} %copy-done.5) | copy-start | bytes 6291460
  60.8 8.3 %copy-start.8 = (bf16[4,256,256]{2,1,0:T(8,128)(2,1)S(1)}, bf16[4,256,256]{2,1,0:T(8,128)(2,1)}, u32[]{:S(2)}) copy-start(bf16[4,256,256]{2,1,0:T(8,128)(2,1)} %copy-done.7) | copy-start | bytes 1572868
  60.8 8.3 %copy-start.10 = (bf16[2,4,128,256]{3,2,1,0:T(8,128)(2,1)S(1)}, bf16[2,4,128,256]{3,2,1,0:T(8,128)(2,1)}, u32[]{:S(2)}) copy-start(bf16[2,4,128,256]{3,2,1,0:T(8,128)(2,1)} %copy-done.9) | copy-start | bytes 1572868
  60.8 4.4 %collective-permute-start.4 = (bf16[2,16,8,128]{3,2,1,0:T(8,128)(2,1)S(1)}, bf16[2,16,8,128]{3,2,1,0:T(8,128)(2,1)S(1)}, u32[]{:S(2)}, u32[]{:S(2)}) collective-permute-start(bf16[2,16,8,128]{3,2,1,0:T(8,128)(2,1)S(1)} %get-tuple-element.44), channel_id=1, source_target_pairs={{0,16},{16,0},{32,48},{48,32},{64,80},{80,64},{96,112},{112,96},{1... | collective-permute-start | bytes 196616 | tf_op jit(solution)/shard_map/ppermute | solution.py:382
  60.9 5.7 %collective-permute-start.5 = (bf16[2,16,8,128]{3,2,1,0:T(8,128)(2,1)S(1)}, bf16[2,16,8,128]{3,2,1,0:T(8,128)(2,1)S(1)}, u32[]{:S(2)}, u32[]{:S(2)}) collective-permute-start(bf16[2,16,8,128]{3,2,1,0:T(8,128)(2,1)S(1)} %get-tuple-element.45), channel_id=1, source_target_pairs={{0,0},{112,112},{16,32},{32,16},{48,64},{64,48},{80,96},{96,80},{1... | collective-permute-start | bytes 196616 | tf_op jit(solution)/shard_map/ppermute | solution.py:381
  63.5 7.9 %copy-start.4 = (bf16[2,4,256,256]{3,2,1,0:T(8,128)(2,1)S(1)}, bf16[2,4,256,256]{3,2,1,0:T(8,128)(2,1)}, u32[]{:S(2)}) copy-start(bf16[2,4,256,256]{3,2,1,0:T(8,128)(2,1)} %copy-done.3) | copy-start | bytes 3145732
  66.8 4.6 %collective-permute-start.6 = (bf16[2,18,8,128]{3,2,1,0:T(8,128)(2,1)S(1)}, bf16[2,18,8,128]{3,2,1,0:T(8,128)(2,1)S(1)}, u32[]{:S(2)}, u32[]{:S(2)}) collective-permute-start(bf16[2,18,8,128]{3,2,1,0:T(8,128)(2,1)S(1)} %get-tuple-element.47), channel_id=1, source_target_pairs={{0,1},{1,0},{2,3},{3,2},{4,5},{5,4},{6,7},{7,6},{8,9},{9,8},{10,11... | collective-permute-start | bytes 221192 | tf_op jit(solution)/shard_map/ppermute | solution.py:382
  66.9 8.4 %collective-permute-start.7 = (bf16[2,18,8,128]{3,2,1,0:T(8,128)(2,1)S(1)}, bf16[2,18,8,128]{3,2,1,0:T(8,128)(2,1)S(1)}, u32[]{:S(2)}, u32[]{:S(2)}) collective-permute-start(bf16[2,18,8,128]{3,2,1,0:T(8,128)(2,1)S(1)} %get-tuple-element.48), channel_id=1, source_target_pairs={{0,0},{15,15},{1,2},{2,1},{3,4},{4,3},{5,6},{6,5},{7,8},{8,7},{9,1... | collective-permute-start | bytes 221192 | tf_op jit(solution)/shard_map/ppermute | solution.py:381
  69.1 6.1 %copy-start.2 = (f32[16,128,128]{2,1,0:T(8,128)S(1)}, f32[16,128,128]{2,1,0:T(8,128)}, u32[]{:S(2)}) copy-start(f32[16,128,128]{2,1,0:T(8,128)} %estimate_ref.1) | copy-start | bytes 3145732

commit v11 on v7

--- a/solution.py
+++ b/solution.py
@@ -330,10 +330,25 @@
         copy.wait()
 
 
-def swap(first, second, axis):
+def swap(first, second, axis, everyone=True):
+    both = ("gx", "gy")
+    rows, cols = (lax.axis_size(name) for name in both)
     count = lax.axis_size(axis)
-    pairs = lambda begin: [p for i in range(begin, count, 2) for p in ((i, (i + 1) % count), ((i + 1) % count, i))]
-    return lax.ppermute(first, axis, pairs(0)), lax.ppermute(second, axis, pairs(1))
+    at = lambda p, q: p * cols + q
+    partner = lambda i, begin: begin + ((i - begin) ^ 1)
+    pairs = []
+    for begin in range(2):
+        found = []
+        for p in range(rows):
+            for q in range(cols):
+                i = partner(p if axis == "gx" else q, begin)
+                if 0 <= i < count:
+                    found.append((at(p, q), at(i, q) if axis == "gx" else at(p, i)))
+                elif everyone:
+                    found.append((at(p, q), at(rows - 1 - p, q) if axis == "gx" else at(p ^ 1, q)))
+        pairs.append(found)
+    late = lax.ppermute(second, both, pairs[1])
+    return lax.ppermute(first, both, pairs[0]), late
 
 
 def place(count, at):
@@ -371,7 +386,6 @@
         60,
     )(me, group_shift, group_length, measured)
     outgoing = outgoing.reshape(devices * views * CAP, depth, tile_cols)
-    ex, ox = (pltpu.with_memory_space_constraint(x, pltpu.HBM) for x in (ex, ox))
     outgoing, ex, ox, cells = lax.optimization_barrier((outgoing, ex, ox, estimate))
     arrived = lax.all_to_all(outgoing, ("gx", "gy"), split_axis=0, concat_axis=0, tiled=True)
 
@@ -380,7 +394,7 @@
     dense = lambda lead, *args: call(
         dense_slab_kernel, [SMEM] * 2 + [VMEM] * 3, (like((lead, tiles, HW, tile_rows), BF16),) * 2
     )(place_x, place_y, *args)
-    ey, oy = swap(*dense(1, cols[None], ex, ox), "gy")
+    ey, oy = swap(*dense(1, cols[None], ex, ox), "gy", everyone=False)
 
     norm = kernels / jnp.sum(kernels, axis=3, keepdims=True)
     tap_rows = jnp.stack([norm, norm[..., ::-1]])

time: 77.3 us -> 73.2 us (0.947)
  the two profiles are of different devices: /device:TPU:0 before, /device:TPU:30 now
where the time goes in v11:
time: 73.2 us; the launch traced here: 72 us
  Pallas kernels  23.1 us (32%)
  waiting for transfers between devices  22.1 us (30%)
  starting transfers between devices  18.8 us (26%)
  local copies, waits for them, and re-layouts  6.57 us (9%)
  other arithmetic  1.16 us (2%)
    ppermute x4, waiting for transfers between devices, swap(): return (lax.ppermute(first, both, pairs[0]), late)  14.4 us
    all_to_all x1, starting transfers between devices, body(): lax.all_to_all(outgoing, ('gx', 'gy'), split_axis=0, concat_axis=0, tiled...  10.8 us
    pallas_call x1, Pallas kernels, body(): call(forward_kernel, [SMEM] * 2 + [VMEM] * 4, (like(measured.shape, F32),...  10.8 us
    ppermute x4, waiting for transfers between devices, swap(): late = lax.ppermute(second, both, pairs[1])  7.78 us
    unnamed x30, local copies, waits for them, and re-layouts  6.47 us
    ppermute x4, starting transfers between devices, swap(): late = lax.ppermute(second, both, pairs[1])  5.81 us
    pallas_call x1, Pallas kernels, body(): call(functools.partial(pack_kernel, devices), [SMEM, HBM, HBM, HBM], like...  2.92 us
    pallas_call x1, Pallas kernels, body(): call(near_kernel, [SMEM] * 2 + [VMEM] * 6, like(estimate.shape, F32), [pl...  2.36 us
  transfers between devices with their start and end apart: 9, of which 6 were waited for; matrix products, arithmetic and copies ran while one was open for 1% of the time, Pallas kernels for 28%

profile of v11, /device:TPU:30, one launch (start us, length us, event | category | flops | bytes accessed | tf_op | source)
XLA Modules:
  0.0 72.0 jit_solution(5243657877585688771)
XLA Ops:
  0.0 0.9 %slice_select_fusion = (f32[16,8,128]{2,1,0:T(8,128)S(1)}, f32[16,8,128]{2,1,0:T(8,128)S(1)}) fusion(f32[16,128,128]{2,1,0:T(8,128)} %estimate_ref.1, pred[]{:T(512)S(6)} %eq.13), kind=kLoop, calls=%fused_computation | loop fusion | flops 32768 | bytes 262145 | tf_op jit(solution)/shard_map/jit(_where)/select_n | solution.py:373
  0.9 0.3 collective-permute-start.1
  1.2 0.3 collective-permute-start
  1.6 2.9 %shard_map.64 = bf16[128,2,3,16,128]{4,3,2,1,0:T(8,128)(2,1)} custom-call(s32[1]{0:T(128)} %bitcast.4.me_ref, s32[2,64]{1,0:T(2,128)} %shift_ref.3, s32[2,64]{1,0:T(2,128)} %length_ref.3, bf16[2,16,128,128]{3,2,1,0:T(8,128)(2,1)} %measured_hbm.1), custom_call_target="tpu_custom_call" | custom-call | tf_op jit(solution)/shard_map/pallas_call | solution.py:374
  4.5 0.2 collective-permute-done.1.other_ref
  4.7 10.8 %all-to-all-start = ((bf16[768,16,128]{2,1,0:T(8,128)(2,1)}), bf16[768,16,128]{2,1,0:T(8,128)(2,1)S(1)}, u32[]{:S(2)}, u32[]{:S(2)}) async-start(bf16[768,16,128]{2,1,0:T(8,128)(2,1)} %bitcast.9), calls=%async_computation | async-start | bytes 6291456 | tf_op jit(solution)/shard_map/all_to_all | solution.py:390
  15.6 0.1 reduce_sum.9
  15.7 0.1 rev.3
  16.0 1.2 %copy-done = f32[16,128,128]{2,1,0:T(8,128)S(1)} copy-done((f32[16,128,128]{2,1,0:T(8,128)S(1)}, f32[16,128,128]{2,1,0:T(8,128)}, u32[]{:S(2)}) %copy-start) | copy-done | bytes 1048600
  17.2 0.4 shard_map.66
  17.5 0.2 shard_map.67
  17.7 1.7 %collective-permute-start.2 = (bf16[1,18,8,128]{3,2,1,0:T(8,128)(2,1)S(1)}, bf16[1,18,8,128]{3,2,1,0:T(8,128)(2,1)S(1)}, u32[]{:S(2)}, u32[]{:S(2)}) collective-permute-start(bf16[1,18,8,128]{3,2,1,0:T(8,128)(2,1)S(1)} %get-tuple-element.38), channel_id=1, source_target_pairs={{0,1},{1,0},{2,3},{3,2},{4,5},{5,4},{6,7},{7,6},{8,9},{9,8},{10,11... | collective-permute-start | bytes 110600 | tf_op jit(solution)/shard_map/ppermute | solution.py:351
  19.5 4.5 %collective-permute-start.3 = (bf16[1,18,8,128]{3,2,1,0:T(8,128)(2,1)S(1)}, bf16[1,18,8,128]{3,2,1,0:T(8,128)(2,1)S(1)}, u32[]{:S(2)}, u32[]{:S(2)}) collective-permute-start(bf16[1,18,8,128]{3,2,1,0:T(8,128)(2,1)S(1)} %get-tuple-element.39), channel_id=1, source_target_pairs={{1,2},{2,1},{3,4},{4,3},{5,6},{6,5},{7,8},{8,7},{9,10},{10,9},{11,... | collective-permute-start | bytes 110600 | tf_op jit(solution)/shard_map/ppermute | solution.py:350
  24.0 1.2 %copy-done.1 = f32[16,128,128]{2,1,0:T(8,128)S(1)} copy-done((f32[16,128,128]{2,1,0:T(8,128)S(1)}, f32[16,128,128]{2,1,0:T(8,128)}, u32[]{:S(2)}) %copy-start.1) | copy-done | bytes 1048600
  25.2 10.8 %shard_map.65 = (f32[2,16,128,128]{3,2,1,0:T(8,128)S(1)}, bf16[2,4,256,256]{3,2,1,0:T(8,128)(2,1)S(1)}, bf16[4,2,48,128]{3,2,1,0:T(8,128)(2,1)S(1)}, bf16[4,256,...) custom-call(s32[16]{0:T(128)S(1)} %copy-done.13, ...), custom_call_target="tpu_custom_call" | custom-call | tf_op jit(solution)/shard_map/pallas_call | solution.py:404
  36.0 1.0 %copy-done.5 = bf16[2,4,256,256]{3,2,1,0:T(8,128)(2,1)} copy-done((bf16[2,4,256,256]{3,2,1,0:T(8,128)(2,1)}, bf16[2,4,256,256]{3,2,1,0:T(8,128)(2,1)S(1)}, u32[]{:S(2)}) %copy-start.5) | copy-done | bytes 1048600
  37.0 0.8 %copy-done.7 = bf16[4,256,256]{2,1,0:T(8,128)(2,1)} copy-done((bf16[4,256,256]{2,1,0:T(8,128)(2,1)}, bf16[4,256,256]{2,1,0:T(8,128)(2,1)S(1)}, u32[]{:S(2)}) %copy-start.7) | copy-done | bytes 524312
  37.8 0.8 %copy-done.9 = bf16[2,4,128,256]{3,2,1,0:T(8,128)(2,1)} copy-done((bf16[2,4,128,256]{3,2,1,0:T(8,128)(2,1)}, bf16[2,4,128,256]{3,2,1,0:T(8,128)(2,1)S(1)}, u32[]{:S(2)}) %copy-start.9) | copy-done | bytes 524312
  38.6 12.5 %collective-permute-done.2.even_ref = bf16[1,18,8,128]{3,2,1,0:T(8,128)(2,1)S(1)} collective-permute-done((bf16[1,18,8,128]{3,2,1,0:T(8,128)(2,1)S(1)}, bf16[1,18,8,128]{3,2,1,0:T(8,128)(2,1)S(1)}, u32[]{:S(2)}, u32[]{:S(2)}) %collective-permute-start.2) | collective-permute-done | bytes 36896 | tf_op jit(solution)/shard_map/ppermute | solution.py:351
  51.1 4.1 %collective-permute-done.3.other_ref = bf16[1,18,8,128]{3,2,1,0:T(8,128)(2,1)S(1)} collective-permute-done((bf16[1,18,8,128]{3,2,1,0:T(8,128)(2,1)S(1)}, bf16[1,18,8,128]{3,2,1,0:T(8,128)(2,1)S(1)}, u32[]{:S(2)}, u32[]{:S(2)}) %collective-permute-start.3) | collective-permute-done | bytes 36896 | tf_op jit(solution)/shard_map/ppermute | solution.py:350
  55.3 1.5 %shard_map.68 = (f32[2,16,128,128]{3,2,1,0:T(8,128)S(1)}, f32[2,16,16,128]{3,2,1,0:T(8,128)S(1)}) custom-call(s32[16]{0:T(128)S(1)} %copy-done.13, s32[1]{0:T(128)} %bitcast.place_y_ref.place_ref, bf16[2,4,256,256]{3,2,1,0:T(8,128)(2,1)S(1)} %get-tuple-element.36.turned_ref, bf16[4,2,48,128]{3,2,1,0:T(8,128)(2,1)S(1)} %get-tuple-element.37.far_ref, ...), custom_call_target="tpu_custom_call" | custom-call | tf_op jit(solution)/shard_map/pallas_call | solution.py:423
  56.8 1.3 %copy-done.3 = f32[2,16,128,128]{3,2,1,0:T(8,128)} copy-done((f32[2,16,128,128]{3,2,1,0:T(8,128)}, f32[2,16,128,128]{3,2,1,0:T(8,128)S(1)}, u32[]{:S(2)}) %copy-start.3) | copy-done | bytes 2097176
  58.2 0.7 %shard_map.70 = (bf16[2,16,8,128]{3,2,1,0:T(8,128)(2,1)S(1)}, bf16[2,16,8,128]{3,2,1,0:T(8,128)(2,1)S(1)}) custom-call(s32[1]{0:T(128)} %bitcast.4.me_ref, s32[1]{0:T(128)} %bitcast.1.place_ref.place_x_ref, s32[2,64]{1,0:T(2,128)S(1)} %copy-done.11, s32[2,64]{1,0:T(2,128)S(1)} %copy-done.12, bf16[768,16,128]{2,1,0:T(8,128)(2,1)S(1)} %all-to-all-done.arrived_ref, ...), custom_call_target="tpu_custom_call" | custom-call | tf_op jit(solution)/shard_map/pallas_call | solution.py:433
  59.0 0.6 collective-permute-start.5
  59.8 1.7 %shard_map.69 = (bf16[2,16,128,128]{3,2,1,0:T(8,128)(2,1)S(1)}, bf16[2,16,16,128]{3,2,1,0:T(8,128)(2,1)S(1)}) custom-call(s32[1]{0:T(128)} %bitcast.4.me_ref, s32[2,64]{1,0:T(2,128)S(1)} %copy-done.11, s32[2,64]{1,0:T(2,128)S(1)} %copy-done.12, bf16[768,16,128]{2,1,0:T(8,128)(2,1)S(1)} %all-to-all-done.arrived_ref, f32[2,16,128,128]{3,2,1,0:T(8,128)S(1)} %copy-done.4), custom_call_target="tpu_custom_call" | custom-call | tf_op jit(solution)/shard_map/pallas_call | solution.py:440
  61.5 1.3 %collective-permute-done.5.other_ref = bf16[2,16,8,128]{3,2,1,0:T(8,128)(2,1)S(1)} collective-permute-done((bf16[2,16,8,128]{3,2,1,0:T(8,128)(2,1)S(1)}, bf16[2,16,8,128]{3,2,1,0:T(8,128)(2,1)S(1)}, u32[]{:S(2)}, u32[]{:S(2)}) %collective-permute-start.5) | collective-permute-done | bytes 65568 | tf_op jit(solution)/shard_map/ppermute | solution.py:350
  62.8 0.2 shard_map.72
  63.0 0.4 collective-permute-start.7
  63.4 2.4 %shard_map.71.near_ref = f32[16,128,128]{2,1,0:T(8,128)S(1)} custom-call(s32[16]{0:T(128)S(1)} %copy-done.13, s32[1]{0:T(128)} %bitcast.1.place_ref.place_x_ref, bf16[4,256,256]{2,1,0:T(8,128)(2,1)S(1)} %copy-done.8, bf16[4,32,32]{2,1,0:T(8,128)(2,1)S(1)} %get-tuple-element.33.ends_ref, bf16[2,4,128,256]{3,2,1,0:T(8,128)(2,1)S(1)} %copy-done.10, ...), custom_call_target="tpu_custom_call" | custom-call | tf_op jit(solution)/shard_map/pallas_call | solution.py:447
  65.7 1.8 %collective-permute-done.6.even_ref = bf16[2,18,8,128]{3,2,1,0:T(8,128)(2,1)S(1)} collective-permute-done((bf16[2,18,8,128]{3,2,1,0:T(8,128)(2,1)S(1)}, bf16[2,18,8,128]{3,2,1,0:T(8,128)(2,1)S(1)}, u32[]{:S(2)}, u32[]{:S(2)}) %collective-permute-start.6) | collective-permute-done | bytes 73760 | tf_op jit(solution)/shard_map/ppermute | solution.py:351
  67.5 2.2 %collective-permute-done.7.other_ref = bf16[2,18,8,128]{3,2,1,0:T(8,128)(2,1)S(1)} collective-permute-done((bf16[2,18,8,128]{3,2,1,0:T(8,128)(2,1)S(1)}, bf16[2,18,8,128]{3,2,1,0:T(8,128)(2,1)S(1)}, u32[]{:S(2)}, u32[]{:S(2)}) %collective-permute-start.7) | collective-permute-done | bytes 73760 | tf_op jit(solution)/shard_map/ppermute | solution.py:350
  69.7 2.2 %shard_map.73 = f32[16,128,128]{2,1,0:T(8,128)} custom-call(s32[16]{0:T(128)S(1)} %copy-done.13, s32[1]{0:T(128)} %bitcast.place_y_ref.place_ref, bf16[2,4,256,256]{3,2,1,0:T(8,128)(2,1)S(1)} %copy-done.6, bf16[4,2,48,128]{3,2,1,0:T(8,128)(2,1)S(1)} %get-tuple-element.31.far_ref, f32[16,128,128]{2,1,0:T(8,128)S(1)} %shard_map.71.near_ref, ...), custom_call_target="tpu_custom_call" | custom-call | tf_op jit(solution)/shard_map/pallas_call | solution.py:456
  (32 shorter events, 0.4 us)
Async XLA Ops:
  0.9 3.8 %collective-permute-start.1 = (f32[16,8,128]{2,1,0:T(8,128)S(1)}, f32[16,8,128]{2,1,0:T(8,128)S(1)}, u32[]{:S(2)}, u32[]{:S(2)}) collective-permute-start(f32[16,8,128]{2,1,0:T(8,128)S(1)} %get-tuple-element.49), channel_id=1, source_target_pairs={{0,112},{1,113},{2,114},{3,115},{4,116},{5,117},{6,118},{7,119},{8... | collective-permute-start | bytes 196616 | tf_op jit(solution)/shard_map/ppermute | solution.py:350
  1.2 3.4 %collective-permute-start = (f32[16,8,128]{2,1,0:T(8,128)S(1)}, f32[16,8,128]{2,1,0:T(8,128)S(1)}, u32[]{:S(2)}, u32[]{:S(2)}) collective-permute-start(f32[16,8,128]{2,1,0:T(8,128)S(1)} %get-tuple-element.50), channel_id=1, source_target_pairs={{0,16},{1,17},{2,18},{3,19},{4,20},{5,21},{6,22},{7,23},{8,24},{9,... | collective-permute-start | bytes 196616 | tf_op jit(solution)/shard_map/ppermute | solution.py:351
  4.7 10.9 %copy-start.14 = (f32[2,4,2,17]{3,2,1,0:T(2,128)S(1)}, f32[2,4,2,17]{3,2,1,0:T(2,128)}, u32[]{:S(2)}) copy-start(f32[2,4,2,17]{3,2,1,0:T(2,128)} %param.8) | copy-start | bytes 3268
  4.7 19.3 %copy-start.13 = (s32[16]{0:T(128)S(1)}, s32[16]{0:T(128)}, u32[]{:S(2)}) copy-start(s32[16]{0:T(128)} %band_ref.7) | copy-start | bytes 196
  4.7 53.5 %all-to-all-start = ((bf16[768,16,128]{2,1,0:T(8,128)(2,1)}), bf16[768,16,128]{2,1,0:T(8,128)(2,1)S(1)}, u32[]{:S(2)}, u32[]{:S(2)}) async-start(bf16[768,16,128]{2,1,0:T(8,128)(2,1)} %bitcast.9), calls=%async_computation | async-start | bytes 6291456 | tf_op jit(solution)/shard_map/all_to_all | solution.py:390
  15.5 42.6 %copy-start.11 = (s32[2,64]{1,0:T(2,128)S(1)}, s32[2,64]{1,0:T(2,128)}, u32[]{:S(2)}) copy-start(s32[2,64]{1,0:T(2,128)} %shift_ref.3) | copy-start | bytes 1540
  15.5 42.6 %copy-start.12 = (s32[2,64]{1,0:T(2,128)S(1)}, s32[2,64]{1,0:T(2,128)}, u32[]{:S(2)}) copy-start(s32[2,64]{1,0:T(2,128)} %length_ref.3) | copy-start | bytes 1540
  15.9 1.2 %copy-start = (f32[16,128,128]{2,1,0:T(8,128)S(1)}, f32[16,128,128]{2,1,0:T(8,128)}, u32[]{:S(2)}) copy-start(f32[16,128,128]{2,1,0:T(8,128)} %estimate_ref.1) | copy-start | bytes 3145732
  17.7 33.4 %collective-permute-start.2 = (bf16[1,18,8,128]{3,2,1,0:T(8,128)(2,1)S(1)}, bf16[1,18,8,128]{3,2,1,0:T(8,128)(2,1)S(1)}, u32[]{:S(2)}, u32[]{:S(2)}) collective-permute-start(bf16[1,18,8,128]{3,2,1,0:T(8,128)(2,1)S(1)} %get-tuple-element.38), channel_id=1, source_target_pairs={{0,1},{1,0},{2,3},{3,2},{4,5},{5,4},{6,7},{7,6},{8,9},{9,8},{10,11... | collective-permute-start | bytes 110600 | tf_op jit(solution)/shard_map/ppermute | solution.py:351
  19.5 35.8 %collective-permute-start.3 = (bf16[1,18,8,128]{3,2,1,0:T(8,128)(2,1)S(1)}, bf16[1,18,8,128]{3,2,1,0:T(8,128)(2,1)S(1)}, u32[]{:S(2)}, u32[]{:S(2)}) collective-permute-start(bf16[1,18,8,128]{3,2,1,0:T(8,128)(2,1)S(1)} %get-tuple-element.39), channel_id=1, source_target_pairs={{1,2},{2,1},{3,4},{4,3},{5,6},{6,5},{7,8},{8,7},{9,10},{10,9},{11,... | collective-permute-start | bytes 110600 | tf_op jit(solution)/shard_map/ppermute | solution.py:350
  24.0 1.2 %copy-start.1 = (f32[16,128,128]{2,1,0:T(8,128)S(1)}, f32[16,128,128]{2,1,0:T(8,128)}, u32[]{:S(2)}) copy-start(f32[16,128,128]{2,1,0:T(8,128)} %estimate_ref.1) | copy-start | bytes 3145732
  36.0 1.0 %copy-start.5 = (bf16[2,4,256,256]{3,2,1,0:T(8,128)(2,1)}, bf16[2,4,256,256]{3,2,1,0:T(8,128)(2,1)S(1)}, u32[]{:S(2)}) copy-start(bf16[2,4,256,256]{3,2,1,0:T(8,128)(2,1)S(1)} %get-tuple-element.30.turned_ref) | copy-start | bytes 3145732
  37.0 0.8 %copy-start.7 = (bf16[4,256,256]{2,1,0:T(8,128)(2,1)}, bf16[4,256,256]{2,1,0:T(8,128)(2,1)S(1)}, u32[]{:S(2)}) copy-start(bf16[4,256,256]{2,1,0:T(8,128)(2,1)S(1)} %get-tuple-element.32.rows_ref) | copy-start | bytes 1572868
  37.8 0.8 %copy-start.9 = (bf16[2,4,128,256]{3,2,1,0:T(8,128)(2,1)}, bf16[2,4,128,256]{3,2,1,0:T(8,128)(2,1)S(1)}, u32[]{:S(2)}) copy-start(bf16[2,4,128,256]{3,2,1,0:T(8,128)(2,1)S(1)} %get-tuple-element.34.cols_ref) | copy-start | bytes 1572868
  56.8 1.4 %copy-start.3 = (f32[2,16,128,128]{3,2,1,0:T(8,128)}, f32[2,16,128,128]{3,2,1,0:T(8,128)S(1)}, u32[]{:S(2)}) copy-start(f32[2,16,128,128]{3,2,1,0:T(8,128)S(1)} %get-tuple-element.41.recip_ref) | copy-start | bytes 6291460
  58.2 1.6 %copy-start.4 = (f32[2,16,128,128]{3,2,1,0:T(8,128)S(1)}, f32[2,16,128,128]{3,2,1,0:T(8,128)}, u32[]{:S(2)}) copy-start(f32[2,16,128,128]{3,2,1,0:T(8,128)} %copy-done.3) | copy-start | bytes 6291460
  58.9 4.4 %copy-start.8 = (bf16[4,256,256]{2,1,0:T(8,128)(2,1)S(1)}, bf16[4,256,256]{2,1,0:T(8,128)(2,1)}, u32[]{:S(2)}) copy-start(bf16[4,256,256]{2,1,0:T(8,128)(2,1)} %copy-done.7) | copy-start | bytes 1572868
  58.9 4.4 %copy-start.10 = (bf16[2,4,128,256]{3,2,1,0:T(8,128)(2,1)S(1)}, bf16[2,4,128,256]{3,2,1,0:T(8,128)(2,1)}, u32[]{:S(2)}) copy-start(bf16[2,4,128,256]{3,2,1,0:T(8,128)(2,1)} %copy-done.9) | copy-start | bytes 1572868
  58.9 2.6 %collective-permute-start.4 = (bf16[2,16,8,128]{3,2,1,0:T(8,128)(2,1)S(1)}, bf16[2,16,8,128]{3,2,1,0:T(8,128)(2,1)S(1)}, u32[]{:S(2)}, u32[]{:S(2)}) collective-permute-start(bf16[2,16,8,128]{3,2,1,0:T(8,128)(2,1)S(1)} %get-tuple-element.44), channel_id=1, source_target_pairs={{0,16},{1,17},{2,18},{3,19},{4,20},{5,21},{6,22},{7,23},{8,24},{9,... | collective-permute-start | bytes 196616 | tf_op jit(solution)/shard_map/ppermute | solution.py:351
  59.0 3.8 %collective-permute-start.5 = (bf16[2,16,8,128]{3,2,1,0:T(8,128)(2,1)S(1)}, bf16[2,16,8,128]{3,2,1,0:T(8,128)(2,1)S(1)}, u32[]{:S(2)}, u32[]{:S(2)}) collective-permute-start(bf16[2,16,8,128]{3,2,1,0:T(8,128)(2,1)S(1)} %get-tuple-element.45), channel_id=1, source_target_pairs={{0,112},{1,113},{2,114},{3,115},{4,116},{5,117},{6,118},{7,119},{8... | collective-permute-start | bytes 196616 | tf_op jit(solution)/shard_map/ppermute | solution.py:350
  59.8 10.0 %copy-start.2 = (f32[16,128,128]{2,1,0:T(8,128)S(1)}, f32[16,128,128]{2,1,0:T(8,128)}, u32[]{:S(2)}) copy-start(f32[16,128,128]{2,1,0:T(8,128)} %estimate_ref.1) | copy-start | bytes 3145732
  59.8 10.0 %copy-start.6 = (bf16[2,4,256,256]{3,2,1,0:T(8,128)(2,1)S(1)}, bf16[2,4,256,256]{3,2,1,0:T(8,128)(2,1)}, u32[]{:S(2)}) copy-start(bf16[2,4,256,256]{3,2,1,0:T(8,128)(2,1)} %copy-done.5) | copy-start | bytes 3145732
  63.0 4.5 %collective-permute-start.6 = (bf16[2,18,8,128]{3,2,1,0:T(8,128)(2,1)S(1)}, bf16[2,18,8,128]{3,2,1,0:T(8,128)(2,1)S(1)}, u32[]{:S(2)}, u32[]{:S(2)}) collective-permute-start(bf16[2,18,8,128]{3,2,1,0:T(8,128)(2,1)S(1)} %get-tuple-element.47), channel_id=1, source_target_pairs={{0,1},{1,0},{2,3},{3,2},{4,5},{5,4},{6,7},{7,6},{8,9},{9,8},{10,11... | collective-permute-start | bytes 221192 | tf_op jit(solution)/shard_map/ppermute | solution.py:351
  63.0 6.7 %collective-permute-start.7 = (bf16[2,18,8,128]{3,2,1,0:T(8,128)(2,1)S(1)}, bf16[2,18,8,128]{3,2,1,0:T(8,128)(2,1)S(1)}, u32[]{:S(2)}, u32[]{:S(2)}) collective-permute-start(bf16[2,18,8,128]{3,2,1,0:T(8,128)(2,1)S(1)} %get-tuple-element.48), channel_id=1, source_target_pairs={{0,16},{1,2},{2,1},{3,4},{4,3},{5,6},{6,5},{7,8},{8,7},{9,10},{10,... | collective-permute-start | bytes 221192 | tf_op jit(solution)/shard_map/ppermute | solution.py:350

commit v12 on v11

--- a/solution.py
+++ b/solution.py
@@ -165,7 +165,7 @@
         second_ref[view] = jnp.where(odd, tail, head).astype(BF16)
 
 
-def unpack_kernel(devices, me_ref, shift_ref, length_ref, arrived_ref, recip_ref, out_ref, cols_ref, rows_ref):
+def unpack_kernel(devices, me_ref, shift_ref, length_ref, arrived_ref, forward_ref, out_ref, cols_ref, rows_ref):
     views, depth, tile_rows, tile_cols = out_ref.shape
     groups = shift_ref.shape[1]
     me = me_ref[0]
@@ -182,7 +182,8 @@
         lax.fori_loop(0, groups, group, 0, unroll=True)
         for r0 in range(0, tile_rows, 16):
             x = jnp.transpose(rows_ref[view, r0 : r0 + 16], (1, 0, 2))
-            out_ref[view, :, r0 : r0 + 16, :] = (x * recip_ref[view, :, r0 : r0 + 16, :]).astype(BF16)
+            forward = forward_ref[view, :, r0 : r0 + 16, :].astype(F32)
+            out_ref[view, :, r0 : r0 + 16, :] = (x / forward).astype(BF16)
         for z in range(depth):
             cols_ref[view, z] = dot(pick, out_ref[view, z], NT).astype(BF16)
 
@@ -264,7 +265,7 @@
     lax.fori_loop(0, depth, plane, 0, unroll=2)
 
 
-def recip_kernel(
+def late_kernel(
     band_ref, place_ref, turned_ref, far_ref, even_ref, other_ref, blurred_ref, out_ref, edge_ref, slab_ref, along_ref
 ):
     views, depth, tile_rows, tile_cols = blurred_ref.shape
@@ -275,8 +276,9 @@
             b = band_ref[z]
             along = jnp.concatenate(far_parts(along_ref, view, b, z), axis=0)
             blurred = blurred_ref[view, z] + dot(along, far_ref[b, view], ((0,), (0,)))
-            recip = 1.0 / blurred.astype(BF16).astype(F32)
-            out_ref[view, z] = recip
+            blurred = blurred.astype(BF16)
+            out_ref[view, z] = blurred
+            recip = 1.0 / blurred.astype(F32)
             edge_ref[view, z, :HW] = recip[:HW]
             edge_ref[view, z, HW:] = recip[tile_rows - HW :]
 
@@ -345,7 +347,7 @@
                 if 0 <= i < count:
                     found.append((at(p, q), at(i, q) if axis == "gx" else at(p, i)))
                 elif everyone:
-                    found.append((at(p, q), at(rows - 1 - p, q) if axis == "gx" else at(p ^ 1, q)))
+                    found.append((at(p, q), at(p, q ^ 1) if axis == "gx" else at(p ^ 1, q)))
         pairs.append(found)
     late = lax.ppermute(second, both, pairs[1])
     return lax.ppermute(first, both, pairs[0]), late
@@ -420,10 +422,10 @@
         ],
     )(depth_band, place_x, tap_rows, cells, ex, ox)
 
-    recip, edge_recip = call(
-        recip_kernel,
+    forward, edge_recip = call(
+        late_kernel,
         [SMEM] * 2 + [VMEM] * 5,
-        (like(measured.shape, F32), like((views, depth, 2 * HW, tile_cols), F32)),
+        (whole, like((views, depth, 2 * HW, tile_cols), F32)),
         [
             pltpu.VMEM((depth * 2 * HW, 2 * tile_rows), BF16),
             pltpu.VMEM((views, bands, 2, depth * 2 * HW, tile_rows), BF16),
@@ -442,7 +444,7 @@
         [SMEM] * 3 + [VMEM] * 2,
         (whole, edge_cols),
         [pltpu.VMEM((views, spare, depth, tile_cols), F32)],
-    )(me, group_shift, group_length, arrived, recip)
+    )(me, group_shift, group_length, arrived, forward)
     ey, oy = swap(*dense(views, cols, ex, ox), "gy")
     near = call(
         near_kernel,

time: 73.2 us -> 71.7 us (0.980); the launches traced: 72 us -> 71.3 us
    ppermute x4, starting transfers between devices: 2.15 us -> 3.03 us  [swap(): return (lax.ppermute(first, both, pairs[0]), late)]
    all_to_all x1, starting transfers between devices: 10.8 us -> 10.1 us  [body(): lax.all_to_all(outgoing, ('gx', 'gy'), split_axis=0, concat_axis=0, tiled...]
  transfers between devices with their start and end apart: 9 -> 9, of which waited for: 6 -> 5; matrix products, arithmetic and copies ran while one was open for 1% -> 1% of each run, Pallas kernels for 28% -> 28%
where the time goes in v12:
time: 71.7 us; the launch traced here: 71.3 us
  Pallas kernels  23.1 us (32%)
  waiting for transfers between devices  21.7 us (30%)
  starting transfers between devices  18.9 us (26%)
  local copies, waits for them, and re-layouts  6.11 us (9%)
  other arithmetic  1.16 us (2%)
    ppermute x4, waiting for transfers between devices, swap(): return (lax.ppermute(first, both, pairs[0]), late)  14.2 us
    pallas_call x1, Pallas kernels, body(): call(forward_kernel, [SMEM] * 2 + [VMEM] * 4, (like(measured.shape, F32),...  10.8 us
    all_to_all x1, starting transfers between devices, body(): lax.all_to_all(outgoing, ('gx', 'gy'), split_axis=0, concat_axis=0, tiled...  10.1 us
    ppermute x4, waiting for transfers between devices, swap(): late = lax.ppermute(second, both, pairs[1])  7.55 us
    unnamed x30, local copies, waits for them, and re-layouts  6.01 us
    ppermute x4, starting transfers between devices, swap(): late = lax.ppermute(second, both, pairs[1])  5.82 us
    ppermute x4, starting transfers between devices, swap(): return (lax.ppermute(first, both, pairs[0]), late)  3.03 us
    pallas_call x1, Pallas kernels, body(): call(functools.partial(pack_kernel, devices), [SMEM, HBM, HBM, HBM], like...  2.91 us
  transfers between devices with their start and end apart: 9, of which 5 were waited for; matrix products, arithmetic and copies ran while one was open for 1% of the time, Pallas kernels for 28%

profile of v12, /device:TPU:30, one launch (start us, length us, event | category | flops | bytes accessed | tf_op | source)
XLA Modules:
  0.0 71.3 jit_solution(831736095584369936)
XLA Ops:
  0.0 0.9 %slice_select_fusion = (f32[16,8,128]{2,1,0:T(8,128)S(1)}, f32[16,8,128]{2,1,0:T(8,128)S(1)}) fusion(f32[16,128,128]{2,1,0:T(8,128)} %estimate_ref.1, pred[]{:T(512)S(6)} %eq.13), kind=kLoop, calls=%fused_computation | loop fusion | flops 32768 | bytes 262145 | tf_op jit(solution)/shard_map/jit(_where)/select_n | solution.py:375
  0.9 0.3 collective-permute-start.1
  1.2 1.2 %collective-permute-start = (f32[16,8,128]{2,1,0:T(8,128)S(1)}, f32[16,8,128]{2,1,0:T(8,128)S(1)}, u32[]{:S(2)}, u32[]{:S(2)}) collective-permute-start(f32[16,8,128]{2,1,0:T(8,128)S(1)} %get-tuple-element.50), channel_id=1, source_target_pairs={{0,16},{1,17},{2,18},{3,19},{4,20},{5,21},{6,22},{7,23},{8,24},{9,... | collective-permute-start | bytes 196616 | tf_op jit(solution)/shard_map/ppermute | solution.py:353
  2.4 2.9 %shard_map.64 = bf16[128,2,3,16,128]{4,3,2,1,0:T(8,128)(2,1)} custom-call(s32[1]{0:T(128)} %bitcast.4.me_ref, s32[2,64]{1,0:T(2,128)} %shift_ref.3, s32[2,64]{1,0:T(2,128)} %length_ref.3, bf16[2,16,128,128]{3,2,1,0:T(8,128)(2,1)} %measured_hbm.1), custom_call_target="tpu_custom_call" | custom-call | tf_op jit(solution)/shard_map/pallas_call | solution.py:376
  5.4 10.1 %all-to-all-start = ((bf16[768,16,128]{2,1,0:T(8,128)(2,1)}), bf16[768,16,128]{2,1,0:T(8,128)(2,1)S(1)}, u32[]{:S(2)}, u32[]{:S(2)}) async-start(bf16[768,16,128]{2,1,0:T(8,128)(2,1)} %bitcast.9), calls=%async_computation | async-start | bytes 6291456 | tf_op jit(solution)/shard_map/all_to_all | solution.py:392
  15.5 0.1 reduce_sum.9
  15.6 0.1 broadcast_divide_fusion
  15.7 0.1 rev.3
  15.9 1.2 %copy-done = f32[16,128,128]{2,1,0:T(8,128)S(1)} copy-done((f32[16,128,128]{2,1,0:T(8,128)S(1)}, f32[16,128,128]{2,1,0:T(8,128)}, u32[]{:S(2)}) %copy-start) | copy-done | bytes 1048600
  17.2 0.4 shard_map.66
  17.5 0.2 shard_map.67
  17.7 1.7 %collective-permute-start.2 = (bf16[1,18,8,128]{3,2,1,0:T(8,128)(2,1)S(1)}, bf16[1,18,8,128]{3,2,1,0:T(8,128)(2,1)S(1)}, u32[]{:S(2)}, u32[]{:S(2)}) collective-permute-start(bf16[1,18,8,128]{3,2,1,0:T(8,128)(2,1)S(1)} %get-tuple-element.38), channel_id=1, source_target_pairs={{0,1},{1,0},{2,3},{3,2},{4,5},{5,4},{6,7},{7,6},{8,9},{9,8},{10,11... | collective-permute-start | bytes 110600 | tf_op jit(solution)/shard_map/ppermute | solution.py:353
  19.4 4.5 %collective-permute-start.3 = (bf16[1,18,8,128]{3,2,1,0:T(8,128)(2,1)S(1)}, bf16[1,18,8,128]{3,2,1,0:T(8,128)(2,1)S(1)}, u32[]{:S(2)}, u32[]{:S(2)}) collective-permute-start(bf16[1,18,8,128]{3,2,1,0:T(8,128)(2,1)S(1)} %get-tuple-element.39), channel_id=1, source_target_pairs={{1,2},{2,1},{3,4},{4,3},{5,6},{6,5},{7,8},{8,7},{9,10},{10,9},{11,... | collective-permute-start | bytes 110600 | tf_op jit(solution)/shard_map/ppermute | solution.py:352
  24.0 1.2 %copy-done.1 = f32[16,128,128]{2,1,0:T(8,128)S(1)} copy-done((f32[16,128,128]{2,1,0:T(8,128)S(1)}, f32[16,128,128]{2,1,0:T(8,128)}, u32[]{:S(2)}) %copy-start.1) | copy-done | bytes 1048600
  25.2 10.8 %shard_map.65 = (f32[2,16,128,128]{3,2,1,0:T(8,128)S(1)}, bf16[2,4,256,256]{3,2,1,0:T(8,128)(2,1)S(1)}, bf16[4,2,48,128]{3,2,1,0:T(8,128)(2,1)S(1)}, bf16[4,256,...) custom-call(s32[16]{0:T(128)S(1)} %copy-done.13, ...), custom_call_target="tpu_custom_call" | custom-call | tf_op jit(solution)/shard_map/pallas_call | solution.py:406
  36.0 1.0 %copy-done.3 = bf16[2,4,256,256]{3,2,1,0:T(8,128)(2,1)} copy-done((bf16[2,4,256,256]{3,2,1,0:T(8,128)(2,1)}, bf16[2,4,256,256]{3,2,1,0:T(8,128)(2,1)S(1)}, u32[]{:S(2)}) %copy-start.3) | copy-done | bytes 1048600
  37.0 0.8 %copy-done.7 = bf16[4,256,256]{2,1,0:T(8,128)(2,1)} copy-done((bf16[4,256,256]{2,1,0:T(8,128)(2,1)}, bf16[4,256,256]{2,1,0:T(8,128)(2,1)S(1)}, u32[]{:S(2)}) %copy-start.7) | copy-done | bytes 524312
  37.8 0.8 %copy-done.9 = bf16[2,4,128,256]{3,2,1,0:T(8,128)(2,1)} copy-done((bf16[2,4,128,256]{3,2,1,0:T(8,128)(2,1)}, bf16[2,4,128,256]{3,2,1,0:T(8,128)(2,1)S(1)}, u32[]{:S(2)}) %copy-start.9) | copy-done | bytes 524312
  38.6 12.5 %collective-permute-done.2.even_ref = bf16[1,18,8,128]{3,2,1,0:T(8,128)(2,1)S(1)} collective-permute-done((bf16[1,18,8,128]{3,2,1,0:T(8,128)(2,1)S(1)}, bf16[1,18,8,128]{3,2,1,0:T(8,128)(2,1)S(1)}, u32[]{:S(2)}, u32[]{:S(2)}) %collective-permute-start.2) | collective-permute-done | bytes 36896 | tf_op jit(solution)/shard_map/ppermute | solution.py:353
  51.1 4.1 %collective-permute-done.3.other_ref = bf16[1,18,8,128]{3,2,1,0:T(8,128)(2,1)S(1)} collective-permute-done((bf16[1,18,8,128]{3,2,1,0:T(8,128)(2,1)S(1)}, bf16[1,18,8,128]{3,2,1,0:T(8,128)(2,1)S(1)}, u32[]{:S(2)}, u32[]{:S(2)}) %collective-permute-start.3) | collective-permute-done | bytes 36896 | tf_op jit(solution)/shard_map/ppermute | solution.py:352
  55.2 1.5 %shard_map.68 = (bf16[2,16,128,128]{3,2,1,0:T(8,128)(2,1)S(1)}, f32[2,16,16,128]{3,2,1,0:T(8,128)S(1)}) custom-call(s32[16]{0:T(128)S(1)} %copy-done.13, s32[1]{0:T(128)} %bitcast.place_y_ref.place_ref, bf16[2,4,256,256]{3,2,1,0:T(8,128)(2,1)S(1)} %get-tuple-element.36.turned_ref, bf16[4,2,48,128]{3,2,1,0:T(8,128)(2,1)S(1)} %get-tuple-element.37.far_ref, ...), custom_call_target="tpu_custom_call" | custom-call | tf_op jit(solution)/shard_map/pallas_call | solution.py:425
  56.8 0.9 %copy-done.5 = bf16[2,16,128,128]{3,2,1,0:T(8,128)(2,1)} copy-done((bf16[2,16,128,128]{3,2,1,0:T(8,128)(2,1)}, bf16[2,16,128,128]{3,2,1,0:T(8,128)(2,1)S(1)}, u32[]{:S(2)}) %copy-start.5) | copy-done | bytes 1048600
  57.7 0.7 %shard_map.70 = (bf16[2,16,8,128]{3,2,1,0:T(8,128)(2,1)S(1)}, bf16[2,16,8,128]{3,2,1,0:T(8,128)(2,1)S(1)}) custom-call(s32[1]{0:T(128)} %bitcast.4.me_ref, s32[1]{0:T(128)} %bitcast.1.place_ref.place_x_ref, s32[2,64]{1,0:T(2,128)S(1)} %copy-done.11, s32[2,64]{1,0:T(2,128)S(1)} %copy-done.12, bf16[768,16,128]{2,1,0:T(8,128)(2,1)S(1)} %all-to-all-done.arrived_ref, ...), custom_call_target="tpu_custom_call" | custom-call | tf_op jit(solution)/shard_map/pallas_call | solution.py:435
  58.6 0.7 collective-permute-start.5
  59.2 1.9 %shard_map.69 = (bf16[2,16,128,128]{3,2,1,0:T(8,128)(2,1)S(1)}, bf16[2,16,16,128]{3,2,1,0:T(8,128)(2,1)S(1)}) custom-call(s32[1]{0:T(128)} %bitcast.4.me_ref, s32[2,64]{1,0:T(2,128)S(1)} %copy-done.11, s32[2,64]{1,0:T(2,128)S(1)} %copy-done.12, bf16[768,16,128]{2,1,0:T(8,128)(2,1)S(1)} %all-to-all-done.arrived_ref, bf16[2,16,128,128]{3,2,1,0:T(8,128)(2,1)S(1)} %copy-done.6), custom_call_target="tpu_custom_call" | custom-call | tf_op jit(solution)/shard_map/pallas_call | solution.py:442
  61.1 1.2 %collective-permute-done.5.other_ref = bf16[2,16,8,128]{3,2,1,0:T(8,128)(2,1)S(1)} collective-permute-done((bf16[2,16,8,128]{3,2,1,0:T(8,128)(2,1)S(1)}, bf16[2,16,8,128]{3,2,1,0:T(8,128)(2,1)S(1)}, u32[]{:S(2)}, u32[]{:S(2)}) %collective-permute-start.5) | collective-permute-done | bytes 65568 | tf_op jit(solution)/shard_map/ppermute | solution.py:352
  62.4 0.2 shard_map.72
  62.6 0.4 collective-permute-start.7
  62.9 2.3 %shard_map.71.near_ref = f32[16,128,128]{2,1,0:T(8,128)S(1)} custom-call(s32[16]{0:T(128)S(1)} %copy-done.13, s32[1]{0:T(128)} %bitcast.1.place_ref.place_x_ref, bf16[4,256,256]{2,1,0:T(8,128)(2,1)S(1)} %copy-done.8, bf16[4,32,32]{2,1,0:T(8,128)(2,1)S(1)} %get-tuple-element.33.ends_ref, bf16[2,4,128,256]{3,2,1,0:T(8,128)(2,1)S(1)} %copy-done.10, ...), custom_call_target="tpu_custom_call" | custom-call | tf_op jit(solution)/shard_map/pallas_call | solution.py:449
  65.3 1.6 %collective-permute-done.6.even_ref = bf16[2,18,8,128]{3,2,1,0:T(8,128)(2,1)S(1)} collective-permute-done((bf16[2,18,8,128]{3,2,1,0:T(8,128)(2,1)S(1)}, bf16[2,18,8,128]{3,2,1,0:T(8,128)(2,1)S(1)}, u32[]{:S(2)}, u32[]{:S(2)}) %collective-permute-start.6) | collective-permute-done | bytes 73760 | tf_op jit(solution)/shard_map/ppermute | solution.py:353
  66.9 2.2 %collective-permute-done.7.other_ref = bf16[2,18,8,128]{3,2,1,0:T(8,128)(2,1)S(1)} collective-permute-done((bf16[2,18,8,128]{3,2,1,0:T(8,128)(2,1)S(1)}, bf16[2,18,8,128]{3,2,1,0:T(8,128)(2,1)S(1)}, u32[]{:S(2)}, u32[]{:S(2)}) %collective-permute-start.7) | collective-permute-done | bytes 73760 | tf_op jit(solution)/shard_map/ppermute | solution.py:352
  69.1 2.2 %shard_map.73 = f32[16,128,128]{2,1,0:T(8,128)} custom-call(s32[16]{0:T(128)S(1)} %copy-done.13, s32[1]{0:T(128)} %bitcast.place_y_ref.place_ref, bf16[2,4,256,256]{3,2,1,0:T(8,128)(2,1)S(1)} %copy-done.4, bf16[4,2,48,128]{3,2,1,0:T(8,128)(2,1)S(1)} %get-tuple-element.31.far_ref, f32[16,128,128]{2,1,0:T(8,128)S(1)} %shard_map.71.near_ref, ...), custom_call_target="tpu_custom_call" | custom-call | tf_op jit(solution)/shard_map/pallas_call | solution.py:458
  (32 shorter events, 0.3 us)
Async XLA Ops:
  0.9 4.5 %collective-permute-start.1 = (f32[16,8,128]{2,1,0:T(8,128)S(1)}, f32[16,8,128]{2,1,0:T(8,128)S(1)}, u32[]{:S(2)}, u32[]{:S(2)}) collective-permute-start(f32[16,8,128]{2,1,0:T(8,128)S(1)} %get-tuple-element.49), channel_id=1, source_target_pairs={{0,1},{1,0},{2,3},{3,2},{4,5},{5,4},{6,7},{7,6},{8,9},{9,8},{10,11... | collective-permute-start | bytes 196616 | tf_op jit(solution)/shard_map/ppermute | solution.py:352
  1.2 4.1 %collective-permute-start = (f32[16,8,128]{2,1,0:T(8,128)S(1)}, f32[16,8,128]{2,1,0:T(8,128)S(1)}, u32[]{:S(2)}, u32[]{:S(2)}) collective-permute-start(f32[16,8,128]{2,1,0:T(8,128)S(1)} %get-tuple-element.50), channel_id=1, source_target_pairs={{0,16},{1,17},{2,18},{3,19},{4,20},{5,21},{6,22},{7,23},{8,24},{9,... | collective-permute-start | bytes 196616 | tf_op jit(solution)/shard_map/ppermute | solution.py:353
  5.4 10.2 %copy-start.14 = (f32[2,4,2,17]{3,2,1,0:T(2,128)S(1)}, f32[2,4,2,17]{3,2,1,0:T(2,128)}, u32[]{:S(2)}) copy-start(f32[2,4,2,17]{3,2,1,0:T(2,128)} %param.8) | copy-start | bytes 3268
  5.4 18.6 %copy-start.13 = (s32[16]{0:T(128)S(1)}, s32[16]{0:T(128)}, u32[]{:S(2)}) copy-start(s32[16]{0:T(128)} %band_ref.7) | copy-start | bytes 196
  5.4 52.3 %all-to-all-start = ((bf16[768,16,128]{2,1,0:T(8,128)(2,1)}), bf16[768,16,128]{2,1,0:T(8,128)(2,1)S(1)}, u32[]{:S(2)}, u32[]{:S(2)}) async-start(bf16[768,16,128]{2,1,0:T(8,128)(2,1)} %bitcast.9), calls=%async_computation | async-start | bytes 6291456 | tf_op jit(solution)/shard_map/all_to_all | solution.py:392
  15.5 42.2 %copy-start.11 = (s32[2,64]{1,0:T(2,128)S(1)}, s32[2,64]{1,0:T(2,128)}, u32[]{:S(2)}) copy-start(s32[2,64]{1,0:T(2,128)} %shift_ref.3) | copy-start | bytes 1540
  15.5 42.2 %copy-start.12 = (s32[2,64]{1,0:T(2,128)S(1)}, s32[2,64]{1,0:T(2,128)}, u32[]{:S(2)}) copy-start(s32[2,64]{1,0:T(2,128)} %length_ref.3) | copy-start | bytes 1540
  15.9 1.2 %copy-start = (f32[16,128,128]{2,1,0:T(8,128)S(1)}, f32[16,128,128]{2,1,0:T(8,128)}, u32[]{:S(2)}) copy-start(f32[16,128,128]{2,1,0:T(8,128)} %estimate_ref.1) | copy-start | bytes 3145732
  17.7 33.4 %collective-permute-start.2 = (bf16[1,18,8,128]{3,2,1,0:T(8,128)(2,1)S(1)}, bf16[1,18,8,128]{3,2,1,0:T(8,128)(2,1)S(1)}, u32[]{:S(2)}, u32[]{:S(2)}) collective-permute-start(bf16[1,18,8,128]{3,2,1,0:T(8,128)(2,1)S(1)} %get-tuple-element.38), channel_id=1, source_target_pairs={{0,1},{1,0},{2,3},{3,2},{4,5},{5,4},{6,7},{7,6},{8,9},{9,8},{10,11... | collective-permute-start | bytes 110600 | tf_op jit(solution)/shard_map/ppermute | solution.py:353
  19.4 35.8 %collective-permute-start.3 = (bf16[1,18,8,128]{3,2,1,0:T(8,128)(2,1)S(1)}, bf16[1,18,8,128]{3,2,1,0:T(8,128)(2,1)S(1)}, u32[]{:S(2)}, u32[]{:S(2)}) collective-permute-start(bf16[1,18,8,128]{3,2,1,0:T(8,128)(2,1)S(1)} %get-tuple-element.39), channel_id=1, source_target_pairs={{1,2},{2,1},{3,4},{4,3},{5,6},{6,5},{7,8},{8,7},{9,10},{10,9},{11,... | collective-permute-start | bytes 110600 | tf_op jit(solution)/shard_map/ppermute | solution.py:352
  23.9 1.2 %copy-start.1 = (f32[16,128,128]{2,1,0:T(8,128)S(1)}, f32[16,128,128]{2,1,0:T(8,128)}, u32[]{:S(2)}) copy-start(f32[16,128,128]{2,1,0:T(8,128)} %estimate_ref.1) | copy-start | bytes 3145732
  36.0 1.0 %copy-start.3 = (bf16[2,4,256,256]{3,2,1,0:T(8,128)(2,1)}, bf16[2,4,256,256]{3,2,1,0:T(8,128)(2,1)S(1)}, u32[]{:S(2)}) copy-start(bf16[2,4,256,256]{3,2,1,0:T(8,128)(2,1)S(1)} %get-tuple-element.30.turned_ref) | copy-start | bytes 3145732
  37.0 0.8 %copy-start.7 = (bf16[4,256,256]{2,1,0:T(8,128)(2,1)}, bf16[4,256,256]{2,1,0:T(8,128)(2,1)S(1)}, u32[]{:S(2)}) copy-start(bf16[4,256,256]{2,1,0:T(8,128)(2,1)S(1)} %get-tuple-element.32.rows_ref) | copy-start | bytes 1572868
  37.8 0.8 %copy-start.9 = (bf16[2,4,128,256]{3,2,1,0:T(8,128)(2,1)}, bf16[2,4,128,256]{3,2,1,0:T(8,128)(2,1)S(1)}, u32[]{:S(2)}) copy-start(bf16[2,4,128,256]{3,2,1,0:T(8,128)(2,1)S(1)} %get-tuple-element.34.cols_ref) | copy-start | bytes 1572868
  56.7 1.0 %copy-start.5 = (bf16[2,16,128,128]{3,2,1,0:T(8,128)(2,1)}, bf16[2,16,128,128]{3,2,1,0:T(8,128)(2,1)S(1)}, u32[]{:S(2)}) copy-start(bf16[2,16,128,128]{3,2,1,0:T(8,128)(2,1)S(1)} %get-tuple-element.41.forward_ref) | copy-start | bytes 3145732
  57.7 1.5 %copy-start.6 = (bf16[2,16,128,128]{3,2,1,0:T(8,128)(2,1)S(1)}, bf16[2,16,128,128]{3,2,1,0:T(8,128)(2,1)}, u32[]{:S(2)}) copy-start(bf16[2,16,128,128]{3,2,1,0:T(8,128)(2,1)} %copy-done.5) | copy-start | bytes 3145732
  57.7 5.2 %copy-start.8 = (bf16[4,256,256]{2,1,0:T(8,128)(2,1)S(1)}, bf16[4,256,256]{2,1,0:T(8,128)(2,1)}, u32[]{:S(2)}) copy-start(bf16[4,256,256]{2,1,0:T(8,128)(2,1)} %copy-done.7) | copy-start | bytes 1572868
  57.7 5.2 %copy-start.10 = (bf16[2,4,128,256]{3,2,1,0:T(8,128)(2,1)S(1)}, bf16[2,4,128,256]{3,2,1,0:T(8,128)(2,1)}, u32[]{:S(2)}) copy-start(bf16[2,4,128,256]{3,2,1,0:T(8,128)(2,1)} %copy-done.9) | copy-start | bytes 1572868
  58.5 2.6 %collective-permute-start.4 = (bf16[2,16,8,128]{3,2,1,0:T(8,128)(2,1)S(1)}, bf16[2,16,8,128]{3,2,1,0:T(8,128)(2,1)S(1)}, u32[]{:S(2)}, u32[]{:S(2)}) collective-permute-start(bf16[2,16,8,128]{3,2,1,0:T(8,128)(2,1)S(1)} %get-tuple-element.44), channel_id=1, source_target_pairs={{0,16},{1,17},{2,18},{3,19},{4,20},{5,21},{6,22},{7,23},{8,24},{9,... | collective-permute-start | bytes 196616 | tf_op jit(solution)/shard_map/ppermute | solution.py:353
  58.6 3.8 %collective-permute-start.5 = (bf16[2,16,8,128]{3,2,1,0:T(8,128)(2,1)S(1)}, bf16[2,16,8,128]{3,2,1,0:T(8,128)(2,1)S(1)}, u32[]{:S(2)}, u32[]{:S(2)}) collective-permute-start(bf16[2,16,8,128]{3,2,1,0:T(8,128)(2,1)S(1)} %get-tuple-element.45), channel_id=1, source_target_pairs={{0,1},{1,0},{2,3},{3,2},{4,5},{5,4},{6,7},{7,6},{8,9},{9,8},{10,11... | collective-permute-start | bytes 196616 | tf_op jit(solution)/shard_map/ppermute | solution.py:352
  59.2 9.9 %copy-start.2 = (f32[16,128,128]{2,1,0:T(8,128)S(1)}, f32[16,128,128]{2,1,0:T(8,128)}, u32[]{:S(2)}) copy-start(f32[16,128,128]{2,1,0:T(8,128)} %estimate_ref.1) | copy-start | bytes 3145732
  59.2 9.9 %copy-start.4 = (bf16[2,4,256,256]{3,2,1,0:T(8,128)(2,1)S(1)}, bf16[2,4,256,256]{3,2,1,0:T(8,128)(2,1)}, u32[]{:S(2)}) copy-start(bf16[2,4,256,256]{3,2,1,0:T(8,128)(2,1)} %copy-done.3) | copy-start | bytes 3145732
  62.5 4.4 %collective-permute-start.6 = (bf16[2,18,8,128]{3,2,1,0:T(8,128)(2,1)S(1)}, bf16[2,18,8,128]{3,2,1,0:T(8,128)(2,1)S(1)}, u32[]{:S(2)}, u32[]{:S(2)}) collective-permute-start(bf16[2,18,8,128]{3,2,1,0:T(8,128)(2,1)S(1)} %get-tuple-element.47), channel_id=1, source_target_pairs={{0,1},{1,0},{2,3},{3,2},{4,5},{5,4},{6,7},{7,6},{8,9},{9,8},{10,11... | collective-permute-start | bytes 221192 | tf_op jit(solution)/shard_map/ppermute | solution.py:353
  62.6 6.5 %collective-permute-start.7 = (bf16[2,18,8,128]{3,2,1,0:T(8,128)(2,1)S(1)}, bf16[2,18,8,128]{3,2,1,0:T(8,128)(2,1)S(1)}, u32[]{:S(2)}, u32[]{:S(2)}) collective-permute-start(bf16[2,18,8,128]{3,2,1,0:T(8,128)(2,1)S(1)} %get-tuple-element.48), channel_id=1, source_target_pairs={{0,16},{1,2},{2,1},{3,4},{4,3},{5,6},{6,5},{7,8},{8,7},{9,10},{10,... | collective-permute-start | bytes 221192 | tf_op jit(solution)/shard_map/ppermute | solution.py:352

commit v13 on v12

--- a/solution.py
+++ b/solution.py
@@ -140,9 +140,9 @@
 
 
 def edges_kernel(
-    devices, tile_rows, me_ref, place_ref, shift_ref, length_ref, arrived_ref, recip_ref, first_ref, second_ref, rows_ref
-):
-    views = recip_ref.shape[0]
+    devices, tile_rows, me_ref, place_ref, shift_ref, length_ref, arrived_ref, edge_ref, first_ref, second_ref, rows_ref
+):
+    views = edge_ref.shape[0]
     odd = is_odd(place_ref)
     groups = shift_ref.shape[1]
     me = me_ref[0]
@@ -158,14 +158,18 @@
                 for k in range(CAP):
                     rows_ref[view, side, start + k] = arrived_ref[base + k].astype(F32)
                 start = start + length_ref[view, g]
-        head = jnp.transpose(rows_ref[view, 0, :HW], (1, 0, 2)) * recip_ref[view, :, :HW]
+        edge = edge_ref[view, :, 4 * HW :].astype(F32)
+        head = jnp.transpose(rows_ref[view, 0, :HW], (1, 0, 2)) / edge[:, :HW]
         tail = rows_ref[view, 1, (CAP - 1) * HW : CAP * HW]
-        tail = jnp.transpose(tail, (1, 0, 2)) * recip_ref[view, :, HW:]
+        tail = jnp.transpose(tail, (1, 0, 2)) / edge[:, HW:]
         first_ref[view] = jnp.where(odd, head, tail).astype(BF16)
         second_ref[view] = jnp.where(odd, tail, head).astype(BF16)
 
 
-def unpack_kernel(devices, me_ref, shift_ref, length_ref, arrived_ref, forward_ref, out_ref, cols_ref, rows_ref):
+def unpack_kernel(
+    devices, me_ref, band_ref, shift_ref, length_ref, arrived_ref, blurred_ref, far_ref, parts_ref,
+    out_ref, cols_ref, rows_ref, forward_ref,
+):
     views, depth, tile_rows, tile_cols = out_ref.shape
     groups = shift_ref.shape[1]
     me = me_ref[0]
@@ -180,6 +184,11 @@
             return start + length_ref[view, g]
 
         lax.fori_loop(0, groups, group, 0, unroll=True)
+        for z in range(depth):
+            parts = parts_ref[view, z, : 4 * HW]
+            parts = jnp.concatenate([parts, parts[: 2 * HW]], axis=0)
+            across = dot(parts, far_ref[band_ref[z], view], ((0,), (0,)))
+            forward_ref[view, z] = (blurred_ref[view, z] + across).astype(BF16)
         for r0 in range(0, tile_rows, 16):
             x = jnp.transpose(rows_ref[view, r0 : r0 + 16], (1, 0, 2))
             forward = forward_ref[view, :, r0 : r0 + 16, :].astype(F32)
@@ -222,7 +231,7 @@
 
 def forward_kernel(
     band_ref, place_ref, taps_ref, cells_ref, even_ref, other_ref,
-    blurred_ref, fwd_turned_ref, fwd_far_ref, rows_ref, ends_ref, cols_ref, turned_ref, far_ref, fwd_rows, fwd_cols,
+    blurred_ref, edge_ref, fwd_turned_ref, fwd_far_ref, later_far_ref, rows_ref, ends_ref, cols_ref, turned_ref, far_ref, fwd_rows, fwd_cols,
 ):
     views, depth, tile_rows, tile_cols = blurred_ref.shape
     bands = taps_ref.shape[2]
@@ -250,6 +259,7 @@
                     cols_ref[view, b] = inner
         ends = jnp.concatenate([ends[:HW], ends[tile_rows - HW :]], axis=0)
         ends_ref[b] = stacked(ends[:, : 2 * HW * views], 0)
+        later_far_ref[b] = fwd_far_ref[b]
 
     def plane(z, carry):
         b = band_ref[z]
@@ -260,27 +270,28 @@
             blurred = quarters(dot(rows[:, :tile_rows], cells)) + halves(dot(rows[:, tile_rows:], ends))
             blurred = quarters(dot(stacked(blurred, 0), fwd_cols[view, b]))
             blurred_ref[view, z] = blurred
+            edge_ref[view, z, :HW] = blurred[:HW]
+            edge_ref[view, z, HW:] = blurred[tile_rows - HW :]
         return carry
 
     lax.fori_loop(0, depth, plane, 0, unroll=2)
 
 
 def late_kernel(
-    band_ref, place_ref, turned_ref, far_ref, even_ref, other_ref, blurred_ref, out_ref, edge_ref, slab_ref, along_ref
-):
-    views, depth, tile_rows, tile_cols = blurred_ref.shape
+    band_ref, place_ref, turned_ref, far_ref, even_ref, other_ref, blurred_ref, out_ref, slab_ref, along_ref
+):
+    views, depth = blurred_ref.shape[:2]
+    tile_rows = along_ref.shape[-1]
     weights = [turned_ref.at[view] for view in range(views)]
     far_products(place_ref, even_ref.at[0], other_ref.at[0], weights, slab_ref, [along_ref.at[v] for v in range(views)])
     for view in range(views):
         for z in range(depth):
             b = band_ref[z]
-            along = jnp.concatenate(far_parts(along_ref, view, b, z), axis=0)
-            blurred = blurred_ref[view, z] + dot(along, far_ref[b, view], ((0,), (0,)))
-            blurred = blurred.astype(BF16)
-            out_ref[view, z] = blurred
-            recip = 1.0 / blurred.astype(F32)
-            edge_ref[view, z, :HW] = recip[:HW]
-            edge_ref[view, z, HW:] = recip[tile_rows - HW :]
+            parts = far_parts(along_ref, view, b, z)
+            out_ref[view, z, : 4 * HW] = jnp.concatenate(parts[:2], axis=0)
+            across = dot(jnp.concatenate(parts, axis=0), far_ref[b, view], ((0,), (0,)))
+            ends = jnp.concatenate([across[:HW], across[tile_rows - HW :]], axis=0)
+            out_ref[view, z, 4 * HW :] = (blurred_ref[view, z] + ends).astype(BF16)
 
 
 def near_kernel(
@@ -403,12 +414,14 @@
     tap_rows = jnp.pad(tap_rows, ((0, 0),) * 4 + ((0, LANES - kernels.shape[3]),))
     turned_like = like((views, bands, 2 * tile_rows, 2 * tile_rows), BF16)
     far_like = like((bands, views, 6 * HW, tile_cols), BF16)
-    blurred, fwd_turned, fwd_far, rows_mat, ends_mat, cols_mat, turned_mat, far_mat = call(
+    blurred, edge, fwd_turned, fwd_far, later_far, rows_mat, ends_mat, cols_mat, turned_mat, far_mat = call(
         forward_kernel,
         [SMEM] * 2 + [VMEM] * 4,
         (
             like(measured.shape, F32),
+            like((views, depth, 2 * HW, tile_cols), F32),
             turned_like,
+            far_like,
             far_like,
             like((bands, 2 * tile_rows, views * tile_rows), BF16),
             like((bands, 4 * HW, views * 2 * HW), BF16),
@@ -422,29 +435,29 @@
         ],
     )(depth_band, place_x, tap_rows, cells, ex, ox)
 
-    forward, edge_recip = call(
+    parts = call(
         late_kernel,
         [SMEM] * 2 + [VMEM] * 5,
-        (whole, like((views, depth, 2 * HW, tile_cols), F32)),
+        like((views, depth, 6 * HW, tile_rows), BF16),
         [
             pltpu.VMEM((depth * 2 * HW, 2 * tile_rows), BF16),
             pltpu.VMEM((views, bands, 2, depth * 2 * HW, tile_rows), BF16),
         ],
-    )(depth_band, place_y, fwd_turned, fwd_far, ey, oy, blurred)
+    )(depth_band, place_y, fwd_turned, fwd_far, ey, oy, edge)
 
     first, second = call(
         functools.partial(edges_kernel, devices, tile_rows),
         [SMEM] * 4 + [VMEM] * 2,
         (edge_rows, edge_rows),
         [pltpu.VMEM((views, 2, CAP * HW + 8, depth, tile_cols), F32)],
-    )(me, place_x, group_shift, group_length, arrived, edge_recip)
+    )(me, place_x, group_shift, group_length, arrived, parts)
     ex, ox = swap(first, second, "gx")
     ratio, cols = call(
         functools.partial(unpack_kernel, devices),
-        [SMEM] * 3 + [VMEM] * 2,
+        [SMEM] * 4 + [VMEM] * 4,
         (whole, edge_cols),
-        [pltpu.VMEM((views, spare, depth, tile_cols), F32)],
-    )(me, group_shift, group_length, arrived, forward)
+        [pltpu.VMEM((views, spare, depth, tile_cols), F32), pltpu.VMEM(measured.shape, BF16)],
+    )(me, depth_band, group_shift, group_length, arrived, blurred, later_far, parts)
     ey, oy = swap(*dense(views, cols, ex, ox), "gy")
     near = call(
         near_kernel,

time: 71.7 us -> 71.8 us (level)
  waiting for transfers between devices: 21.7 us -> 18.2 us
  local copies, waits for them, and re-layouts: 6.11 us -> 8.46 us
    ppermute x4, waiting for transfers between devices: 14.2 us -> 10.8 us  [swap(): return (lax.ppermute(first, both, pairs[0]), late)]
    unnamed x30 -> x42, local copies, waits for them, and re-layouts: 6.01 us -> 8.36 us
  transfers between devices with their start and end apart: 9 -> 9, of which waited for: 5 -> 5; matrix products, arithmetic and copies ran while one was open for 1% -> 1% of each run, Pallas kernels for 28% -> 29%
where the time goes in v13:
time: 71.8 us; the launch traced here: 70.8 us
  Pallas kernels  23.4 us (33%)
  starting transfers between devices  19 us (26%)
  waiting for transfers between devices  18.2 us (25%)
  local copies, waits for them, and re-layouts  8.46 us (12%)
  other arithmetic  1.16 us (2%)
    pallas_call x1, Pallas kernels, body(): call(forward_kernel, [SMEM] * 2 + [VMEM] * 4, (like(measured.shape, F32),...  10.8 us
    ppermute x4, waiting for transfers between devices, swap(): return (lax.ppermute(first, both, pairs[0]), late)  10.8 us
    all_to_all x1, starting transfers between devices, body(): lax.all_to_all(outgoing, ('gx', 'gy'), split_axis=0, concat_axis=0, tiled...  10.1 us
    unnamed x42, local copies, waits for them, and re-layouts  8.36 us
    ppermute x4, waiting for transfers between devices, swap(): late = lax.ppermute(second, both, pairs[1])  7.37 us
    ppermute x4, starting transfers between devices, swap(): late = lax.ppermute(second, both, pairs[1])  5.91 us
    ppermute x4, starting transfers between devices, swap(): return (lax.ppermute(first, both, pairs[0]), late)  3.03 us
    pallas_call x1, Pallas kernels, body(): call(functools.partial(pack_kernel, devices), [SMEM, HBM, HBM, HBM], like...  2.92 us
  transfers between devices with their start and end apart: 9, of which 5 were waited for; matrix products, arithmetic and copies ran while one was open for 1% of the time, Pallas kernels for 29%

profile of v13, /device:TPU:30, one launch (start us, length us, event | category | flops | bytes accessed | tf_op | source)
XLA Modules:
  0.0 70.8 jit_solution(8251913033434157633)
XLA Ops:
  0.0 0.9 %slice_select_fusion = (f32[16,8,128]{2,1,0:T(8,128)S(1)}, f32[16,8,128]{2,1,0:T(8,128)S(1)}) fusion(f32[16,128,128]{2,1,0:T(8,128)} %estimate_ref.1, pred[]{:T(512)S(6)} %eq.13), kind=kLoop, calls=%fused_computation | loop fusion | flops 32768 | bytes 262145 | tf_op jit(solution)/shard_map/jit(_where)/select_n | solution.py:386
  0.9 0.3 collective-permute-start.1
  1.2 1.2 %collective-permute-start = (f32[16,8,128]{2,1,0:T(8,128)S(1)}, f32[16,8,128]{2,1,0:T(8,128)S(1)}, u32[]{:S(2)}, u32[]{:S(2)}) collective-permute-start(f32[16,8,128]{2,1,0:T(8,128)S(1)} %get-tuple-element.50), channel_id=1, source_target_pairs={{0,16},{1,17},{2,18},{3,19},{4,20},{5,21},{6,22},{7,23},{8,24},{9,... | collective-permute-start | bytes 196616 | tf_op jit(solution)/shard_map/ppermute | solution.py:364
  2.4 2.9 %shard_map.64 = bf16[128,2,3,16,128]{4,3,2,1,0:T(8,128)(2,1)} custom-call(s32[1]{0:T(128)} %bitcast.4.me_ref, s32[2,64]{1,0:T(2,128)} %shift_ref.3, s32[2,64]{1,0:T(2,128)} %length_ref.3, bf16[2,16,128,128]{3,2,1,0:T(8,128)(2,1)} %measured_hbm.1), custom_call_target="tpu_custom_call" | custom-call | tf_op jit(solution)/shard_map/pallas_call | solution.py:387
  5.4 10.1 %all-to-all-start = ((bf16[768,16,128]{2,1,0:T(8,128)(2,1)}), bf16[768,16,128]{2,1,0:T(8,128)(2,1)S(1)}, u32[]{:S(2)}, u32[]{:S(2)}) async-start(bf16[768,16,128]{2,1,0:T(8,128)(2,1)} %bitcast.9), calls=%async_computation | async-start | bytes 6291456 | tf_op jit(solution)/shard_map/all_to_all | solution.py:403
  16.0 1.2 %copy-done = f32[16,128,128]{2,1,0:T(8,128)S(1)} copy-done((f32[16,128,128]{2,1,0:T(8,128)S(1)}, f32[16,128,128]{2,1,0:T(8,128)}, u32[]{:S(2)}) %copy-start) | copy-done | bytes 1048600
  17.2 0.4 shard_map.66
  17.5 0.2 shard_map.67
  17.7 1.7 %collective-permute-start.2 = (bf16[1,18,8,128]{3,2,1,0:T(8,128)(2,1)S(1)}, bf16[1,18,8,128]{3,2,1,0:T(8,128)(2,1)S(1)}, u32[]{:S(2)}, u32[]{:S(2)}) collective-permute-start(bf16[1,18,8,128]{3,2,1,0:T(8,128)(2,1)S(1)} %get-tuple-element.40), channel_id=1, source_target_pairs={{0,1},{1,0},{2,3},{3,2},{4,5},{5,4},{6,7},{7,6},{8,9},{9,8},{10,11... | collective-permute-start | bytes 110600 | tf_op jit(solution)/shard_map/ppermute | solution.py:364
  19.5 4.5 %collective-permute-start.3 = (bf16[1,18,8,128]{3,2,1,0:T(8,128)(2,1)S(1)}, bf16[1,18,8,128]{3,2,1,0:T(8,128)(2,1)S(1)}, u32[]{:S(2)}, u32[]{:S(2)}) collective-permute-start(bf16[1,18,8,128]{3,2,1,0:T(8,128)(2,1)S(1)} %get-tuple-element.41), channel_id=1, source_target_pairs={{1,2},{2,1},{3,4},{4,3},{5,6},{6,5},{7,8},{8,7},{9,10},{10,9},{11,... | collective-permute-start | bytes 110600 | tf_op jit(solution)/shard_map/ppermute | solution.py:363
  24.0 1.2 %copy-done.1 = f32[16,128,128]{2,1,0:T(8,128)S(1)} copy-done((f32[16,128,128]{2,1,0:T(8,128)S(1)}, f32[16,128,128]{2,1,0:T(8,128)}, u32[]{:S(2)}) %copy-start.1) | copy-done | bytes 1048600
  25.2 10.8 %shard_map.65 = (f32[2,16,128,128]{3,2,1,0:T(8,128)S(1)}, f32[2,16,16,128]{3,2,1,0:T(8,128)S(1)}, bf16[2,4,256,256]{3,2,1,0:T(8,128)(2,1)S(1)}, bf16[4,2,48,128]...) custom-call(s32[16]{0:T(128)S(1)} %copy-done.17, ...), custom_call_target="tpu_custom_call" | custom-call | tf_op jit(solution)/shard_map/pallas_call | solution.py:417
  36.0 1.3 %copy-done.3 = f32[2,16,128,128]{3,2,1,0:T(8,128)} copy-done((f32[2,16,128,128]{3,2,1,0:T(8,128)}, f32[2,16,128,128]{3,2,1,0:T(8,128)S(1)}, u32[]{:S(2)}) %copy-start.3) | copy-done | bytes 2097176
  37.4 1.0 %copy-done.5 = bf16[2,4,256,256]{3,2,1,0:T(8,128)(2,1)} copy-done((bf16[2,4,256,256]{3,2,1,0:T(8,128)(2,1)}, bf16[2,4,256,256]{3,2,1,0:T(8,128)(2,1)S(1)}, u32[]{:S(2)}) %copy-start.5) | copy-done | bytes 1048600
  38.4 0.8 %copy-done.7 = bf16[4,256,256]{2,1,0:T(8,128)(2,1)} copy-done((bf16[4,256,256]{2,1,0:T(8,128)(2,1)}, bf16[4,256,256]{2,1,0:T(8,128)(2,1)S(1)}, u32[]{:S(2)}) %copy-start.7) | copy-done | bytes 524312
  39.2 0.8 %copy-done.9 = bf16[2,4,128,256]{3,2,1,0:T(8,128)(2,1)} copy-done((bf16[2,4,128,256]{3,2,1,0:T(8,128)(2,1)}, bf16[2,4,128,256]{3,2,1,0:T(8,128)(2,1)S(1)}, u32[]{:S(2)}) %copy-start.9) | copy-done | bytes 524312
  40.0 0.6 copy-done.11
  40.6 0.6 copy-done.13
  41.2 0.6 copy-done.15
  41.9 9.3 %collective-permute-done.2.even_ref = bf16[1,18,8,128]{3,2,1,0:T(8,128)(2,1)S(1)} collective-permute-done((bf16[1,18,8,128]{3,2,1,0:T(8,128)(2,1)S(1)}, bf16[1,18,8,128]{3,2,1,0:T(8,128)(2,1)S(1)}, u32[]{:S(2)}, u32[]{:S(2)}) %collective-permute-start.2) | collective-permute-done | bytes 36896 | tf_op jit(solution)/shard_map/ppermute | solution.py:364
  51.1 4.1 %collective-permute-done.3.other_ref = bf16[1,18,8,128]{3,2,1,0:T(8,128)(2,1)S(1)} collective-permute-done((bf16[1,18,8,128]{3,2,1,0:T(8,128)(2,1)S(1)}, bf16[1,18,8,128]{3,2,1,0:T(8,128)(2,1)S(1)}, u32[]{:S(2)}, u32[]{:S(2)}) %collective-permute-start.3) | collective-permute-done | bytes 36896 | tf_op jit(solution)/shard_map/ppermute | solution.py:363
  55.3 1.5 %shard_map.68.parts_ref.edge_ref = bf16[2,16,48,128]{3,2,1,0:T(8,128)(2,1)S(1)} custom-call(s32[16]{0:T(128)S(1)} %copy-done.17, s32[1]{0:T(128)} %bitcast.place_y_ref.place_ref, bf16[2,4,256,256]{3,2,1,0:T(8,128)(2,1)S(1)} %get-tuple-element.38.turned_ref, bf16[4,2,48,128]{3,2,1,0:T(8,128)(2,1)S(1)} %get-tuple-element.39.far_ref, ...), custom_call_target="tpu_custom_call" | custom-call | tf_op jit(solution)/shard_map/pallas_call | solution.py:438
  56.8 0.7 %shard_map.70 = (bf16[2,16,8,128]{3,2,1,0:T(8,128)(2,1)S(1)}, bf16[2,16,8,128]{3,2,1,0:T(8,128)(2,1)S(1)}) custom-call(s32[1]{0:T(128)} %bitcast.4.me_ref, s32[1]{0:T(128)} %bitcast.1.place_ref.place_x_ref, s32[2,64]{1,0:T(2,128)S(1)} %copy-done.18, s32[2,64]{1,0:T(2,128)S(1)} %copy-done.19, bf16[768,16,128]{2,1,0:T(8,128)(2,1)S(1)} %all-to-all-done.arrived_ref, ...), custom_call_target="tpu_custom_call" | custom-call | tf_op jit(solution)/shard_map/pallas_call | solution.py:448
  57.7 0.6 collective-permute-start.5
  58.4 2.2 %shard_map.69 = (bf16[2,16,128,128]{3,2,1,0:T(8,128)(2,1)S(1)}, bf16[2,16,16,128]{3,2,1,0:T(8,128)(2,1)S(1)}) custom-call(s32[1]{0:T(128)} %bitcast.4.me_ref, s32[16]{0:T(128)S(1)} %copy-done.17, s32[2,64]{1,0:T(2,128)S(1)} %copy-done.18, s32[2,64]{1,0:T(2,128)S(1)} %copy-done.19, bf16[768,16,128]{2,1,0:T(8,128)(2,1)S(1)} %all-to-all-done.arrived_ref, ...), custom_call_target="tpu_custom_call" | custom-call | tf_op jit(solution)/shard_map/pallas_call | solution.py:455
  60.6 0.9 %collective-permute-done.5.other_ref = bf16[2,16,8,128]{3,2,1,0:T(8,128)(2,1)S(1)} collective-permute-done((bf16[2,16,8,128]{3,2,1,0:T(8,128)(2,1)S(1)}, bf16[2,16,8,128]{3,2,1,0:T(8,128)(2,1)S(1)}, u32[]{:S(2)}, u32[]{:S(2)}) %collective-permute-start.5) | collective-permute-done | bytes 65568 | tf_op jit(solution)/shard_map/ppermute | solution.py:363
  61.5 0.2 shard_map.72
  61.7 0.5 collective-permute-start.7
  62.1 2.3 %shard_map.71.near_ref = f32[16,128,128]{2,1,0:T(8,128)S(1)} custom-call(s32[16]{0:T(128)S(1)} %copy-done.17, s32[1]{0:T(128)} %bitcast.1.place_ref.place_x_ref, bf16[4,256,256]{2,1,0:T(8,128)(2,1)S(1)} %copy-done.8, bf16[4,32,32]{2,1,0:T(8,128)(2,1)S(1)} %copy-done.16, bf16[2,4,128,256]{3,2,1,0:T(8,128)(2,1)S(1)} %copy-done.10, ...), custom_call_target="tpu_custom_call" | custom-call | tf_op jit(solution)/shard_map/pallas_call | solution.py:462
  64.5 1.5 %collective-permute-done.6.even_ref = bf16[2,18,8,128]{3,2,1,0:T(8,128)(2,1)S(1)} collective-permute-done((bf16[2,18,8,128]{3,2,1,0:T(8,128)(2,1)S(1)}, bf16[2,18,8,128]{3,2,1,0:T(8,128)(2,1)S(1)}, u32[]{:S(2)}, u32[]{:S(2)}) %collective-permute-start.6) | collective-permute-done | bytes 73760 | tf_op jit(solution)/shard_map/ppermute | solution.py:364
  66.0 2.4 %collective-permute-done.7.other_ref = bf16[2,18,8,128]{3,2,1,0:T(8,128)(2,1)S(1)} collective-permute-done((bf16[2,18,8,128]{3,2,1,0:T(8,128)(2,1)S(1)}, bf16[2,18,8,128]{3,2,1,0:T(8,128)(2,1)S(1)}, u32[]{:S(2)}, u32[]{:S(2)}) %collective-permute-start.7) | collective-permute-done | bytes 73760 | tf_op jit(solution)/shard_map/ppermute | solution.py:363
  68.4 2.2 %shard_map.73 = f32[16,128,128]{2,1,0:T(8,128)} custom-call(s32[16]{0:T(128)S(1)} %copy-done.17, s32[1]{0:T(128)} %bitcast.place_y_ref.place_ref, bf16[2,4,256,256]{3,2,1,0:T(8,128)(2,1)S(1)} %copy-done.6, bf16[4,2,48,128]{3,2,1,0:T(8,128)(2,1)S(1)} %copy-done.12, f32[16,128,128]{2,1,0:T(8,128)S(1)} %shard_map.71.near_ref, ...), custom_call_target="tpu_custom_call" | custom-call | tf_op jit(solution)/shard_map/pallas_call | solution.py:471
  (44 shorter events, 0.6 us)
Async XLA Ops:
  0.9 4.5 %collective-permute-start.1 = (f32[16,8,128]{2,1,0:T(8,128)S(1)}, f32[16,8,128]{2,1,0:T(8,128)S(1)}, u32[]{:S(2)}, u32[]{:S(2)}) collective-permute-start(f32[16,8,128]{2,1,0:T(8,128)S(1)} %get-tuple-element.49), channel_id=1, source_target_pairs={{0,1},{1,0},{2,3},{3,2},{4,5},{5,4},{6,7},{7,6},{8,9},{9,8},{10,11... | collective-permute-start | bytes 196616 | tf_op jit(solution)/shard_map/ppermute | solution.py:363
  1.2 4.1 %collective-permute-start = (f32[16,8,128]{2,1,0:T(8,128)S(1)}, f32[16,8,128]{2,1,0:T(8,128)S(1)}, u32[]{:S(2)}, u32[]{:S(2)}) collective-permute-start(f32[16,8,128]{2,1,0:T(8,128)S(1)} %get-tuple-element.50), channel_id=1, source_target_pairs={{0,16},{1,17},{2,18},{3,19},{4,20},{5,21},{6,22},{7,23},{8,24},{9,... | collective-permute-start | bytes 196616 | tf_op jit(solution)/shard_map/ppermute | solution.py:364
  5.4 10.2 %copy-start.20 = (f32[2,4,2,17]{3,2,1,0:T(2,128)S(1)}, f32[2,4,2,17]{3,2,1,0:T(2,128)}, u32[]{:S(2)}) copy-start(f32[2,4,2,17]{3,2,1,0:T(2,128)} %param.8) | copy-start | bytes 3268
  5.4 18.6 %copy-start.17 = (s32[16]{0:T(128)S(1)}, s32[16]{0:T(128)}, u32[]{:S(2)}) copy-start(s32[16]{0:T(128)} %band_ref.9) | copy-start | bytes 196
  5.4 51.3 %all-to-all-start = ((bf16[768,16,128]{2,1,0:T(8,128)(2,1)}), bf16[768,16,128]{2,1,0:T(8,128)(2,1)S(1)}, u32[]{:S(2)}, u32[]{:S(2)}) async-start(bf16[768,16,128]{2,1,0:T(8,128)(2,1)} %bitcast.9), calls=%async_computation | async-start | bytes 6291456 | tf_op jit(solution)/shard_map/all_to_all | solution.py:403
  15.5 41.3 %copy-start.18 = (s32[2,64]{1,0:T(2,128)S(1)}, s32[2,64]{1,0:T(2,128)}, u32[]{:S(2)}) copy-start(s32[2,64]{1,0:T(2,128)} %shift_ref.3) | copy-start | bytes 1540
  15.5 41.3 %copy-start.19 = (s32[2,64]{1,0:T(2,128)S(1)}, s32[2,64]{1,0:T(2,128)}, u32[]{:S(2)}) copy-start(s32[2,64]{1,0:T(2,128)} %length_ref.3) | copy-start | bytes 1540
  15.9 1.2 %copy-start = (f32[16,128,128]{2,1,0:T(8,128)S(1)}, f32[16,128,128]{2,1,0:T(8,128)}, u32[]{:S(2)}) copy-start(f32[16,128,128]{2,1,0:T(8,128)} %estimate_ref.1) | copy-start | bytes 3145732
  17.7 33.4 %collective-permute-start.2 = (bf16[1,18,8,128]{3,2,1,0:T(8,128)(2,1)S(1)}, bf16[1,18,8,128]{3,2,1,0:T(8,128)(2,1)S(1)}, u32[]{:S(2)}, u32[]{:S(2)}) collective-permute-start(bf16[1,18,8,128]{3,2,1,0:T(8,128)(2,1)S(1)} %get-tuple-element.40), channel_id=1, source_target_pairs={{0,1},{1,0},{2,3},{3,2},{4,5},{5,4},{6,7},{7,6},{8,9},{9,8},{10,11... | collective-permute-start | bytes 110600 | tf_op jit(solution)/shard_map/ppermute | solution.py:364
  19.5 35.8 %collective-permute-start.3 = (bf16[1,18,8,128]{3,2,1,0:T(8,128)(2,1)S(1)}, bf16[1,18,8,128]{3,2,1,0:T(8,128)(2,1)S(1)}, u32[]{:S(2)}, u32[]{:S(2)}) collective-permute-start(bf16[1,18,8,128]{3,2,1,0:T(8,128)(2,1)S(1)} %get-tuple-element.41), channel_id=1, source_target_pairs={{1,2},{2,1},{3,4},{4,3},{5,6},{6,5},{7,8},{8,7},{9,10},{10,9},{11,... | collective-permute-start | bytes 110600 | tf_op jit(solution)/shard_map/ppermute | solution.py:363
  24.0 1.2 %copy-start.1 = (f32[16,128,128]{2,1,0:T(8,128)S(1)}, f32[16,128,128]{2,1,0:T(8,128)}, u32[]{:S(2)}) copy-start(f32[16,128,128]{2,1,0:T(8,128)} %estimate_ref.1) | copy-start | bytes 3145732
  36.0 1.4 %copy-start.3 = (f32[2,16,128,128]{3,2,1,0:T(8,128)}, f32[2,16,128,128]{3,2,1,0:T(8,128)S(1)}, u32[]{:S(2)}) copy-start(f32[2,16,128,128]{3,2,1,0:T(8,128)S(1)} %get-tuple-element.36.blurred_ref) | copy-start | bytes 6291460
  37.4 1.0 %copy-start.5 = (bf16[2,4,256,256]{3,2,1,0:T(8,128)(2,1)}, bf16[2,4,256,256]{3,2,1,0:T(8,128)(2,1)S(1)}, u32[]{:S(2)}) copy-start(bf16[2,4,256,256]{3,2,1,0:T(8,128)(2,1)S(1)} %get-tuple-element.30.turned_ref) | copy-start | bytes 3145732
  38.4 0.8 %copy-start.7 = (bf16[4,256,256]{2,1,0:T(8,128)(2,1)}, bf16[4,256,256]{2,1,0:T(8,128)(2,1)S(1)}, u32[]{:S(2)}) copy-start(bf16[4,256,256]{2,1,0:T(8,128)(2,1)S(1)} %get-tuple-element.32.rows_ref) | copy-start | bytes 1572868
  39.2 0.8 %copy-start.9 = (bf16[2,4,128,256]{3,2,1,0:T(8,128)(2,1)}, bf16[2,4,128,256]{3,2,1,0:T(8,128)(2,1)S(1)}, u32[]{:S(2)}) copy-start(bf16[2,4,128,256]{3,2,1,0:T(8,128)(2,1)S(1)} %get-tuple-element.34.cols_ref) | copy-start | bytes 1572868
  40.0 0.6 copy-start.11
  40.6 0.6 copy-start.13
  41.2 0.6 copy-start.15
  56.8 1.6 %copy-start.4 = (f32[2,16,128,128]{3,2,1,0:T(8,128)S(1)}, f32[2,16,128,128]{3,2,1,0:T(8,128)}, u32[]{:S(2)}) copy-start(f32[2,16,128,128]{3,2,1,0:T(8,128)} %copy-done.3) | copy-start | bytes 6291460
  56.8 1.6 %copy-start.14 = (bf16[4,2,48,128]{3,2,1,0:T(8,128)(2,1)S(1)}, bf16[4,2,48,128]{3,2,1,0:T(8,128)(2,1)}, u32[]{:S(2)}) copy-start(bf16[4,2,48,128]{3,2,1,0:T(8,128)(2,1)} %copy-done.13) | copy-start | bytes 294916
  57.6 4.6 %copy-start.8 = (bf16[4,256,256]{2,1,0:T(8,128)(2,1)S(1)}, bf16[4,256,256]{2,1,0:T(8,128)(2,1)}, u32[]{:S(2)}) copy-start(bf16[4,256,256]{2,1,0:T(8,128)(2,1)} %copy-done.7) | copy-start | bytes 1572868
  57.6 4.6 %copy-start.10 = (bf16[2,4,128,256]{3,2,1,0:T(8,128)(2,1)S(1)}, bf16[2,4,128,256]{3,2,1,0:T(8,128)(2,1)}, u32[]{:S(2)}) copy-start(bf16[2,4,128,256]{3,2,1,0:T(8,128)(2,1)} %copy-done.9) | copy-start | bytes 1572868
  57.6 4.5 %copy-start.16 = (bf16[4,32,32]{2,1,0:T(8,128)(2,1)S(1)}, bf16[4,32,32]{2,1,0:T(8,128)(2,1)}, u32[]{:S(2)}) copy-start(bf16[4,32,32]{2,1,0:T(8,128)(2,1)} %copy-done.15) | copy-start | bytes 24580
  57.6 3.0 %collective-permute-start.4 = (bf16[2,16,8,128]{3,2,1,0:T(8,128)(2,1)S(1)}, bf16[2,16,8,128]{3,2,1,0:T(8,128)(2,1)S(1)}, u32[]{:S(2)}, u32[]{:S(2)}) collective-permute-start(bf16[2,16,8,128]{3,2,1,0:T(8,128)(2,1)S(1)} %get-tuple-element.44), channel_id=1, source_target_pairs={{0,16},{1,17},{2,18},{3,19},{4,20},{5,21},{6,22},{7,23},{8,24},{9,... | collective-permute-start | bytes 196616 | tf_op jit(solution)/shard_map/ppermute | solution.py:364
  57.7 3.8 %collective-permute-start.5 = (bf16[2,16,8,128]{3,2,1,0:T(8,128)(2,1)S(1)}, bf16[2,16,8,128]{3,2,1,0:T(8,128)(2,1)S(1)}, u32[]{:S(2)}, u32[]{:S(2)}) collective-permute-start(bf16[2,16,8,128]{3,2,1,0:T(8,128)(2,1)S(1)} %get-tuple-element.45), channel_id=1, source_target_pairs={{0,1},{1,0},{2,3},{3,2},{4,5},{5,4},{6,7},{7,6},{8,9},{9,8},{10,11... | collective-permute-start | bytes 196616 | tf_op jit(solution)/shard_map/ppermute | solution.py:363
  60.5 7.8 %copy-start.2 = (f32[16,128,128]{2,1,0:T(8,128)S(1)}, f32[16,128,128]{2,1,0:T(8,128)}, u32[]{:S(2)}) copy-start(f32[16,128,128]{2,1,0:T(8,128)} %estimate_ref.1) | copy-start | bytes 3145732
  60.5 7.8 %copy-start.6 = (bf16[2,4,256,256]{3,2,1,0:T(8,128)(2,1)S(1)}, bf16[2,4,256,256]{3,2,1,0:T(8,128)(2,1)}, u32[]{:S(2)}) copy-start(bf16[2,4,256,256]{3,2,1,0:T(8,128)(2,1)} %copy-done.5) | copy-start | bytes 3145732
  60.6 7.8 %copy-start.12 = (bf16[4,2,48,128]{3,2,1,0:T(8,128)(2,1)S(1)}, bf16[4,2,48,128]{3,2,1,0:T(8,128)(2,1)}, u32[]{:S(2)}) copy-start(bf16[4,2,48,128]{3,2,1,0:T(8,128)(2,1)} %copy-done.11) | copy-start | bytes 294916
  61.6 4.4 %collective-permute-start.6 = (bf16[2,18,8,128]{3,2,1,0:T(8,128)(2,1)S(1)}, bf16[2,18,8,128]{3,2,1,0:T(8,128)(2,1)S(1)}, u32[]{:S(2)}, u32[]{:S(2)}) collective-permute-start(bf16[2,18,8,128]{3,2,1,0:T(8,128)(2,1)S(1)} %get-tuple-element.47), channel_id=1, source_target_pairs={{0,1},{1,0},{2,3},{3,2},{4,5},{5,4},{6,7},{7,6},{8,9},{9,8},{10,11... | collective-permute-start | bytes 221192 | tf_op jit(solution)/shard_map/ppermute | solution.py:364
  61.7 6.7 %collective-permute-start.7 = (bf16[2,18,8,128]{3,2,1,0:T(8,128)(2,1)S(1)}, bf16[2,18,8,128]{3,2,1,0:T(8,128)(2,1)S(1)}, u32[]{:S(2)}, u32[]{:S(2)}) collective-permute-start(bf16[2,18,8,128]{3,2,1,0:T(8,128)(2,1)S(1)} %get-tuple-element.48), channel_id=1, source_target_pairs={{0,16},{1,2},{2,1},{3,4},{4,3},{5,6},{6,5},{7,8},{8,7},{9,10},{10,... | collective-permute-start | bytes 221192 | tf_op jit(solution)/shard_map/ppermute | solution.py:363

commit v14 on v13

--- a/solution.py
+++ b/solution.py
@@ -343,7 +343,7 @@
         copy.wait()
 
 
-def swap(first, second, axis, everyone=True):
+def swap(first, second, axis):
     both = ("gx", "gy")
     rows, cols = (lax.axis_size(name) for name in both)
     count = lax.axis_size(axis)
@@ -357,7 +357,7 @@
                 i = partner(p if axis == "gx" else q, begin)
                 if 0 <= i < count:
                     found.append((at(p, q), at(i, q) if axis == "gx" else at(p, i)))
-                elif everyone:
+                else:
                     found.append((at(p, q), at(p, q ^ 1) if axis == "gx" else at(p ^ 1, q)))
         pairs.append(found)
     late = lax.ppermute(second, both, pairs[1])
@@ -407,7 +407,7 @@
     dense = lambda lead, *args: call(
         dense_slab_kernel, [SMEM] * 2 + [VMEM] * 3, (like((lead, tiles, HW, tile_rows), BF16),) * 2
     )(place_x, place_y, *args)
-    ey, oy = swap(*dense(1, cols[None], ex, ox), "gy", everyone=False)
+    ey, oy = swap(*dense(1, cols[None], ex, ox), "gy")
 
     norm = kernels / jnp.sum(kernels, axis=3, keepdims=True)
     tap_rows = jnp.stack([norm, norm[..., ::-1]])

time: 71.8 us -> 71.8 us (level)
  waiting for transfers between devices: 18.2 us -> 20.1 us
  starting transfers between devices: 19 us -> 17.1 us
    ppermute x4, waiting for transfers between devices: 10.8 us -> 12.7 us  [swap(): return (lax.ppermute(first, both, pairs[0]), late)]
    ppermute x4, starting transfers between devices: 5.91 us -> 4.04 us  [swap(): late = lax.ppermute(second, both, pairs[1])]
where the time goes in v14:
time: 71.8 us; the launch traced here: 70.7 us
  Pallas kernels  23.5 us (33%)
  waiting for transfers between devices  20.1 us (28%)
  starting transfers between devices  17.1 us (24%)
  local copies, waits for them, and re-layouts  8.45 us (12%)
  other arithmetic  1.16 us (2%)
    ppermute x4, waiting for transfers between devices, swap(): return (lax.ppermute(first, both, pairs[0]), late)  12.7 us
    pallas_call x1, Pallas kernels, body(): call(forward_kernel, [SMEM] * 2 + [VMEM] * 4, (like(measured.shape, F32),...  10.8 us
    all_to_all x1, starting transfers between devices, body(): lax.all_to_all(outgoing, ('gx', 'gy'), split_axis=0, concat_axis=0, tiled...  10 us
    unnamed x42, local copies, waits for them, and re-layouts  8.35 us
    ppermute x4, waiting for transfers between devices, swap(): late = lax.ppermute(second, both, pairs[1])  7.36 us
    ppermute x4, starting transfers between devices, swap(): late = lax.ppermute(second, both, pairs[1])  4.04 us
    ppermute x4, starting transfers between devices, swap(): return (lax.ppermute(first, both, pairs[0]), late)  3.03 us
    pallas_call x1, Pallas kernels, body(): call(functools.partial(pack_kernel, devices), [SMEM, HBM, HBM, HBM], like...  2.96 us
  transfers between devices with their start and end apart: 9, of which 5 were waited for; matrix products, arithmetic and copies ran while one was open for 1% of the time, Pallas kernels for 29%

profile of v14, /device:TPU:30, one launch (start us, length us, event | category | flops | bytes accessed | tf_op | source)
XLA Modules:
  0.0 70.7 jit_solution(6153290680741327343)
XLA Ops:
  0.0 0.9 %slice_select_fusion = (f32[16,8,128]{2,1,0:T(8,128)S(1)}, f32[16,8,128]{2,1,0:T(8,128)S(1)}) fusion(f32[16,128,128]{2,1,0:T(8,128)} %estimate_ref.1, pred[]{:T(512)S(6)} %eq.13), kind=kLoop, calls=%fused_computation | loop fusion | flops 32768 | bytes 262145 | tf_op jit(solution)/shard_map/jit(_where)/select_n | solution.py:386
  0.9 0.3 collective-permute-start.1
  1.2 1.2 %collective-permute-start = (f32[16,8,128]{2,1,0:T(8,128)S(1)}, f32[16,8,128]{2,1,0:T(8,128)S(1)}, u32[]{:S(2)}, u32[]{:S(2)}) collective-permute-start(f32[16,8,128]{2,1,0:T(8,128)S(1)} %get-tuple-element.50), channel_id=1, source_target_pairs={{0,16},{1,17},{2,18},{3,19},{4,20},{5,21},{6,22},{7,23},{8,24},{9,... | collective-permute-start | bytes 196616 | tf_op jit(solution)/shard_map/ppermute | solution.py:364
  2.4 3.0 %shard_map.64 = bf16[128,2,3,16,128]{4,3,2,1,0:T(8,128)(2,1)} custom-call(s32[1]{0:T(128)} %bitcast.4.me_ref, s32[2,64]{1,0:T(2,128)} %shift_ref.3, s32[2,64]{1,0:T(2,128)} %length_ref.3, bf16[2,16,128,128]{3,2,1,0:T(8,128)(2,1)} %measured_hbm.1), custom_call_target="tpu_custom_call" | custom-call | tf_op jit(solution)/shard_map/pallas_call | solution.py:387
  5.5 10.0 %all-to-all-start = ((bf16[768,16,128]{2,1,0:T(8,128)(2,1)}), bf16[768,16,128]{2,1,0:T(8,128)(2,1)S(1)}, u32[]{:S(2)}, u32[]{:S(2)}) async-start(bf16[768,16,128]{2,1,0:T(8,128)(2,1)} %bitcast.9), calls=%async_computation | async-start | bytes 6291456 | tf_op jit(solution)/shard_map/all_to_all | solution.py:403
  15.9 1.2 %copy-done = f32[16,128,128]{2,1,0:T(8,128)S(1)} copy-done((f32[16,128,128]{2,1,0:T(8,128)S(1)}, f32[16,128,128]{2,1,0:T(8,128)}, u32[]{:S(2)}) %copy-start) | copy-done | bytes 1048600
  17.1 0.4 shard_map.66
  17.5 0.2 shard_map.67
  17.7 1.7 %collective-permute-start.2 = (bf16[1,18,8,128]{3,2,1,0:T(8,128)(2,1)S(1)}, bf16[1,18,8,128]{3,2,1,0:T(8,128)(2,1)S(1)}, u32[]{:S(2)}, u32[]{:S(2)}) collective-permute-start(bf16[1,18,8,128]{3,2,1,0:T(8,128)(2,1)S(1)} %get-tuple-element.40), channel_id=1, source_target_pairs={{0,1},{1,0},{2,3},{3,2},{4,5},{5,4},{6,7},{7,6},{8,9},{9,8},{10,11... | collective-permute-start | bytes 110600 | tf_op jit(solution)/shard_map/ppermute | solution.py:364
  19.4 2.6 %collective-permute-start.3 = (bf16[1,18,8,128]{3,2,1,0:T(8,128)(2,1)S(1)}, bf16[1,18,8,128]{3,2,1,0:T(8,128)(2,1)S(1)}, u32[]{:S(2)}, u32[]{:S(2)}) collective-permute-start(bf16[1,18,8,128]{3,2,1,0:T(8,128)(2,1)S(1)} %get-tuple-element.41), channel_id=1, source_target_pairs={{0,16},{1,2},{2,1},{3,4},{4,3},{5,6},{6,5},{7,8},{8,7},{9,10},{10,... | collective-permute-start | bytes 110600 | tf_op jit(solution)/shard_map/ppermute | solution.py:363
  22.0 1.2 %copy-done.1 = f32[16,128,128]{2,1,0:T(8,128)S(1)} copy-done((f32[16,128,128]{2,1,0:T(8,128)S(1)}, f32[16,128,128]{2,1,0:T(8,128)}, u32[]{:S(2)}) %copy-start.1) | copy-done | bytes 1048600
  23.2 10.8 %shard_map.65 = (f32[2,16,128,128]{3,2,1,0:T(8,128)S(1)}, f32[2,16,16,128]{3,2,1,0:T(8,128)S(1)}, bf16[2,4,256,256]{3,2,1,0:T(8,128)(2,1)S(1)}, bf16[4,2,48,128]...) custom-call(s32[16]{0:T(128)S(1)} %copy-done.17, ...), custom_call_target="tpu_custom_call" | custom-call | tf_op jit(solution)/shard_map/pallas_call | solution.py:417
  34.1 1.3 %copy-done.3 = f32[2,16,128,128]{3,2,1,0:T(8,128)} copy-done((f32[2,16,128,128]{3,2,1,0:T(8,128)}, f32[2,16,128,128]{3,2,1,0:T(8,128)S(1)}, u32[]{:S(2)}) %copy-start.3) | copy-done | bytes 2097176
  35.4 1.0 %copy-done.5 = bf16[2,4,256,256]{3,2,1,0:T(8,128)(2,1)} copy-done((bf16[2,4,256,256]{3,2,1,0:T(8,128)(2,1)}, bf16[2,4,256,256]{3,2,1,0:T(8,128)(2,1)S(1)}, u32[]{:S(2)}) %copy-start.5) | copy-done | bytes 1048600
  36.4 0.8 %copy-done.7 = bf16[4,256,256]{2,1,0:T(8,128)(2,1)} copy-done((bf16[4,256,256]{2,1,0:T(8,128)(2,1)}, bf16[4,256,256]{2,1,0:T(8,128)(2,1)S(1)}, u32[]{:S(2)}) %copy-start.7) | copy-done | bytes 524312
  37.2 0.8 %copy-done.9 = bf16[2,4,128,256]{3,2,1,0:T(8,128)(2,1)} copy-done((bf16[2,4,128,256]{3,2,1,0:T(8,128)(2,1)}, bf16[2,4,128,256]{3,2,1,0:T(8,128)(2,1)S(1)}, u32[]{:S(2)}) %copy-start.9) | copy-done | bytes 524312
  38.0 0.6 copy-done.11
  38.6 0.6 copy-done.13
  39.3 0.6 copy-done.15
  39.9 11.2 %collective-permute-done.2.even_ref = bf16[1,18,8,128]{3,2,1,0:T(8,128)(2,1)S(1)} collective-permute-done((bf16[1,18,8,128]{3,2,1,0:T(8,128)(2,1)S(1)}, bf16[1,18,8,128]{3,2,1,0:T(8,128)(2,1)S(1)}, u32[]{:S(2)}, u32[]{:S(2)}) %collective-permute-start.2) | collective-permute-done | bytes 36896 | tf_op jit(solution)/shard_map/ppermute | solution.py:364
  51.1 4.1 %collective-permute-done.3.other_ref = bf16[1,18,8,128]{3,2,1,0:T(8,128)(2,1)S(1)} collective-permute-done((bf16[1,18,8,128]{3,2,1,0:T(8,128)(2,1)S(1)}, bf16[1,18,8,128]{3,2,1,0:T(8,128)(2,1)S(1)}, u32[]{:S(2)}, u32[]{:S(2)}) %collective-permute-start.3) | collective-permute-done | bytes 36896 | tf_op jit(solution)/shard_map/ppermute | solution.py:363
  55.2 1.5 %shard_map.68.parts_ref.edge_ref = bf16[2,16,48,128]{3,2,1,0:T(8,128)(2,1)S(1)} custom-call(s32[16]{0:T(128)S(1)} %copy-done.17, s32[1]{0:T(128)} %bitcast.place_y_ref.place_ref, bf16[2,4,256,256]{3,2,1,0:T(8,128)(2,1)S(1)} %get-tuple-element.38.turned_ref, bf16[4,2,48,128]{3,2,1,0:T(8,128)(2,1)S(1)} %get-tuple-element.39.far_ref, ...), custom_call_target="tpu_custom_call" | custom-call | tf_op jit(solution)/shard_map/pallas_call | solution.py:438
  56.8 0.7 %shard_map.70 = (bf16[2,16,8,128]{3,2,1,0:T(8,128)(2,1)S(1)}, bf16[2,16,8,128]{3,2,1,0:T(8,128)(2,1)S(1)}) custom-call(s32[1]{0:T(128)} %bitcast.4.me_ref, s32[1]{0:T(128)} %bitcast.1.place_ref.place_x_ref, s32[2,64]{1,0:T(2,128)S(1)} %copy-done.18, s32[2,64]{1,0:T(2,128)S(1)} %copy-done.19, bf16[768,16,128]{2,1,0:T(8,128)(2,1)S(1)} %all-to-all-done.arrived_ref, ...), custom_call_target="tpu_custom_call" | custom-call | tf_op jit(solution)/shard_map/pallas_call | solution.py:448
  57.6 0.7 collective-permute-start.5
  58.3 2.2 %shard_map.69 = (bf16[2,16,128,128]{3,2,1,0:T(8,128)(2,1)S(1)}, bf16[2,16,16,128]{3,2,1,0:T(8,128)(2,1)S(1)}) custom-call(s32[1]{0:T(128)} %bitcast.4.me_ref, s32[16]{0:T(128)S(1)} %copy-done.17, s32[2,64]{1,0:T(2,128)S(1)} %copy-done.18, s32[2,64]{1,0:T(2,128)S(1)} %copy-done.19, bf16[768,16,128]{2,1,0:T(8,128)(2,1)S(1)} %all-to-all-done.arrived_ref, ...), custom_call_target="tpu_custom_call" | custom-call | tf_op jit(solution)/shard_map/pallas_call | solution.py:455
  60.5 0.9 %collective-permute-done.5.other_ref = bf16[2,16,8,128]{3,2,1,0:T(8,128)(2,1)S(1)} collective-permute-done((bf16[2,16,8,128]{3,2,1,0:T(8,128)(2,1)S(1)}, bf16[2,16,8,128]{3,2,1,0:T(8,128)(2,1)S(1)}, u32[]{:S(2)}, u32[]{:S(2)}) %collective-permute-start.5) | collective-permute-done | bytes 65568 | tf_op jit(solution)/shard_map/ppermute | solution.py:363
  61.4 0.2 shard_map.72
  61.6 0.5 collective-permute-start.7
  62.1 2.3 %shard_map.71.near_ref = f32[16,128,128]{2,1,0:T(8,128)S(1)} custom-call(s32[16]{0:T(128)S(1)} %copy-done.17, s32[1]{0:T(128)} %bitcast.1.place_ref.place_x_ref, bf16[4,256,256]{2,1,0:T(8,128)(2,1)S(1)} %copy-done.8, bf16[4,32,32]{2,1,0:T(8,128)(2,1)S(1)} %copy-done.16, bf16[2,4,128,256]{3,2,1,0:T(8,128)(2,1)S(1)} %copy-done.10, ...), custom_call_target="tpu_custom_call" | custom-call | tf_op jit(solution)/shard_map/pallas_call | solution.py:462
  64.4 1.5 %collective-permute-done.6.even_ref = bf16[2,18,8,128]{3,2,1,0:T(8,128)(2,1)S(1)} collective-permute-done((bf16[2,18,8,128]{3,2,1,0:T(8,128)(2,1)S(1)}, bf16[2,18,8,128]{3,2,1,0:T(8,128)(2,1)S(1)}, u32[]{:S(2)}, u32[]{:S(2)}) %collective-permute-start.6) | collective-permute-done | bytes 73760 | tf_op jit(solution)/shard_map/ppermute | solution.py:364
  66.0 2.4 %collective-permute-done.7.other_ref = bf16[2,18,8,128]{3,2,1,0:T(8,128)(2,1)S(1)} collective-permute-done((bf16[2,18,8,128]{3,2,1,0:T(8,128)(2,1)S(1)}, bf16[2,18,8,128]{3,2,1,0:T(8,128)(2,1)S(1)}, u32[]{:S(2)}, u32[]{:S(2)}) %collective-permute-start.7) | collective-permute-done | bytes 73760 | tf_op jit(solution)/shard_map/ppermute | solution.py:363
  68.3 2.2 %shard_map.73 = f32[16,128,128]{2,1,0:T(8,128)} custom-call(s32[16]{0:T(128)S(1)} %copy-done.17, s32[1]{0:T(128)} %bitcast.place_y_ref.place_ref, bf16[2,4,256,256]{3,2,1,0:T(8,128)(2,1)S(1)} %copy-done.6, bf16[4,2,48,128]{3,2,1,0:T(8,128)(2,1)S(1)} %copy-done.12, f32[16,128,128]{2,1,0:T(8,128)S(1)} %shard_map.71.near_ref, ...), custom_call_target="tpu_custom_call" | custom-call | tf_op jit(solution)/shard_map/pallas_call | solution.py:471
  (44 shorter events, 0.6 us)
Async XLA Ops:
  0.9 4.5 %collective-permute-start.1 = (f32[16,8,128]{2,1,0:T(8,128)S(1)}, f32[16,8,128]{2,1,0:T(8,128)S(1)}, u32[]{:S(2)}, u32[]{:S(2)}) collective-permute-start(f32[16,8,128]{2,1,0:T(8,128)S(1)} %get-tuple-element.49), channel_id=1, source_target_pairs={{0,1},{1,0},{2,3},{3,2},{4,5},{5,4},{6,7},{7,6},{8,9},{9,8},{10,11... | collective-permute-start | bytes 196616 | tf_op jit(solution)/shard_map/ppermute | solution.py:363
  1.2 4.2 %collective-permute-start = (f32[16,8,128]{2,1,0:T(8,128)S(1)}, f32[16,8,128]{2,1,0:T(8,128)S(1)}, u32[]{:S(2)}, u32[]{:S(2)}) collective-permute-start(f32[16,8,128]{2,1,0:T(8,128)S(1)} %get-tuple-element.50), channel_id=1, source_target_pairs={{0,16},{1,17},{2,18},{3,19},{4,20},{5,21},{6,22},{7,23},{8,24},{9,... | collective-permute-start | bytes 196616 | tf_op jit(solution)/shard_map/ppermute | solution.py:364
  5.4 10.1 %copy-start.20 = (f32[2,4,2,17]{3,2,1,0:T(2,128)S(1)}, f32[2,4,2,17]{3,2,1,0:T(2,128)}, u32[]{:S(2)}) copy-start(f32[2,4,2,17]{3,2,1,0:T(2,128)} %param.8) | copy-start | bytes 3268
  5.4 16.6 %copy-start.17 = (s32[16]{0:T(128)S(1)}, s32[16]{0:T(128)}, u32[]{:S(2)}) copy-start(s32[16]{0:T(128)} %band_ref.9) | copy-start | bytes 196
  5.5 51.3 %all-to-all-start = ((bf16[768,16,128]{2,1,0:T(8,128)(2,1)}), bf16[768,16,128]{2,1,0:T(8,128)(2,1)S(1)}, u32[]{:S(2)}, u32[]{:S(2)}) async-start(bf16[768,16,128]{2,1,0:T(8,128)(2,1)} %bitcast.9), calls=%async_computation | async-start | bytes 6291456 | tf_op jit(solution)/shard_map/all_to_all | solution.py:403
  15.5 41.2 %copy-start.18 = (s32[2,64]{1,0:T(2,128)S(1)}, s32[2,64]{1,0:T(2,128)}, u32[]{:S(2)}) copy-start(s32[2,64]{1,0:T(2,128)} %shift_ref.3) | copy-start | bytes 1540
  15.5 41.2 %copy-start.19 = (s32[2,64]{1,0:T(2,128)S(1)}, s32[2,64]{1,0:T(2,128)}, u32[]{:S(2)}) copy-start(s32[2,64]{1,0:T(2,128)} %length_ref.3) | copy-start | bytes 1540
  15.9 1.2 %copy-start = (f32[16,128,128]{2,1,0:T(8,128)S(1)}, f32[16,128,128]{2,1,0:T(8,128)}, u32[]{:S(2)}) copy-start(f32[16,128,128]{2,1,0:T(8,128)} %estimate_ref.1) | copy-start | bytes 3145732
  17.7 33.4 %collective-permute-start.2 = (bf16[1,18,8,128]{3,2,1,0:T(8,128)(2,1)S(1)}, bf16[1,18,8,128]{3,2,1,0:T(8,128)(2,1)S(1)}, u32[]{:S(2)}, u32[]{:S(2)}) collective-permute-start(bf16[1,18,8,128]{3,2,1,0:T(8,128)(2,1)S(1)} %get-tuple-element.40), channel_id=1, source_target_pairs={{0,1},{1,0},{2,3},{3,2},{4,5},{5,4},{6,7},{7,6},{8,9},{9,8},{10,11... | collective-permute-start | bytes 110600 | tf_op jit(solution)/shard_map/ppermute | solution.py:364
  19.4 35.8 %collective-permute-start.3 = (bf16[1,18,8,128]{3,2,1,0:T(8,128)(2,1)S(1)}, bf16[1,18,8,128]{3,2,1,0:T(8,128)(2,1)S(1)}, u32[]{:S(2)}, u32[]{:S(2)}) collective-permute-start(bf16[1,18,8,128]{3,2,1,0:T(8,128)(2,1)S(1)} %get-tuple-element.41), channel_id=1, source_target_pairs={{0,16},{1,2},{2,1},{3,4},{4,3},{5,6},{6,5},{7,8},{8,7},{9,10},{10,... | collective-permute-start | bytes 110600 | tf_op jit(solution)/shard_map/ppermute | solution.py:363
  22.0 1.2 %copy-start.1 = (f32[16,128,128]{2,1,0:T(8,128)S(1)}, f32[16,128,128]{2,1,0:T(8,128)}, u32[]{:S(2)}) copy-start(f32[16,128,128]{2,1,0:T(8,128)} %estimate_ref.1) | copy-start | bytes 3145732
  34.1 1.4 %copy-start.3 = (f32[2,16,128,128]{3,2,1,0:T(8,128)}, f32[2,16,128,128]{3,2,1,0:T(8,128)S(1)}, u32[]{:S(2)}) copy-start(f32[2,16,128,128]{3,2,1,0:T(8,128)S(1)} %get-tuple-element.36.blurred_ref) | copy-start | bytes 6291460
  35.4 1.0 %copy-start.5 = (bf16[2,4,256,256]{3,2,1,0:T(8,128)(2,1)}, bf16[2,4,256,256]{3,2,1,0:T(8,128)(2,1)S(1)}, u32[]{:S(2)}) copy-start(bf16[2,4,256,256]{3,2,1,0:T(8,128)(2,1)S(1)} %get-tuple-element.30.turned_ref) | copy-start | bytes 3145732
  36.4 0.8 %copy-start.7 = (bf16[4,256,256]{2,1,0:T(8,128)(2,1)}, bf16[4,256,256]{2,1,0:T(8,128)(2,1)S(1)}, u32[]{:S(2)}) copy-start(bf16[4,256,256]{2,1,0:T(8,128)(2,1)S(1)} %get-tuple-element.32.rows_ref) | copy-start | bytes 1572868
  37.2 0.8 %copy-start.9 = (bf16[2,4,128,256]{3,2,1,0:T(8,128)(2,1)}, bf16[2,4,128,256]{3,2,1,0:T(8,128)(2,1)S(1)}, u32[]{:S(2)}) copy-start(bf16[2,4,128,256]{3,2,1,0:T(8,128)(2,1)S(1)} %get-tuple-element.34.cols_ref) | copy-start | bytes 1572868
  38.0 0.6 copy-start.11
  38.6 0.6 copy-start.13
  39.3 0.6 copy-start.15
  56.7 1.6 %copy-start.4 = (f32[2,16,128,128]{3,2,1,0:T(8,128)S(1)}, f32[2,16,128,128]{3,2,1,0:T(8,128)}, u32[]{:S(2)}) copy-start(f32[2,16,128,128]{3,2,1,0:T(8,128)} %copy-done.3) | copy-start | bytes 6291460
  56.7 1.6 %copy-start.14 = (bf16[4,2,48,128]{3,2,1,0:T(8,128)(2,1)S(1)}, bf16[4,2,48,128]{3,2,1,0:T(8,128)(2,1)}, u32[]{:S(2)}) copy-start(bf16[4,2,48,128]{3,2,1,0:T(8,128)(2,1)} %copy-done.13) | copy-start | bytes 294916
  57.5 4.6 %copy-start.8 = (bf16[4,256,256]{2,1,0:T(8,128)(2,1)S(1)}, bf16[4,256,256]{2,1,0:T(8,128)(2,1)}, u32[]{:S(2)}) copy-start(bf16[4,256,256]{2,1,0:T(8,128)(2,1)} %copy-done.7) | copy-start | bytes 1572868
  57.5 4.6 %copy-start.10 = (bf16[2,4,128,256]{3,2,1,0:T(8,128)(2,1)S(1)}, bf16[2,4,128,256]{3,2,1,0:T(8,128)(2,1)}, u32[]{:S(2)}) copy-start(bf16[2,4,128,256]{3,2,1,0:T(8,128)(2,1)} %copy-done.9) | copy-start | bytes 1572868
  57.5 4.6 %copy-start.16 = (bf16[4,32,32]{2,1,0:T(8,128)(2,1)S(1)}, bf16[4,32,32]{2,1,0:T(8,128)(2,1)}, u32[]{:S(2)}) copy-start(bf16[4,32,32]{2,1,0:T(8,128)(2,1)} %copy-done.15) | copy-start | bytes 24580
  57.5 3.0 %collective-permute-start.4 = (bf16[2,16,8,128]{3,2,1,0:T(8,128)(2,1)S(1)}, bf16[2,16,8,128]{3,2,1,0:T(8,128)(2,1)S(1)}, u32[]{:S(2)}, u32[]{:S(2)}) collective-permute-start(bf16[2,16,8,128]{3,2,1,0:T(8,128)(2,1)S(1)} %get-tuple-element.44), channel_id=1, source_target_pairs={{0,16},{1,17},{2,18},{3,19},{4,20},{5,21},{6,22},{7,23},{8,24},{9,... | collective-permute-start | bytes 196616 | tf_op jit(solution)/shard_map/ppermute | solution.py:364
  57.6 3.8 %collective-permute-start.5 = (bf16[2,16,8,128]{3,2,1,0:T(8,128)(2,1)S(1)}, bf16[2,16,8,128]{3,2,1,0:T(8,128)(2,1)S(1)}, u32[]{:S(2)}, u32[]{:S(2)}) collective-permute-start(bf16[2,16,8,128]{3,2,1,0:T(8,128)(2,1)S(1)} %get-tuple-element.45), channel_id=1, source_target_pairs={{0,1},{1,0},{2,3},{3,2},{4,5},{5,4},{6,7},{7,6},{8,9},{9,8},{10,11... | collective-permute-start | bytes 196616 | tf_op jit(solution)/shard_map/ppermute | solution.py:363
  60.5 7.8 %copy-start.2 = (f32[16,128,128]{2,1,0:T(8,128)S(1)}, f32[16,128,128]{2,1,0:T(8,128)}, u32[]{:S(2)}) copy-start(f32[16,128,128]{2,1,0:T(8,128)} %estimate_ref.1) | copy-start | bytes 3145732
  60.5 7.8 %copy-start.6 = (bf16[2,4,256,256]{3,2,1,0:T(8,128)(2,1)S(1)}, bf16[2,4,256,256]{3,2,1,0:T(8,128)(2,1)}, u32[]{:S(2)}) copy-start(bf16[2,4,256,256]{3,2,1,0:T(8,128)(2,1)} %copy-done.5) | copy-start | bytes 3145732
  60.5 7.8 %copy-start.12 = (bf16[4,2,48,128]{3,2,1,0:T(8,128)(2,1)S(1)}, bf16[4,2,48,128]{3,2,1,0:T(8,128)(2,1)}, u32[]{:S(2)}) copy-start(bf16[4,2,48,128]{3,2,1,0:T(8,128)(2,1)} %copy-done.11) | copy-start | bytes 294916
  61.6 4.4 %collective-permute-start.6 = (bf16[2,18,8,128]{3,2,1,0:T(8,128)(2,1)S(1)}, bf16[2,18,8,128]{3,2,1,0:T(8,128)(2,1)S(1)}, u32[]{:S(2)}, u32[]{:S(2)}) collective-permute-start(bf16[2,18,8,128]{3,2,1,0:T(8,128)(2,1)S(1)} %get-tuple-element.47), channel_id=1, source_target_pairs={{0,1},{1,0},{2,3},{3,2},{4,5},{5,4},{6,7},{7,6},{8,9},{9,8},{10,11... | collective-permute-start | bytes 221192 | tf_op jit(solution)/shard_map/ppermute | solution.py:364
  61.6 6.7 %collective-permute-start.7 = (bf16[2,18,8,128]{3,2,1,0:T(8,128)(2,1)S(1)}, bf16[2,18,8,128]{3,2,1,0:T(8,128)(2,1)S(1)}, u32[]{:S(2)}, u32[]{:S(2)}) collective-permute-start(bf16[2,18,8,128]{3,2,1,0:T(8,128)(2,1)S(1)} %get-tuple-element.48), channel_id=1, source_target_pairs={{0,16},{1,2},{2,1},{3,4},{4,3},{5,6},{6,5},{7,8},{8,7},{9,10},{10,... | collective-permute-start | bytes 221192 | tf_op jit(solution)/shard_map/ppermute | solution.py:363

commit v15 on v13

--- a/solution.py
+++ b/solution.py
@@ -91,25 +91,32 @@
     sub = lax.broadcasted_iota(jnp.int32, (tile_cols, tile_cols), 0)
     turn = (lane + sub == tile_cols - 1).astype(BF16)
     me = me_ref[0]
+
+    def leave(view, begin, end, start):
+        for g in range(begin, end):
+            peer = lax.rem(me + shift_ref[view, g], devices)
+            blocks = rows_ref.at[view, pl.ds(start, CAP)]
+            pltpu.make_async_copy(blocks, out_hbm.at[peer, view], sems.at[views + 2 + view]).start()
+            start = start + length_ref[view, g]
+        return start
+
+    share = groups * 16 // tile_rows
     for view in range(views):
         loads[view].wait()
+        start = 0
         for r0 in range(0, tile_rows, 16):
             x = measured_ref[view, :, r0 : r0 + 16, :]
             if view % 2 == 1:
                 x = dot(x.reshape(depth * 16, tile_cols), turn).reshape(depth, 16, tile_cols)
             x = jnp.transpose(x.astype(F32), (1, 0, 2))
             rows_ref[view, r0 : r0 + 16] = x.astype(BF16)
+            if view > 0:
+                at = r0 // 16 * share
+                start = leave(view - 1, at, at + share, start)
         if view == 0:
             for copy in tables:
                 copy.wait()
-
-        def group(g, start, view=view):
-            peer = lax.rem(me + shift_ref[view, g], devices)
-            blocks = rows_ref.at[view, pl.ds(start, CAP)]
-            pltpu.make_async_copy(blocks, out_hbm.at[peer, view], sems.at[views + 2 + view]).start()
-            return start + length_ref[view, g]
-
-        lax.fori_loop(0, groups, group, 0, unroll=True)
+    leave(views - 1, 0, groups, 0)
     for view in range(views):
         sent = out_hbm.at[pl.ds(0, groups), view]
         pltpu.make_async_copy(sent, sent, sems.at[views + 2 + view]).wait()

time: 71.8 us -> 71.7 us (level)
  no operation moved by 1% of the time
where the time goes in v15:
time: 71.7 us; the launch traced here: 70.7 us
  Pallas kernels  23.4 us (33%)
  starting transfers between devices  18.9 us (26%)
  waiting for transfers between devices  18.2 us (25%)
  local copies, waits for them, and re-layouts  8.46 us (12%)
  other arithmetic  1.16 us (2%)
    ppermute x4, waiting for transfers between devices, swap(): return (lax.ppermute(first, both, pairs[0]), late)  10.8 us
    pallas_call x1, Pallas kernels, body(): call(forward_kernel, [SMEM] * 2 + [VMEM] * 4, (like(measured.shape, F32),...  10.8 us
    all_to_all x1, starting transfers between devices, body(): lax.all_to_all(outgoing, ('gx', 'gy'), split_axis=0, concat_axis=0, tiled...  10 us
    unnamed x42, local copies, waits for them, and re-layouts  8.36 us
    ppermute x4, waiting for transfers between devices, swap(): late = lax.ppermute(second, both, pairs[1])  7.37 us
    ppermute x4, starting transfers between devices, swap(): late = lax.ppermute(second, both, pairs[1])  5.91 us
    ppermute x4, starting transfers between devices, swap(): return (lax.ppermute(first, both, pairs[0]), late)  3.03 us
    pallas_call x1, Pallas kernels, body(): call(functools.partial(pack_kernel, devices), [SMEM, HBM, HBM, HBM], like...  2.92 us
  transfers between devices with their start and end apart: 9, of which 5 were waited for; matrix products, arithmetic and copies ran while one was open for 1% of the time, Pallas kernels for 29%

profile of v15, /device:TPU:30, one launch (start us, length us, event | category | flops | bytes accessed | tf_op | source)
XLA Modules:
  0.0 70.7 jit_solution(1264259001721312378)
XLA Ops:
  0.0 0.9 %slice_select_fusion = (f32[16,8,128]{2,1,0:T(8,128)S(1)}, f32[16,8,128]{2,1,0:T(8,128)S(1)}) fusion(f32[16,128,128]{2,1,0:T(8,128)} %estimate_ref.1, pred[]{:T(512)S(6)} %eq.13), kind=kLoop, calls=%fused_computation | loop fusion | flops 32768 | bytes 262145 | tf_op jit(solution)/shard_map/jit(_where)/select_n | solution.py:393
  0.9 0.3 collective-permute-start.1
  1.2 1.2 %collective-permute-start = (f32[16,8,128]{2,1,0:T(8,128)S(1)}, f32[16,8,128]{2,1,0:T(8,128)S(1)}, u32[]{:S(2)}, u32[]{:S(2)}) collective-permute-start(f32[16,8,128]{2,1,0:T(8,128)S(1)} %get-tuple-element.50), channel_id=1, source_target_pairs={{0,16},{1,17},{2,18},{3,19},{4,20},{5,21},{6,22},{7,23},{8,24},{9,... | collective-permute-start | bytes 196616 | tf_op jit(solution)/shard_map/ppermute | solution.py:371
  2.4 2.9 %shard_map.64 = bf16[128,2,3,16,128]{4,3,2,1,0:T(8,128)(2,1)} custom-call(s32[1]{0:T(128)} %bitcast.4.me_ref, s32[2,64]{1,0:T(2,128)} %shift_ref.3, s32[2,64]{1,0:T(2,128)} %length_ref.3, bf16[2,16,128,128]{3,2,1,0:T(8,128)(2,1)} %measured_hbm.1), custom_call_target="tpu_custom_call" | custom-call | tf_op jit(solution)/shard_map/pallas_call | solution.py:394
  5.4 10.0 %all-to-all-start = ((bf16[768,16,128]{2,1,0:T(8,128)(2,1)}), bf16[768,16,128]{2,1,0:T(8,128)(2,1)S(1)}, u32[]{:S(2)}, u32[]{:S(2)}) async-start(bf16[768,16,128]{2,1,0:T(8,128)(2,1)} %bitcast.9), calls=%async_computation | async-start | bytes 6291456 | tf_op jit(solution)/shard_map/all_to_all | solution.py:410
  15.9 1.2 %copy-done = f32[16,128,128]{2,1,0:T(8,128)S(1)} copy-done((f32[16,128,128]{2,1,0:T(8,128)S(1)}, f32[16,128,128]{2,1,0:T(8,128)}, u32[]{:S(2)}) %copy-start) | copy-done | bytes 1048600
  17.1 0.4 shard_map.66
  17.4 0.2 shard_map.67
  17.6 1.7 %collective-permute-start.2 = (bf16[1,18,8,128]{3,2,1,0:T(8,128)(2,1)S(1)}, bf16[1,18,8,128]{3,2,1,0:T(8,128)(2,1)S(1)}, u32[]{:S(2)}, u32[]{:S(2)}) collective-permute-start(bf16[1,18,8,128]{3,2,1,0:T(8,128)(2,1)S(1)} %get-tuple-element.40), channel_id=1, source_target_pairs={{0,1},{1,0},{2,3},{3,2},{4,5},{5,4},{6,7},{7,6},{8,9},{9,8},{10,11... | collective-permute-start | bytes 110600 | tf_op jit(solution)/shard_map/ppermute | solution.py:371
  19.4 4.5 %collective-permute-start.3 = (bf16[1,18,8,128]{3,2,1,0:T(8,128)(2,1)S(1)}, bf16[1,18,8,128]{3,2,1,0:T(8,128)(2,1)S(1)}, u32[]{:S(2)}, u32[]{:S(2)}) collective-permute-start(bf16[1,18,8,128]{3,2,1,0:T(8,128)(2,1)S(1)} %get-tuple-element.41), channel_id=1, source_target_pairs={{1,2},{2,1},{3,4},{4,3},{5,6},{6,5},{7,8},{8,7},{9,10},{10,9},{11,... | collective-permute-start | bytes 110600 | tf_op jit(solution)/shard_map/ppermute | solution.py:370
  23.9 1.2 %copy-done.1 = f32[16,128,128]{2,1,0:T(8,128)S(1)} copy-done((f32[16,128,128]{2,1,0:T(8,128)S(1)}, f32[16,128,128]{2,1,0:T(8,128)}, u32[]{:S(2)}) %copy-start.1) | copy-done | bytes 1048600
  25.1 10.8 %shard_map.65 = (f32[2,16,128,128]{3,2,1,0:T(8,128)S(1)}, f32[2,16,16,128]{3,2,1,0:T(8,128)S(1)}, bf16[2,4,256,256]{3,2,1,0:T(8,128)(2,1)S(1)}, bf16[4,2,48,128]...) custom-call(s32[16]{0:T(128)S(1)} %copy-done.17, ...), custom_call_target="tpu_custom_call" | custom-call | tf_op jit(solution)/shard_map/pallas_call | solution.py:424
  35.9 1.3 %copy-done.3 = f32[2,16,128,128]{3,2,1,0:T(8,128)} copy-done((f32[2,16,128,128]{3,2,1,0:T(8,128)}, f32[2,16,128,128]{3,2,1,0:T(8,128)S(1)}, u32[]{:S(2)}) %copy-start.3) | copy-done | bytes 2097176
  37.3 1.0 %copy-done.5 = bf16[2,4,256,256]{3,2,1,0:T(8,128)(2,1)} copy-done((bf16[2,4,256,256]{3,2,1,0:T(8,128)(2,1)}, bf16[2,4,256,256]{3,2,1,0:T(8,128)(2,1)S(1)}, u32[]{:S(2)}) %copy-start.5) | copy-done | bytes 1048600
  38.3 0.8 %copy-done.7 = bf16[4,256,256]{2,1,0:T(8,128)(2,1)} copy-done((bf16[4,256,256]{2,1,0:T(8,128)(2,1)}, bf16[4,256,256]{2,1,0:T(8,128)(2,1)S(1)}, u32[]{:S(2)}) %copy-start.7) | copy-done | bytes 524312
  39.1 0.8 %copy-done.9 = bf16[2,4,128,256]{3,2,1,0:T(8,128)(2,1)} copy-done((bf16[2,4,128,256]{3,2,1,0:T(8,128)(2,1)}, bf16[2,4,128,256]{3,2,1,0:T(8,128)(2,1)S(1)}, u32[]{:S(2)}) %copy-start.9) | copy-done | bytes 524312
  39.9 0.6 copy-done.11
  40.5 0.6 copy-done.13
  41.1 0.6 copy-done.15
  41.8 9.3 %collective-permute-done.2.even_ref = bf16[1,18,8,128]{3,2,1,0:T(8,128)(2,1)S(1)} collective-permute-done((bf16[1,18,8,128]{3,2,1,0:T(8,128)(2,1)S(1)}, bf16[1,18,8,128]{3,2,1,0:T(8,128)(2,1)S(1)}, u32[]{:S(2)}, u32[]{:S(2)}) %collective-permute-start.2) | collective-permute-done | bytes 36896 | tf_op jit(solution)/shard_map/ppermute | solution.py:371
  51.0 4.1 %collective-permute-done.3.other_ref = bf16[1,18,8,128]{3,2,1,0:T(8,128)(2,1)S(1)} collective-permute-done((bf16[1,18,8,128]{3,2,1,0:T(8,128)(2,1)S(1)}, bf16[1,18,8,128]{3,2,1,0:T(8,128)(2,1)S(1)}, u32[]{:S(2)}, u32[]{:S(2)}) %collective-permute-start.3) | collective-permute-done | bytes 36896 | tf_op jit(solution)/shard_map/ppermute | solution.py:370
  55.2 1.5 %shard_map.68.parts_ref.edge_ref = bf16[2,16,48,128]{3,2,1,0:T(8,128)(2,1)S(1)} custom-call(s32[16]{0:T(128)S(1)} %copy-done.17, s32[1]{0:T(128)} %bitcast.place_y_ref.place_ref, bf16[2,4,256,256]{3,2,1,0:T(8,128)(2,1)S(1)} %get-tuple-element.38.turned_ref, bf16[4,2,48,128]{3,2,1,0:T(8,128)(2,1)S(1)} %get-tuple-element.39.far_ref, ...), custom_call_target="tpu_custom_call" | custom-call | tf_op jit(solution)/shard_map/pallas_call | solution.py:445
  56.7 0.7 %shard_map.70 = (bf16[2,16,8,128]{3,2,1,0:T(8,128)(2,1)S(1)}, bf16[2,16,8,128]{3,2,1,0:T(8,128)(2,1)S(1)}) custom-call(s32[1]{0:T(128)} %bitcast.4.me_ref, s32[1]{0:T(128)} %bitcast.1.place_ref.place_x_ref, s32[2,64]{1,0:T(2,128)S(1)} %copy-done.18, s32[2,64]{1,0:T(2,128)S(1)} %copy-done.19, bf16[768,16,128]{2,1,0:T(8,128)(2,1)S(1)} %all-to-all-done.arrived_ref, ...), custom_call_target="tpu_custom_call" | custom-call | tf_op jit(solution)/shard_map/pallas_call | solution.py:455
  57.6 0.6 collective-permute-start.5
  58.3 2.2 %shard_map.69 = (bf16[2,16,128,128]{3,2,1,0:T(8,128)(2,1)S(1)}, bf16[2,16,16,128]{3,2,1,0:T(8,128)(2,1)S(1)}) custom-call(s32[1]{0:T(128)} %bitcast.4.me_ref, s32[16]{0:T(128)S(1)} %copy-done.17, s32[2,64]{1,0:T(2,128)S(1)} %copy-done.18, s32[2,64]{1,0:T(2,128)S(1)} %copy-done.19, bf16[768,16,128]{2,1,0:T(8,128)(2,1)S(1)} %all-to-all-done.arrived_ref, ...), custom_call_target="tpu_custom_call" | custom-call | tf_op jit(solution)/shard_map/pallas_call | solution.py:462
  60.5 0.9 %collective-permute-done.5.other_ref = bf16[2,16,8,128]{3,2,1,0:T(8,128)(2,1)S(1)} collective-permute-done((bf16[2,16,8,128]{3,2,1,0:T(8,128)(2,1)S(1)}, bf16[2,16,8,128]{3,2,1,0:T(8,128)(2,1)S(1)}, u32[]{:S(2)}, u32[]{:S(2)}) %collective-permute-start.5) | collective-permute-done | bytes 65568 | tf_op jit(solution)/shard_map/ppermute | solution.py:370
  61.4 0.2 shard_map.72
  61.6 0.5 collective-permute-start.7
  62.0 2.3 %shard_map.71.near_ref = f32[16,128,128]{2,1,0:T(8,128)S(1)} custom-call(s32[16]{0:T(128)S(1)} %copy-done.17, s32[1]{0:T(128)} %bitcast.1.place_ref.place_x_ref, bf16[4,256,256]{2,1,0:T(8,128)(2,1)S(1)} %copy-done.8, bf16[4,32,32]{2,1,0:T(8,128)(2,1)S(1)} %copy-done.16, bf16[2,4,128,256]{3,2,1,0:T(8,128)(2,1)S(1)} %copy-done.10, ...), custom_call_target="tpu_custom_call" | custom-call | tf_op jit(solution)/shard_map/pallas_call | solution.py:469
  64.4 1.5 %collective-permute-done.6.even_ref = bf16[2,18,8,128]{3,2,1,0:T(8,128)(2,1)S(1)} collective-permute-done((bf16[2,18,8,128]{3,2,1,0:T(8,128)(2,1)S(1)}, bf16[2,18,8,128]{3,2,1,0:T(8,128)(2,1)S(1)}, u32[]{:S(2)}, u32[]{:S(2)}) %collective-permute-start.6) | collective-permute-done | bytes 73760 | tf_op jit(solution)/shard_map/ppermute | solution.py:371
  65.9 2.4 %collective-permute-done.7.other_ref = bf16[2,18,8,128]{3,2,1,0:T(8,128)(2,1)S(1)} collective-permute-done((bf16[2,18,8,128]{3,2,1,0:T(8,128)(2,1)S(1)}, bf16[2,18,8,128]{3,2,1,0:T(8,128)(2,1)S(1)}, u32[]{:S(2)}, u32[]{:S(2)}) %collective-permute-start.7) | collective-permute-done | bytes 73760 | tf_op jit(solution)/shard_map/ppermute | solution.py:370
  68.3 2.2 %shard_map.73 = f32[16,128,128]{2,1,0:T(8,128)} custom-call(s32[16]{0:T(128)S(1)} %copy-done.17, s32[1]{0:T(128)} %bitcast.place_y_ref.place_ref, bf16[2,4,256,256]{3,2,1,0:T(8,128)(2,1)S(1)} %copy-done.6, bf16[4,2,48,128]{3,2,1,0:T(8,128)(2,1)S(1)} %copy-done.12, f32[16,128,128]{2,1,0:T(8,128)S(1)} %shard_map.71.near_ref, ...), custom_call_target="tpu_custom_call" | custom-call | tf_op jit(solution)/shard_map/pallas_call | solution.py:478
  (44 shorter events, 0.6 us)
Async XLA Ops:
  0.9 4.5 %collective-permute-start.1 = (f32[16,8,128]{2,1,0:T(8,128)S(1)}, f32[16,8,128]{2,1,0:T(8,128)S(1)}, u32[]{:S(2)}, u32[]{:S(2)}) collective-permute-start(f32[16,8,128]{2,1,0:T(8,128)S(1)} %get-tuple-element.49), channel_id=1, source_target_pairs={{0,1},{1,0},{2,3},{3,2},{4,5},{5,4},{6,7},{7,6},{8,9},{9,8},{10,11... | collective-permute-start | bytes 196616 | tf_op jit(solution)/shard_map/ppermute | solution.py:370
  1.2 4.1 %collective-permute-start = (f32[16,8,128]{2,1,0:T(8,128)S(1)}, f32[16,8,128]{2,1,0:T(8,128)S(1)}, u32[]{:S(2)}, u32[]{:S(2)}) collective-permute-start(f32[16,8,128]{2,1,0:T(8,128)S(1)} %get-tuple-element.50), channel_id=1, source_target_pairs={{0,16},{1,17},{2,18},{3,19},{4,20},{5,21},{6,22},{7,23},{8,24},{9,... | collective-permute-start | bytes 196616 | tf_op jit(solution)/shard_map/ppermute | solution.py:371
  5.4 10.1 %copy-start.20 = (f32[2,4,2,17]{3,2,1,0:T(2,128)S(1)}, f32[2,4,2,17]{3,2,1,0:T(2,128)}, u32[]{:S(2)}) copy-start(f32[2,4,2,17]{3,2,1,0:T(2,128)} %param.8) | copy-start | bytes 3268
  5.4 18.5 %copy-start.17 = (s32[16]{0:T(128)S(1)}, s32[16]{0:T(128)}, u32[]{:S(2)}) copy-start(s32[16]{0:T(128)} %band_ref.9) | copy-start | bytes 196
  5.4 51.3 %all-to-all-start = ((bf16[768,16,128]{2,1,0:T(8,128)(2,1)}), bf16[768,16,128]{2,1,0:T(8,128)(2,1)S(1)}, u32[]{:S(2)}, u32[]{:S(2)}) async-start(bf16[768,16,128]{2,1,0:T(8,128)(2,1)} %bitcast.9), calls=%async_computation | async-start | bytes 6291456 | tf_op jit(solution)/shard_map/all_to_all | solution.py:410
  15.4 41.3 %copy-start.18 = (s32[2,64]{1,0:T(2,128)S(1)}, s32[2,64]{1,0:T(2,128)}, u32[]{:S(2)}) copy-start(s32[2,64]{1,0:T(2,128)} %shift_ref.3) | copy-start | bytes 1540
  15.4 41.2 %copy-start.19 = (s32[2,64]{1,0:T(2,128)S(1)}, s32[2,64]{1,0:T(2,128)}, u32[]{:S(2)}) copy-start(s32[2,64]{1,0:T(2,128)} %length_ref.3) | copy-start | bytes 1540
  15.9 1.2 %copy-start = (f32[16,128,128]{2,1,0:T(8,128)S(1)}, f32[16,128,128]{2,1,0:T(8,128)}, u32[]{:S(2)}) copy-start(f32[16,128,128]{2,1,0:T(8,128)} %estimate_ref.1) | copy-start | bytes 3145732
  17.6 33.4 %collective-permute-start.2 = (bf16[1,18,8,128]{3,2,1,0:T(8,128)(2,1)S(1)}, bf16[1,18,8,128]{3,2,1,0:T(8,128)(2,1)S(1)}, u32[]{:S(2)}, u32[]{:S(2)}) collective-permute-start(bf16[1,18,8,128]{3,2,1,0:T(8,128)(2,1)S(1)} %get-tuple-element.40), channel_id=1, source_target_pairs={{0,1},{1,0},{2,3},{3,2},{4,5},{5,4},{6,7},{7,6},{8,9},{9,8},{10,11... | collective-permute-start | bytes 110600 | tf_op jit(solution)/shard_map/ppermute | solution.py:371
  19.4 35.8 %collective-permute-start.3 = (bf16[1,18,8,128]{3,2,1,0:T(8,128)(2,1)S(1)}, bf16[1,18,8,128]{3,2,1,0:T(8,128)(2,1)S(1)}, u32[]{:S(2)}, u32[]{:S(2)}) collective-permute-start(bf16[1,18,8,128]{3,2,1,0:T(8,128)(2,1)S(1)} %get-tuple-element.41), channel_id=1, source_target_pairs={{1,2},{2,1},{3,4},{4,3},{5,6},{6,5},{7,8},{8,7},{9,10},{10,9},{11,... | collective-permute-start | bytes 110600 | tf_op jit(solution)/shard_map/ppermute | solution.py:370
  23.9 1.2 %copy-start.1 = (f32[16,128,128]{2,1,0:T(8,128)S(1)}, f32[16,128,128]{2,1,0:T(8,128)}, u32[]{:S(2)}) copy-start(f32[16,128,128]{2,1,0:T(8,128)} %estimate_ref.1) | copy-start | bytes 3145732
  35.9 1.4 %copy-start.3 = (f32[2,16,128,128]{3,2,1,0:T(8,128)}, f32[2,16,128,128]{3,2,1,0:T(8,128)S(1)}, u32[]{:S(2)}) copy-start(f32[2,16,128,128]{3,2,1,0:T(8,128)S(1)} %get-tuple-element.36.blurred_ref) | copy-start | bytes 6291460
  37.3 1.0 %copy-start.5 = (bf16[2,4,256,256]{3,2,1,0:T(8,128)(2,1)}, bf16[2,4,256,256]{3,2,1,0:T(8,128)(2,1)S(1)}, u32[]{:S(2)}) copy-start(bf16[2,4,256,256]{3,2,1,0:T(8,128)(2,1)S(1)} %get-tuple-element.30.turned_ref) | copy-start | bytes 3145732
  38.3 0.8 %copy-start.7 = (bf16[4,256,256]{2,1,0:T(8,128)(2,1)}, bf16[4,256,256]{2,1,0:T(8,128)(2,1)S(1)}, u32[]{:S(2)}) copy-start(bf16[4,256,256]{2,1,0:T(8,128)(2,1)S(1)} %get-tuple-element.32.rows_ref) | copy-start | bytes 1572868
  39.1 0.8 %copy-start.9 = (bf16[2,4,128,256]{3,2,1,0:T(8,128)(2,1)}, bf16[2,4,128,256]{3,2,1,0:T(8,128)(2,1)S(1)}, u32[]{:S(2)}) copy-start(bf16[2,4,128,256]{3,2,1,0:T(8,128)(2,1)S(1)} %get-tuple-element.34.cols_ref) | copy-start | bytes 1572868
  39.9 0.6 copy-start.11
  40.5 0.6 copy-start.13
  41.1 0.6 copy-start.15
  56.7 1.6 %copy-start.4 = (f32[2,16,128,128]{3,2,1,0:T(8,128)S(1)}, f32[2,16,128,128]{3,2,1,0:T(8,128)}, u32[]{:S(2)}) copy-start(f32[2,16,128,128]{3,2,1,0:T(8,128)} %copy-done.3) | copy-start | bytes 6291460
  56.7 1.6 %copy-start.14 = (bf16[4,2,48,128]{3,2,1,0:T(8,128)(2,1)S(1)}, bf16[4,2,48,128]{3,2,1,0:T(8,128)(2,1)}, u32[]{:S(2)}) copy-start(bf16[4,2,48,128]{3,2,1,0:T(8,128)(2,1)} %copy-done.13) | copy-start | bytes 294916
  57.5 4.6 %copy-start.8 = (bf16[4,256,256]{2,1,0:T(8,128)(2,1)S(1)}, bf16[4,256,256]{2,1,0:T(8,128)(2,1)}, u32[]{:S(2)}) copy-start(bf16[4,256,256]{2,1,0:T(8,128)(2,1)} %copy-done.7) | copy-start | bytes 1572868
  57.5 4.5 %copy-start.10 = (bf16[2,4,128,256]{3,2,1,0:T(8,128)(2,1)S(1)}, bf16[2,4,128,256]{3,2,1,0:T(8,128)(2,1)}, u32[]{:S(2)}) copy-start(bf16[2,4,128,256]{3,2,1,0:T(8,128)(2,1)} %copy-done.9) | copy-start | bytes 1572868
  57.5 4.5 %copy-start.16 = (bf16[4,32,32]{2,1,0:T(8,128)(2,1)S(1)}, bf16[4,32,32]{2,1,0:T(8,128)(2,1)}, u32[]{:S(2)}) copy-start(bf16[4,32,32]{2,1,0:T(8,128)(2,1)} %copy-done.15) | copy-start | bytes 24580
  57.5 3.0 %collective-permute-start.4 = (bf16[2,16,8,128]{3,2,1,0:T(8,128)(2,1)S(1)}, bf16[2,16,8,128]{3,2,1,0:T(8,128)(2,1)S(1)}, u32[]{:S(2)}, u32[]{:S(2)}) collective-permute-start(bf16[2,16,8,128]{3,2,1,0:T(8,128)(2,1)S(1)} %get-tuple-element.44), channel_id=1, source_target_pairs={{0,16},{1,17},{2,18},{3,19},{4,20},{5,21},{6,22},{7,23},{8,24},{9,... | collective-permute-start | bytes 196616 | tf_op jit(solution)/shard_map/ppermute | solution.py:371
  57.6 3.8 %collective-permute-start.5 = (bf16[2,16,8,128]{3,2,1,0:T(8,128)(2,1)S(1)}, bf16[2,16,8,128]{3,2,1,0:T(8,128)(2,1)S(1)}, u32[]{:S(2)}, u32[]{:S(2)}) collective-permute-start(bf16[2,16,8,128]{3,2,1,0:T(8,128)(2,1)S(1)} %get-tuple-element.45), channel_id=1, source_target_pairs={{0,1},{1,0},{2,3},{3,2},{4,5},{5,4},{6,7},{7,6},{8,9},{9,8},{10,11... | collective-permute-start | bytes 196616 | tf_op jit(solution)/shard_map/ppermute | solution.py:370
  60.4 7.8 %copy-start.2 = (f32[16,128,128]{2,1,0:T(8,128)S(1)}, f32[16,128,128]{2,1,0:T(8,128)}, u32[]{:S(2)}) copy-start(f32[16,128,128]{2,1,0:T(8,128)} %estimate_ref.1) | copy-start | bytes 3145732
  60.4 7.8 %copy-start.6 = (bf16[2,4,256,256]{3,2,1,0:T(8,128)(2,1)S(1)}, bf16[2,4,256,256]{3,2,1,0:T(8,128)(2,1)}, u32[]{:S(2)}) copy-start(bf16[2,4,256,256]{3,2,1,0:T(8,128)(2,1)} %copy-done.5) | copy-start | bytes 3145732
  60.5 7.8 %copy-start.12 = (bf16[4,2,48,128]{3,2,1,0:T(8,128)(2,1)S(1)}, bf16[4,2,48,128]{3,2,1,0:T(8,128)(2,1)}, u32[]{:S(2)}) copy-start(bf16[4,2,48,128]{3,2,1,0:T(8,128)(2,1)} %copy-done.11) | copy-start | bytes 294916
  61.5 4.4 %collective-permute-start.6 = (bf16[2,18,8,128]{3,2,1,0:T(8,128)(2,1)S(1)}, bf16[2,18,8,128]{3,2,1,0:T(8,128)(2,1)S(1)}, u32[]{:S(2)}, u32[]{:S(2)}) collective-permute-start(bf16[2,18,8,128]{3,2,1,0:T(8,128)(2,1)S(1)} %get-tuple-element.47), channel_id=1, source_target_pairs={{0,1},{1,0},{2,3},{3,2},{4,5},{5,4},{6,7},{7,6},{8,9},{9,8},{10,11... | collective-permute-start | bytes 221192 | tf_op jit(solution)/shard_map/ppermute | solution.py:371
  61.6 6.7 %collective-permute-start.7 = (bf16[2,18,8,128]{3,2,1,0:T(8,128)(2,1)S(1)}, bf16[2,18,8,128]{3,2,1,0:T(8,128)(2,1)S(1)}, u32[]{:S(2)}, u32[]{:S(2)}) collective-permute-start(bf16[2,18,8,128]{3,2,1,0:T(8,128)(2,1)S(1)} %get-tuple-element.48), channel_id=1, source_target_pairs={{0,16},{1,2},{2,1},{3,4},{4,3},{5,6},{6,5},{7,8},{8,7},{9,10},{10,... | collective-permute-start | bytes 221192 | tf_op jit(solution)/shard_map/ppermute | solution.py:370

commit v16 on v13

--- a/solution.py
+++ b/solution.py
@@ -137,6 +137,23 @@
                 edge = dot(pick, jnp.concatenate(ends, axis=0), NT)
             first_ref[view, i] = jnp.where(odd, edge[:HW], edge[HW:]).astype(BF16)
             second_ref[view, i] = jnp.where(odd, edge[HW:], edge[:HW]).astype(BF16)
+
+
+def half_slab_kernel(late, place_x_ref, place_y_ref, cols_ref, even_ref, other_ref, *refs):
+    out_ref = refs[-1]
+    views, depth, _, tile_rows = cols_ref.shape
+    count = tile_rows // (2 * HW)
+    pick = edge_picker(even_ref.shape[-1])
+    head = is_odd(place_y_ref) != late
+    for view in range(views):
+        for i in range(out_ref.shape[1]):
+            if i < depth:
+                edge = cols_ref[view, i].astype(F32)
+            else:
+                planes = range((i - depth) * count, (i - depth + 1) * count)
+                ends = [halo(place_x_ref, even_ref[view, z], other_ref[view, z]) for z in planes]
+                edge = dot(pick, jnp.concatenate(ends, axis=0), NT)
+            out_ref[view, i] = jnp.where(head, edge[:HW], edge[HW:]).astype(BF16)
 
 
 def edges_kernel(
@@ -458,7 +475,11 @@
         (whole, edge_cols),
         [pltpu.VMEM((views, spare, depth, tile_cols), F32), pltpu.VMEM(measured.shape, BF16)],
     )(me, depth_band, group_shift, group_length, arrived, blurred, later_far, parts)
-    ey, oy = swap(*dense(views, cols, ex, ox), "gy")
+    slab = lambda late, *args: call(
+        functools.partial(half_slab_kernel, late), [SMEM] * 2 + [VMEM] * (len(args)), like((views, tiles, HW, tile_rows), BF16)
+    )(place_x, place_y, *args)
+    second = slab(True, cols, ex, ox)
+    ey, oy = swap(slab(False, cols, ex, ox, second), second, "gy")
     near = call(
         near_kernel,
         [SMEM] * 2 + [VMEM] * 6,

time: 71.8 us -> 72 us (level)
  no operation moved by 1% of the time
where the time goes in v16:
time: 72 us; the launch traced here: 70.9 us
  Pallas kernels  23.7 us (33%)
  starting transfers between devices  19.1 us (27%)
  waiting for transfers between devices  18.1 us (25%)
  local copies, waits for them, and re-layouts  8.46 us (12%)
  other arithmetic  1.16 us (2%)
    pallas_call x1, Pallas kernels, body(): call(forward_kernel, [SMEM] * 2 + [VMEM] * 4, (like(measured.shape, F32),...  10.8 us
    ppermute x4, waiting for transfers between devices, swap(): return (lax.ppermute(first, both, pairs[0]), late)  10.8 us
    all_to_all x1, starting transfers between devices, body(): lax.all_to_all(outgoing, ('gx', 'gy'), split_axis=0, concat_axis=0, tiled...  10.1 us
    unnamed x42, local copies, waits for them, and re-layouts  8.36 us
    ppermute x4, waiting for transfers between devices, swap(): late = lax.ppermute(second, both, pairs[1])  7.31 us
    ppermute x4, starting transfers between devices, swap(): late = lax.ppermute(second, both, pairs[1])  5.94 us
    ppermute x4, starting transfers between devices, swap(): return (lax.ppermute(first, both, pairs[0]), late)  3.03 us
    pallas_call x1, Pallas kernels, body(): call(functools.partial(pack_kernel, devices), [SMEM, HBM, HBM, HBM], like...  2.94 us
  transfers between devices with their start and end apart: 9, of which 5 were waited for; matrix products, arithmetic and copies ran while one was open for 1% of the time, Pallas kernels for 29%

profile of v16, /device:TPU:30, one launch (start us, length us, event | category | flops | bytes accessed | tf_op | source)
XLA Modules:
  0.0 70.9 jit_solution(5315916148996377751)
XLA Ops:
  0.0 0.9 %slice_select_fusion = (f32[16,8,128]{2,1,0:T(8,128)S(1)}, f32[16,8,128]{2,1,0:T(8,128)S(1)}) fusion(f32[16,128,128]{2,1,0:T(8,128)} %estimate_ref.1, pred[]{:T(512)S(6)} %eq.13), kind=kLoop, calls=%fused_computation | loop fusion | flops 32768 | bytes 262145 | tf_op jit(solution)/shard_map/jit(_where)/select_n | solution.py:403
  0.9 0.3 collective-permute-start.1
  1.2 1.2 %collective-permute-start = (f32[16,8,128]{2,1,0:T(8,128)S(1)}, f32[16,8,128]{2,1,0:T(8,128)S(1)}, u32[]{:S(2)}, u32[]{:S(2)}) collective-permute-start(f32[16,8,128]{2,1,0:T(8,128)S(1)} %get-tuple-element.46), channel_id=1, source_target_pairs={{0,16},{1,17},{2,18},{3,19},{4,20},{5,21},{6,22},{7,23},{8,24},{9,... | collective-permute-start | bytes 196616 | tf_op jit(solution)/shard_map/ppermute | solution.py:381
  2.4 2.9 %shard_map.64 = bf16[128,2,3,16,128]{4,3,2,1,0:T(8,128)(2,1)} custom-call(s32[1]{0:T(128)} %bitcast.4.me_ref, s32[2,64]{1,0:T(2,128)} %shift_ref.3, s32[2,64]{1,0:T(2,128)} %length_ref.3, bf16[2,16,128,128]{3,2,1,0:T(8,128)(2,1)} %measured_hbm.1), custom_call_target="tpu_custom_call" | custom-call | tf_op jit(solution)/shard_map/pallas_call | solution.py:404
  5.4 10.1 %all-to-all-start = ((bf16[768,16,128]{2,1,0:T(8,128)(2,1)}), bf16[768,16,128]{2,1,0:T(8,128)(2,1)S(1)}, u32[]{:S(2)}, u32[]{:S(2)}) async-start(bf16[768,16,128]{2,1,0:T(8,128)(2,1)} %bitcast.9), calls=%async_computation | async-start | bytes 6291456 | tf_op jit(solution)/shard_map/all_to_all | solution.py:420
  16.0 1.2 %copy-done = f32[16,128,128]{2,1,0:T(8,128)S(1)} copy-done((f32[16,128,128]{2,1,0:T(8,128)S(1)}, f32[16,128,128]{2,1,0:T(8,128)}, u32[]{:S(2)}) %copy-start) | copy-done | bytes 1048600
  17.2 0.4 shard_map.66
  17.7 1.7 %collective-permute-start.2 = (bf16[1,18,8,128]{3,2,1,0:T(8,128)(2,1)S(1)}, bf16[1,18,8,128]{3,2,1,0:T(8,128)(2,1)S(1)}, u32[]{:S(2)}, u32[]{:S(2)}) collective-permute-start(bf16[1,18,8,128]{3,2,1,0:T(8,128)(2,1)S(1)} %get-tuple-element.38), channel_id=1, source_target_pairs={{0,1},{1,0},{2,3},{3,2},{4,5},{5,4},{6,7},{7,6},{8,9},{9,8},{10,11... | collective-permute-start | bytes 110600 | tf_op jit(solution)/shard_map/ppermute | solution.py:381
  19.5 4.5 %collective-permute-start.3 = (bf16[1,18,8,128]{3,2,1,0:T(8,128)(2,1)S(1)}, bf16[1,18,8,128]{3,2,1,0:T(8,128)(2,1)S(1)}, u32[]{:S(2)}, u32[]{:S(2)}) collective-permute-start(bf16[1,18,8,128]{3,2,1,0:T(8,128)(2,1)S(1)} %get-tuple-element.39), channel_id=1, source_target_pairs={{1,2},{2,1},{3,4},{4,3},{5,6},{6,5},{7,8},{8,7},{9,10},{10,9},{11,... | collective-permute-start | bytes 110600 | tf_op jit(solution)/shard_map/ppermute | solution.py:380
  24.0 1.2 %copy-done.1 = f32[16,128,128]{2,1,0:T(8,128)S(1)} copy-done((f32[16,128,128]{2,1,0:T(8,128)S(1)}, f32[16,128,128]{2,1,0:T(8,128)}, u32[]{:S(2)}) %copy-start.1) | copy-done | bytes 1048600
  25.2 10.8 %shard_map.65 = (f32[2,16,128,128]{3,2,1,0:T(8,128)S(1)}, f32[2,16,16,128]{3,2,1,0:T(8,128)S(1)}, bf16[2,4,256,256]{3,2,1,0:T(8,128)(2,1)S(1)}, bf16[4,2,48,128]...) custom-call(s32[16]{0:T(128)S(1)} %copy-done.17, ...), custom_call_target="tpu_custom_call" | custom-call | tf_op jit(solution)/shard_map/pallas_call | solution.py:434
  36.0 1.3 %copy-done.3 = f32[2,16,128,128]{3,2,1,0:T(8,128)} copy-done((f32[2,16,128,128]{3,2,1,0:T(8,128)}, f32[2,16,128,128]{3,2,1,0:T(8,128)S(1)}, u32[]{:S(2)}) %copy-start.3) | copy-done | bytes 2097176
  37.4 1.0 %copy-done.5 = bf16[2,4,256,256]{3,2,1,0:T(8,128)(2,1)} copy-done((bf16[2,4,256,256]{3,2,1,0:T(8,128)(2,1)}, bf16[2,4,256,256]{3,2,1,0:T(8,128)(2,1)S(1)}, u32[]{:S(2)}) %copy-start.5) | copy-done | bytes 1048600
  38.4 0.8 %copy-done.7 = bf16[4,256,256]{2,1,0:T(8,128)(2,1)} copy-done((bf16[4,256,256]{2,1,0:T(8,128)(2,1)}, bf16[4,256,256]{2,1,0:T(8,128)(2,1)S(1)}, u32[]{:S(2)}) %copy-start.7) | copy-done | bytes 524312
  39.2 0.8 %copy-done.9 = bf16[2,4,128,256]{3,2,1,0:T(8,128)(2,1)} copy-done((bf16[2,4,128,256]{3,2,1,0:T(8,128)(2,1)}, bf16[2,4,128,256]{3,2,1,0:T(8,128)(2,1)S(1)}, u32[]{:S(2)}) %copy-start.9) | copy-done | bytes 524312
  40.0 0.6 copy-done.11
  40.6 0.6 copy-done.13
  41.2 0.6 copy-done.15
  41.8 9.3 %collective-permute-done.2.even_ref = bf16[1,18,8,128]{3,2,1,0:T(8,128)(2,1)S(1)} collective-permute-done((bf16[1,18,8,128]{3,2,1,0:T(8,128)(2,1)S(1)}, bf16[1,18,8,128]{3,2,1,0:T(8,128)(2,1)S(1)}, u32[]{:S(2)}, u32[]{:S(2)}) %collective-permute-start.2) | collective-permute-done | bytes 36896 | tf_op jit(solution)/shard_map/ppermute | solution.py:381
  51.1 4.1 %collective-permute-done.3.other_ref = bf16[1,18,8,128]{3,2,1,0:T(8,128)(2,1)S(1)} collective-permute-done((bf16[1,18,8,128]{3,2,1,0:T(8,128)(2,1)S(1)}, bf16[1,18,8,128]{3,2,1,0:T(8,128)(2,1)S(1)}, u32[]{:S(2)}, u32[]{:S(2)}) %collective-permute-start.3) | collective-permute-done | bytes 36896 | tf_op jit(solution)/shard_map/ppermute | solution.py:380
  55.3 1.5 %shard_map.68.parts_ref.edge_ref = bf16[2,16,48,128]{3,2,1,0:T(8,128)(2,1)S(1)} custom-call(s32[16]{0:T(128)S(1)} %copy-done.17, s32[1]{0:T(128)} %bitcast.place_y_ref.place_ref, bf16[2,4,256,256]{3,2,1,0:T(8,128)(2,1)S(1)} %get-tuple-element.36.turned_ref, bf16[4,2,48,128]{3,2,1,0:T(8,128)(2,1)S(1)} %get-tuple-element.37.far_ref, ...), custom_call_target="tpu_custom_call" | custom-call | tf_op jit(solution)/shard_map/pallas_call | solution.py:455
  56.8 0.7 %shard_map.70 = (bf16[2,16,8,128]{3,2,1,0:T(8,128)(2,1)S(1)}, bf16[2,16,8,128]{3,2,1,0:T(8,128)(2,1)S(1)}) custom-call(s32[1]{0:T(128)} %bitcast.4.me_ref, s32[1]{0:T(128)} %bitcast.1.place_ref.place_x_ref, s32[2,64]{1,0:T(2,128)S(1)} %copy-done.18, s32[2,64]{1,0:T(2,128)S(1)} %copy-done.19, bf16[768,16,128]{2,1,0:T(8,128)(2,1)S(1)} %all-to-all-done.arrived_ref, ...), custom_call_target="tpu_custom_call" | custom-call | tf_op jit(solution)/shard_map/pallas_call | solution.py:465
  57.7 0.6 collective-permute-start.5
  58.4 2.2 %shard_map.69 = (bf16[2,16,128,128]{3,2,1,0:T(8,128)(2,1)S(1)}, bf16[2,16,16,128]{3,2,1,0:T(8,128)(2,1)S(1)}) custom-call(s32[1]{0:T(128)} %bitcast.4.me_ref, s32[16]{0:T(128)S(1)} %copy-done.17, s32[2,64]{1,0:T(2,128)S(1)} %copy-done.18, s32[2,64]{1,0:T(2,128)S(1)} %copy-done.19, bf16[768,16,128]{2,1,0:T(8,128)(2,1)S(1)} %all-to-all-done.arrived_ref, ...), custom_call_target="tpu_custom_call" | custom-call | tf_op jit(solution)/shard_map/pallas_call | solution.py:472
  60.6 0.8 %collective-permute-done.5.other_ref = bf16[2,16,8,128]{3,2,1,0:T(8,128)(2,1)S(1)} collective-permute-done((bf16[2,16,8,128]{3,2,1,0:T(8,128)(2,1)S(1)}, bf16[2,16,8,128]{3,2,1,0:T(8,128)(2,1)S(1)}, u32[]{:S(2)}, u32[]{:S(2)}) %collective-permute-start.5) | collective-permute-done | bytes 65568 | tf_op jit(solution)/shard_map/ppermute | solution.py:380
  61.4 0.2 shard_map.72.refs_0_
  61.6 0.2 shard_map.73
  61.8 0.5 collective-permute-start.7
  62.3 2.3 %shard_map.71.near_ref = f32[16,128,128]{2,1,0:T(8,128)S(1)} custom-call(s32[16]{0:T(128)S(1)} %copy-done.17, s32[1]{0:T(128)} %bitcast.1.place_ref.place_x_ref, bf16[4,256,256]{2,1,0:T(8,128)(2,1)S(1)} %copy-done.8, bf16[4,32,32]{2,1,0:T(8,128)(2,1)S(1)} %copy-done.16, bf16[2,4,128,256]{3,2,1,0:T(8,128)(2,1)S(1)} %copy-done.10, ...), custom_call_target="tpu_custom_call" | custom-call | tf_op jit(solution)/shard_map/pallas_call | solution.py:483
  64.6 1.5 %collective-permute-done.6.even_ref = bf16[2,18,8,128]{3,2,1,0:T(8,128)(2,1)S(1)} collective-permute-done((bf16[2,18,8,128]{3,2,1,0:T(8,128)(2,1)S(1)}, bf16[2,18,8,128]{3,2,1,0:T(8,128)(2,1)S(1)}, u32[]{:S(2)}, u32[]{:S(2)}) %collective-permute-start.6) | collective-permute-done | bytes 73760 | tf_op jit(solution)/shard_map/ppermute | solution.py:381
  66.2 2.4 %collective-permute-done.7.other_ref = bf16[2,18,8,128]{3,2,1,0:T(8,128)(2,1)S(1)} collective-permute-done((bf16[2,18,8,128]{3,2,1,0:T(8,128)(2,1)S(1)}, bf16[2,18,8,128]{3,2,1,0:T(8,128)(2,1)S(1)}, u32[]{:S(2)}, u32[]{:S(2)}) %collective-permute-start.7) | collective-permute-done | bytes 73760 | tf_op jit(solution)/shard_map/ppermute | solution.py:380
  68.5 2.2 %shard_map.74 = f32[16,128,128]{2,1,0:T(8,128)} custom-call(s32[16]{0:T(128)S(1)} %copy-done.17, s32[1]{0:T(128)} %bitcast.place_y_ref.place_ref, bf16[2,4,256,256]{3,2,1,0:T(8,128)(2,1)S(1)} %copy-done.6, bf16[4,2,48,128]{3,2,1,0:T(8,128)(2,1)S(1)} %copy-done.12, f32[16,128,128]{2,1,0:T(8,128)S(1)} %shard_map.71.near_ref, ...), custom_call_target="tpu_custom_call" | custom-call | tf_op jit(solution)/shard_map/pallas_call | solution.py:492
  (45 shorter events, 0.8 us)
Async XLA Ops:
  0.9 4.5 %collective-permute-start.1 = (f32[16,8,128]{2,1,0:T(8,128)S(1)}, f32[16,8,128]{2,1,0:T(8,128)S(1)}, u32[]{:S(2)}, u32[]{:S(2)}) collective-permute-start(f32[16,8,128]{2,1,0:T(8,128)S(1)} %get-tuple-element.45), channel_id=1, source_target_pairs={{0,1},{1,0},{2,3},{3,2},{4,5},{5,4},{6,7},{7,6},{8,9},{9,8},{10,11... | collective-permute-start | bytes 196616 | tf_op jit(solution)/shard_map/ppermute | solution.py:380
  1.2 4.2 %collective-permute-start = (f32[16,8,128]{2,1,0:T(8,128)S(1)}, f32[16,8,128]{2,1,0:T(8,128)S(1)}, u32[]{:S(2)}, u32[]{:S(2)}) collective-permute-start(f32[16,8,128]{2,1,0:T(8,128)S(1)} %get-tuple-element.46), channel_id=1, source_target_pairs={{0,16},{1,17},{2,18},{3,19},{4,20},{5,21},{6,22},{7,23},{8,24},{9,... | collective-permute-start | bytes 196616 | tf_op jit(solution)/shard_map/ppermute | solution.py:381
  5.4 10.1 %copy-start.20 = (f32[2,4,2,17]{3,2,1,0:T(2,128)S(1)}, f32[2,4,2,17]{3,2,1,0:T(2,128)}, u32[]{:S(2)}) copy-start(f32[2,4,2,17]{3,2,1,0:T(2,128)} %param.8) | copy-start | bytes 3268
  5.4 18.5 %copy-start.17 = (s32[16]{0:T(128)S(1)}, s32[16]{0:T(128)}, u32[]{:S(2)}) copy-start(s32[16]{0:T(128)} %band_ref.9) | copy-start | bytes 196
  5.4 51.3 %all-to-all-start = ((bf16[768,16,128]{2,1,0:T(8,128)(2,1)}), bf16[768,16,128]{2,1,0:T(8,128)(2,1)S(1)}, u32[]{:S(2)}, u32[]{:S(2)}) async-start(bf16[768,16,128]{2,1,0:T(8,128)(2,1)} %bitcast.9), calls=%async_computation | async-start | bytes 6291456 | tf_op jit(solution)/shard_map/all_to_all | solution.py:420
  15.5 41.3 %copy-start.18 = (s32[2,64]{1,0:T(2,128)S(1)}, s32[2,64]{1,0:T(2,128)}, u32[]{:S(2)}) copy-start(s32[2,64]{1,0:T(2,128)} %shift_ref.3) | copy-start | bytes 1540
  15.5 41.2 %copy-start.19 = (s32[2,64]{1,0:T(2,128)S(1)}, s32[2,64]{1,0:T(2,128)}, u32[]{:S(2)}) copy-start(s32[2,64]{1,0:T(2,128)} %length_ref.3) | copy-start | bytes 1540
  15.9 1.2 %copy-start = (f32[16,128,128]{2,1,0:T(8,128)S(1)}, f32[16,128,128]{2,1,0:T(8,128)}, u32[]{:S(2)}) copy-start(f32[16,128,128]{2,1,0:T(8,128)} %estimate_ref.1) | copy-start | bytes 3145732
  17.7 33.4 %collective-permute-start.2 = (bf16[1,18,8,128]{3,2,1,0:T(8,128)(2,1)S(1)}, bf16[1,18,8,128]{3,2,1,0:T(8,128)(2,1)S(1)}, u32[]{:S(2)}, u32[]{:S(2)}) collective-permute-start(bf16[1,18,8,128]{3,2,1,0:T(8,128)(2,1)S(1)} %get-tuple-element.38), channel_id=1, source_target_pairs={{0,1},{1,0},{2,3},{3,2},{4,5},{5,4},{6,7},{7,6},{8,9},{9,8},{10,11... | collective-permute-start | bytes 110600 | tf_op jit(solution)/shard_map/ppermute | solution.py:381
  19.5 35.8 %collective-permute-start.3 = (bf16[1,18,8,128]{3,2,1,0:T(8,128)(2,1)S(1)}, bf16[1,18,8,128]{3,2,1,0:T(8,128)(2,1)S(1)}, u32[]{:S(2)}, u32[]{:S(2)}) collective-permute-start(bf16[1,18,8,128]{3,2,1,0:T(8,128)(2,1)S(1)} %get-tuple-element.39), channel_id=1, source_target_pairs={{1,2},{2,1},{3,4},{4,3},{5,6},{6,5},{7,8},{8,7},{9,10},{10,9},{11,... | collective-permute-start | bytes 110600 | tf_op jit(solution)/shard_map/ppermute | solution.py:380
  24.0 1.2 %copy-start.1 = (f32[16,128,128]{2,1,0:T(8,128)S(1)}, f32[16,128,128]{2,1,0:T(8,128)}, u32[]{:S(2)}) copy-start(f32[16,128,128]{2,1,0:T(8,128)} %estimate_ref.1) | copy-start | bytes 3145732
  36.0 1.3 %copy-start.3 = (f32[2,16,128,128]{3,2,1,0:T(8,128)}, f32[2,16,128,128]{3,2,1,0:T(8,128)S(1)}, u32[]{:S(2)}) copy-start(f32[2,16,128,128]{3,2,1,0:T(8,128)S(1)} %get-tuple-element.34.blurred_ref) | copy-start | bytes 6291460
  37.4 1.0 %copy-start.5 = (bf16[2,4,256,256]{3,2,1,0:T(8,128)(2,1)}, bf16[2,4,256,256]{3,2,1,0:T(8,128)(2,1)S(1)}, u32[]{:S(2)}) copy-start(bf16[2,4,256,256]{3,2,1,0:T(8,128)(2,1)S(1)} %get-tuple-element.28.turned_ref) | copy-start | bytes 3145732
  38.4 0.8 %copy-start.7 = (bf16[4,256,256]{2,1,0:T(8,128)(2,1)}, bf16[4,256,256]{2,1,0:T(8,128)(2,1)S(1)}, u32[]{:S(2)}) copy-start(bf16[4,256,256]{2,1,0:T(8,128)(2,1)S(1)} %get-tuple-element.30.rows_ref) | copy-start | bytes 1572868
  39.2 0.8 %copy-start.9 = (bf16[2,4,128,256]{3,2,1,0:T(8,128)(2,1)}, bf16[2,4,128,256]{3,2,1,0:T(8,128)(2,1)S(1)}, u32[]{:S(2)}) copy-start(bf16[2,4,128,256]{3,2,1,0:T(8,128)(2,1)S(1)} %get-tuple-element.32.cols_ref) | copy-start | bytes 1572868
  40.0 0.6 copy-start.11
  40.6 0.6 copy-start.13
  41.2 0.6 copy-start.15
  56.8 1.6 %copy-start.4 = (f32[2,16,128,128]{3,2,1,0:T(8,128)S(1)}, f32[2,16,128,128]{3,2,1,0:T(8,128)}, u32[]{:S(2)}) copy-start(f32[2,16,128,128]{3,2,1,0:T(8,128)} %copy-done.3) | copy-start | bytes 6291460
  56.8 1.6 %copy-start.14 = (bf16[4,2,48,128]{3,2,1,0:T(8,128)(2,1)S(1)}, bf16[4,2,48,128]{3,2,1,0:T(8,128)(2,1)}, u32[]{:S(2)}) copy-start(bf16[4,2,48,128]{3,2,1,0:T(8,128)(2,1)} %copy-done.13) | copy-start | bytes 294916
  57.6 3.0 %collective-permute-start.4 = (bf16[2,16,8,128]{3,2,1,0:T(8,128)(2,1)S(1)}, bf16[2,16,8,128]{3,2,1,0:T(8,128)(2,1)S(1)}, u32[]{:S(2)}, u32[]{:S(2)}) collective-permute-start(bf16[2,16,8,128]{3,2,1,0:T(8,128)(2,1)S(1)} %get-tuple-element.42), channel_id=1, source_target_pairs={{0,16},{1,17},{2,18},{3,19},{4,20},{5,21},{6,22},{7,23},{8,24},{9,... | collective-permute-start | bytes 196616 | tf_op jit(solution)/shard_map/ppermute | solution.py:381
  57.7 3.8 %collective-permute-start.5 = (bf16[2,16,8,128]{3,2,1,0:T(8,128)(2,1)S(1)}, bf16[2,16,8,128]{3,2,1,0:T(8,128)(2,1)S(1)}, u32[]{:S(2)}, u32[]{:S(2)}) collective-permute-start(bf16[2,16,8,128]{3,2,1,0:T(8,128)(2,1)S(1)} %get-tuple-element.43), channel_id=1, source_target_pairs={{0,1},{1,0},{2,3},{3,2},{4,5},{5,4},{6,7},{7,6},{8,9},{9,8},{10,11... | collective-permute-start | bytes 196616 | tf_op jit(solution)/shard_map/ppermute | solution.py:380
  58.4 3.9 %copy-start.8 = (bf16[4,256,256]{2,1,0:T(8,128)(2,1)S(1)}, bf16[4,256,256]{2,1,0:T(8,128)(2,1)}, u32[]{:S(2)}) copy-start(bf16[4,256,256]{2,1,0:T(8,128)(2,1)} %copy-done.7) | copy-start | bytes 1572868
  58.4 3.9 %copy-start.10 = (bf16[2,4,128,256]{3,2,1,0:T(8,128)(2,1)S(1)}, bf16[2,4,128,256]{3,2,1,0:T(8,128)(2,1)}, u32[]{:S(2)}) copy-start(bf16[2,4,128,256]{3,2,1,0:T(8,128)(2,1)} %copy-done.9) | copy-start | bytes 1572868
  58.4 3.9 %copy-start.16 = (bf16[4,32,32]{2,1,0:T(8,128)(2,1)S(1)}, bf16[4,32,32]{2,1,0:T(8,128)(2,1)}, u32[]{:S(2)}) copy-start(bf16[4,32,32]{2,1,0:T(8,128)(2,1)} %copy-done.15) | copy-start | bytes 24580
  60.6 8.0 %copy-start.2 = (f32[16,128,128]{2,1,0:T(8,128)S(1)}, f32[16,128,128]{2,1,0:T(8,128)}, u32[]{:S(2)}) copy-start(f32[16,128,128]{2,1,0:T(8,128)} %estimate_ref.1) | copy-start | bytes 3145732
  60.6 8.0 %copy-start.6 = (bf16[2,4,256,256]{3,2,1,0:T(8,128)(2,1)S(1)}, bf16[2,4,256,256]{3,2,1,0:T(8,128)(2,1)}, u32[]{:S(2)}) copy-start(bf16[2,4,256,256]{3,2,1,0:T(8,128)(2,1)} %copy-done.5) | copy-start | bytes 3145732
  60.6 8.0 %copy-start.12 = (bf16[4,2,48,128]{3,2,1,0:T(8,128)(2,1)S(1)}, bf16[4,2,48,128]{3,2,1,0:T(8,128)(2,1)}, u32[]{:S(2)}) copy-start(bf16[4,2,48,128]{3,2,1,0:T(8,128)(2,1)} %copy-done.11) | copy-start | bytes 294916
  61.8 4.4 %collective-permute-start.6 = (bf16[2,18,8,128]{3,2,1,0:T(8,128)(2,1)S(1)}, bf16[2,18,8,128]{3,2,1,0:T(8,128)(2,1)S(1)}, u32[]{:S(2)}, u32[]{:S(2)}) collective-permute-start(bf16[2,18,8,128]{3,2,1,0:T(8,128)(2,1)S(1)} %shard_map.73), channel_id=1, source_target_pairs={{0,1},{1,0},{2,3},{3,2},{4,5},{5,4},{6,7},{7,6},{8,9},{9,8},{10,11... | collective-permute-start | bytes 221192 | tf_op jit(solution)/shard_map/ppermute | solution.py:381
  61.8 6.7 %collective-permute-start.7 = (bf16[2,18,8,128]{3,2,1,0:T(8,128)(2,1)S(1)}, bf16[2,18,8,128]{3,2,1,0:T(8,128)(2,1)S(1)}, u32[]{:S(2)}, u32[]{:S(2)}) collective-permute-start(bf16[2,18,8,128]{3,2,1,0:T(8,128)(2,1)S(1)} %shard_map.72.refs_0_), channel_id=1, source_target_pairs={{0,16},{1,2},{2,1},{3,4},{4,3},{5,6},{6,5},{7,8},{8,7},{9,10},{10,... | collective-permute-start | bytes 221192 | tf_op jit(solution)/shard_map/ppermute | solution.py:380
